TPU v7x, 128 devices: a whole 4x4x4 slice. The times are simulated.
128 devices in a mesh: defocus: 8 (over x_lo, y), blk: 16 (over z, x_hi, core).
Axes of the slice: x: 4 (x_hi: 2, x_lo: 2; x = x_hi * 2 + x_lo), y: 4, z: 4, core: 2. Of those that a mesh axis runs over, the one named last changes fastest.
Arguments:
- images: bfloat16 [8, 16, 384, 384], P('defocus', 'blk'), may hold values from -6 to 6
- projections: bfloat16 [16, 384, 384], P('blk', 'defocus'), may hold values from -6 to 6
- ctf_row: int32 [8, 16], P('defocus', 'blk'), may hold values from 0 to 63
- defocus_term: float32 [64], replicated, may hold values from 100 to 400
- astig_term: float32 [64], replicated, may hold values from -40 to 40
- astig_cross: float32 [64], replicated, may hold values from -40 to 40
- phase_shift: float32 [64], replicated, may hold values from 0.1 to 1.5
Outputs:
- peak: float32 [8, 16, 384, 384], P('defocus', 'blk')
All inputs are finite; a program needn't handle non-finite values.
Results may differ from a plain program's by a relative error of at most 0.0095.
Values may be sent and summed in bfloat16 or wider, within the bound.
No kernel may reach another device: no remote copies, remote signals or barrier semaphores. Data moves between devices by JAX's collectives and lax.ppermute only.
A program may use at most 64 MiB of HBM per device.

v0:
```python
import math

import jax
import jax.numpy as jnp
from jax import lax
from jax.sharding import PartitionSpec as P


def section_tables(pixels):
    indices = jnp.arange(pixels, dtype=jnp.int32)
    phases = indices[:, None] * indices[None, :] % pixels
    angles = phases.astype(jnp.float32) * (2.0 * math.pi / pixels)
    cosine_table = jnp.cos(angles).astype(jnp.bfloat16)
    sine_table = jnp.sin(angles).astype(jnp.bfloat16)
    boundary_table = jnp.concatenate([cosine_table, -sine_table], axis=1)
    squared_lookup = jnp.concatenate(
        [
            jnp.concatenate([cosine_table, sine_table], axis=1),
            jnp.concatenate([-sine_table, cosine_table], axis=1),
        ],
        axis=0,
    )
    return (boundary_table, squared_lookup)


def transform(template_stack, boundary_table, squared_lookup):
    pixels = template_stack.shape[-1]
    halves = jnp.einsum(
        "xgs,so->xgo", template_stack, boundary_table, preferred_element_type=jnp.float32
    ).astype(jnp.bfloat16)
    stacked = jnp.concatenate([halves[:, :, :pixels], halves[:, :, pixels:]], axis=1)
    result = jnp.einsum("ua,tab->tub", squared_lookup, stacked, preferred_element_type=jnp.float32)
    return (result[:, :pixels], result[:, pixels:])


def ctf_gains(row_ids, defocus_term, astig_term, astig_cross, phase_shift, pixels):
    indices = jnp.arange(pixels, dtype=jnp.int32)
    signed = jnp.where(indices < pixels // 2, indices, indices - pixels)
    frequency = signed.astype(jnp.float32) / pixels
    row_freq = frequency[:, None]
    col_freq = frequency[None, :]
    radial = row_freq * row_freq + col_freq * col_freq
    stretch = row_freq * row_freq - col_freq * col_freq
    skewed = 2.0 * row_freq * col_freq
    matches = row_ids[:, None] == jnp.arange(defocus_term.shape[0], dtype=jnp.int32)[None, :]

    def select_row(lookup_table):
        return jnp.sum(jnp.where(matches, lookup_table[None, :], 0.0), axis=1)[:, None, None]

    chi_angle = (
        select_row(defocus_term) * radial
        + select_row(astig_term) * stretch
        + select_row(astig_cross) * skewed
        + select_row(phase_shift)
    )
    return -jnp.sin(chi_angle)


def correlate(
    spectrum_re, spectrum_im, factor, ctf_weight, plane_re, plane_im, boundary_table, squared_lookup
):
    pixels = spectrum_re.shape[-1]
    wide_re = plane_re.astype(jnp.float32)
    wide_im = plane_im.astype(jnp.float32)
    template_norm = jnp.sum((wide_re * wide_re + wide_im * wide_im)[None] * ctf_weight, axis=(1, 2))
    scaling = factor / jnp.sqrt(template_norm + 1e-06)[:, None, None]
    product_re = ((spectrum_re * wide_re + spectrum_im * wide_im) * scaling).astype(jnp.bfloat16)
    product_im = ((spectrum_im * wide_re - spectrum_re * wide_im) * scaling).astype(jnp.bfloat16)
    combined_parts = jnp.concatenate([product_re, product_im], axis=2)
    halves = jnp.einsum(
        "xgs,so->xgo", combined_parts, squared_lookup, preferred_element_type=jnp.float32
    ).astype(jnp.bfloat16)
    stacked = jnp.concatenate([halves[:, :, :pixels], halves[:, :, pixels:]], axis=1)
    return jnp.einsum("ua,tab->tub", boundary_table, stacked, preferred_element_type=jnp.float32)


def per_device(images, projections, ctf_row, defocus_term, astig_term, astig_cross, phase_shift):
    micrographs = images[0]
    pixels = micrographs.shape[-1]
    boundary_table, squared_lookup = section_tables(pixels)
    spectrum_re, spectrum_im = transform(micrographs, boundary_table, squared_lookup)
    power_local = jnp.sum(spectrum_re * spectrum_re + spectrum_im * spectrum_im, axis=0)
    power_total = lax.psum(power_local.astype(jnp.bfloat16), "blk").astype(jnp.float32)
    mean_power = power_total / (lax.axis_size("blk") * micrographs.shape[0])
    noise_power = mean_power + 0.05 * jnp.mean(mean_power)
    transfer_gain = ctf_gains(
        ctf_row[0], defocus_term, astig_term, astig_cross, phase_shift, pixels
    )
    factor = transfer_gain / noise_power[None]
    ctf_weight = transfer_gain * factor
    library = lax.all_gather(projections, "defocus", axis=1, tiled=True)
    initial = jnp.full(micrographs.shape, -jnp.inf, jnp.float32)
    arrived_re, arrived_im = transform(
        lax.all_gather(library, "blk", axis=0, tiled=True), boundary_table, squared_lookup
    )
    rounded = lax.optimization_barrier(
        (arrived_re.astype(jnp.bfloat16), arrived_im.astype(jnp.bfloat16))
    )

    def one_plane(current, planes):
        scores = correlate(
            spectrum_re,
            spectrum_im,
            factor,
            ctf_weight,
            planes[0],
            planes[1],
            boundary_table,
            squared_lookup,
        )
        return (jnp.maximum(current, scores), None)

    result, _ = lax.scan(one_plane, initial, (rounded[0], rounded[1]))
    return result[None]


def solution(mesh):
    in_specs = (
        P("defocus", "blk", None, None),
        P("blk", "defocus", None),
        P("defocus", "blk"),
        P(),
        P(),
        P(),
        P(),
    )
    out_specs = P("defocus", "blk", None, None)
    return jax.shard_map(
        per_device, mesh=mesh, in_specs=in_specs, out_specs=out_specs, check_vma=False
    )
```

profile of v0, /device:TPU:1, one launch (start us, length us, event | category | flops | bytes accessed | tf_op | source)
XLA Modules:
  0.0 378.4 jit_solution(12518729024491444624)
XLA Ops:
  6.5 2.3 fusion.36
  8.9 2.3 cosine_convert_fusion
  11.2 2.3 sine_convert_fusion
  15.7 25.8 %all_gather.6 = bf16[1,384,384]{2,1,0:T(8,128)(2,1)} all-gather(bf16[1,48,384]{2,1,0:T(8,128)(2,1)S(1)} %copy-done.2), channel_id=1, replica_groups=mesh['defocus'=8,'blk'=16] {'defocus'}, dimensions={1}, use_global_device_ids=true | all-gather | bytes 331776 | tf_op jit(solution)/shard_map/all_gather | solution.py:91
  44.9 1.1 maximum_maximum_fusion
  46.1 104.6 %all-reduce.2.cloned.1.call-done = bf16[384,384]{0,1:T(8,128)(2,1)} async-done(((bf16[384,384]{0,1:T(8,128)(2,1)}), bf16[384,384]{0,1:T(8,128)(2,1)}) %all-reduce.2.cloned.1.call-update) | async-done | bytes 294928 | tf_op jit(solution)/shard_map/psum | solution.py:83
  150.6 1.7 fusion.30
  153.0 6.9 %fusion.43 = (f32[1,384,384]{1,2,0:T(8,128)}, f32[1,384,384]{1,2,0:T(8,128)S(1)}) fusion(f32[]{:T(128)S(6)} %mul_shard_map.3, bf16[384,384]{0,1:T(8,128)(2,1)} %all-reduce.2.cloned.1.call-done, f32[]{:T(128)} %get-tuple-element.152, f32[384]{0:T(512)S(1)} %get-tuple-element.157, f32[384]{0:T(512)S(1)} %get-tuple-element.156, f32[]{:T(128)} %get-tuple-element.153, ...), kind=kLoop, calls=%fused_computation.76 | loop fusion | flops 2211840 | bytes 1479188 | tf_op jit(solution)/shard_map/div | solution.py:89
  160.2 1.3 copy.22
  161.5 49.6 %all-gather.2.cloned.1.call-done = bf16[16,384,384]{2,1,0:T(8,128)(2,1)} async-done(((bf16[1,384,384]{2,1,0:T(8,128)(2,1)}), bf16[16,384,384]{2,1,0:T(8,128)(2,1)}) %all-gather.2.cloned.1.call-update) | async-done | bytes 4718608 | tf_op jit(solution)/shard_map/all_gather | solution.py:94
  211.0 9.7 %convert_bitcast_fusion.1 = bf16[16,384,768]{2,1,0:T(8,128)(2,1)} fusion(bf16[16,384,384]{2,1,0:T(8,128)(2,1)} %all-gather.2.cloned.1.call-done, bf16[384,384]{1,0:T(8,128)(2,1)S(1)} %fusion.36, bf16[384,384]{1,0:T(8,128)(2,1)S(1)} %cosine_convert_fusion), kind=kOutput, calls=%fused_computation.35 | convolution fusion | flops 3629776896 | bytes 14745600 | tf_op jit(solution)/shard_map/xgs,so->xgo/dot_general | solution.py:28
  220.8 7.3 %fusion.46 = (bf16[16,384,384]{2,1,0:T(8,128)(2,1)S(1)}, bf16[16,384,384]{2,1,0:T(8,128)(2,1)}) fusion(bf16[16,384,768]{2,1,0:T(8,128)(2,1)} %convert_bitcast_fusion.1), kind=kLoop, calls=%fused_computation.79 | loop fusion | bytes 18874368 | tf_op jit(solution)/shard_map/slice | solution.py:31
  228.1 11.7 %convert_bitcast_fusion = bf16[16,768,384]{1,2,0:T(8,128)(2,1)} fusion(bf16[16,384,384]{2,1,0:T(8,128)(2,1)} %get-tuple-element.144, bf16[16,384,384]{2,1,0:T(8,128)(2,1)S(1)} %get-tuple-element.143, bf16[384,384]{1,0:T(8,128)(2,1)S(1)} %cosine_convert_fusion, bf16[384,384]{1,0:T(8,128)(2,1)S(1)} %fusion.36, bf16[384,384]{1,0:T(8,128)(2,1)S(1)} %sine_convert_fusion), kind=kOutput, calls=%fused_computation.34 | convolution fusion | flops 7276068864 | bytes 19759104 | tf_op jit(solution)/shard_map/ua,tab->tub/dot_general | solution.py:32
  239.8 8.9 %fusion.45 = (bf16[16,384,384]{1,2,0:T(8,128)(2,1)}, bf16[16,384,384]{1,2,0:T(8,128)(2,1)}) fusion(bf16[16,768,384]{1,2,0:T(8,128)(2,1)} %convert_bitcast_fusion), kind=kLoop, calls=%fused_computation.78 | loop fusion | bytes 18874368 | tf_op jit(solution)/shard_map/slice | solution.py:33
  248.7 120.8 %while.11 = (s32[]{:T(128)}, f32[1,384,384]{1,2,0:T(8,128)}, bf16[16,384,384]{1,2,0:T(8,128)(2,1)}, f32[1,384,384]{2,1,0:T(8,128)S(1)}, bf16[16,384,384]{1,2,0:T...) while((s32[]{:T(128)}, f32[1,384,384]{1,2,0:T(8,128)}, ...), condition=%wide.region_8.9_spmd.clone, body=%wide.region_6.8_spmd.clone.sunk | while | flops 685375488 | bytes 17105100 | solution.py:113
  248.7 1.1 constant_dynamic-slice_fusion.3
  251.9 1.0 copy-done.1
  253.7 2.4 fusion.64
  256.1 1.1 constant_dynamic-slice_fusion.3
  259.3 1.0 copy-done.1
  261.0 2.6 fusion.64
  263.6 1.1 constant_dynamic-slice_fusion.3
  266.9 1.0 copy-done.1
  268.6 2.6 fusion.64
  271.2 1.1 constant_dynamic-slice_fusion.3
  274.4 1.0 copy-done.1
  276.2 2.6 fusion.64
  278.7 1.1 constant_dynamic-slice_fusion.3
  282.0 1.0 copy-done.1
  283.7 2.6 fusion.64
  286.3 1.1 constant_dynamic-slice_fusion.3
  289.6 1.0 copy-done.1
  291.3 2.6 fusion.64
  293.9 1.1 constant_dynamic-slice_fusion.3
  297.1 1.0 copy-done.1
  298.8 2.6 fusion.64
  301.4 1.1 constant_dynamic-slice_fusion.3
  304.7 1.0 copy-done.1
  306.4 2.6 fusion.64
  309.0 1.1 constant_dynamic-slice_fusion.3
  312.2 1.0 copy-done.1
  314.0 2.6 fusion.64
  316.5 1.1 constant_dynamic-slice_fusion.3
  319.8 1.0 copy-done.1
  321.5 2.6 fusion.64
  324.1 1.1 constant_dynamic-slice_fusion.3
  327.4 1.0 copy-done.1
  329.1 2.6 fusion.64
  331.7 1.1 constant_dynamic-slice_fusion.3
  334.9 1.0 copy-done.1
  336.6 2.6 fusion.64
  339.2 1.1 constant_dynamic-slice_fusion.3
  342.5 1.0 copy-done.1
  344.2 2.6 fusion.64
  346.8 1.1 constant_dynamic-slice_fusion.3
  350.0 1.0 copy-done.1
  351.8 2.6 fusion.64
  354.3 1.1 constant_dynamic-slice_fusion.3
  357.6 1.0 copy-done.1
  359.3 2.6 fusion.64
  361.9 1.1 constant_dynamic-slice_fusion.3
  365.2 1.0 copy-done.1
  366.9 2.6 fusion.64
  369.5 2.1 copy.23
  (141 shorter events, 39.1 us)
Async XLA Ops:
  6.5 7.0 %copy-start = (bf16[1,1,384,384]{3,2,1,0:T(8,128)(2,1)S(1)}, bf16[1,1,384,384]{3,2,1,0:T(8,128)(2,1)}, u32[]{:S(2)}) copy-start(bf16[1,1,384,384]{3,2,1,0:T(8,128)(2,1)} %param.9) | copy-start | bytes 884740
  6.5 144.1 %all-reduce.2.cloned.1.call-start = ((), (), s32[]{:S(2)}) async-start(), calls=%async_computation.1 | async-start | bytes 589824 | tf_op jit(solution)/shard_map/psum | solution.py:83
  14.7 1.0 copy-start.2
  14.8 27.9 %copy-start.3 = (f32[64]{0:T(128)S(1)}, f32[64]{0:T(128)}, u32[]{:S(2)}) copy-start(f32[64]{0:T(128)} %param.15) | copy-start | bytes 772
  14.8 27.9 %copy-start.4 = (f32[64]{0:T(128)S(1)}, f32[64]{0:T(128)}, u32[]{:S(2)}) copy-start(f32[64]{0:T(128)} %param.14) | copy-start | bytes 772
  14.8 28.6 %copy-start.5 = (f32[64]{0:T(128)S(1)}, f32[64]{0:T(128)}, u32[]{:S(2)}) copy-start(f32[64]{0:T(128)} %param.13) | copy-start | bytes 772
  14.8 28.6 %copy-start.6 = (f32[64]{0:T(128)S(1)}, f32[64]{0:T(128)}, u32[]{:S(2)}) copy-start(f32[64]{0:T(128)} %param.12) | copy-start | bytes 772
  15.7 195.4 %all-gather.2.cloned.1.call-start = ((), (), s32[]{:S(2)}) async-start(), calls=%async_computation | async-start | bytes 5013504 | tf_op jit(solution)/shard_map/all_gather | solution.py:94
  251.7 1.3 copy-start.1
  259.1 1.3 copy-start.1
  266.6 1.3 copy-start.1
  274.2 1.3 copy-start.1
  281.7 1.3 copy-start.1
  289.3 1.3 copy-start.1
  296.9 1.3 copy-start.1
  304.4 1.3 copy-start.1
  312.0 1.3 copy-start.1
  319.5 1.3 copy-start.1
  327.1 1.3 copy-start.1
  334.7 1.3 copy-start.1
  342.2 1.3 copy-start.1
  349.8 1.3 copy-start.1
  357.3 1.3 copy-start.1
  364.9 1.3 copy-start.1
Sparse Core Ops, SparseCore 0:
  15.8 134.7 all-reduce.1
  153.4 57.6 all-gather.1
where the time goes:
time: 380 us; the launch traced here: 378 us
  waiting for transfers between devices  154 us (41%)
  matrix products  73.6 us (19%)
  local copies, waits for them, and re-layouts  62.3 us (16%)
  other arithmetic  35.8 us (9%)
  blocking collectives  25.8 us (7%)
  between operations  14.9 us (4%)
  loops' own time  11.8 us (3%)
    psum x1, waiting for transfers between devices, per_device(): lax.psum(power_local.astype(jnp.bfloat16), 'blk').astype(jnp.float32)  105 us
    all_gather x1, waiting for transfers between devices, per_device(): lax.all_gather(library, 'blk', axis=0, tiled=True)  49.6 us
    dot_general x16, matrix products, correlate(): jnp.einsum('ua,tab->tub', boundary_table, stacked, preferred_element_type...  41 us
    all_gather x1, blocking collectives, per_device(): library = lax.all_gather(projections, 'defocus', axis=1, tiled=True)  25.8 us
    dynamic_slice x48, local copies, waits for them, and re-layouts, per_device(): result, _ = lax.scan(one_plane, initial, (rounded[0], rounded[1]))  24.7 us
    while x32, local copies, waits for them, and re-layouts  16.2 us
    dot_general x2, matrix products, transform(): jnp.einsum('ua,tab->tub', squared_lookup, stacked, preferred_element_type...  12.4 us
    reduce_sum x16, other arithmetic, correlate(): jnp.sum((wide_re * wide_re + wide_im * wide_im)[None] * ctf_weight, axis=...  12.1 us
  transfers between devices with their start and end apart: 2, of which 2 were waited for; matrix products, arithmetic and copies ran while one was open for 4% of the time, Pallas kernels for 0%

commit v1 on v0

v1 whole, which is shorter than its diff:
```python
import math

import jax
import jax.numpy as jnp
import ml_dtypes
import numpy as np
from jax import lax
from jax.experimental import pallas as pl
from jax.experimental.pallas import tpu as pltpu
from jax.sharding import Mesh
from jax.sharding import PartitionSpec as P

DEF = ("xlo", "y")
BLK = ("z", "xhi", "core")
CHIPS = ("xlo", "y", "z", "xhi")
N = 384
HALF = N // 2
ROWS = 208
PART = ROWS // 2
F32 = jnp.float32
BF16 = jnp.bfloat16


def tables():
    j = np.arange(N)
    phase = (j[:, None] * j[None, :]) % N
    cos = np.cos(2.0 * np.pi * phase / N)
    sin = np.sin(2.0 * np.pi * phase / N)
    bf = ml_dtypes.bfloat16
    first = np.zeros((2 * ROWS, N))
    first[: HALF + 1] = cos[: HALF + 1]
    first[ROWS : ROWS + HALF + 1] = -sin[: HALF + 1]
    forward = np.block([[cos, -sin], [sin, cos]])
    inverse = np.block([[cos, sin], [-sin, cos]])
    weight = np.full(HALF + 1, 2.0)
    weight[0] = weight[HALF] = 1.0
    fold = np.zeros((2, ROWS, ROWS))
    fold[0, : HALF + 1, : HALF + 1] = cos[: HALF + 1, : HALF + 1].astype(bf).astype(float) * weight
    fold[1, : HALF + 1, : HALF + 1] = sin[: HALF + 1, : HALF + 1].astype(bf).astype(float) * weight
    unfold = np.zeros((HALF, 2 * ROWS))
    unfold[0, HALF] = 1.0
    for i in range(1, HALF):
        unfold[i, ROWS + HALF - i] = 1.0
    return [a.astype(bf) for a in (first, forward, inverse, fold, unfold)]


def dot(a, b):
    return jnp.dot(a, b, preferred_element_type=F32)


def half_spectrum(image, first, forward):
    part = dot(first, image).astype(BF16)
    both = jnp.concatenate([part[:ROWS], part[ROWS:]], axis=1)
    out = dot(both, forward)
    return out[:, :N], out[:, N:]


def tile_kernel(core_ref, own_ref, other_ref, first_ref, forward_ref, spec_ref, power_ref, total_ref):
    for t, ref in enumerate((own_ref, other_ref)):
        re, im = half_spectrum(ref[...], first_ref[...], forward_ref[...])
        spec_ref[t, 0] = re
        spec_ref[t, 1] = im
        square = re * re + im * im
        total_ref[...] = square if t == 0 else total_ref[...] + square
    start = pl.multiple_of(core_ref[0] * PART, 8)
    power_ref[...] = total_ref[pl.ds(start, PART), :].astype(BF16)


def sine(x):
    x = x - jnp.round(x)
    a = jnp.abs(x)
    a = jnp.minimum(a, 0.5 - a)
    s = a * a
    p = jnp.full_like(x, -15.0946425768229800)
    for c in (
        42.0586939448600400,
        -76.7058597530613900,
        81.6052492760750400,
        -41.3417022403997600,
        6.28318530717958648,
    ):
        p = p * s + c
    p = p * a
    return jnp.where(x < 0.0, -p, p)


def gain_kernel(row_ref, mark_ref, d_ref, a_ref, x_ref, p_ref, gain_ref, weight_ref):
    other = jnp.max(mark_ref[...].astype(F32)).astype(jnp.int32)
    u = lax.broadcasted_iota(jnp.int32, (ROWS, N), 0)
    v = lax.broadcasted_iota(jnp.int32, (ROWS, N), 1)
    row = jnp.where(u < HALF, u, u - N).astype(F32) * (1.0 / N)
    col = jnp.where(v < HALF, v, v - N).astype(F32) * (1.0 / N)
    radial = row * row + col * col
    stretch = row * row - col * col
    skew = 2.0 * row * col
    inner = (u > 0) & (u < HALF)
    scale = jnp.where(inner, 2.0, jnp.where(u <= HALF, 1.0, 0.0))
    turn = 1.0 / (2.0 * math.pi)
    for t, r in enumerate((row_ref[0, 0], other)):
        base = (d_ref[r] * turn) * radial + (a_ref[r] * turn) * stretch + p_ref[r] * turn
        cross = (x_ref[r] * turn) * skew
        plus = -sine(base + cross)
        minus = -sine(base - cross)
        mirror = jnp.where(inner & (v == HALF), minus, plus)
        gain_ref[t] = 0.5 * (plus + mirror)
        weight_ref[t] = (0.5 * scale) * (plus * plus + mirror * mirror)


def match_kernel(
    image_ref,
    spec_ref,
    low_ref,
    high_ref,
    gain_ref,
    weight_ref,
    first_ref,
    forward_ref,
    inverse_ref,
    fold_ref,
    best_ref,
    give_ref,
    spec_sc,
    weight_sc,
    best_sc,
):
    step = pl.program_id(0)

    @pl.when(step == 0)
    def _():
        power = jnp.concatenate([low_ref[...], high_ref[...]], axis=0).astype(F32) * (1.0 / 16.0)
        u = lax.broadcasted_iota(jnp.int32, (ROWS, N), 0)
        scale = jnp.where((u > 0) & (u < HALF), 2.0, jnp.where(u <= HALF, 1.0, 0.0))
        mean = jnp.sum(power * scale) * (1.0 / (N * N))
        inverse_noise = 1.0 / (jnp.where(u <= HALF, power, 1.0) + 0.05 * mean)
        for t in range(2):
            factor = gain_ref[t] * inverse_noise
            spec_sc[t, 0] = spec_ref[t, 0] * factor
            spec_sc[t, 1] = spec_ref[t, 1] * factor
            weight_sc[t] = weight_ref[t] * inverse_noise
        best_sc[...] = jnp.full_like(best_sc, -jnp.inf)

    image = image_ref[...].reshape(N, N)
    re, im = half_spectrum(image, first_ref[...], forward_ref[...])
    re = re.astype(BF16).astype(F32)
    im = im.astype(BF16).astype(F32)
    square = re * re + im * im
    for t in range(2):
        norm = jnp.sum(square * weight_sc[t])
        scale = lax.rsqrt(jnp.full((1, 2 * N), norm + 1e-06, F32))
        s_re, s_im = spec_sc[t, 0], spec_sc[t, 1]
        both = jnp.concatenate(
            [
                (s_re * re + s_im * im).astype(BF16),
                (s_im * re - s_re * im).astype(BF16),
            ],
            axis=1,
        )
        half = (dot(both, inverse_ref[...]) * scale).astype(BF16)
        even = dot(fold_ref[0], half[:, :N])
        odd = dot(fold_ref[1], half[:, N:])
        best_sc[t, 0] = jnp.maximum(best_sc[t, 0], even - odd)
        best_sc[t, 1] = jnp.maximum(best_sc[t, 1], even + odd)

    @pl.when(step == pl.num_programs(0) - 1)
    def _():
        best_ref[...] = best_sc[0]
        give_ref[...] = best_sc[1].astype(BF16)


def join_kernel(best_ref, got_ref, unfold_ref, out_ref):
    best = jnp.maximum(best_ref[...], got_ref[...].astype(F32))
    out_ref[:HALF] = best[0, :HALF]
    rest = best.reshape(2 * ROWS, N)
    total = None
    for _ in range(3):
        part = rest.astype(BF16)
        rest = rest - part.astype(F32)
        moved = dot(unfold_ref[...], part)
        total = moved if total is None else total + moved
    out_ref[HALF:] = total


def vmem(count):
    return [pl.BlockSpec(memory_space=pltpu.VMEM)] * count


def smem(count):
    return [pl.BlockSpec(memory_space=pltpu.SMEM)] * count


def cost(flops, size):
    return pl.CostEstimate(flops=flops, bytes_accessed=size, transcendentals=0)


def per_device(images, projections, ctf_row, defocus_term, astig_term, astig_cross, phase_shift):
    first, forward, inverse, fold, unfold = (jnp.asarray(a) for a in tables())
    chips = math.prod(lax.axis_size(a) for a in CHIPS)
    groups = math.prod(lax.axis_size(a) for a in DEF)
    planes = chips // groups
    core = lax.axis_index("core")
    swap = [(0, 1), (1, 0)]

    block = projections[0]
    library = lax.all_to_all(
        jnp.broadcast_to(block[None], (chips,) + block.shape), CHIPS, 0, 0, tiled=False
    )

    tile = images[0, 0]
    mark = jnp.broadcast_to(ctf_row.astype(BF16), (16, N))
    sent = jnp.concatenate([tile, mark], axis=0)
    received = lax.ppermute(sent, "core", swap)

    limit = pltpu.CompilerParams(vmem_limit_bytes=40 << 20)
    spec, power = pl.pallas_call(
        tile_kernel,
        out_shape=[
            jax.ShapeDtypeStruct((2, 2, ROWS, N), F32),
            jax.ShapeDtypeStruct((PART, N), BF16),
        ],
        grid=(1,),
        in_specs=smem(1)
        + [
            pl.BlockSpec((N, N), lambda i: (0, 0)),
            pl.BlockSpec((N, N), lambda i: (0, 0)),
            pl.BlockSpec((2 * ROWS, N), lambda i: (0, 0)),
            pl.BlockSpec((2 * N, 2 * N), lambda i: (0, 0)),
        ],
        out_specs=[
            pl.BlockSpec((2, 2, ROWS, N), lambda i: (0, 0, 0, 0)),
            pl.BlockSpec((PART, N), lambda i: (0, 0)),
        ],
        scratch_shapes=[pltpu.VMEM((ROWS, N), F32)],
        compiler_params=limit,
        cost_estimate=cost(2 * 2 * ROWS * N * N * 6, 4 << 20),
        name="tile",
    )(core[None].astype(jnp.int32), tile, received, first, forward)

    gain, weight = pl.pallas_call(
        gain_kernel,
        out_shape=[jax.ShapeDtypeStruct((2, ROWS, N), F32)] * 2,
        grid=(1,),
        in_specs=smem(1)
        + [pl.BlockSpec((16, N), lambda i: (N // 16, 0))]
        + smem(4),
        out_specs=[pl.BlockSpec((2, ROWS, N), lambda i: (0, 0, 0))] * 2,
        compiler_params=limit,
        cost_estimate=cost(2 * ROWS * N * 60, 2 << 20),
        name="gain",
    )(ctf_row, received, defocus_term, astig_term, astig_cross, phase_shift)

    deep = lax.axis_size("z")
    sums = power.astype(F32)
    for s in range(1, deep):
        moved = lax.ppermute(power, "z", [(i, (i + s) % deep) for i in range(deep)])
        sums = sums + moved.astype(F32)
    sums = sums.astype(BF16)
    moved = lax.ppermute(sums, "xhi", swap)
    mine = (sums.astype(F32) + moved.astype(F32)).astype(BF16)
    theirs = lax.ppermute(mine, "core", swap)
    low = jnp.where(core == 0, mine, theirs)
    high = jnp.where(core == 0, theirs, mine)

    library = library.reshape(groups, planes, N // groups, N)
    best, give = pl.pallas_call(
        match_kernel,
        out_shape=[
            jax.ShapeDtypeStruct((2, ROWS, N), F32),
            jax.ShapeDtypeStruct((2, ROWS, N), BF16),
        ],
        grid=(planes,),
        in_specs=[
            pl.BlockSpec((groups, None, N // groups, N), lambda i: (0, i, 0, 0)),
            pl.BlockSpec((2, 2, ROWS, N), lambda i: (0, 0, 0, 0)),
            pl.BlockSpec((PART, N), lambda i: (0, 0)),
            pl.BlockSpec((PART, N), lambda i: (0, 0)),
            pl.BlockSpec((2, ROWS, N), lambda i: (0, 0, 0)),
            pl.BlockSpec((2, ROWS, N), lambda i: (0, 0, 0)),
            pl.BlockSpec((2 * ROWS, N), lambda i: (0, 0)),
            pl.BlockSpec((2 * N, 2 * N), lambda i: (0, 0)),
            pl.BlockSpec((2 * N, 2 * N), lambda i: (0, 0)),
            pl.BlockSpec((2, ROWS, ROWS), lambda i: (0, 0, 0)),
        ],
        out_specs=[
            pl.BlockSpec((2, ROWS, N), lambda i: (0, 0, 0)),
            pl.BlockSpec((2, ROWS, N), lambda i: (0, 0, 0)),
        ],
        scratch_shapes=[
            pltpu.VMEM((2, 2, ROWS, N), F32),
            pltpu.VMEM((2, ROWS, N), F32),
            pltpu.VMEM((2, 2, ROWS, N), F32),
        ],
        compiler_params=limit,
        cost_estimate=cost(planes * 2 * ROWS * N * N * 16, 8 << 20),
        name="match",
    )(library, spec, low, high, gain, weight, first, forward, inverse, fold)

    got = lax.ppermute(give, "core", swap)
    peak = pl.pallas_call(
        join_kernel,
        out_shape=jax.ShapeDtypeStruct((N, N), F32),
        compiler_params=limit,
        cost_estimate=cost(3 * 2 * HALF * 2 * ROWS * N, 2 << 20),
        name="join",
    )(best, got, unfold)
    return peak[None, None]


def solution(mesh):
    fine = Mesh(mesh.devices.reshape(2, 4, 4, 2, 2), DEF + BLK)
    in_specs = (P(DEF, BLK, None, None), P(BLK, DEF, None), P(DEF, BLK), P(), P(), P(), P())
    out_specs = P(DEF, BLK, None, None)
    return jax.shard_map(
        per_device, mesh=fine, in_specs=in_specs, out_specs=out_specs, check_vma=False
    )
```

time: 380 us -> 85.5 us (0.23)
  waiting for transfers between devices: 154 us -> 29.8 us
  matrix products: 73.6 us -> 0 us
  local copies, waits for them, and re-layouts: 62.3 us -> 13.1 us
  other arithmetic: 35.8 us -> 0.09 us
  blocking collectives: 25.8 us -> 0 us
  Pallas kernels: 0 us -> 21 us
  starting transfers between devices: 0.04 us -> 20.1 us
  between operations: 14.9 us -> 0.77 us
  loops' own time: 11.8 us -> 0 us
    psum x1 -> x0, waiting for transfers between devices: 105 us -> none  [per_device(): lax.psum(power_local.astype(jnp.bfloat16), 'blk').astype(jnp.float32)]
    dot_general x36 -> x0, matrix products: 73.6 us -> none  [the longest x16 41 us: correlate(): jnp.einsum('ua,tab->tub', boundary_table, stacked, preferred_element_type...]
    all_gather x1 -> x0, waiting for transfers between devices: 49.6 us -> none  [per_device(): lax.all_gather(library, 'blk', axis=0, tiled=True)]
    ppermute x0 -> x7, waiting for transfers between devices: none -> 29.8 us  [the longest x3 23.6 us: per_device(): moved = lax.ppermute(power, 'z', [(i, (i + s) % deep) for i in range(deep)])]
    all_gather x1 -> x0, blocking collectives: 25.8 us -> none  [per_device(): library = lax.all_gather(projections, 'defocus', axis=1, tiled=True)]
    dynamic_slice x48 -> x0, local copies, waits for them, and re-layouts: 24.7 us -> none  [per_device(): result, _ = lax.scan(one_plane, initial, (rounded[0], rounded[1]))]
    pallas_call x0 -> x4, Pallas kernels: none -> 21 us  [the longest x1 16.5 us: per_device(): pl.pallas_call(match_kernel, out_shape=[jax.ShapeDtypeStruct((2, ROWS, N)...]
    while x33 -> x0, local copies, waits for them, and re-layouts: 18.3 us -> none
  transfers between devices with their start and end apart: 2 -> 8, of which waited for: 2 -> 6; matrix products, arithmetic and copies ran while one was open for 4% -> 1% of each run, Pallas kernels for 0% -> 4%
where the time goes in v1:
time: 85.5 us; the launch traced here: 85 us
  waiting for transfers between devices  29.8 us (35%)
  Pallas kernels  21 us (25%)
  starting transfers between devices  20.1 us (24%)
  local copies, waits for them, and re-layouts  13.1 us (15%)
    ppermute x3, waiting for transfers between devices, per_device(): moved = lax.ppermute(power, 'z', [(i, (i + s) % deep) for i in range(deep)])  23.6 us
    pallas_call x1, Pallas kernels, per_device(): pl.pallas_call(match_kernel, out_shape=[jax.ShapeDtypeStruct((2, ROWS, N)...  16.5 us
    all_to_all x1, starting transfers between devices, per_device(): lax.all_to_all(jnp.broadcast_to(block[None], (chips,) + block.shape), CHI...  12.1 us
    unnamed x34, local copies, waits for them, and re-layouts  9.99 us
    ppermute x3, starting transfers between devices, per_device(): moved = lax.ppermute(power, 'z', [(i, (i + s) % deep) for i in range(deep)])  3.66 us
    ppermute x1, waiting for transfers between devices, per_device(): moved = lax.ppermute(sums, 'xhi', swap)  3.19 us
    broadcast_in_dim x1, local copies, waits for them, and re-layouts, per_device(): jnp.broadcast_to(block[None], (chips,) + block.shape)  2.4 us
    pallas_call x1, Pallas kernels, per_device(): pl.pallas_call(gain_kernel, out_shape=[jax.ShapeDtypeStruct((2, ROWS, N),...  1.93 us
  transfers between devices with their start and end apart: 8, of which 6 were waited for; matrix products, arithmetic and copies ran while one was open for 1% of the time, Pallas kernels for 4%

profile of v1, /device:TPU:1, one launch (start us, length us, event | category | flops | bytes accessed | tf_op | source)
XLA Modules:
  0.0 85.0 jit_solution(2379965667705762800)
XLA Ops:
  0.0 2.4 %broadcast_in_dim.19 = bf16[64,48,384]{2,1,0:T(8,128)(2,1)} broadcast(bf16[48,384]{1,0:T(8,128)(2,1)} %bitcast.9), dimensions={1,2} | broadcast | bytes 2396160 | tf_op jit(solution)/shard_map/broadcast_in_dim | solution.py:205
  2.4 0.0 copy-start
  2.4 0.0 copy-start.13
  2.4 12.1 %all-to-all-start = ((bf16[64,48,384]{2,1,0:T(8,128)(2,1)}), bf16[64,48,384]{2,1,0:T(8,128)(2,1)S(1)}, u32[]{:S(2)}, u32[]{:S(2)}) async-start(bf16[64,48,384]{2,1,0:T(8,128)(2,1)} %broadcast_in_dim.19), calls=%async_computation | async-start | bytes 4718592 | tf_op jit(solution)/shard_map/all_to_all | solution.py:204
  15.2 0.0 copy-done
  15.2 0.8 concatenate.3
  15.9 1.0 %collective-permute-start = (bf16[400,384]{1,0:T(8,128)(2,1)}, bf16[400,384]{1,0:T(8,128)(2,1)S(1)}, u32[]{:S(2)}, u32[]{:S(2)}) collective-permute-start(bf16[400,384]{1,0:T(8,128)(2,1)} %concatenate.3), channel_id=1, source_target_pairs={{0,1},{1,0},{2,3},{3,2},{4,5},{5,4},{6,7},{7,6},{8,9},{9,8},{10,11... | collective-permute-start | bytes 921608 | tf_op jit(solution)/shard_map/ppermute | solution.py:211
  16.9 1.4 %collective-permute-done.other_ref.mark_ref = bf16[400,384]{1,0:T(8,128)(2,1)S(1)} collective-permute-done((bf16[400,384]{1,0:T(8,128)(2,1)}, bf16[400,384]{1,0:T(8,128)(2,1)S(1)}, u32[]{:S(2)}, u32[]{:S(2)}) %collective-permute-start) | collective-permute-done | bytes 307232 | tf_op jit(solution)/shard_map/ppermute | solution.py:211
  18.3 0.0 copy-done.13
  18.3 0.0 copy-start.10
  18.3 1.3 %copy-done.10 = bf16[768,768]{1,0:T(8,128)(2,1)S(1)} copy-done((bf16[768,768]{1,0:T(8,128)(2,1)S(1)}, bf16[768,768]{1,0:T(8,128)(2,1)}, u32[]{:S(2)}) %copy-start.10) | copy-done | bytes 1179672
  19.6 0.0 copy-start.2
  19.6 0.0 copy-start.3
  19.6 0.0 copy-start.4
  19.6 0.0 copy-start.5
  19.6 1.3 %tile.1 = (f32[2,2,208,384]{3,2,1,0:T(8,128)S(1)}, bf16[104,384]{1,0:T(8,128)(2,1)S(1)}) custom-call(s32[1]{0:T(128)} %bitcast.2.core_ref, bf16[384,384]{1,0:T(8,128)(2,1)S(1)} %bitcast.8, bf16[400,384]{1,0:T(8,128)(2,1)S(1)} %collective-permute-done.other_ref.mark_ref, bf16[416,384]{1,0:T(8,128)(2,1)S(1)} %copy-done.13, bf16[768,768]{1,0:T(8,128)(2,1)S(1)} %copy-done.10), custom_call_target="tpu_custom_call" | custom-call | flops 736100352 | bytes 4194304 | tf_op jit(solution)/shard_map/tile/pallas_call | solution.py:214
  20.9 0.0 copy-start.15
  20.9 1.0 %copy-done.15 = f32[2,2,208,384]{3,2,1,0:T(8,128)} copy-done((f32[2,2,208,384]{3,2,1,0:T(8,128)}, f32[2,2,208,384]{3,2,1,0:T(8,128)S(1)}, u32[]{:S(2)}) %copy-start.15) | copy-done | bytes 1277976
  21.9 0.0 copy-start.14
  21.9 2.5 %collective-permute-start.3 = (bf16[104,384]{1,0:T(8,128)(2,1)S(1)}, bf16[104,384]{1,0:T(8,128)(2,1)S(1)}, u32[]{:S(2)}, u32[]{:S(2)}) collective-permute-start(bf16[104,384]{1,0:T(8,128)(2,1)S(1)} %get-tuple-element.12), channel_id=1, source_target_pairs={{0,12},{4,0},{8,4},{12,8},{1,13},{5,1},{9,5},{13,9},{2,14},{6,2},{... | collective-permute-start | bytes 239624 | tf_op jit(solution)/shard_map/ppermute | solution.py:254
  24.4 0.6 collective-permute-start.2
  25.0 0.6 collective-permute-start.1
  25.6 18.3 %collective-permute-done.3 = bf16[104,384]{1,0:T(8,128)(2,1)S(1)} collective-permute-done((bf16[104,384]{1,0:T(8,128)(2,1)S(1)}, bf16[104,384]{1,0:T(8,128)(2,1)S(1)}, u32[]{:S(2)}, u32[]{:S(2)}) %collective-permute-start.3) | collective-permute-done | bytes 79904 | tf_op jit(solution)/shard_map/ppermute | solution.py:254
  43.9 1.6 %collective-permute-done.2 = bf16[104,384]{1,0:T(8,128)(2,1)S(1)} collective-permute-done((bf16[104,384]{1,0:T(8,128)(2,1)S(1)}, bf16[104,384]{1,0:T(8,128)(2,1)S(1)}, u32[]{:S(2)}, u32[]{:S(2)}) %collective-permute-start.2) | collective-permute-done | bytes 79904 | tf_op jit(solution)/shard_map/ppermute | solution.py:254
  45.4 3.8 %collective-permute-done.1 = bf16[104,384]{1,0:T(8,128)(2,1)S(1)} collective-permute-done((bf16[104,384]{1,0:T(8,128)(2,1)S(1)}, bf16[104,384]{1,0:T(8,128)(2,1)S(1)}, u32[]{:S(2)}, u32[]{:S(2)}) %collective-permute-start.1) | collective-permute-done | bytes 79904 | tf_op jit(solution)/shard_map/ppermute | solution.py:254
  49.3 1.7 %collective-permute-start.4 = (bf16[104,384]{1,0:T(8,128)(2,1)S(1)}, bf16[104,384]{1,0:T(8,128)(2,1)S(1)}, u32[]{:S(2)}, u32[]{:S(2)}) collective-permute-start(bf16[104,384]{1,0:T(8,128)(2,1)S(1)} %add_convert_fusion.1), channel_id=1, source_target_pairs={{0,2},{2,0},{1,3},{3,1},{4,6},{6,4},{5,7},{7,5},{8,10},{10,8},{9,1... | collective-permute-start | bytes 239624 | tf_op jit(solution)/shard_map/ppermute | solution.py:257
  50.9 3.2 %collective-permute-done.4 = bf16[104,384]{1,0:T(8,128)(2,1)S(1)} collective-permute-done((bf16[104,384]{1,0:T(8,128)(2,1)S(1)}, bf16[104,384]{1,0:T(8,128)(2,1)S(1)}, u32[]{:S(2)}, u32[]{:S(2)}) %collective-permute-start.4) | collective-permute-done | bytes 79904 | tf_op jit(solution)/shard_map/ppermute | solution.py:257
  54.1 1.6 %collective-permute-start.5 = (bf16[104,384]{1,0:T(8,128)(2,1)S(1)}, bf16[104,384]{1,0:T(8,128)(2,1)S(1)}, u32[]{:S(2)}, u32[]{:S(2)}) collective-permute-start(bf16[104,384]{1,0:T(8,128)(2,1)S(1)} %add_convert_fusion), channel_id=1, source_target_pairs={{0,1},{1,0},{2,3},{3,2},{4,5},{5,4},{6,7},{7,6},{8,9},{9,8},{10,11... | collective-permute-start | bytes 239624 | tf_op jit(solution)/shard_map/ppermute | solution.py:259
  55.8 0.0 copy-done.2
  55.8 0.0 copy-done.3
  55.8 0.0 copy-done.4
  55.8 0.0 copy-done.5
  55.8 1.9 %gain.1 = (f32[2,208,384]{2,1,0:T(8,128)S(1)}, f32[2,208,384]{2,1,0:T(8,128)S(1)}) custom-call(s32[1,1]{1,0:T(1,128)S(6)} %copy.13.row_ref, bf16[400,384]{1,0:T(8,128)(2,1)S(1)} %collective-permute-done.other_ref.mark_ref, f32[64]{0:T(128)S(1)} %copy-done.2, f32[64]{0:T(128)S(1)} %copy-done.3, f32[64]{0:T(128)S(1)} %copy-done.4, f32[64]{0:T(128)S(1)} %copy-done.5), custom_call_target="tpu_custom_call" | custom-call | flops 9584640 | bytes 2097152 | tf_op jit(solution)/shard_map/gain/pallas_call | solution.py:238
  57.7 0.0 copy-start.6
  57.7 0.8 copy-done.6
  58.6 0.0 copy-start.8
  58.6 0.8 copy-done.8
  59.4 0.0 collective-permute-done.5
  59.4 0.0 all-to-all-done
  59.4 0.0 copy-done.14
  59.4 0.0 copy-start.7
  59.5 1.1 %copy-done.7 = f32[2,208,384]{2,1,0:T(8,128)S(1)} copy-done((f32[2,208,384]{2,1,0:T(8,128)S(1)}, f32[2,208,384]{2,1,0:T(8,128)}, u32[]{:S(2)}) %copy-start.7) | copy-done | bytes 639000
  60.5 0.0 copy-start.9
  60.5 1.1 %copy-done.9 = f32[2,208,384]{2,1,0:T(8,128)S(1)} copy-done((f32[2,208,384]{2,1,0:T(8,128)S(1)}, f32[2,208,384]{2,1,0:T(8,128)}, u32[]{:S(2)}) %copy-start.9) | copy-done | bytes 639000
  61.6 0.0 copy-start.11
  61.6 1.3 %copy-done.11 = bf16[768,768]{1,0:T(8,128)(2,1)S(1)} copy-done((bf16[768,768]{1,0:T(8,128)(2,1)S(1)}, bf16[768,768]{1,0:T(8,128)(2,1)}, u32[]{:S(2)}) %copy-start.11) | copy-done | bytes 1179672
  62.9 0.0 copy-start.12
  62.9 1.3 %copy-done.12 = bf16[768,768]{1,0:T(8,128)(2,1)S(1)} copy-done((bf16[768,768]{1,0:T(8,128)(2,1)S(1)}, bf16[768,768]{1,0:T(8,128)(2,1)}, u32[]{:S(2)}) %copy-start.12) | copy-done | bytes 1179672
  64.2 0.0 copy-start.16
  64.2 1.3 %copy-done.16 = f32[2,2,208,384]{3,2,1,0:T(8,128)S(1)} copy-done((f32[2,2,208,384]{3,2,1,0:T(8,128)S(1)}, f32[2,2,208,384]{3,2,1,0:T(8,128)}, u32[]{:S(2)}) %copy-start.16) | copy-done | bytes 1277976
  65.5 0.0 copy-start.1
  65.5 16.5 %match.1 = (f32[2,208,384]{2,1,0:T(8,128)S(1)}, bf16[2,208,384]{2,1,0:T(8,128)(2,1)S(1)}) custom-call(bf16[8,8,48,384]{3,2,1,0:T(8,128)(2,1)S(1)} %bitcast.6, f32[2,2,208,384]{3,2,1,0:T(8,128)S(1)} %copy-done.16, bf16[104,384]{1,0:T(8,128)(2,1)S(1)} %get-tuple-element.18.low_ref, bf16[104,384]{1,0:T(8,128)(2,1)S(1)} %get-tuple-element.17.high_ref, ...), custom_call_target="tpu_custom_call" | custom-call | flops 7851737088 | bytes 8388608 | tf_op jit(solution)/shard_map/match/pallas_call | solution.py:264
  82.0 0.1 collective-permute-start.6
  82.1 1.6 %collective-permute-done.6.got_ref = bf16[2,208,384]{2,1,0:T(8,128)(2,1)S(1)} collective-permute-done((bf16[2,208,384]{2,1,0:T(8,128)(2,1)S(1)}, bf16[2,208,384]{2,1,0:T(8,128)(2,1)S(1)}, u32[]{:S(2)}, u32[]{:S(2)}) %collective-permute-start.6) | collective-permute-done | bytes 319520 | tf_op jit(solution)/shard_map/ppermute | solution.py:297
  83.7 0.0 copy-done.1
  83.7 1.3 %join.1 = f32[384,384]{1,0:T(8,128)} custom-call(f32[2,208,384]{2,1,0:T(8,128)S(1)} %get-tuple-element.15.best_ref, bf16[2,208,384]{2,1,0:T(8,128)(2,1)S(1)} %collective-permute-done.6.got_ref, bf16[192,416]{1,0:T(8,128)(2,1)S(1)} %copy-done.1), custom_call_target="tpu_custom_call" | custom-call | flops 184025088 | bytes 2097152 | tf_op jit(solution)/shard_map/join/pallas_call | solution.py:298
  (3 shorter events, 0.1 us)
Async XLA Ops:
  2.4 12.8 %copy-start = (bf16[1,1,384,384]{3,2,1,0:T(8,128)(2,1)S(1)}, bf16[1,1,384,384]{3,2,1,0:T(8,128)(2,1)}, u32[]{:S(2)}) copy-start(bf16[1,1,384,384]{3,2,1,0:T(8,128)(2,1)} %param.12) | copy-start | bytes 884740
  2.4 15.9 %copy-start.13 = (bf16[416,384]{1,0:T(8,128)(2,1)S(1)}, bf16[416,384]{1,0:T(8,128)(2,1)}, u32[]{:S(2)}) copy-start(bf16[416,384]{1,0:T(8,128)(2,1)} %constant.16.clone.first_ref) | copy-start | bytes 958468
  2.4 57.0 %all-to-all-start = ((bf16[64,48,384]{2,1,0:T(8,128)(2,1)}), bf16[64,48,384]{2,1,0:T(8,128)(2,1)S(1)}, u32[]{:S(2)}, u32[]{:S(2)}) async-start(bf16[64,48,384]{2,1,0:T(8,128)(2,1)} %broadcast_in_dim.19), calls=%async_computation | async-start | bytes 4718592 | tf_op jit(solution)/shard_map/all_to_all | solution.py:204
  15.9 2.4 %collective-permute-start = (bf16[400,384]{1,0:T(8,128)(2,1)}, bf16[400,384]{1,0:T(8,128)(2,1)S(1)}, u32[]{:S(2)}, u32[]{:S(2)}) collective-permute-start(bf16[400,384]{1,0:T(8,128)(2,1)} %concatenate.3), channel_id=1, source_target_pairs={{0,1},{1,0},{2,3},{3,2},{4,5},{5,4},{6,7},{7,6},{8,9},{9,8},{10,11... | collective-permute-start | bytes 921608 | tf_op jit(solution)/shard_map/ppermute | solution.py:211
  18.3 1.3 %copy-start.10 = (bf16[768,768]{1,0:T(8,128)(2,1)S(1)}, bf16[768,768]{1,0:T(8,128)(2,1)}, u32[]{:S(2)}) copy-start(bf16[768,768]{1,0:T(8,128)(2,1)} %constant.17.clone.forward_ref) | copy-start | bytes 3538948
  19.6 36.2 %copy-start.2 = (f32[64]{0:T(128)S(1)}, f32[64]{0:T(128)}, u32[]{:S(2)}) copy-start(f32[64]{0:T(128)} %d_ref.1) | copy-start | bytes 772
  19.6 36.2 %copy-start.3 = (f32[64]{0:T(128)S(1)}, f32[64]{0:T(128)}, u32[]{:S(2)}) copy-start(f32[64]{0:T(128)} %a_ref.1) | copy-start | bytes 772
  19.6 36.2 %copy-start.4 = (f32[64]{0:T(128)S(1)}, f32[64]{0:T(128)}, u32[]{:S(2)}) copy-start(f32[64]{0:T(128)} %x_ref.1) | copy-start | bytes 772
  19.6 36.2 %copy-start.5 = (f32[64]{0:T(128)S(1)}, f32[64]{0:T(128)}, u32[]{:S(2)}) copy-start(f32[64]{0:T(128)} %p_ref.1) | copy-start | bytes 772
  20.9 1.0 %copy-start.15 = (f32[2,2,208,384]{3,2,1,0:T(8,128)}, f32[2,2,208,384]{3,2,1,0:T(8,128)S(1)}, u32[]{:S(2)}) copy-start(f32[2,2,208,384]{3,2,1,0:T(8,128)S(1)} %get-tuple-element.11.spec_ref) | copy-start | bytes 3833860
  21.9 37.5 %copy-start.14 = (bf16[2,208,208]{2,1,0:T(8,128)(2,1)S(1)}, bf16[2,208,208]{2,1,0:T(8,128)(2,1)}, u32[]{:S(2)}) copy-start(bf16[2,208,208]{2,1,0:T(8,128)(2,1)} %constant.19.clone.fold_ref) | copy-start | bytes 519172
  21.9 22.0 %collective-permute-start.3 = (bf16[104,384]{1,0:T(8,128)(2,1)S(1)}, bf16[104,384]{1,0:T(8,128)(2,1)S(1)}, u32[]{:S(2)}, u32[]{:S(2)}) collective-permute-start(bf16[104,384]{1,0:T(8,128)(2,1)S(1)} %get-tuple-element.12), channel_id=1, source_target_pairs={{0,12},{4,0},{8,4},{12,8},{1,13},{5,1},{9,5},{13,9},{2,14},{6,2},{... | collective-permute-start | bytes 239624 | tf_op jit(solution)/shard_map/ppermute | solution.py:254
  24.4 21.0 %collective-permute-start.2 = (bf16[104,384]{1,0:T(8,128)(2,1)S(1)}, bf16[104,384]{1,0:T(8,128)(2,1)S(1)}, u32[]{:S(2)}, u32[]{:S(2)}) collective-permute-start(bf16[104,384]{1,0:T(8,128)(2,1)S(1)} %get-tuple-element.12), channel_id=1, source_target_pairs={{0,8},{4,12},{8,0},{12,4},{1,9},{5,13},{9,1},{13,5},{2,10},{6,14},... | collective-permute-start | bytes 239624 | tf_op jit(solution)/shard_map/ppermute | solution.py:254
  25.0 24.2 %collective-permute-start.1 = (bf16[104,384]{1,0:T(8,128)(2,1)S(1)}, bf16[104,384]{1,0:T(8,128)(2,1)S(1)}, u32[]{:S(2)}, u32[]{:S(2)}) collective-permute-start(bf16[104,384]{1,0:T(8,128)(2,1)S(1)} %get-tuple-element.12), channel_id=1, source_target_pairs={{0,4},{4,8},{8,12},{12,0},{1,5},{5,9},{9,13},{13,1},{2,6},{6,10},{... | collective-permute-start | bytes 239624 | tf_op jit(solution)/shard_map/ppermute | solution.py:254
  49.3 4.9 %collective-permute-start.4 = (bf16[104,384]{1,0:T(8,128)(2,1)S(1)}, bf16[104,384]{1,0:T(8,128)(2,1)S(1)}, u32[]{:S(2)}, u32[]{:S(2)}) collective-permute-start(bf16[104,384]{1,0:T(8,128)(2,1)S(1)} %add_convert_fusion.1), channel_id=1, source_target_pairs={{0,2},{2,0},{1,3},{3,1},{4,6},{6,4},{5,7},{7,5},{8,10},{10,8},{9,1... | collective-permute-start | bytes 239624 | tf_op jit(solution)/shard_map/ppermute | solution.py:257
  54.1 5.3 %collective-permute-start.5 = (bf16[104,384]{1,0:T(8,128)(2,1)S(1)}, bf16[104,384]{1,0:T(8,128)(2,1)S(1)}, u32[]{:S(2)}, u32[]{:S(2)}) collective-permute-start(bf16[104,384]{1,0:T(8,128)(2,1)S(1)} %add_convert_fusion), channel_id=1, source_target_pairs={{0,1},{1,0},{2,3},{3,2},{4,5},{5,4},{6,7},{7,6},{8,9},{9,8},{10,11... | collective-permute-start | bytes 239624 | tf_op jit(solution)/shard_map/ppermute | solution.py:259
  57.7 0.8 copy-start.6
  58.6 0.8 copy-start.8
  59.4 1.1 %copy-start.7 = (f32[2,208,384]{2,1,0:T(8,128)S(1)}, f32[2,208,384]{2,1,0:T(8,128)}, u32[]{:S(2)}) copy-start(f32[2,208,384]{2,1,0:T(8,128)} %copy-done.6) | copy-start | bytes 1916932
  60.5 1.1 %copy-start.9 = (f32[2,208,384]{2,1,0:T(8,128)S(1)}, f32[2,208,384]{2,1,0:T(8,128)}, u32[]{:S(2)}) copy-start(f32[2,208,384]{2,1,0:T(8,128)} %copy-done.8) | copy-start | bytes 1916932
  61.6 1.3 %copy-start.11 = (bf16[768,768]{1,0:T(8,128)(2,1)S(1)}, bf16[768,768]{1,0:T(8,128)(2,1)}, u32[]{:S(2)}) copy-start(bf16[768,768]{1,0:T(8,128)(2,1)} %constant.17.clone.forward_ref) | copy-start | bytes 3538948
  62.9 1.3 %copy-start.12 = (bf16[768,768]{1,0:T(8,128)(2,1)S(1)}, bf16[768,768]{1,0:T(8,128)(2,1)}, u32[]{:S(2)}) copy-start(bf16[768,768]{1,0:T(8,128)(2,1)} %constant.18.clone.inverse_ref) | copy-start | bytes 3538948
  64.2 1.3 %copy-start.16 = (f32[2,2,208,384]{3,2,1,0:T(8,128)S(1)}, f32[2,2,208,384]{3,2,1,0:T(8,128)}, u32[]{:S(2)}) copy-start(f32[2,2,208,384]{3,2,1,0:T(8,128)} %copy-done.15) | copy-start | bytes 3833860
  65.5 18.2 %copy-start.1 = (bf16[192,416]{1,0:T(8,128)(2,1)S(1)}, bf16[192,416]{1,0:T(8,128)(2,1)}, u32[]{:S(2)}) copy-start(bf16[192,416]{1,0:T(8,128)(2,1)} %constant.20.clone.unfold_ref) | copy-start | bytes 479236
  82.0 1.7 %collective-permute-start.6 = (bf16[2,208,384]{2,1,0:T(8,128)(2,1)S(1)}, bf16[2,208,384]{2,1,0:T(8,128)(2,1)S(1)}, u32[]{:S(2)}, u32[]{:S(2)}) collective-permute-start(bf16[2,208,384]{2,1,0:T(8,128)(2,1)S(1)} %get-tuple-element.16), channel_id=1, source_target_pairs={{0,1},{1,0},{2,3},{3,2},{4,5},{5,4},{6,7},{7,6},{8,9},{9,8},{10,11... | collective-permute-start | bytes 958472 | tf_op jit(solution)/shard_map/ppermute | solution.py:297

commit v2 on v1

v2 whole, which is shorter than its diff:
```python
import math

import jax
import jax.numpy as jnp
import ml_dtypes
import numpy as np
from jax import lax
from jax.experimental import pallas as pl
from jax.experimental.pallas import tpu as pltpu
from jax.sharding import Mesh
from jax.sharding import PartitionSpec as P

DEF = ("xlo", "y")
BLK = ("z", "xhi", "core")
CHIPS = ("xlo", "y", "z", "xhi")
ZX = ("z", "xhi")
N = 384
HALF = N // 2
THIRD = N // 3
BLOCKS = (80, 64, 64)
ROWS = sum(BLOCKS)
PART = ROWS // 2
ROOT = math.sqrt(3.0) / 2.0
F32 = jnp.float32
BF16 = jnp.bfloat16


def tables():
    j = np.arange(N)
    phase = (j[:, None] * j[None, :]) % N
    cos = np.cos(2.0 * np.pi * phase / N)
    sin = np.sin(2.0 * np.pi * phase / N)
    bf = ml_dtypes.bfloat16
    u = np.concatenate([3 * np.arange(b) + c for c, b in enumerate(BLOCKS)])
    keep = (u <= HALF)[:, None]
    u = np.minimum(u, HALF)
    v = np.concatenate([3 * np.arange(THIRD) + c for c in range(3)])
    first = np.concatenate([keep * cos[u], keep * -sin[u]])
    c, s = cos[:, v], sin[:, v]
    forward = np.block([[c, -s], [s, c]])
    r = np.arange(THIRD)
    b0, b1 = BLOCKS[0], BLOCKS[0] + BLOCKS[1]
    real = np.concatenate([(keep * cos[u])[:b0, r], (keep * -sin[u])[:b0, r]])
    c1, s1 = cos[u[b0:b1]][:, r], sin[u[b0:b1]][:, r]
    c2, s2 = cos[u[b1:]][:, r], sin[u[b1:]][:, r]
    pair = np.block([[c1, s1], [c2, -s2], [-s1, c1], [-s2, -c2]])
    ahead, back = [], []
    for k in range(3):
        ck = cos[r][:, 3 * r + k]
        sk = sin[r][:, 3 * r + k]
        ahead.append(np.block([[ck, -sk], [sk, ck]]))
        back.append(np.block([[ck.T, sk.T], [-sk.T, ck.T]]))
    ahead, back = np.stack(ahead), np.stack(back)
    weight = np.where((u == 0) | (u == HALF), 1.0, 2.0) * keep[:, 0]
    fold = np.zeros((2, ROWS, ROWS))
    fold[0, : HALF + 1] = cos[: HALF + 1][:, u].astype(bf).astype(float) * weight
    fold[1, : HALF + 1] = sin[: HALF + 1][:, u].astype(bf).astype(float) * weight
    unfold = np.zeros((HALF, 2 * ROWS))
    unfold[0, HALF] = 1.0
    for i in range(1, HALF):
        unfold[i, ROWS + HALF - i] = 1.0
    names = ("first", "forward", "real", "pair", "ahead", "back", "fold", "unfold")
    arrays = (first, forward, real, pair, ahead, back, fold, unfold)
    return {n: jnp.asarray(a.astype(bf)) for n, a in zip(names, arrays)}


def dot(a, b):
    return jnp.dot(a, b, preferred_element_type=F32)


def row_numbers():
    i = lax.broadcasted_iota(jnp.int32, (ROWS, N), 0)
    k = lax.broadcasted_iota(jnp.int32, (ROWS, N), 1)
    b0, b1 = BLOCKS[0], BLOCKS[0] + BLOCKS[1]
    u = jnp.where(i < b0, 3 * i, jnp.where(i < b1, 3 * (i - b0) + 1, 3 * (i - b1) + 2))
    v = jnp.where(
        k < THIRD, 3 * k, jnp.where(k < 2 * THIRD, 3 * (k - THIRD) + 1, 3 * (k - 2 * THIRD) + 2)
    )
    return u, v


def row_scale(u):
    return jnp.where((u > 0) & (u < HALF), 2.0, jnp.where(u <= HALF, 1.0, 0.0))


def copy_kernel(block_ref, out_ref, wide_sc, sems):
    count = wide_sc.shape[0]
    wide_sc[...] = jnp.broadcast_to(block_ref[...][None], wide_sc.shape)
    moves = [
        pltpu.make_async_copy(wide_sc, out_ref.at[pl.ds(i * count, count)], sems.at[i])
        for i in range(out_ref.shape[0] // count)
    ]
    for move in moves:
        move.start()
    for move in moves:
        move.wait()


def sine(x):
    x = x - jnp.round(x)
    a = jnp.abs(x)
    a = jnp.minimum(a, 0.5 - a)
    s = a * a
    p = jnp.full_like(x, -15.0946425768229800)
    for c in (
        42.0586939448600400,
        -76.7058597530613900,
        81.6052492760750400,
        -41.3417022403997600,
        6.28318530717958648,
    ):
        p = p * s + c
    p = p * a
    return jnp.where(x < 0.0, -p, p)


def tile_kernel(
    core_ref,
    row_ref,
    d_ref,
    a_ref,
    x_ref,
    p_ref,
    own_ref,
    other_ref,
    first_ref,
    forward_ref,
    spec_ref,
    weight_ref,
    power_ref,
    total_ref,
):
    mark = other_ref[N:, :].astype(F32)
    other = jnp.max(mark).astype(jnp.int32)
    u, v = row_numbers()
    row = jnp.where(u < HALF, u, u - N).astype(F32) * (1.0 / N)
    col = jnp.where(v < HALF, v, v - N).astype(F32) * (1.0 / N)
    radial = row * row + col * col
    stretch = row * row - col * col
    skew = 2.0 * row * col
    inner = (u > 0) & (u < HALF)
    scale = row_scale(u)
    turn = 1.0 / (2.0 * math.pi)
    for t, r in enumerate((row_ref[0, 0], other)):
        image = own_ref[...] if t == 0 else other_ref[:N, :]
        part = dot(first_ref[...], image).astype(BF16)
        both = jnp.concatenate([part[:ROWS], part[ROWS:]], axis=1)
        out = dot(both, forward_ref[...])
        re, im = out[:, :N], out[:, N:]
        square = re * re + im * im
        total_ref[...] = square if t == 0 else total_ref[...] + square
        base = (d_ref[r] * turn) * radial + (a_ref[r] * turn) * stretch + p_ref[r] * turn
        cross = (x_ref[r] * turn) * skew
        plus = -sine(base + cross)
        minus = -sine(base - cross)
        mirror = jnp.where(inner & (v == HALF), minus, plus)
        gain = 0.5 * (plus + mirror)
        spec_ref[t, 0] = re * gain
        spec_ref[t, 1] = im * gain
        weight_ref[t] = (0.5 * scale) * (plus * plus + mirror * mirror)
    start = pl.multiple_of(core_ref[0] * PART, 8)
    power_ref[...] = total_ref[pl.ds(start, PART), :].astype(BF16)


def library_kernel(image_ref, real_ref, pair_ref, ahead_ref, out_ref):
    image = image_ref[...].reshape(N, N).astype(F32)
    x0, x1, x2 = image[:THIRD], image[THIRD : 2 * THIRD], image[2 * THIRD :]
    plus, minus = x1 + x2, x1 - x2
    f0 = (x0 + plus).astype(BF16)
    f1 = jnp.concatenate(
        [(x0 - 0.5 * plus).astype(BF16), (-ROOT * minus).astype(BF16)], axis=0
    )
    low = dot(real_ref[...], f0)
    high = dot(pair_ref[...], f1)
    b0 = BLOCKS[0]
    b2 = BLOCKS[1] + BLOCKS[2]
    re = jnp.concatenate([low[:b0], high[:b2]], axis=0)
    im = jnp.concatenate([low[b0:], high[b2:]], axis=0)
    r0, r1, r2 = re[:, :THIRD], re[:, THIRD : 2 * THIRD], re[:, 2 * THIRD :]
    i0, i1, i2 = im[:, :THIRD], im[:, THIRD : 2 * THIRD], im[:, 2 * THIRD :]
    rp, rm = r1 + r2, ROOT * (r1 - r2)
    ip, im_ = i1 + i2, ROOT * (i1 - i2)
    rh, ih = r0 - 0.5 * rp, i0 - 0.5 * ip
    parts = ((r0 + rp, i0 + ip), (rh + im_, ih - rm), (rh - im_, ih + rm))
    for k, (a, b) in enumerate(parts):
        lhs = jnp.concatenate([a.astype(BF16), b.astype(BF16)], axis=1)
        out = dot(lhs, ahead_ref[k]).astype(BF16)
        out_ref[0, :, k * THIRD : (k + 1) * THIRD] = out[:, :THIRD]
        out_ref[1, :, k * THIRD : (k + 1) * THIRD] = out[:, THIRD:]


def match_kernel(
    lib_ref,
    spec_ref,
    weight_ref,
    low_ref,
    high_ref,
    back_ref,
    fold_ref,
    out_ref,
    spec_sc,
    weight_sc,
    best_sc,
):
    step = pl.program_id(0)

    @pl.when(step == 0)
    def _():
        power = jnp.concatenate([low_ref[...], high_ref[...]], axis=0).astype(F32) * (1.0 / 16.0)
        u, _ = row_numbers()
        mean = jnp.sum(power * row_scale(u)) * (1.0 / (N * N))
        inverse_noise = 1.0 / (jnp.where(u <= HALF, power, 1.0) + 0.05 * mean)
        spec_sc[0] = spec_ref[0] * inverse_noise
        spec_sc[1] = spec_ref[1] * inverse_noise
        weight_sc[...] = weight_ref[...] * inverse_noise
        best_sc[...] = jnp.full_like(best_sc, -jnp.inf)

    re = lib_ref[0].astype(F32)
    im = lib_ref[1].astype(F32)
    norm = jnp.sum((re * re + im * im) * weight_sc[...])
    scale = lax.rsqrt(jnp.full((1, THIRD), norm + 1e-06, F32))
    s_re, s_im = spec_sc[0], spec_sc[1]
    p_re = (s_re * re + s_im * im).astype(BF16)
    p_im = (s_im * re - s_re * im).astype(BF16)
    g = []
    for k in range(3):
        at = slice(k * THIRD, (k + 1) * THIRD)
        g.append(dot(jnp.concatenate([p_re[:, at], p_im[:, at]], axis=1), back_ref[k]))
    (r0, i0), (r1, i1), (r2, i2) = ((x[:, :THIRD], x[:, THIRD:]) for x in g)
    slant = scale * ROOT
    rp, rm = r1 + r2, slant * (r1 - r2)
    ip, im_ = i1 + i2, slant * (i1 - i2)
    rh, ih = scale * (r0 - 0.5 * rp), scale * (i0 - 0.5 * ip)
    h_re = [scale * (r0 + rp), rh - im_, rh + im_]
    h_im = [scale * (i0 + ip), ih + rm, ih - rm]
    h_re = jnp.concatenate([h.astype(BF16) for h in h_re], axis=1)
    h_im = jnp.concatenate([h.astype(BF16) for h in h_im], axis=1)
    even = dot(fold_ref[0], h_re)
    odd = dot(fold_ref[1], h_im)
    best_sc[0] = jnp.maximum(best_sc[0], even - odd)
    best_sc[1] = jnp.maximum(best_sc[1], even + odd)

    @pl.when(step == pl.num_programs(0) - 1)
    def _():
        out_ref[...] = best_sc[...].astype(out_ref.dtype)


def join_kernel(best_ref, got_ref, unfold_ref, out_ref):
    best = jnp.maximum(best_ref[...], got_ref[...].astype(F32))
    out_ref[:HALF] = best[0, :HALF]
    rest = best.reshape(2 * ROWS, N)
    total = None
    for _ in range(3):
        part = rest.astype(BF16)
        rest = rest - part.astype(F32)
        moved = dot(unfold_ref[...], part)
        total = moved if total is None else total + moved
    out_ref[HALF:] = total


def vmem(count):
    return [pl.BlockSpec(memory_space=pltpu.VMEM)] * count


def smem(count):
    return [pl.BlockSpec(memory_space=pltpu.SMEM)] * count


def cost(flops, size):
    return pl.CostEstimate(flops=flops, bytes_accessed=size, transcendentals=0)


def params(mib):
    return pltpu.CompilerParams(vmem_limit_bytes=mib << 20)


def per_device(images, projections, ctf_row, defocus_term, astig_term, astig_cross, phase_shift):
    tab = tables()
    chips = math.prod(lax.axis_size(a) for a in CHIPS)
    groups = math.prod(lax.axis_size(a) for a in DEF)
    planes = chips // groups
    core = lax.axis_index("core")
    swap = [(0, 1), (1, 0)]

    block = projections[0]
    copies = pl.pallas_call(
        copy_kernel,
        out_shape=jax.ShapeDtypeStruct((chips,) + block.shape, BF16),
        in_specs=vmem(1),
        out_specs=pl.BlockSpec(memory_space=pltpu.HBM),
        scratch_shapes=[
            pltpu.VMEM((groups,) + block.shape, BF16),
            pltpu.SemaphoreType.DMA((planes,)),
        ],
        compiler_params=params(4),
        cost_estimate=cost(0, 3 << 20),
        name="copies",
    )(block)
    library = lax.all_to_all(copies, CHIPS, 0, 0, tiled=False)

    tile = images[0, 0]
    mark = jnp.broadcast_to(ctf_row.astype(BF16), (16, N))
    received = lax.ppermute(jnp.concatenate([tile, mark], axis=0), "core", swap)

    spec, weight, power = pl.pallas_call(
        tile_kernel,
        out_shape=[
            jax.ShapeDtypeStruct((2, 2, ROWS, N), F32),
            jax.ShapeDtypeStruct((2, ROWS, N), F32),
            jax.ShapeDtypeStruct((PART, N), BF16),
        ],
        in_specs=smem(6) + vmem(4),
        out_specs=vmem(3),
        scratch_shapes=[pltpu.VMEM((ROWS, N), F32)],
        compiler_params=params(16),
        cost_estimate=cost(2 * 2 * ROWS * N * N * 6, 4 << 20),
        name="tile",
    )(
        core[None].astype(jnp.int32),
        ctf_row,
        defocus_term,
        astig_term,
        astig_cross,
        phase_shift,
        tile,
        received,
        tab["first"],
        tab["forward"],
    )

    deep, wide = (lax.axis_size(a) for a in ZX)
    sums = power.astype(F32)
    for dz in range(deep):
        for dx in range(wide):
            if dz or dx:
                perm = [
                    (z * wide + x, (z + dz) % deep * wide + (x + dx) % wide)
                    for z in range(deep)
                    for x in range(wide)
                ]
                sums = sums + lax.ppermute(power, ZX, perm).astype(F32)
    mine = sums.astype(BF16)
    theirs = lax.ppermute(mine, "core", swap)
    low = jnp.where(core == 0, mine, theirs)
    high = jnp.where(core == 0, theirs, mine)

    library = library.reshape(groups, planes, N // groups, N)
    spectra = pl.pallas_call(
        library_kernel,
        out_shape=jax.ShapeDtypeStruct((planes, 2, ROWS, N), BF16),
        grid=(planes,),
        in_specs=[pl.BlockSpec((groups, None, N // groups, N), lambda i: (0, i, 0, 0))] + vmem(3),
        out_specs=pl.BlockSpec((None, 2, ROWS, N), lambda i: (i, 0, 0, 0)),
        compiler_params=params(16),
        cost_estimate=cost(planes * 2 * ROWS * 768 * 256 * 2, 5 << 20),
        name="library",
    )(library, tab["real"], tab["pair"], tab["ahead"])

    def match(t, dtype, name):
        return pl.pallas_call(
            match_kernel,
            out_shape=jax.ShapeDtypeStruct((2, ROWS, N), dtype),
            grid=(planes,),
            in_specs=[
                pl.BlockSpec((None, 2, ROWS, N), lambda i: (i, 0, 0, 0)),
                pl.BlockSpec((None, 2, ROWS, N), lambda i: (t, 0, 0, 0)),
                pl.BlockSpec((None, ROWS, N), lambda i: (t, 0, 0)),
            ]
            + vmem(4),
            out_specs=vmem(1)[0],
            scratch_shapes=[
                pltpu.VMEM((2, ROWS, N), F32),
                pltpu.VMEM((ROWS, N), F32),
                pltpu.VMEM((2, ROWS, N), F32),
            ],
            compiler_params=params(16),
            cost_estimate=cost(planes * 2 * ROWS * 768 * 256 * 2, 4 << 20),
            name=name,
        )(spectra, spec, weight, low, high, tab["back"], tab["fold"])

    give = match(1, BF16, "other")
    got = lax.ppermute(give, "core", swap)
    best = match(0, F32, "own")
    peak = pl.pallas_call(
        join_kernel,
        out_shape=jax.ShapeDtypeStruct((N, N), F32),
        in_specs=vmem(3),
        out_specs=vmem(1)[0],
        compiler_params=params(16),
        cost_estimate=cost(3 * 2 * HALF * 2 * ROWS * N, 2 << 20),
        name="join",
    )(best, got, tab["unfold"])
    return peak[None, None]


def solution(mesh):
    fine = Mesh(mesh.devices.reshape(2, 4, 4, 2, 2), DEF + BLK)
    in_specs = (P(DEF, BLK, None, None), P(BLK, DEF, None), P(DEF, BLK), P(), P(), P(), P())
    out_specs = P(DEF, BLK, None, None)
    return jax.shard_map(
        per_device, mesh=fine, in_specs=in_specs, out_specs=out_specs, check_vma=False
    )
```

time: 85.5 us -> 78 us (0.912)
  waiting for transfers between devices: 29.8 us -> 15.6 us
  starting transfers between devices: 20.1 us -> 30.2 us
  local copies, waits for them, and re-layouts: 13.1 us -> 9.87 us
  Pallas kernels: 21 us -> 19.8 us
  other arithmetic: 0.09 us -> 1.03 us
    ppermute x5 -> x8, waiting for transfers between devices: 28.2 us -> 14.6 us  [the longest x7 13.3 us: per_device(): sums = sums + lax.ppermute(power, ZX, perm).astype(F32)]
    ppermute x5 -> x8, starting transfers between devices: 6.27 us -> 15.7 us  [the longest x7 14.7 us: per_device(): sums = sums + lax.ppermute(power, ZX, perm).astype(F32)]
    pallas_call x2 -> x4, Pallas kernels: 18.4 us -> 15.8 us  [the longest x2 10.7 us: match(): pl.pallas_call(match_kernel, out_shape=jax.ShapeDtypeStruct((2, ROWS, N),...]
    broadcast_in_dim x1 -> x0, local copies, waits for them, and re-layouts: 2.4 us -> none  [per_device(): jnp.broadcast_to(block[None], (chips,) + block.shape)]
    ppermute x1, waiting for transfers between devices: 1.58 us -> 0.01 us  [per_device(): got = lax.ppermute(give, 'core', swap)]
    pallas_call x1, Pallas kernels: 1.27 us -> 2.65 us  [per_device(): pl.pallas_call(tile_kernel, out_shape=[jax.ShapeDtypeStruct((2, 2, ROWS,...]
    ppermute x1, waiting for transfers between devices: 0.01 us -> 1.05 us  [per_device(): theirs = lax.ppermute(mine, 'core', swap)]
    select_n x1, other arithmetic: 0.02 us -> 0.94 us  [per_device(): high = jnp.where(core == 0, theirs, mine)]
  transfers between devices with their start and end apart: 8 -> 11, of which waited for: 6 -> 7; matrix products, arithmetic and copies ran while one was open for 1% -> 1% of each run, Pallas kernels for 4% -> 10%
where the time goes in v2:
time: 78 us; the launch traced here: 77.4 us
  starting transfers between devices  30.2 us (39%)
  Pallas kernels  19.8 us (25%)
  waiting for transfers between devices  15.6 us (20%)
  local copies, waits for them, and re-layouts  9.87 us (13%)
  other arithmetic  1.03 us (1%)
  between operations  0.92 us (1%)
    ppermute x7, starting transfers between devices, per_device(): sums = sums + lax.ppermute(power, ZX, perm).astype(F32)  14.7 us
    ppermute x7, waiting for transfers between devices, per_device(): sums = sums + lax.ppermute(power, ZX, perm).astype(F32)  13.3 us
    all_to_all x1, starting transfers between devices, per_device(): library = lax.all_to_all(copies, CHIPS, 0, 0, tiled=False)  12.1 us
    pallas_call x2, Pallas kernels, match(): pl.pallas_call(match_kernel, out_shape=jax.ShapeDtypeStruct((2, ROWS, N),...  10.7 us
    unnamed x42, local copies, waits for them, and re-layouts  9.84 us
    pallas_call x1, Pallas kernels, per_device(): pl.pallas_call(library_kernel, out_shape=jax.ShapeDtypeStruct((planes, 2,...  4.48 us
    pallas_call x1, Pallas kernels, per_device(): pl.pallas_call(tile_kernel, out_shape=[jax.ShapeDtypeStruct((2, 2, ROWS,...  2.65 us
    ppermute x1, starting transfers between devices, per_device(): theirs = lax.ppermute(mine, 'core', swap)  1.94 us
  transfers between devices with their start and end apart: 11, of which 7 were waited for; matrix products, arithmetic and copies ran while one was open for 1% of the time, Pallas kernels for 10%

profile of v2, /device:TPU:1, one launch (start us, length us, event | category | flops | bytes accessed | tf_op | source)
XLA Modules:
  0.0 77.4 jit_solution(4120948082274748088)
XLA Ops:
  0.0 0.0 copy-start.11
  0.0 0.8 copy-done.11
  0.8 0.6 copies.1
  1.4 0.0 copy-start
  1.4 1.4 %copy-done = bf16[64,48,384]{2,1,0:T(8,128)(2,1)} copy-done((bf16[64,48,384]{2,1,0:T(8,128)(2,1)}, bf16[64,48,384]{2,1,0:T(8,128)(2,1)S(1)}, u32[]{:S(2)}) %copy-start) | copy-done | bytes 2359320
  2.8 0.0 copy-start.6
  2.8 0.0 copy-start.14
  2.8 0.0 copy-start.15
  2.8 0.0 copy-start.16
  2.8 0.0 copy-start.17
  2.8 12.1 %all-to-all-start = ((bf16[64,48,384]{2,1,0:T(8,128)(2,1)}), bf16[64,48,384]{2,1,0:T(8,128)(2,1)S(1)}, u32[]{:S(2)}, u32[]{:S(2)}) async-start(bf16[64,48,384]{2,1,0:T(8,128)(2,1)} %copy-done), calls=%async_computation | async-start | bytes 4718592 | tf_op jit(solution)/shard_map/all_to_all | solution.py:299
  14.9 0.0 copy-start.5
  15.6 0.0 copy-done.6
  15.7 1.0 %collective-permute-start = (bf16[400,384]{1,0:T(8,128)(2,1)S(1)}, bf16[400,384]{1,0:T(8,128)(2,1)S(1)}, u32[]{:S(2)}, u32[]{:S(2)}) collective-permute-start(bf16[400,384]{1,0:T(8,128)(2,1)S(1)} %concatenate.3), channel_id=1, source_target_pairs={{0,1},{1,0},{2,3},{3,2},{4,5},{5,4},{6,7},{7,6},{8,9},{9,8},{10,11... | collective-permute-start | bytes 921608 | tf_op jit(solution)/shard_map/ppermute | solution.py:303
  16.7 1.2 %collective-permute-done.other_ref = bf16[400,384]{1,0:T(8,128)(2,1)S(1)} collective-permute-done((bf16[400,384]{1,0:T(8,128)(2,1)S(1)}, bf16[400,384]{1,0:T(8,128)(2,1)S(1)}, u32[]{:S(2)}, u32[]{:S(2)}) %collective-permute-start) | collective-permute-done | bytes 307232 | tf_op jit(solution)/shard_map/ppermute | solution.py:303
  18.0 0.7 copy-done.12
  18.7 0.0 copy-done.14
  18.7 0.0 copy-done.15
  18.7 0.0 copy-done.16
  18.7 0.0 copy-done.17
  18.7 0.0 copy-start.7
  18.7 1.0 %copy-done.7 = bf16[1,1,384,384]{3,2,1,0:T(8,128)(2,1)S(1)} copy-done((bf16[1,1,384,384]{3,2,1,0:T(8,128)(2,1)S(1)}, bf16[1,1,384,384]{3,2,1,0:T(8,128)(2,1)}, u32[]{:S(2)}) %copy-start.7) | copy-done | bytes 294936
  19.7 1.0 %copy-done.13 = bf16[400,384]{1,0:T(8,128)(2,1)S(1)} copy-done((bf16[400,384]{1,0:T(8,128)(2,1)S(1)}, bf16[400,384]{1,0:T(8,128)(2,1)}, u32[]{:S(2)}) %copy-start.13) | copy-done | bytes 307224
  20.6 1.3 %copy-done.18 = bf16[768,768]{1,0:T(8,128)(2,1)S(1)} copy-done((bf16[768,768]{1,0:T(8,128)(2,1)S(1)}, bf16[768,768]{1,0:T(8,128)(2,1)}, u32[]{:S(2)}) %copy-start.18) | copy-done | bytes 1179672
  21.9 1.0 %copy-done.19 = bf16[416,384]{1,0:T(8,128)(2,1)S(1)} copy-done((bf16[416,384]{1,0:T(8,128)(2,1)S(1)}, bf16[416,384]{1,0:T(8,128)(2,1)}, u32[]{:S(2)}) %copy-start.19) | copy-done | bytes 319512
  22.9 2.7 %tile.1 = (f32[2,2,208,384]{3,2,1,0:T(8,128)S(1)}, f32[2,208,384]{2,1,0:T(8,128)S(1)}, bf16[104,384]{1,0:T(8,128)(2,1)S(1)}) custom-call(s32[1]{0:T(128)} %bitcast.2.core_ref, s32[1,1]{1,0:T(1,128)S(6)} %copy.16.row_ref, f32[64]{0:T(128)S(1)} %copy-done.14, f32[64]{0:T(128)S(1)} %copy-done.15, f32[64]{0:T(128)S(1)} %copy-done.16, f32[64]{0:T(128)S(1)} %copy-done.17, ...), custom_call_target="tpu_custom_call" | custom-call | flops 736100352 | bytes 4194304 | tf_op jit(solution)/shard_map/tile/pallas_call | solution.py:305
  25.5 0.0 copy-start.1
  25.5 1.0 %copy-done.1 = f32[2,2,208,384]{3,2,1,0:T(8,128)} copy-done((f32[2,2,208,384]{3,2,1,0:T(8,128)}, f32[2,2,208,384]{3,2,1,0:T(8,128)S(1)}, u32[]{:S(2)}) %copy-start.1) | copy-done | bytes 1277976
  26.6 4.9 %collective-permute-start.7 = (bf16[104,384]{1,0:T(8,128)(2,1)S(1)}, bf16[104,384]{1,0:T(8,128)(2,1)S(1)}, u32[]{:S(2)}, u32[]{:S(2)}) collective-permute-start(bf16[104,384]{1,0:T(8,128)(2,1)S(1)} %get-tuple-element.10), channel_id=1, source_target_pairs={{0,14},{2,12},{4,2},{6,0},{8,6},{10,4},{12,10},{14,8},{1,15},{3,13... | collective-permute-start | bytes 239624 | tf_op jit(solution)/shard_map/ppermute | solution.py:341
  31.5 0.6 collective-permute-start.6
  32.1 0.2 collective-permute-start.5
  32.2 2.8 %collective-permute-start.4 = (bf16[104,384]{1,0:T(8,128)(2,1)S(1)}, bf16[104,384]{1,0:T(8,128)(2,1)S(1)}, u32[]{:S(2)}, u32[]{:S(2)}) collective-permute-start(bf16[104,384]{1,0:T(8,128)(2,1)S(1)} %get-tuple-element.10), channel_id=1, source_target_pairs={{0,8},{2,10},{4,12},{6,14},{8,0},{10,2},{12,4},{14,6},{1,9},{3,11}... | collective-permute-start | bytes 239624 | tf_op jit(solution)/shard_map/ppermute | solution.py:341
  35.0 3.3 %collective-permute-start.3 = (bf16[104,384]{1,0:T(8,128)(2,1)S(1)}, bf16[104,384]{1,0:T(8,128)(2,1)S(1)}, u32[]{:S(2)}, u32[]{:S(2)}) collective-permute-start(bf16[104,384]{1,0:T(8,128)(2,1)S(1)} %get-tuple-element.10), channel_id=1, source_target_pairs={{0,6},{2,4},{4,10},{6,8},{8,14},{10,12},{12,2},{14,0},{1,7},{3,5},... | collective-permute-start | bytes 239624 | tf_op jit(solution)/shard_map/ppermute | solution.py:341
  38.3 6.6 %collective-permute-done.7 = bf16[104,384]{1,0:T(8,128)(2,1)S(1)} collective-permute-done((bf16[104,384]{1,0:T(8,128)(2,1)S(1)}, bf16[104,384]{1,0:T(8,128)(2,1)S(1)}, u32[]{:S(2)}, u32[]{:S(2)}) %collective-permute-start.7) | collective-permute-done | bytes 79904 | tf_op jit(solution)/shard_map/ppermute | solution.py:341
  45.0 1.5 %collective-permute-start.2 = (bf16[104,384]{1,0:T(8,128)(2,1)S(1)}, bf16[104,384]{1,0:T(8,128)(2,1)S(1)}, u32[]{:S(2)}, u32[]{:S(2)}) collective-permute-start(bf16[104,384]{1,0:T(8,128)(2,1)S(1)} %get-tuple-element.10), channel_id=1, source_target_pairs={{0,4},{2,6},{4,8},{6,10},{8,12},{10,14},{12,0},{14,2},{1,5},{3,7},... | collective-permute-start | bytes 239624 | tf_op jit(solution)/shard_map/ppermute | solution.py:341
  46.4 3.4 %collective-permute-done.6 = bf16[104,384]{1,0:T(8,128)(2,1)S(1)} collective-permute-done((bf16[104,384]{1,0:T(8,128)(2,1)S(1)}, bf16[104,384]{1,0:T(8,128)(2,1)S(1)}, u32[]{:S(2)}, u32[]{:S(2)}) %collective-permute-start.6) | collective-permute-done | bytes 79904 | tf_op jit(solution)/shard_map/ppermute | solution.py:341
  49.9 1.5 %collective-permute-start.1 = (bf16[104,384]{1,0:T(8,128)(2,1)S(1)}, bf16[104,384]{1,0:T(8,128)(2,1)S(1)}, u32[]{:S(2)}, u32[]{:S(2)}) collective-permute-start(bf16[104,384]{1,0:T(8,128)(2,1)S(1)} %get-tuple-element.10), channel_id=1, source_target_pairs={{0,2},{2,0},{4,6},{6,4},{8,10},{10,8},{12,14},{14,12},{1,3},{3,1},... | collective-permute-start | bytes 239624 | tf_op jit(solution)/shard_map/ppermute | solution.py:341
  51.4 0.0 collective-permute-done.5
  51.4 0.6 collective-permute-done.4
  52.0 0.0 collective-permute-done.3
  52.0 0.5 collective-permute-done.2
  52.4 2.2 %collective-permute-done.1 = bf16[104,384]{1,0:T(8,128)(2,1)S(1)} collective-permute-done((bf16[104,384]{1,0:T(8,128)(2,1)S(1)}, bf16[104,384]{1,0:T(8,128)(2,1)S(1)}, u32[]{:S(2)}, u32[]{:S(2)}) %collective-permute-start.1) | collective-permute-done | bytes 79904 | tf_op jit(solution)/shard_map/ppermute | solution.py:341
  54.6 0.1 add_convert_fusion
  54.7 0.0 copy-start.20
  54.7 1.9 %collective-permute-start.8 = (bf16[104,384]{1,0:T(8,128)(2,1)S(1)}, bf16[104,384]{1,0:T(8,128)(2,1)}, u32[]{:S(2)}, u32[]{:S(2)}) collective-permute-start(bf16[104,384]{1,0:T(8,128)(2,1)S(1)} %add_convert_fusion), channel_id=1, source_target_pairs={{0,1},{1,0},{2,3},{3,2},{4,5},{5,4},{6,7},{7,6},{8,9},{9,8},{10,11... | collective-permute-start | bytes 239624 | tf_op jit(solution)/shard_map/ppermute | solution.py:343
  56.7 0.0 copy-done.20
  56.7 1.0 %collective-permute-done.8 = bf16[104,384]{1,0:T(8,128)(2,1)} collective-permute-done((bf16[104,384]{1,0:T(8,128)(2,1)S(1)}, bf16[104,384]{1,0:T(8,128)(2,1)}, u32[]{:S(2)}, u32[]{:S(2)}) %collective-permute-start.8) | collective-permute-done | bytes 79904 | tf_op jit(solution)/shard_map/ppermute | solution.py:343
  57.7 0.9 %broadcast_select_fusion = (bf16[104,384]{1,0:T(8,128)(2,1)S(1)}, bf16[104,384]{1,0:T(8,128)(2,1)S(1)}) fusion(bf16[104,384]{1,0:T(8,128)(2,1)} %collective-permute-done.8, bf16[104,384]{1,0:T(8,128)(2,1)} %copy-done.20, pred[]{:T(512)S(6)} %eq.4), kind=kLoop, calls=%fused_computation.1 | loop fusion | flops 79872 | bytes 319489 | tf_op jit(solution)/shard_map/jit(_where)/select_n | solution.py:345
  58.7 0.0 all-to-all-done
  58.7 0.0 copy-done.5
  58.7 0.0 copy-start.9
  58.7 0.9 %copy-done.9 = bf16[256,256]{1,0:T(8,128)(2,1)S(1)} copy-done((bf16[256,256]{1,0:T(8,128)(2,1)S(1)}, bf16[256,256]{1,0:T(8,128)(2,1)}, u32[]{:S(2)}) %copy-start.9) | copy-done | bytes 131096
  59.6 0.8 %copy-done.10 = bf16[160,128]{1,0:T(8,128)(2,1)S(1)} copy-done((bf16[160,128]{1,0:T(8,128)(2,1)S(1)}, bf16[160,128]{1,0:T(8,128)(2,1)}, u32[]{:S(2)}) %copy-start.10) | copy-done | bytes 40984
  60.4 4.5 %library.1.lib_ref = bf16[8,2,208,384]{3,2,1,0:T(8,128)(2,1)S(1)} custom-call(bf16[8,8,48,384]{3,2,1,0:T(8,128)(2,1)S(1)} %bitcast.6, bf16[160,128]{1,0:T(8,128)(2,1)S(1)} %copy-done.10, bf16[256,256]{1,0:T(8,128)(2,1)S(1)} %copy-done.9, bf16[3,256,256]{2,1,0:T(8,128)(2,1)S(1)} %copy-done.5), custom_call_target="tpu_custom_call" | custom-call | flops 1308622848 | bytes 5242880 | tf_op jit(solution)/shard_map/library/pallas_call | solution.py:348
  64.9 0.0 copy-done.2
  64.9 0.0 copy-done.3
  64.9 0.0 copy-done.4
  64.9 5.4 %other.1 = bf16[2,208,384]{2,1,0:T(8,128)(2,1)S(1)} custom-call(bf16[8,2,208,384]{3,2,1,0:T(8,128)(2,1)S(1)} %library.1.lib_ref, f32[2,2,208,384]{3,2,1,0:T(8,128)S(1)} %copy-done.2, f32[2,208,384]{2,1,0:T(8,128)S(1)} %get-tuple-element.9.weight_ref, bf16[104,384]{1,0:T(8,128)(2,1)S(1)} %get-tuple-element.12.low_ref, ...), custom_call_target="tpu_custom_call" | custom-call | flops 1308622848 | bytes 4194304 | tf_op jit(solution)/shard_map/other/pallas_call | solution.py:360
  70.3 0.0 copy-start.8
  70.3 0.4 collective-permute-start.9
  70.7 5.4 %own.1.best_ref = f32[2,208,384]{2,1,0:T(8,128)S(1)} custom-call(bf16[8,2,208,384]{3,2,1,0:T(8,128)(2,1)S(1)} %library.1.lib_ref, f32[2,2,208,384]{3,2,1,0:T(8,128)S(1)} %copy-done.2, f32[2,208,384]{2,1,0:T(8,128)S(1)} %get-tuple-element.9.weight_ref, bf16[104,384]{1,0:T(8,128)(2,1)S(1)} %get-tuple-element.12.low_ref, ...), custom_call_target="tpu_custom_call" | custom-call | flops 1308622848 | bytes 4194304 | tf_op jit(solution)/shard_map/own/pallas_call | solution.py:360
  76.1 0.0 collective-permute-done.9.got_ref
  76.1 0.0 copy-done.8
  76.1 1.3 %join.1 = f32[384,384]{1,0:T(8,128)} custom-call(f32[2,208,384]{2,1,0:T(8,128)S(1)} %own.1.best_ref, bf16[2,208,384]{2,1,0:T(8,128)(2,1)S(1)} %collective-permute-done.9.got_ref, bf16[192,416]{1,0:T(8,128)(2,1)S(1)} %copy-done.8), custom_call_target="tpu_custom_call" | custom-call | flops 184025088 | bytes 2097152 | tf_op jit(solution)/shard_map/join/pallas_call | solution.py:384
  (9 shorter events, 0.0 us)
Async XLA Ops:
  0.0 0.8 copy-start.11
  1.4 1.4 %copy-start = (bf16[64,48,384]{2,1,0:T(8,128)(2,1)}, bf16[64,48,384]{2,1,0:T(8,128)(2,1)S(1)}, u32[]{:S(2)}) copy-start(bf16[64,48,384]{2,1,0:T(8,128)(2,1)S(1)} %copies.1) | copy-start | bytes 7077892
  2.8 12.9 %copy-start.6 = (bf16[1,1,384,384]{3,2,1,0:T(8,128)(2,1)S(1)}, bf16[1,1,384,384]{3,2,1,0:T(8,128)(2,1)}, u32[]{:S(2)}) copy-start(bf16[1,1,384,384]{3,2,1,0:T(8,128)(2,1)} %param.15) | copy-start | bytes 884740
  2.8 15.9 %copy-start.14 = (f32[64]{0:T(128)S(1)}, f32[64]{0:T(128)}, u32[]{:S(2)}) copy-start(f32[64]{0:T(128)} %d_ref.1) | copy-start | bytes 772
  2.8 15.9 %copy-start.15 = (f32[64]{0:T(128)S(1)}, f32[64]{0:T(128)}, u32[]{:S(2)}) copy-start(f32[64]{0:T(128)} %a_ref.1) | copy-start | bytes 772
  2.8 15.9 %copy-start.16 = (f32[64]{0:T(128)S(1)}, f32[64]{0:T(128)}, u32[]{:S(2)}) copy-start(f32[64]{0:T(128)} %x_ref.1) | copy-start | bytes 772
  2.8 15.9 %copy-start.17 = (f32[64]{0:T(128)S(1)}, f32[64]{0:T(128)}, u32[]{:S(2)}) copy-start(f32[64]{0:T(128)} %p_ref.1) | copy-start | bytes 772
  2.8 55.9 %all-to-all-start = ((bf16[64,48,384]{2,1,0:T(8,128)(2,1)}), bf16[64,48,384]{2,1,0:T(8,128)(2,1)S(1)}, u32[]{:S(2)}, u32[]{:S(2)}) async-start(bf16[64,48,384]{2,1,0:T(8,128)(2,1)} %copy-done), calls=%async_computation | async-start | bytes 4718592 | tf_op jit(solution)/shard_map/all_to_all | solution.py:299
  14.9 43.7 %copy-start.5 = (bf16[3,256,256]{2,1,0:T(8,128)(2,1)S(1)}, bf16[3,256,256]{2,1,0:T(8,128)(2,1)}, u32[]{:S(2)}) copy-start(bf16[3,256,256]{2,1,0:T(8,128)(2,1)} %constant.26.clone.ahead_ref) | copy-start | bytes 1179652
  15.7 2.3 %collective-permute-start = (bf16[400,384]{1,0:T(8,128)(2,1)S(1)}, bf16[400,384]{1,0:T(8,128)(2,1)S(1)}, u32[]{:S(2)}, u32[]{:S(2)}) collective-permute-start(bf16[400,384]{1,0:T(8,128)(2,1)S(1)} %concatenate.3), channel_id=1, source_target_pairs={{0,1},{1,0},{2,3},{3,2},{4,5},{5,4},{6,7},{7,6},{8,9},{9,8},{10,11... | collective-permute-start | bytes 921608 | tf_op jit(solution)/shard_map/ppermute | solution.py:303
  18.0 0.7 copy-start.12
  18.7 1.0 %copy-start.7 = (bf16[1,1,384,384]{3,2,1,0:T(8,128)(2,1)S(1)}, bf16[1,1,384,384]{3,2,1,0:T(8,128)(2,1)}, u32[]{:S(2)}) copy-start(bf16[1,1,384,384]{3,2,1,0:T(8,128)(2,1)} %param.15) | copy-start | bytes 884740
  19.7 1.0 %copy-start.13 = (bf16[400,384]{1,0:T(8,128)(2,1)S(1)}, bf16[400,384]{1,0:T(8,128)(2,1)}, u32[]{:S(2)}) copy-start(bf16[400,384]{1,0:T(8,128)(2,1)} %copy-done.12) | copy-start | bytes 921604
  20.6 1.3 %copy-start.18 = (bf16[768,768]{1,0:T(8,128)(2,1)S(1)}, bf16[768,768]{1,0:T(8,128)(2,1)}, u32[]{:S(2)}) copy-start(bf16[768,768]{1,0:T(8,128)(2,1)} %constant.23.clone.forward_ref) | copy-start | bytes 3538948
  21.9 1.0 %copy-start.19 = (bf16[416,384]{1,0:T(8,128)(2,1)S(1)}, bf16[416,384]{1,0:T(8,128)(2,1)}, u32[]{:S(2)}) copy-start(bf16[416,384]{1,0:T(8,128)(2,1)} %constant.22.clone.first_ref) | copy-start | bytes 958468
  25.5 1.1 %copy-start.1 = (f32[2,2,208,384]{3,2,1,0:T(8,128)}, f32[2,2,208,384]{3,2,1,0:T(8,128)S(1)}, u32[]{:S(2)}) copy-start(f32[2,2,208,384]{3,2,1,0:T(8,128)S(1)} %get-tuple-element.8.spec_ref) | copy-start | bytes 3833860
  26.6 18.4 %collective-permute-start.7 = (bf16[104,384]{1,0:T(8,128)(2,1)S(1)}, bf16[104,384]{1,0:T(8,128)(2,1)S(1)}, u32[]{:S(2)}, u32[]{:S(2)}) collective-permute-start(bf16[104,384]{1,0:T(8,128)(2,1)S(1)} %get-tuple-element.10), channel_id=1, source_target_pairs={{0,14},{2,12},{4,2},{6,0},{8,6},{10,4},{12,10},{14,8},{1,15},{3,13... | collective-permute-start | bytes 239624 | tf_op jit(solution)/shard_map/ppermute | solution.py:341
  31.5 18.4 %collective-permute-start.6 = (bf16[104,384]{1,0:T(8,128)(2,1)S(1)}, bf16[104,384]{1,0:T(8,128)(2,1)S(1)}, u32[]{:S(2)}, u32[]{:S(2)}) collective-permute-start(bf16[104,384]{1,0:T(8,128)(2,1)S(1)} %get-tuple-element.10), channel_id=1, source_target_pairs={{0,12},{2,14},{4,0},{6,2},{8,4},{10,6},{12,8},{14,10},{1,13},{3,15... | collective-permute-start | bytes 239624 | tf_op jit(solution)/shard_map/ppermute | solution.py:341
  32.1 19.3 %collective-permute-start.5 = (bf16[104,384]{1,0:T(8,128)(2,1)S(1)}, bf16[104,384]{1,0:T(8,128)(2,1)S(1)}, u32[]{:S(2)}, u32[]{:S(2)}) collective-permute-start(bf16[104,384]{1,0:T(8,128)(2,1)S(1)} %get-tuple-element.10), channel_id=1, source_target_pairs={{0,10},{2,8},{4,14},{6,12},{8,2},{10,0},{12,6},{14,4},{1,11},{3,9}... | collective-permute-start | bytes 239624 | tf_op jit(solution)/shard_map/ppermute | solution.py:341
  32.2 19.7 %collective-permute-start.4 = (bf16[104,384]{1,0:T(8,128)(2,1)S(1)}, bf16[104,384]{1,0:T(8,128)(2,1)S(1)}, u32[]{:S(2)}, u32[]{:S(2)}) collective-permute-start(bf16[104,384]{1,0:T(8,128)(2,1)S(1)} %get-tuple-element.10), channel_id=1, source_target_pairs={{0,8},{2,10},{4,12},{6,14},{8,0},{10,2},{12,4},{14,6},{1,9},{3,11}... | collective-permute-start | bytes 239624 | tf_op jit(solution)/shard_map/ppermute | solution.py:341
  35.0 16.9 %collective-permute-start.3 = (bf16[104,384]{1,0:T(8,128)(2,1)S(1)}, bf16[104,384]{1,0:T(8,128)(2,1)S(1)}, u32[]{:S(2)}, u32[]{:S(2)}) collective-permute-start(bf16[104,384]{1,0:T(8,128)(2,1)S(1)} %get-tuple-element.10), channel_id=1, source_target_pairs={{0,6},{2,4},{4,10},{6,8},{8,14},{10,12},{12,2},{14,0},{1,7},{3,5},... | collective-permute-start | bytes 239624 | tf_op jit(solution)/shard_map/ppermute | solution.py:341
  45.0 7.5 %collective-permute-start.2 = (bf16[104,384]{1,0:T(8,128)(2,1)S(1)}, bf16[104,384]{1,0:T(8,128)(2,1)S(1)}, u32[]{:S(2)}, u32[]{:S(2)}) collective-permute-start(bf16[104,384]{1,0:T(8,128)(2,1)S(1)} %get-tuple-element.10), channel_id=1, source_target_pairs={{0,4},{2,6},{4,8},{6,10},{8,12},{10,14},{12,0},{14,2},{1,5},{3,7},... | collective-permute-start | bytes 239624 | tf_op jit(solution)/shard_map/ppermute | solution.py:341
  49.9 4.8 %collective-permute-start.1 = (bf16[104,384]{1,0:T(8,128)(2,1)S(1)}, bf16[104,384]{1,0:T(8,128)(2,1)S(1)}, u32[]{:S(2)}, u32[]{:S(2)}) collective-permute-start(bf16[104,384]{1,0:T(8,128)(2,1)S(1)} %get-tuple-element.10), channel_id=1, source_target_pairs={{0,2},{2,0},{4,6},{6,4},{8,10},{10,8},{12,14},{14,12},{1,3},{3,1},... | collective-permute-start | bytes 239624 | tf_op jit(solution)/shard_map/ppermute | solution.py:341
  54.7 2.0 %copy-start.20 = (bf16[104,384]{1,0:T(8,128)(2,1)}, bf16[104,384]{1,0:T(8,128)(2,1)S(1)}, u32[]{:S(2)}) copy-start(bf16[104,384]{1,0:T(8,128)(2,1)S(1)} %add_convert_fusion) | copy-start | bytes 239620
  54.7 3.0 %collective-permute-start.8 = (bf16[104,384]{1,0:T(8,128)(2,1)S(1)}, bf16[104,384]{1,0:T(8,128)(2,1)}, u32[]{:S(2)}, u32[]{:S(2)}) collective-permute-start(bf16[104,384]{1,0:T(8,128)(2,1)S(1)} %add_convert_fusion), channel_id=1, source_target_pairs={{0,1},{1,0},{2,3},{3,2},{4,5},{5,4},{6,7},{7,6},{8,9},{9,8},{10,11... | collective-permute-start | bytes 239624 | tf_op jit(solution)/shard_map/ppermute | solution.py:343
  58.7 0.9 %copy-start.9 = (bf16[256,256]{1,0:T(8,128)(2,1)S(1)}, bf16[256,256]{1,0:T(8,128)(2,1)}, u32[]{:S(2)}) copy-start(bf16[256,256]{1,0:T(8,128)(2,1)} %constant.25.clone.pair_ref) | copy-start | bytes 393220
  59.6 0.8 %copy-start.10 = (bf16[160,128]{1,0:T(8,128)(2,1)S(1)}, bf16[160,128]{1,0:T(8,128)(2,1)}, u32[]{:S(2)}) copy-start(bf16[160,128]{1,0:T(8,128)(2,1)} %constant.24.clone.real_ref) | copy-start | bytes 122884
  60.4 4.5 %copy-start.2 = (f32[2,2,208,384]{3,2,1,0:T(8,128)S(1)}, f32[2,2,208,384]{3,2,1,0:T(8,128)}, u32[]{:S(2)}) copy-start(f32[2,2,208,384]{3,2,1,0:T(8,128)} %copy-done.1) | copy-start | bytes 3833860
  60.4 4.5 %copy-start.3 = (bf16[3,256,256]{2,1,0:T(8,128)(2,1)S(1)}, bf16[3,256,256]{2,1,0:T(8,128)(2,1)}, u32[]{:S(2)}) copy-start(bf16[3,256,256]{2,1,0:T(8,128)(2,1)} %constant.27.clone.back_ref) | copy-start | bytes 1179652
  60.4 4.5 %copy-start.4 = (bf16[2,208,208]{2,1,0:T(8,128)(2,1)S(1)}, bf16[2,208,208]{2,1,0:T(8,128)(2,1)}, u32[]{:S(2)}) copy-start(bf16[2,208,208]{2,1,0:T(8,128)(2,1)} %constant.28.clone.fold_ref) | copy-start | bytes 519172
  70.3 5.8 %copy-start.8 = (bf16[192,416]{1,0:T(8,128)(2,1)S(1)}, bf16[192,416]{1,0:T(8,128)(2,1)}, u32[]{:S(2)}) copy-start(bf16[192,416]{1,0:T(8,128)(2,1)} %constant.29.clone.unfold_ref) | copy-start | bytes 479236
  70.3 5.8 %collective-permute-start.9 = (bf16[2,208,384]{2,1,0:T(8,128)(2,1)S(1)}, bf16[2,208,384]{2,1,0:T(8,128)(2,1)S(1)}, u32[]{:S(2)}, u32[]{:S(2)}) collective-permute-start(bf16[2,208,384]{2,1,0:T(8,128)(2,1)S(1)} %other.1), channel_id=1, source_target_pairs={{0,1},{1,0},{2,3},{3,2},{4,5},{5,4},{6,7},{7,6},{8,9},{9,8},{10,11... | collective-permute-start | bytes 958472 | tf_op jit(solution)/shard_map/ppermute | solution.py:382

commit v3 on v2

v3 whole, which is shorter than its diff:
```python
import functools
import math

import jax
import jax.numpy as jnp
import ml_dtypes
import numpy as np
from jax import lax
from jax.experimental import pallas as pl
from jax.experimental.pallas import tpu as pltpu
from jax.sharding import Mesh
from jax.sharding import PartitionSpec as P

DEF = ("xlo", "y")
BLK = ("z", "xhi", "core")
N = 384
HALF = N // 2
THIRD = N // 3
BLOCKS = (64, 64, 72)
ROWS = sum(BLOCKS)
ROOT = math.sqrt(3.0) / 2.0
F32 = jnp.float32
BF16 = jnp.bfloat16


def tables():
    j = np.arange(N)
    phase = (j[:, None] * j[None, :]) % N
    cos = np.cos(2.0 * np.pi * phase / N)
    sin = np.sin(2.0 * np.pi * phase / N)
    bf = ml_dtypes.bfloat16
    u = np.concatenate([3 * np.arange(b) + c for c, b in zip((1, 2, 0), BLOCKS)])
    keep = (u <= HALF)[:, None]
    u = np.minimum(u, HALF)
    r = np.arange(THIRD)
    b1, b2 = BLOCKS[0], BLOCKS[0] + BLOCKS[1]
    real = np.concatenate([(keep * cos[u])[b2:, r], (keep * -sin[u])[b2:, r]])
    c1, s1 = cos[u[:b1]][:, r], sin[u[:b1]][:, r]
    c2, s2 = cos[u[b1:b2]][:, r], sin[u[b1:b2]][:, r]
    pair = np.block([[c1, s1], [c2, -s2], [-s1, c1], [-s2, -c2]])
    ahead, back = [], []
    for k in range(3):
        ck = cos[r][:, 3 * r + k]
        sk = sin[r][:, 3 * r + k]
        ahead.append(np.block([[ck, -sk], [sk, ck]]))
        back.append(np.block([[ck.T, sk.T], [-sk.T, ck.T]]))
    ahead, back = np.stack(ahead), np.stack(back)
    weight = np.where((u == 0) | (u == HALF), 1.0, 2.0) * keep[:, 0]
    fold = np.zeros((2, ROWS, ROWS))
    fold[0, : HALF + 1] = cos[: HALF + 1][:, u].astype(bf).astype(float) * weight
    fold[1, : HALF + 1] = sin[: HALF + 1][:, u].astype(bf).astype(float) * weight
    unfold = np.zeros((HALF, 2 * ROWS))
    unfold[0, HALF] = 1.0
    for i in range(1, HALF):
        unfold[i, ROWS + HALF - i] = 1.0
    names = ("real", "pair", "ahead", "back", "fold", "unfold")
    arrays = (real, pair, ahead, back, fold, unfold)
    return {n: jnp.asarray(a.astype(bf)) for n, a in zip(names, arrays)}


def dot(a, b):
    return jnp.dot(a, b, preferred_element_type=F32)


def row_numbers():
    i = lax.broadcasted_iota(jnp.int32, (ROWS, N), 0)
    k = lax.broadcasted_iota(jnp.int32, (ROWS, N), 1)
    b1, b2 = BLOCKS[0], BLOCKS[0] + BLOCKS[1]
    u = jnp.where(i < b1, 3 * i + 1, jnp.where(i < b2, 3 * (i - b1) + 2, 3 * (i - b2)))
    v = jnp.where(
        k < THIRD, 3 * k, jnp.where(k < 2 * THIRD, 3 * (k - THIRD) + 1, 3 * (k - 2 * THIRD) + 2)
    )
    return u, v


def row_scale(u):
    return jnp.where((u > 0) & (u < HALF), 2.0, jnp.where(u <= HALF, 1.0, 0.0))


def spread(block_ref, out_ref, sems):
    moves = [
        pltpu.make_async_copy(block_ref, out_ref.at[i], sems.at[i]) for i in range(out_ref.shape[0])
    ]
    for move in moves:
        move.start()
    for move in moves:
        move.wait()


def copy_kernel(block_ref, out_ref, sems):
    spread(block_ref, out_ref, sems)


def sine(x):
    x = x - jnp.round(x)
    a = jnp.abs(x)
    a = jnp.minimum(a, 0.5 - a)
    s = a * a
    p = jnp.full_like(x, -15.0946425768229800)
    for c in (
        42.0586939448600400,
        -76.7058597530613900,
        81.6052492760750400,
        -41.3417022403997600,
        6.28318530717958648,
    ):
        p = p * s + c
    p = p * a
    return jnp.where(x < 0.0, -p, p)


def half_spectrum(image, real, pair, ahead):
    image = image.astype(F32)
    x0, x1, x2 = image[:THIRD], image[THIRD : 2 * THIRD], image[2 * THIRD :]
    plus, minus = x1 + x2, x1 - x2
    f0 = (x0 + plus).astype(BF16)
    f1 = jnp.concatenate([(x0 - 0.5 * plus).astype(BF16), (-ROOT * minus).astype(BF16)], axis=0)
    low = dot(real, f0)
    high = dot(pair, f1)
    b, c = BLOCKS[0] + BLOCKS[1], BLOCKS[2]
    re = jnp.concatenate([high[:b], low[:c]], axis=0)
    im = jnp.concatenate([high[b:], low[c:]], axis=0)
    r0, r1, r2 = re[:, :THIRD], re[:, THIRD : 2 * THIRD], re[:, 2 * THIRD :]
    i0, i1, i2 = im[:, :THIRD], im[:, THIRD : 2 * THIRD], im[:, 2 * THIRD :]
    rp, rm = r1 + r2, ROOT * (r1 - r2)
    ip, im_ = i1 + i2, ROOT * (i1 - i2)
    rh, ih = r0 - 0.5 * rp, i0 - 0.5 * ip
    parts = ((r0 + rp, i0 + ip), (rh + im_, ih - rm), (rh - im_, ih + rm))
    result = []
    for k, (a, b) in enumerate(parts):
        out = dot(jnp.concatenate([a.astype(BF16), b.astype(BF16)], axis=1), ahead[k])
        result.append((out[:, :THIRD], out[:, THIRD:]))
    return result


def store_spectrum(ref, parts):
    for k, (re, im) in enumerate(parts):
        at = slice(k * THIRD, (k + 1) * THIRD)
        ref[0, :, at] = re.astype(ref.dtype)
        ref[1, :, at] = im.astype(ref.dtype)


def own_kernel(image_ref, real_ref, pair_ref, ahead_ref, spec_ref):
    parts = half_spectrum(image_ref[...], real_ref[...], pair_ref[...], ahead_ref)
    store_spectrum(spec_ref, parts)


def other_kernel(image_ref, own_ref, real_ref, pair_ref, ahead_ref, spec_ref, power_ref):
    parts = half_spectrum(image_ref[...], real_ref[...], pair_ref[...], ahead_ref)
    store_spectrum(spec_ref, parts)
    for k, (re, im) in enumerate(parts):
        at = slice(k * THIRD, (k + 1) * THIRD)
        a, b = own_ref[0, :, at], own_ref[1, :, at]
        power_ref[:, at] = ((a * a + b * b) + (re * re + im * im)).astype(BF16)


def library_kernel(image_ref, real_ref, pair_ref, ahead_ref, spec_ref, out_ref, sems):
    image = image_ref[...].reshape(N, N)
    store_spectrum(spec_ref, half_spectrum(image, real_ref[...], pair_ref[...], ahead_ref))
    spread(spec_ref, out_ref, sems)


def whiten_kernel(
    row_ref,
    mate_ref,
    d_ref,
    a_ref,
    x_ref,
    p_ref,
    own_ref,
    other_ref,
    mine_ref,
    theirs_ref,
    spec_ref,
    weight_ref,
):
    u, v = row_numbers()
    scale = row_scale(u)
    power = (mine_ref[...].astype(F32) + theirs_ref[...].astype(F32)) * (1.0 / 16.0)
    mean = jnp.sum(power * scale) * (1.0 / (N * N))
    inverse_noise = 1.0 / (jnp.where(u <= HALF, power, 1.0) + 0.05 * mean)
    row = jnp.where(u < HALF, u, u - N).astype(F32) * (1.0 / N)
    col = jnp.where(v < HALF, v, v - N).astype(F32) * (1.0 / N)
    radial = row * row + col * col
    stretch = row * row - col * col
    skew = 2.0 * row * col
    inner = (u > 0) & (u < HALF)
    turn = 1.0 / (2.0 * math.pi)
    for t, r in enumerate((row_ref[0, 0], mate_ref[0, 0])):
        base = (d_ref[r] * turn) * radial + (a_ref[r] * turn) * stretch + p_ref[r] * turn
        cross = (x_ref[r] * turn) * skew
        plus = -sine(base + cross)
        minus = -sine(base - cross)
        mirror = jnp.where(inner & (v == HALF), minus, plus)
        gain = (0.5 * (plus + mirror)) * inverse_noise
        source = own_ref if t == 0 else other_ref
        spec_ref[t, 0] = source[0] * gain
        spec_ref[t, 1] = source[1] * gain
        weight_ref[t] = (0.5 * scale) * (plus * plus + mirror * mirror) * inverse_noise


def match_step(re, im, square, t, spec_ref, weight_ref, back_ref, fold_ref):
    norm = jnp.sum(square * weight_ref[t])
    scale = lax.rsqrt(jnp.full((1, THIRD), norm + 1e-06, F32))
    s_re, s_im = spec_ref[t, 0], spec_ref[t, 1]
    p_re = (s_re * re + s_im * im).astype(BF16)
    p_im = (s_im * re - s_re * im).astype(BF16)
    g = []
    for k in range(3):
        at = slice(k * THIRD, (k + 1) * THIRD)
        g.append(dot(jnp.concatenate([p_re[:, at], p_im[:, at]], axis=1), back_ref[k]))
    (r0, i0), (r1, i1), (r2, i2) = ((x[:, :THIRD], x[:, THIRD:]) for x in g)
    slant = scale * ROOT
    rp, rm = r1 + r2, slant * (r1 - r2)
    ip, im_ = i1 + i2, slant * (i1 - i2)
    rh, ih = scale * (r0 - 0.5 * rp), scale * (i0 - 0.5 * ip)
    h_re = [scale * (r0 + rp), rh - im_, rh + im_]
    h_im = [scale * (i0 + ip), ih + rm, ih - rm]
    h_re = jnp.concatenate([h.astype(BF16) for h in h_re], axis=1)
    h_im = jnp.concatenate([h.astype(BF16) for h in h_im], axis=1)
    even = dot(fold_ref[0], h_re)
    odd = dot(fold_ref[1], h_im)
    return even - odd, even + odd


def near_kernel(lib_ref, spec_ref, weight_ref, back_ref, fold_ref, out_ref):
    step = pl.program_id(0)

    @pl.when(step == 0)
    def _():
        out_ref[...] = jnp.full_like(out_ref, -jnp.inf)

    re = lib_ref[step, 0].astype(F32)
    im = lib_ref[step, 1].astype(F32)
    square = re * re + im * im
    for t in range(2):
        minus, plus = match_step(re, im, square, t, spec_ref, weight_ref, back_ref, fold_ref)
        out_ref[t, 0] = jnp.maximum(out_ref[t, 0], minus)
        out_ref[t, 1] = jnp.maximum(out_ref[t, 1], plus)


def far_kernel(t, lib_ref, spec_ref, weight_ref, back_ref, fold_ref, start_ref, out_ref, best_sc):
    step = pl.program_id(0)

    @pl.when(step == 0)
    def _():
        best_sc[...] = start_ref[t]

    re = lib_ref[step, 0].astype(F32)
    im = lib_ref[step, 1].astype(F32)
    square = re * re + im * im
    minus, plus = match_step(re, im, square, t, spec_ref, weight_ref, back_ref, fold_ref)
    best_sc[0] = jnp.maximum(best_sc[0], minus)
    best_sc[1] = jnp.maximum(best_sc[1], plus)

    @pl.when(step == pl.num_programs(0) - 1)
    def _():
        out_ref[...] = best_sc[...].astype(out_ref.dtype)


def join_kernel(best_ref, got_ref, unfold_ref, out_ref):
    best = jnp.maximum(best_ref[...], got_ref[...].astype(F32))
    out_ref[:HALF] = best[0, :HALF]
    rest = best.reshape(2 * ROWS, N)
    total = None
    for _ in range(3):
        part = rest.astype(BF16)
        rest = rest - part.astype(F32)
        moved = dot(unfold_ref[...], part)
        total = moved if total is None else total + moved
    out_ref[HALF:] = total


def vmem(count):
    return [pl.BlockSpec(memory_space=pltpu.VMEM)] * count


def smem(count):
    return [pl.BlockSpec(memory_space=pltpu.SMEM)] * count


def cost(flops, size):
    return pl.CostEstimate(flops=flops, bytes_accessed=size, transcendentals=0)


def params(mib):
    return pltpu.CompilerParams(vmem_limit_bytes=mib << 20)


def per_device(images, projections, ctf_row, defocus_term, astig_term, astig_cross, phase_shift):
    tab = tables()
    transform = (tab["real"], tab["pair"], tab["ahead"])
    groups = math.prod(lax.axis_size(a) for a in DEF)
    deep, wide = lax.axis_size("z"), lax.axis_size("xhi")
    core = lax.axis_index("core")
    swap = [(0, 1), (1, 0)]
    spectrum = pltpu.VMEM((2, ROWS, N), F32)
    work = 2 * ROWS * 768 * 256 * 2

    block = projections[0]
    image = lax.all_to_all(
        jnp.broadcast_to(block[None], (groups,) + block.shape), DEF, 0, 0, tiled=False
    )

    tile = images[0, 0]
    received = lax.ppermute(tile, "core", swap)
    own = pl.pallas_call(
        own_kernel,
        out_shape=spectrum,
        in_specs=vmem(4),
        out_specs=vmem(1)[0],
        compiler_params=params(16),
        cost_estimate=cost(work, 2 << 20),
        name="own_tile",
    )(tile, *transform)
    other, power = pl.pallas_call(
        other_kernel,
        out_shape=[spectrum, pltpu.VMEM((ROWS, N), BF16)],
        in_specs=vmem(5),
        out_specs=vmem(2),
        compiler_params=params(16),
        cost_estimate=cost(work, 2 << 20),
        name="other_tile",
    )(received, own, *transform)

    image, power = lax.optimization_barrier((image, power))

    sums = jnp.where(core == 0, power.astype(F32), 0.0)
    for dz in range(deep):
        perm = [
            ((z * wide + x) * 2 + c, ((z + dz) % deep * wide + (x ^ c)) * 2 + c)
            for z in range(deep)
            for x in range(wide)
            for c in range(2)
            if dz or c
        ]
        sums = sums + lax.ppermute(power, BLK, perm).astype(F32)
    mine = sums.astype(BF16)
    theirs = lax.ppermute(mine, "core", swap)
    mate = lax.ppermute(ctf_row, "core", swap)
    spec, weight = pl.pallas_call(
        whiten_kernel,
        out_shape=[pltpu.VMEM((2, 2, ROWS, N), F32), pltpu.VMEM((2, ROWS, N), F32)],
        in_specs=smem(6) + vmem(4),
        out_specs=vmem(2),
        compiler_params=params(16),
        cost_estimate=cost(2 * ROWS * N * 60, 4 << 20),
        name="whiten",
    )(ctf_row, mate, defocus_term, astig_term, astig_cross, phase_shift, own, other, mine, theirs)

    wide_shape = (deep, 2, ROWS, N)
    near, near_copies = pl.pallas_call(
        library_kernel,
        out_shape=[pltpu.VMEM((2, ROWS, N), BF16), pltpu.HBM(wide_shape, BF16)],
        in_specs=vmem(4),
        out_specs=[vmem(1)[0], pl.BlockSpec(memory_space=pltpu.HBM)],
        scratch_shapes=[pltpu.SemaphoreType.DMA((deep,))],
        compiler_params=params(16),
        cost_estimate=cost(work, 4 << 20),
        name="library",
    )(image, *transform)
    far, _ = lax.optimization_barrier((lax.ppermute(near, "xhi", swap), mine))
    near_all = lax.all_to_all(near_copies, "z", 0, 0, tiled=False)
    far_copies = pl.pallas_call(
        copy_kernel,
        out_shape=pltpu.HBM(wide_shape, BF16),
        in_specs=vmem(1),
        out_specs=pl.BlockSpec(memory_space=pltpu.HBM),
        scratch_shapes=[pltpu.SemaphoreType.DMA((deep,))],
        compiler_params=params(4),
        cost_estimate=cost(0, 3 << 20),
        name="copies",
    )(far)
    far_all = lax.all_to_all(far_copies, "z", 0, 0, tiled=False)

    near_best = pl.pallas_call(
        near_kernel,
        out_shape=pltpu.VMEM((2, 2, ROWS, N), F32),
        grid=(deep,),
        in_specs=vmem(5),
        out_specs=vmem(1)[0],
        compiler_params=params(16),
        cost_estimate=cost(2 * deep * 2 * work, 8 << 20),
        name="near",
    )(near_all, spec, weight, tab["back"], tab["fold"])
    far_all, near_best = lax.optimization_barrier((far_all, near_best))

    def match(t, dtype, name):
        return pl.pallas_call(
            functools.partial(far_kernel, t),
            out_shape=pltpu.VMEM((2, ROWS, N), dtype),
            grid=(deep,),
            in_specs=vmem(6),
            out_specs=vmem(1)[0],
            scratch_shapes=[pltpu.VMEM((2, ROWS, N), F32)],
            compiler_params=params(16),
            cost_estimate=cost(deep * 2 * work, 4 << 20),
            name=name,
        )(far_all, spec, weight, tab["back"], tab["fold"], near_best)

    got = lax.ppermute(match(1, BF16, "far_other"), "core", swap)
    best = match(0, F32, "far_own")
    peak = pl.pallas_call(
        join_kernel,
        out_shape=jax.ShapeDtypeStruct((N, N), F32),
        in_specs=vmem(3),
        out_specs=vmem(1)[0],
        compiler_params=params(16),
        cost_estimate=cost(3 * 2 * HALF * 2 * ROWS * N, 2 << 20),
        name="join",
    )(best, got, tab["unfold"])
    return peak[None, None]


def solution(mesh):
    fine = Mesh(mesh.devices.reshape(2, 4, 4, 2, 2), DEF + BLK)
    in_specs = (P(DEF, BLK, None, None), P(BLK, DEF, None), P(DEF, BLK), P(), P(), P(), P())
    out_specs = P(DEF, BLK, None, None)
    return jax.shard_map(
        per_device, mesh=fine, in_specs=in_specs, out_specs=out_specs, check_vma=False
    )
```

time: 78 us -> 75.6 us (0.969)
  waiting for transfers between devices: 15.6 us -> 8.72 us
  local copies, waits for them, and re-layouts: 9.87 us -> 14.5 us
  starting transfers between devices: 30.2 us -> 32.5 us
  Pallas kernels: 19.8 us -> 18 us
  other arithmetic: 1.03 us -> 0.11 us
    ppermute x9 -> x8, waiting for transfers between devices: 14.6 us -> 7.88 us  [the longest x4 4.22 us: per_device(): sums = sums + lax.ppermute(power, BLK, perm).astype(F32)]
    unnamed x42 -> x52, local copies, waits for them, and re-layouts: 9.84 us -> 13 us
    pallas_call x5 -> x8, Pallas kernels: 18.5 us -> 16.6 us  [the longest x2 5.19 us: match(): pl.pallas_call(functools.partial(far_kernel, t), out_shape=pltpu.VMEM((2,...]
    ppermute x1, starting transfers between devices: 1.94 us -> 3.62 us  [per_device(): theirs = lax.ppermute(mine, 'core', swap)]
    all_to_all x1 -> x3, starting transfers between devices: 12.1 us -> 13.8 us  [the longest x1 5.2 us: per_device(): lax.all_to_all(jnp.broadcast_to(block[None], (groups,) + block.shape), DE...]
    broadcast_in_dim x0 -> x1, local copies, waits for them, and re-layouts: none -> 1.51 us  [per_device(): jnp.broadcast_to(block[None], (groups,) + block.shape)]
    ppermute x1, waiting for transfers between devices: 1.05 us -> 0.01 us  [per_device(): theirs = lax.ppermute(mine, 'core', swap)]
    ppermute x9 -> x8, starting transfers between devices: 16.2 us -> 15.1 us  [the longest x4 10.8 us: per_device(): sums = sums + lax.ppermute(power, BLK, perm).astype(F32)]
  transfers between devices with their start and end apart: 11 -> 12, of which waited for: 7 -> 6; matrix products, arithmetic and copies ran while one was open for 1% -> 2% of each run, Pallas kernels for 10% -> 17%
where the time goes in v3:
time: 75.6 us; the launch traced here: 74.8 us
  starting transfers between devices  32.5 us (43%)
  Pallas kernels  18 us (24%)
  local copies, waits for them, and re-layouts  14.5 us (19%)
  waiting for transfers between devices  8.72 us (12%)
  between operations  0.93 us (1%)
    unnamed x52, local copies, waits for them, and re-layouts  13 us
    ppermute x4, starting transfers between devices, per_device(): sums = sums + lax.ppermute(power, BLK, perm).astype(F32)  10.8 us
    all_to_all x1, starting transfers between devices, per_device(): lax.all_to_all(jnp.broadcast_to(block[None], (groups,) + block.shape), DE...  5.2 us
    pallas_call x2, Pallas kernels, match(): pl.pallas_call(functools.partial(far_kernel, t), out_shape=pltpu.VMEM((2,...  5.19 us
    all_to_all x1, starting transfers between devices, per_device(): near_all = lax.all_to_all(near_copies, 'z', 0, 0, tiled=False)  5.04 us
    ppermute x4, waiting for transfers between devices, per_device(): sums = sums + lax.ppermute(power, BLK, perm).astype(F32)  4.22 us
    pallas_call x1, Pallas kernels, per_device(): pl.pallas_call(near_kernel, out_shape=pltpu.VMEM((2, 2, ROWS, N), F32), g...  4.08 us
    ppermute x1, starting transfers between devices, per_device(): theirs = lax.ppermute(mine, 'core', swap)  3.62 us
  transfers between devices with their start and end apart: 12, of which 6 were waited for; matrix products, arithmetic and copies ran while one was open for 2% of the time, Pallas kernels for 17%

profile of v3, /device:TPU:1, one launch (start us, length us, event | category | flops | bytes accessed | tf_op | source)
XLA Modules:
  0.0 74.8 jit_solution(1870996898248790381)
XLA Ops:
  0.0 1.4 %collective-permute-start = (bf16[384,384]{1,0:T(8,128)(2,1)}, bf16[384,384]{1,0:T(8,128)(2,1)S(1)}, u32[]{:S(2)}, u32[]{:S(2)}) collective-permute-start(bf16[384,384]{1,0:T(8,128)(2,1)} %bitcast.3), channel_id=1, source_target_pairs={{0,1},{1,0},{2,3},{3,2},{4,5},{5,4},{6,7},{7,6},{8,9},{9,8},{10,11... | collective-permute-start | bytes 884744 | tf_op jit(solution)/shard_map/ppermute | solution.py:306
  1.4 1.5 %broadcast_in_dim.15 = bf16[8,48,384]{2,1,0:T(8,128)(2,1)} broadcast(bf16[48,384]{1,0:T(8,128)(2,1)} %bitcast.5), dimensions={1,2} | broadcast | bytes 331776 | tf_op jit(solution)/shard_map/broadcast_in_dim | solution.py:302
  2.9 5.2 %all-to-all-start = ((bf16[8,48,384]{2,1,0:T(8,128)(2,1)}), bf16[8,48,384]{2,1,0:T(8,128)(2,1)S(1)}, u32[]{:S(2)}, u32[]{:S(2)}) async-start(bf16[8,48,384]{2,1,0:T(8,128)(2,1)} %broadcast_in_dim.15), calls=%async_computation | async-start | bytes 589824 | tf_op jit(solution)/shard_map/all_to_all | solution.py:301
  8.1 1.0 %copy-done.2 = bf16[3,256,256]{2,1,0:T(8,128)(2,1)S(1)} copy-done((bf16[3,256,256]{2,1,0:T(8,128)(2,1)S(1)}, bf16[3,256,256]{2,1,0:T(8,128)(2,1)}, u32[]{:S(2)}) %copy-start.2) | copy-done | bytes 393240
  9.1 0.9 %copy-done.9 = bf16[256,256]{1,0:T(8,128)(2,1)S(1)} copy-done((bf16[256,256]{1,0:T(8,128)(2,1)S(1)}, bf16[256,256]{1,0:T(8,128)(2,1)}, u32[]{:S(2)}) %copy-start.9) | copy-done | bytes 131096
  10.0 0.8 %copy-done.18 = bf16[144,128]{1,0:T(8,128)(2,1)S(1)} copy-done((bf16[144,128]{1,0:T(8,128)(2,1)S(1)}, bf16[144,128]{1,0:T(8,128)(2,1)}, u32[]{:S(2)}) %copy-start.18) | copy-done | bytes 36888
  10.8 1.0 %copy-done.20 = bf16[1,1,384,384]{3,2,1,0:T(8,128)(2,1)S(1)} copy-done((bf16[1,1,384,384]{3,2,1,0:T(8,128)(2,1)S(1)}, bf16[1,1,384,384]{3,2,1,0:T(8,128)(2,1)}, u32[]{:S(2)}) %copy-start.20) | copy-done | bytes 294936
  11.8 0.5 own_tile.1.own_ref
  12.3 0.0 collective-permute-done.image_ref
  12.3 0.5 other_tile.1
  12.9 0.0 copy-start.14
  12.9 0.8 %copy-done.14 = f32[2,200,384]{2,1,0:T(8,128)} copy-done((f32[2,200,384]{2,1,0:T(8,128)}, f32[2,200,384]{2,1,0:T(8,128)S(1)}, u32[]{:S(2)}) %copy-start.14) | copy-done | bytes 614424
  13.7 0.8 %all-to-all-done.image_ref = bf16[8,48,384]{2,1,0:T(8,128)(2,1)S(1)} async-done(((bf16[8,48,384]{2,1,0:T(8,128)(2,1)}), bf16[8,48,384]{2,1,0:T(8,128)(2,1)S(1)}, u32[]{:S(2)}, u32[]{:S(2)}) %all-to-all-start) | async-done | bytes 294944 | tf_op jit(solution)/shard_map/all_to_all | solution.py:301
  14.5 0.0 copy-done.3
  14.5 0.0 copy-done.10
  14.5 0.0 copy-done.19
  14.5 1.6 %library.1 = (bf16[2,200,384]{2,1,0:T(8,128)(2,1)S(1)}, bf16[4,2,200,384]{3,2,1,0:T(8,128)(2,1)}) custom-call(bf16[8,48,384]{2,1,0:T(8,128)(2,1)S(1)} %all-to-all-done.image_ref, bf16[144,128]{1,0:T(8,128)(2,1)S(1)} %copy-done.19, bf16[256,256]{1,0:T(8,128)(2,1)S(1)} %copy-done.10, bf16[3,256,256]{2,1,0:T(8,128)(2,1)S(1)} %copy-done.3), custom_call_target="tpu_custom_call" | custom-call | flops 157286400 | bytes 4194304 | tf_op jit(solution)/shard_map/library/pallas_call | solution.py:352
  16.2 5.0 %all-to-all-start.2 = ((bf16[4,2,200,384]{3,2,1,0:T(8,128)(2,1)}), bf16[4,2,200,384]{3,2,1,0:T(8,128)(2,1)S(1)}, u32[]{:S(2)}, u32[]{:S(2)}) async-start(bf16[4,2,200,384]{3,2,1,0:T(8,128)(2,1)} %get-tuple-element.21), calls=%async_computation.2 | async-start | bytes 2457600 | tf_op jit(solution)/shard_map/all_to_all | solution.py:363
  21.2 4.8 %collective-permute-start.5 = (bf16[200,384]{1,0:T(8,128)(2,1)S(1)}, bf16[200,384]{1,0:T(8,128)(2,1)S(1)}, u32[]{:S(2)}, u32[]{:S(2)}) collective-permute-start(bf16[200,384]{1,0:T(8,128)(2,1)S(1)} %get-tuple-element.19), channel_id=1, source_target_pairs={{0,12},{1,15},{2,14},{3,13},{4,0},{5,3},{6,2},{7,1},{8,4},{9,7},{1... | collective-permute-start | bytes 460808 | tf_op jit(solution)/shard_map/ppermute | solution.py:337
  26.0 0.8 %collective-permute-start.4 = (bf16[200,384]{1,0:T(8,128)(2,1)S(1)}, bf16[200,384]{1,0:T(8,128)(2,1)S(1)}, u32[]{:S(2)}, u32[]{:S(2)}) collective-permute-start(bf16[200,384]{1,0:T(8,128)(2,1)S(1)} %get-tuple-element.19), channel_id=1, source_target_pairs={{0,8},{1,11},{2,10},{3,9},{4,12},{5,15},{6,14},{7,13},{8,0},{9,3},... | collective-permute-start | bytes 460808 | tf_op jit(solution)/shard_map/ppermute | solution.py:337
  26.9 2.7 %collective-permute-start.3 = (bf16[200,384]{1,0:T(8,128)(2,1)S(1)}, bf16[200,384]{1,0:T(8,128)(2,1)S(1)}, u32[]{:S(2)}, u32[]{:S(2)}) collective-permute-start(bf16[200,384]{1,0:T(8,128)(2,1)S(1)} %get-tuple-element.19), channel_id=1, source_target_pairs={{0,4},{1,7},{2,6},{3,5},{4,8},{5,11},{6,10},{7,9},{8,12},{9,15},{1... | collective-permute-start | bytes 460808 | tf_op jit(solution)/shard_map/ppermute | solution.py:337
  29.6 2.4 %collective-permute-start.2 = (bf16[200,384]{1,0:T(8,128)(2,1)S(1)}, bf16[200,384]{1,0:T(8,128)(2,1)S(1)}, u32[]{:S(2)}, u32[]{:S(2)}) collective-permute-start(bf16[200,384]{1,0:T(8,128)(2,1)S(1)} %get-tuple-element.19), channel_id=1, source_target_pairs={{1,3},{3,1},{5,7},{7,5},{9,11},{11,9},{13,15},{15,13},{17,19},{19,... | collective-permute-start | bytes 460808 | tf_op jit(solution)/shard_map/ppermute | solution.py:337
  32.1 2.5 %collective-permute-start.1 = (bf16[2,200,384]{2,1,0:T(8,128)(2,1)S(1)}, bf16[2,200,384]{2,1,0:T(8,128)(2,1)S(1)}, u32[]{:S(2)}, u32[]{:S(2)}) collective-permute-start(bf16[2,200,384]{2,1,0:T(8,128)(2,1)S(1)} %get-tuple-element.18), channel_id=1, source_target_pairs={{0,2},{2,0},{1,3},{3,1},{4,6},{6,4},{5,7},{7,5},{8,10},{10,8},{9,1... | collective-permute-start | bytes 921608 | tf_op jit(solution)/shard_map/ppermute | solution.py:362
  34.6 0.0 collective-permute-done.5
  34.6 0.9 %collective-permute-done.4 = bf16[200,384]{1,0:T(8,128)(2,1)S(1)} collective-permute-done((bf16[200,384]{1,0:T(8,128)(2,1)S(1)}, bf16[200,384]{1,0:T(8,128)(2,1)S(1)}, u32[]{:S(2)}, u32[]{:S(2)}) %collective-permute-start.4) | collective-permute-done | bytes 153632 | tf_op jit(solution)/shard_map/ppermute | solution.py:337
  35.5 0.4 collective-permute-done.3
  35.8 3.0 %collective-permute-done.2 = bf16[200,384]{1,0:T(8,128)(2,1)S(1)} collective-permute-done((bf16[200,384]{1,0:T(8,128)(2,1)S(1)}, bf16[200,384]{1,0:T(8,128)(2,1)S(1)}, u32[]{:S(2)}, u32[]{:S(2)}) %collective-permute-start.2) | collective-permute-done | bytes 153632 | tf_op jit(solution)/shard_map/ppermute | solution.py:337
  38.8 0.1 add_convert_fusion.mine_ref
  38.9 0.0 copy-start.16
  38.9 3.2 %collective-permute-done.1.block_ref = bf16[2,200,384]{2,1,0:T(8,128)(2,1)S(1)} collective-permute-done((bf16[2,200,384]{2,1,0:T(8,128)(2,1)S(1)}, bf16[2,200,384]{2,1,0:T(8,128)(2,1)S(1)}, u32[]{:S(2)}, u32[]{:S(2)}) %collective-permute-start.1) | collective-permute-done | bytes 307232 | tf_op jit(solution)/shard_map/ppermute | solution.py:362
  42.1 1.1 %copies.1 = bf16[4,2,200,384]{3,2,1,0:T(8,128)(2,1)} custom-call(bf16[2,200,384]{2,1,0:T(8,128)(2,1)S(1)} %collective-permute-done.1.block_ref), custom_call_target="tpu_custom_call" | custom-call | bytes 3145728 | tf_op jit(solution)/shard_map/copies/pallas_call | solution.py:364
  43.2 0.0 copy-start.22
  43.2 0.0 copy-start.23
  43.2 0.0 copy-start.24
  43.2 0.0 copy-start.25
  43.2 0.0 all-to-all-done.2.lib_ref
  43.2 1.0 %copy-done.7 = bf16[4,2,200,384]{3,2,1,0:T(8,128)(2,1)} copy-done((bf16[4,2,200,384]{3,2,1,0:T(8,128)(2,1)}, bf16[4,2,200,384]{3,2,1,0:T(8,128)(2,1)S(1)}, u32[]{:S(2)}) %copy-start.7) | copy-done | bytes 1228824
  44.3 3.5 %all-to-all-start.1 = ((bf16[4,2,200,384]{3,2,1,0:T(8,128)(2,1)}), bf16[4,2,200,384]{3,2,1,0:T(8,128)(2,1)S(1)}, u32[]{:S(2)}, u32[]{:S(2)}) async-start(bf16[4,2,200,384]{3,2,1,0:T(8,128)(2,1)} %copies.1), calls=%async_computation.1 | async-start | bytes 2457600 | tf_op jit(solution)/shard_map/all_to_all | solution.py:374
  47.8 0.0 copy-start.6
  47.8 0.0 copy-start.11
  47.8 3.6 %collective-permute-start.7 = (bf16[200,384]{1,0:T(8,128)(2,1)S(1)}, bf16[200,384]{1,0:T(8,128)(2,1)S(1)}, u32[]{:S(2)}, u32[]{:S(2)}) collective-permute-start(bf16[200,384]{1,0:T(8,128)(2,1)S(1)} %add_convert_fusion.mine_ref), channel_id=1, source_target_pairs={{0,1},{1,0},{2,3},{3,2},{4,5},{5,4},{6,7},{7,6},{8,9},{9,8},{10,11... | collective-permute-start | bytes 460808 | tf_op jit(solution)/shard_map/ppermute | solution.py:339
  51.5 0.1 collective-permute-start.6
  52.2 0.5 collective-permute-done.6.mate_ref
  52.7 0.0 collective-permute-done.7.theirs_ref
  52.7 1.1 %copy-done.15 = f32[2,200,384]{2,1,0:T(8,128)S(1)} copy-done((f32[2,200,384]{2,1,0:T(8,128)S(1)}, f32[2,200,384]{2,1,0:T(8,128)}, u32[]{:S(2)}) %copy-start.15) | copy-done | bytes 614424
  53.8 0.9 %copy-done.17 = bf16[200,384]{1,0:T(8,128)(2,1)S(1)} copy-done((bf16[200,384]{1,0:T(8,128)(2,1)S(1)}, bf16[200,384]{1,0:T(8,128)(2,1)}, u32[]{:S(2)}) %copy-start.17) | copy-done | bytes 153624
  54.7 3.6 %whiten.1 = (f32[2,2,200,384]{3,2,1,0:T(8,128)S(1)}, f32[2,200,384]{2,1,0:T(8,128)S(1)}) custom-call(s32[1,1]{1,0:T(1,128)S(6)} %copy.14.row_ref, s32[1,1]{1,0:T(1,128)} %collective-permute-done.6.mate_ref, f32[64]{0:T(128)S(1)} %copy-done.22, f32[64]{0:T(128)S(1)} %copy-done.23, f32[64]{0:T(128)S(1)} %copy-done.24, f32[64]{0:T(128)S(1)} %copy-done.25, ...), custom_call_target="tpu_custom_call" | custom-call | flops 9216000 | bytes 4194304 | tf_op jit(solution)/shard_map/whiten/pallas_call | solution.py:341
  58.3 0.0 copy-done.6
  58.3 0.0 copy-done.11
  58.3 0.0 copy-start.8
  58.3 1.3 %copy-done.8 = bf16[4,2,200,384]{3,2,1,0:T(8,128)(2,1)S(1)} copy-done((bf16[4,2,200,384]{3,2,1,0:T(8,128)(2,1)S(1)}, bf16[4,2,200,384]{3,2,1,0:T(8,128)(2,1)}, u32[]{:S(2)}) %copy-start.8) | copy-done | bytes 1228824
  59.6 4.1 %near.1.start_ref = f32[2,2,200,384]{3,2,1,0:T(8,128)S(1)} custom-call(bf16[4,2,200,384]{3,2,1,0:T(8,128)(2,1)S(1)} %copy-done.8, f32[2,2,200,384]{3,2,1,0:T(8,128)S(1)} %get-tuple-element.23.spec_ref, f32[2,200,384]{2,1,0:T(8,128)S(1)} %get-tuple-element.24.weight_ref, bf16[3,256,256]{2,1,0:T(8,128)(2,1)S(1)} %copy-done.6, bf16[2,200,200]{2,1,0:T(8,128)(2,1)S(1)} %copy-done.11), custom_call_target="tpu_custom_call" | custom-call | flops 2516582400 | bytes 8388608 | tf_op jit(solution)/shard_map/near/pallas_call | solution.py:376
  63.7 1.0 %copy-done = f32[2,2,200,384]{3,2,1,0:T(8,128)} copy-done((f32[2,2,200,384]{3,2,1,0:T(8,128)}, f32[2,2,200,384]{3,2,1,0:T(8,128)S(1)}, u32[]{:S(2)}) %copy-start) | copy-done | bytes 1228824
  64.8 0.8 %copy-done.4 = f32[2,200,384]{2,1,0:T(8,128)} copy-done((f32[2,200,384]{2,1,0:T(8,128)}, f32[2,200,384]{2,1,0:T(8,128)S(1)}, u32[]{:S(2)}) %copy-start.4) | copy-done | bytes 614424
  65.6 0.0 all-to-all-done.1.lib_ref
  65.6 1.3 %copy-done.1 = f32[2,2,200,384]{3,2,1,0:T(8,128)S(1)} copy-done((f32[2,2,200,384]{3,2,1,0:T(8,128)S(1)}, f32[2,2,200,384]{3,2,1,0:T(8,128)}, u32[]{:S(2)}) %copy-start.1) | copy-done | bytes 1228824
  66.9 1.1 %copy-done.5 = f32[2,200,384]{2,1,0:T(8,128)S(1)} copy-done((f32[2,200,384]{2,1,0:T(8,128)S(1)}, f32[2,200,384]{2,1,0:T(8,128)}, u32[]{:S(2)}) %copy-start.5) | copy-done | bytes 614424
  67.9 2.6 %far_other.1 = bf16[2,200,384]{2,1,0:T(8,128)(2,1)S(1)} custom-call(bf16[4,2,200,384]{3,2,1,0:T(8,128)(2,1)S(1)} %all-to-all-done.1.lib_ref, f32[2,2,200,384]{3,2,1,0:T(8,128)S(1)} %get-tuple-element.23.spec_ref, f32[2,200,384]{2,1,0:T(8,128)S(1)} %copy-done.5, bf16[3,256,256]{2,1,0:T(8,128)(2,1)S(1)} %copy-done.6, bf16[2,200,200]{2,1,0:T(8,128)(2,1)S(1)} %copy-done.12, ...), custom_call_target="tpu_custom_call" | custom-call | flops 1258291200 | bytes 4194304 | tf_op jit(solution)/shard_map/far_other/pallas_call | solution.py:389
  70.5 0.0 copy-start.21
  70.5 0.3 collective-permute-start.8
  70.8 0.0 copy-done.13
  70.8 2.6 %far_own.1.best_ref = f32[2,200,384]{2,1,0:T(8,128)S(1)} custom-call(bf16[4,2,200,384]{3,2,1,0:T(8,128)(2,1)S(1)} %all-to-all-done.1.lib_ref, f32[2,2,200,384]{3,2,1,0:T(8,128)S(1)} %get-tuple-element.23.spec_ref, f32[2,200,384]{2,1,0:T(8,128)S(1)} %copy-done.5, bf16[3,256,256]{2,1,0:T(8,128)(2,1)S(1)} %copy-done.6, bf16[2,200,200]{2,1,0:T(8,128)(2,1)S(1)} %copy-done.13, ...), custom_call_target="tpu_custom_call" | custom-call | flops 1258291200 | bytes 4194304 | tf_op jit(solution)/shard_map/far_own/pallas_call | solution.py:389
  73.4 0.0 collective-permute-done.8.got_ref
  73.5 1.3 %join.1 = f32[384,384]{1,0:T(8,128)} custom-call(f32[2,200,384]{2,1,0:T(8,128)S(1)} %far_own.1.best_ref, bf16[2,200,384]{2,1,0:T(8,128)(2,1)S(1)} %collective-permute-done.8.got_ref, bf16[192,400]{1,0:T(8,128)(2,1)S(1)} %copy-done.21), custom_call_target="tpu_custom_call" | custom-call | flops 176947200 | bytes 2097152 | tf_op jit(solution)/shard_map/join/pallas_call | solution.py:403
  (23 shorter events, 0.0 us)
Async XLA Ops:
  0.0 12.3 %collective-permute-start = (bf16[384,384]{1,0:T(8,128)(2,1)}, bf16[384,384]{1,0:T(8,128)(2,1)S(1)}, u32[]{:S(2)}, u32[]{:S(2)}) collective-permute-start(bf16[384,384]{1,0:T(8,128)(2,1)} %bitcast.3), channel_id=1, source_target_pairs={{0,1},{1,0},{2,3},{3,2},{4,5},{5,4},{6,7},{7,6},{8,9},{9,8},{10,11... | collective-permute-start | bytes 884744 | tf_op jit(solution)/shard_map/ppermute | solution.py:306
  2.9 11.6 %all-to-all-start = ((bf16[8,48,384]{2,1,0:T(8,128)(2,1)}), bf16[8,48,384]{2,1,0:T(8,128)(2,1)S(1)}, u32[]{:S(2)}, u32[]{:S(2)}) async-start(bf16[8,48,384]{2,1,0:T(8,128)(2,1)} %broadcast_in_dim.15), calls=%async_computation | async-start | bytes 589824 | tf_op jit(solution)/shard_map/all_to_all | solution.py:301
  8.1 1.0 %copy-start.2 = (bf16[3,256,256]{2,1,0:T(8,128)(2,1)S(1)}, bf16[3,256,256]{2,1,0:T(8,128)(2,1)}, u32[]{:S(2)}) copy-start(bf16[3,256,256]{2,1,0:T(8,128)(2,1)} %constant.22.clone.ahead_ref) | copy-start | bytes 1179652
  9.1 0.9 %copy-start.9 = (bf16[256,256]{1,0:T(8,128)(2,1)S(1)}, bf16[256,256]{1,0:T(8,128)(2,1)}, u32[]{:S(2)}) copy-start(bf16[256,256]{1,0:T(8,128)(2,1)} %constant.21.clone.pair_ref) | copy-start | bytes 393220
  10.0 0.8 %copy-start.18 = (bf16[144,128]{1,0:T(8,128)(2,1)S(1)}, bf16[144,128]{1,0:T(8,128)(2,1)}, u32[]{:S(2)}) copy-start(bf16[144,128]{1,0:T(8,128)(2,1)} %constant.20.clone.real_ref) | copy-start | bytes 110596
  10.8 1.0 %copy-start.20 = (bf16[1,1,384,384]{3,2,1,0:T(8,128)(2,1)S(1)}, bf16[1,1,384,384]{3,2,1,0:T(8,128)(2,1)}, u32[]{:S(2)}) copy-start(bf16[1,1,384,384]{3,2,1,0:T(8,128)(2,1)} %param.13) | copy-start | bytes 884740
  11.8 2.8 %copy-start.3 = (bf16[3,256,256]{2,1,0:T(8,128)(2,1)S(1)}, bf16[3,256,256]{2,1,0:T(8,128)(2,1)}, u32[]{:S(2)}) copy-start(bf16[3,256,256]{2,1,0:T(8,128)(2,1)} %constant.22.clone.ahead_ref) | copy-start | bytes 1179652
  11.8 2.8 %copy-start.10 = (bf16[256,256]{1,0:T(8,128)(2,1)S(1)}, bf16[256,256]{1,0:T(8,128)(2,1)}, u32[]{:S(2)}) copy-start(bf16[256,256]{1,0:T(8,128)(2,1)} %constant.21.clone.pair_ref) | copy-start | bytes 393220
  11.8 2.8 %copy-start.19 = (bf16[144,128]{1,0:T(8,128)(2,1)S(1)}, bf16[144,128]{1,0:T(8,128)(2,1)}, u32[]{:S(2)}) copy-start(bf16[144,128]{1,0:T(8,128)(2,1)} %constant.20.clone.real_ref) | copy-start | bytes 110596
  12.9 0.8 %copy-start.14 = (f32[2,200,384]{2,1,0:T(8,128)}, f32[2,200,384]{2,1,0:T(8,128)S(1)}, u32[]{:S(2)}) copy-start(f32[2,200,384]{2,1,0:T(8,128)S(1)} %get-tuple-element.22.other_ref) | copy-start | bytes 1843204
  16.2 27.0 %all-to-all-start.2 = ((bf16[4,2,200,384]{3,2,1,0:T(8,128)(2,1)}), bf16[4,2,200,384]{3,2,1,0:T(8,128)(2,1)S(1)}, u32[]{:S(2)}, u32[]{:S(2)}) async-start(bf16[4,2,200,384]{3,2,1,0:T(8,128)(2,1)} %get-tuple-element.21), calls=%async_computation.2 | async-start | bytes 2457600 | tf_op jit(solution)/shard_map/all_to_all | solution.py:363
  21.2 13.4 %collective-permute-start.5 = (bf16[200,384]{1,0:T(8,128)(2,1)S(1)}, bf16[200,384]{1,0:T(8,128)(2,1)S(1)}, u32[]{:S(2)}, u32[]{:S(2)}) collective-permute-start(bf16[200,384]{1,0:T(8,128)(2,1)S(1)} %get-tuple-element.19), channel_id=1, source_target_pairs={{0,12},{1,15},{2,14},{3,13},{4,0},{5,3},{6,2},{7,1},{8,4},{9,7},{1... | collective-permute-start | bytes 460808 | tf_op jit(solution)/shard_map/ppermute | solution.py:337
  26.0 9.4 %collective-permute-start.4 = (bf16[200,384]{1,0:T(8,128)(2,1)S(1)}, bf16[200,384]{1,0:T(8,128)(2,1)S(1)}, u32[]{:S(2)}, u32[]{:S(2)}) collective-permute-start(bf16[200,384]{1,0:T(8,128)(2,1)S(1)} %get-tuple-element.19), channel_id=1, source_target_pairs={{0,8},{1,11},{2,10},{3,9},{4,12},{5,15},{6,14},{7,13},{8,0},{9,3},... | collective-permute-start | bytes 460808 | tf_op jit(solution)/shard_map/ppermute | solution.py:337
  26.9 9.0 %collective-permute-start.3 = (bf16[200,384]{1,0:T(8,128)(2,1)S(1)}, bf16[200,384]{1,0:T(8,128)(2,1)S(1)}, u32[]{:S(2)}, u32[]{:S(2)}) collective-permute-start(bf16[200,384]{1,0:T(8,128)(2,1)S(1)} %get-tuple-element.19), channel_id=1, source_target_pairs={{0,4},{1,7},{2,6},{3,5},{4,8},{5,11},{6,10},{7,9},{8,12},{9,15},{1... | collective-permute-start | bytes 460808 | tf_op jit(solution)/shard_map/ppermute | solution.py:337
  29.6 9.2 %collective-permute-start.2 = (bf16[200,384]{1,0:T(8,128)(2,1)S(1)}, bf16[200,384]{1,0:T(8,128)(2,1)S(1)}, u32[]{:S(2)}, u32[]{:S(2)}) collective-permute-start(bf16[200,384]{1,0:T(8,128)(2,1)S(1)} %get-tuple-element.19), channel_id=1, source_target_pairs={{1,3},{3,1},{5,7},{7,5},{9,11},{11,9},{13,15},{15,13},{17,19},{19,... | collective-permute-start | bytes 460808 | tf_op jit(solution)/shard_map/ppermute | solution.py:337
  32.1 10.0 %collective-permute-start.1 = (bf16[2,200,384]{2,1,0:T(8,128)(2,1)S(1)}, bf16[2,200,384]{2,1,0:T(8,128)(2,1)S(1)}, u32[]{:S(2)}, u32[]{:S(2)}) collective-permute-start(bf16[2,200,384]{2,1,0:T(8,128)(2,1)S(1)} %get-tuple-element.18), channel_id=1, source_target_pairs={{0,2},{2,0},{1,3},{3,1},{4,6},{6,4},{5,7},{7,5},{8,10},{10,8},{9,1... | collective-permute-start | bytes 921608 | tf_op jit(solution)/shard_map/ppermute | solution.py:362
  38.9 8.9 %copy-start.16 = (bf16[200,384]{1,0:T(8,128)(2,1)}, bf16[200,384]{1,0:T(8,128)(2,1)S(1)}, u32[]{:S(2)}) copy-start(bf16[200,384]{1,0:T(8,128)(2,1)S(1)} %add_convert_fusion.mine_ref) | copy-start | bytes 460804
  43.2 9.5 %copy-start.22 = (f32[64]{0:T(128)S(1)}, f32[64]{0:T(128)}, u32[]{:S(2)}) copy-start(f32[64]{0:T(128)} %d_ref.1) | copy-start | bytes 772
  43.2 9.5 %copy-start.23 = (f32[64]{0:T(128)S(1)}, f32[64]{0:T(128)}, u32[]{:S(2)}) copy-start(f32[64]{0:T(128)} %a_ref.1) | copy-start | bytes 772
  43.2 9.5 %copy-start.24 = (f32[64]{0:T(128)S(1)}, f32[64]{0:T(128)}, u32[]{:S(2)}) copy-start(f32[64]{0:T(128)} %x_ref.1) | copy-start | bytes 772
  43.2 9.5 %copy-start.25 = (f32[64]{0:T(128)S(1)}, f32[64]{0:T(128)}, u32[]{:S(2)}) copy-start(f32[64]{0:T(128)} %p_ref.1) | copy-start | bytes 772
  43.2 1.0 %copy-start.7 = (bf16[4,2,200,384]{3,2,1,0:T(8,128)(2,1)}, bf16[4,2,200,384]{3,2,1,0:T(8,128)(2,1)S(1)}, u32[]{:S(2)}) copy-start(bf16[4,2,200,384]{3,2,1,0:T(8,128)(2,1)S(1)} %all-to-all-done.2.lib_ref) | copy-start | bytes 3686404
  44.3 21.3 %all-to-all-start.1 = ((bf16[4,2,200,384]{3,2,1,0:T(8,128)(2,1)}), bf16[4,2,200,384]{3,2,1,0:T(8,128)(2,1)S(1)}, u32[]{:S(2)}, u32[]{:S(2)}) async-start(bf16[4,2,200,384]{3,2,1,0:T(8,128)(2,1)} %copies.1), calls=%async_computation.1 | async-start | bytes 2457600 | tf_op jit(solution)/shard_map/all_to_all | solution.py:374
  47.8 10.5 %copy-start.6 = (bf16[3,256,256]{2,1,0:T(8,128)(2,1)S(1)}, bf16[3,256,256]{2,1,0:T(8,128)(2,1)}, u32[]{:S(2)}) copy-start(bf16[3,256,256]{2,1,0:T(8,128)(2,1)} %constant.23.clone.back_ref) | copy-start | bytes 1179652
  47.8 10.5 %copy-start.11 = (bf16[2,200,200]{2,1,0:T(8,128)(2,1)S(1)}, bf16[2,200,200]{2,1,0:T(8,128)(2,1)}, u32[]{:S(2)}) copy-start(bf16[2,200,200]{2,1,0:T(8,128)(2,1)} %constant.24.clone.fold_ref) | copy-start | bytes 480004
  47.8 4.9 %collective-permute-start.7 = (bf16[200,384]{1,0:T(8,128)(2,1)S(1)}, bf16[200,384]{1,0:T(8,128)(2,1)S(1)}, u32[]{:S(2)}, u32[]{:S(2)}) collective-permute-start(bf16[200,384]{1,0:T(8,128)(2,1)S(1)} %add_convert_fusion.mine_ref), channel_id=1, source_target_pairs={{0,1},{1,0},{2,3},{3,2},{4,5},{5,4},{6,7},{7,6},{8,9},{9,8},{10,11... | collective-permute-start | bytes 460808 | tf_op jit(solution)/shard_map/ppermute | solution.py:339
  51.5 1.2 %collective-permute-start.6 = (s32[1,1]{1,0:T(1,128)}, s32[1,1]{1,0:T(1,128)}, u32[]{:S(2)}, u32[]{:S(2)}) collective-permute-start(s32[1,1]{1,0:T(1,128)} %param.15), channel_id=1, source_target_pairs={{0,1},{1,0},{2,3},{3,2},{4,5},{5,4},{6,7},{7,6},{8,9},{9,8},{10,11... | collective-permute-start | bytes 20 | tf_op jit(solution)/shard_map/ppermute | solution.py:340
  52.7 1.1 %copy-start.15 = (f32[2,200,384]{2,1,0:T(8,128)S(1)}, f32[2,200,384]{2,1,0:T(8,128)}, u32[]{:S(2)}) copy-start(f32[2,200,384]{2,1,0:T(8,128)} %copy-done.14) | copy-start | bytes 1843204
  53.8 0.9 %copy-start.17 = (bf16[200,384]{1,0:T(8,128)(2,1)S(1)}, bf16[200,384]{1,0:T(8,128)(2,1)}, u32[]{:S(2)}) copy-start(bf16[200,384]{1,0:T(8,128)(2,1)} %copy-done.16) | copy-start | bytes 460804
  58.3 1.3 %copy-start.8 = (bf16[4,2,200,384]{3,2,1,0:T(8,128)(2,1)S(1)}, bf16[4,2,200,384]{3,2,1,0:T(8,128)(2,1)}, u32[]{:S(2)}) copy-start(bf16[4,2,200,384]{3,2,1,0:T(8,128)(2,1)} %copy-done.7) | copy-start | bytes 3686404
  59.6 6.0 %copy-start.12 = (bf16[2,200,200]{2,1,0:T(8,128)(2,1)S(1)}, bf16[2,200,200]{2,1,0:T(8,128)(2,1)}, u32[]{:S(2)}) copy-start(bf16[2,200,200]{2,1,0:T(8,128)(2,1)} %constant.24.clone.fold_ref) | copy-start | bytes 480004
  63.7 1.0 %copy-start = (f32[2,2,200,384]{3,2,1,0:T(8,128)}, f32[2,2,200,384]{3,2,1,0:T(8,128)S(1)}, u32[]{:S(2)}) copy-start(f32[2,2,200,384]{3,2,1,0:T(8,128)S(1)} %near.1.start_ref) | copy-start | bytes 3686404
  64.7 0.8 %copy-start.4 = (f32[2,200,384]{2,1,0:T(8,128)}, f32[2,200,384]{2,1,0:T(8,128)S(1)}, u32[]{:S(2)}) copy-start(f32[2,200,384]{2,1,0:T(8,128)S(1)} %get-tuple-element.24.weight_ref) | copy-start | bytes 1843204
  65.6 1.3 %copy-start.1 = (f32[2,2,200,384]{3,2,1,0:T(8,128)S(1)}, f32[2,2,200,384]{3,2,1,0:T(8,128)}, u32[]{:S(2)}) copy-start(f32[2,2,200,384]{3,2,1,0:T(8,128)} %copy-done) | copy-start | bytes 3686404
  66.9 1.1 %copy-start.5 = (f32[2,200,384]{2,1,0:T(8,128)S(1)}, f32[2,200,384]{2,1,0:T(8,128)}, u32[]{:S(2)}) copy-start(f32[2,200,384]{2,1,0:T(8,128)} %copy-done.4) | copy-start | bytes 1843204
  67.9 2.9 %copy-start.13 = (bf16[2,200,200]{2,1,0:T(8,128)(2,1)S(1)}, bf16[2,200,200]{2,1,0:T(8,128)(2,1)}, u32[]{:S(2)}) copy-start(bf16[2,200,200]{2,1,0:T(8,128)(2,1)} %constant.24.clone.fold_ref) | copy-start | bytes 480004
  70.5 2.9 %copy-start.21 = (bf16[192,400]{1,0:T(8,128)(2,1)S(1)}, bf16[192,400]{1,0:T(8,128)(2,1)}, u32[]{:S(2)}) copy-start(bf16[192,400]{1,0:T(8,128)(2,1)} %constant.25.clone.unfold_ref) | copy-start | bytes 460804
  70.5 2.9 %collective-permute-start.8 = (bf16[2,200,384]{2,1,0:T(8,128)(2,1)S(1)}, bf16[2,200,384]{2,1,0:T(8,128)(2,1)S(1)}, u32[]{:S(2)}, u32[]{:S(2)}) collective-permute-start(bf16[2,200,384]{2,1,0:T(8,128)(2,1)S(1)} %far_other.1), channel_id=1, source_target_pairs={{0,1},{1,0},{2,3},{3,2},{4,5},{5,4},{6,7},{7,6},{8,9},{9,8},{10,11... | collective-permute-start | bytes 921608 | tf_op jit(solution)/shard_map/ppermute | solution.py:401

commit v4 on v3

--- a/solution.py
+++ b/solution.py
@@ -1,4 +1,3 @@
-import functools
 import math
 
 import jax
@@ -18,6 +17,7 @@
 THIRD = N // 3
 BLOCKS = (64, 64, 72)
 ROWS = sum(BLOCKS)
+FOLD = 208
 ROOT = math.sqrt(3.0) / 2.0
 F32 = jnp.float32
 BF16 = jnp.bfloat16
@@ -53,9 +53,10 @@
     unfold[0, HALF] = 1.0
     for i in range(1, HALF):
         unfold[i, ROWS + HALF - i] = 1.0
-    names = ("real", "pair", "ahead", "back", "fold", "unfold")
-    arrays = (real, pair, ahead, back, fold, unfold)
-    return {n: jnp.asarray(a.astype(bf)) for n, a in zip(names, arrays)}
+    ahead_all = np.concatenate([ahead.reshape(-1, 2 * THIRD), pair, np.pad(real, ((0, 0), (0, THIRD)))])
+    pad = ((0, 0), (0, FOLD - ROWS), (0, 2 * THIRD - ROWS))
+    back_all = np.concatenate([back.reshape(-1, 2 * THIRD), np.pad(fold, pad).reshape(-1, 2 * THIRD)])
+    return [jnp.asarray(a.astype(bf)) for a in (ahead_all, back_all, unfold)]
 
 
 def dot(a, b):
@@ -85,10 +86,6 @@
         move.start()
     for move in moves:
         move.wait()
-
-
-def copy_kernel(block_ref, out_ref, sems):
-    spread(block_ref, out_ref, sems)
 
 
 def sine(x):
@@ -109,7 +106,9 @@
     return jnp.where(x < 0.0, -p, p)
 
 
-def half_spectrum(image, real, pair, ahead):
+def half_spectrum(image, tab):
+    wide = 2 * THIRD
+    pair, real = tab[3 * wide : 4 * wide, :], tab[4 * wide :, :THIRD]
     image = image.astype(F32)
     x0, x1, x2 = image[:THIRD], image[THIRD : 2 * THIRD], image[2 * THIRD :]
     plus, minus = x1 + x2, x1 - x2
@@ -128,7 +127,8 @@
     parts = ((r0 + rp, i0 + ip), (rh + im_, ih - rm), (rh - im_, ih + rm))
     result = []
     for k, (a, b) in enumerate(parts):
-        out = dot(jnp.concatenate([a.astype(BF16), b.astype(BF16)], axis=1), ahead[k])
+        lhs = jnp.concatenate([a.astype(BF16), b.astype(BF16)], axis=1)
+        out = dot(lhs, tab[k * wide : (k + 1) * wide, :])
         result.append((out[:, :THIRD], out[:, THIRD:]))
     return result
 
@@ -140,24 +140,20 @@
         ref[1, :, at] = im.astype(ref.dtype)
 
 
-def own_kernel(image_ref, real_ref, pair_ref, ahead_ref, spec_ref):
-    parts = half_spectrum(image_ref[...], real_ref[...], pair_ref[...], ahead_ref)
-    store_spectrum(spec_ref, parts)
-
-
-def other_kernel(image_ref, own_ref, real_ref, pair_ref, ahead_ref, spec_ref, power_ref):
-    parts = half_spectrum(image_ref[...], real_ref[...], pair_ref[...], ahead_ref)
+def own_kernel(image_ref, tab_ref, spec_ref, power_ref):
+    parts = half_spectrum(image_ref[...].reshape(N, N), tab_ref)
     store_spectrum(spec_ref, parts)
     for k, (re, im) in enumerate(parts):
-        at = slice(k * THIRD, (k + 1) * THIRD)
-        a, b = own_ref[0, :, at], own_ref[1, :, at]
-        power_ref[:, at] = ((a * a + b * b) + (re * re + im * im)).astype(BF16)
-
-
-def library_kernel(image_ref, real_ref, pair_ref, ahead_ref, spec_ref, out_ref, sems):
-    image = image_ref[...].reshape(N, N)
-    store_spectrum(spec_ref, half_spectrum(image, real_ref[...], pair_ref[...], ahead_ref))
-    spread(spec_ref, out_ref, sems)
+        power_ref[:, k * THIRD : (k + 1) * THIRD] = (re * re + im * im).astype(BF16)
+
+
+def other_kernel(image_ref, tab_ref, mate_ref, spec_ref):
+    store_spectrum(spec_ref, half_spectrum(image_ref[...], tab_ref))
+
+
+def library_kernel(image_ref, tab_ref, out_ref, spec_sc, sems):
+    store_spectrum(spec_sc, half_spectrum(image_ref[...].reshape(N, N), tab_ref))
+    spread(spec_sc, out_ref, sems)
 
 
 def whiten_kernel(
@@ -199,7 +195,8 @@
         weight_ref[t] = (0.5 * scale) * (plus * plus + mirror * mirror) * inverse_noise
 
 
-def match_step(re, im, square, t, spec_ref, weight_ref, back_ref, fold_ref):
+def match_step(re, im, square, t, spec_ref, weight_ref, tab):
+    wide = 2 * THIRD
     norm = jnp.sum(square * weight_ref[t])
     scale = lax.rsqrt(jnp.full((1, THIRD), norm + 1e-06, F32))
     s_re, s_im = spec_ref[t, 0], spec_ref[t, 1]
@@ -208,7 +205,8 @@
     g = []
     for k in range(3):
         at = slice(k * THIRD, (k + 1) * THIRD)
-        g.append(dot(jnp.concatenate([p_re[:, at], p_im[:, at]], axis=1), back_ref[k]))
+        lhs = jnp.concatenate([p_re[:, at], p_im[:, at]], axis=1)
+        g.append(dot(lhs, tab[k * wide : (k + 1) * wide, :]))
     (r0, i0), (r1, i1), (r2, i2) = ((x[:, :THIRD], x[:, THIRD:]) for x in g)
     slant = scale * ROOT
     rp, rm = r1 + r2, slant * (r1 - r2)
@@ -218,38 +216,39 @@
     h_im = [scale * (i0 + ip), ih + rm, ih - rm]
     h_re = jnp.concatenate([h.astype(BF16) for h in h_re], axis=1)
     h_im = jnp.concatenate([h.astype(BF16) for h in h_im], axis=1)
-    even = dot(fold_ref[0], h_re)
-    odd = dot(fold_ref[1], h_im)
+    first = 3 * wide
+    even = dot(tab[first : first + ROWS, :ROWS], h_re)
+    odd = dot(tab[first + FOLD : first + FOLD + ROWS, :ROWS], h_im)
     return even - odd, even + odd
 
 
-def near_kernel(lib_ref, spec_ref, weight_ref, back_ref, fold_ref, out_ref):
+def near_kernel(lib_ref, spec_ref, weight_ref, tab_ref, out_ref):
     step = pl.program_id(0)
 
     @pl.when(step == 0)
     def _():
         out_ref[...] = jnp.full_like(out_ref, -jnp.inf)
 
-    re = lib_ref[step, 0].astype(F32)
-    im = lib_ref[step, 1].astype(F32)
+    re = lib_ref[0].astype(F32)
+    im = lib_ref[1].astype(F32)
     square = re * re + im * im
     for t in range(2):
-        minus, plus = match_step(re, im, square, t, spec_ref, weight_ref, back_ref, fold_ref)
+        minus, plus = match_step(re, im, square, t, spec_ref, weight_ref, tab_ref)
         out_ref[t, 0] = jnp.maximum(out_ref[t, 0], minus)
         out_ref[t, 1] = jnp.maximum(out_ref[t, 1], plus)
 
 
-def far_kernel(t, lib_ref, spec_ref, weight_ref, back_ref, fold_ref, start_ref, out_ref, best_sc):
+def far_kernel(lib_ref, spec_ref, weight_ref, tab_ref, start_ref, out_ref, best_sc):
     step = pl.program_id(0)
 
     @pl.when(step == 0)
     def _():
-        best_sc[...] = start_ref[t]
-
-    re = lib_ref[step, 0].astype(F32)
-    im = lib_ref[step, 1].astype(F32)
+        best_sc[...] = start_ref[0]
+
+    re = lib_ref[0].astype(F32)
+    im = lib_ref[1].astype(F32)
     square = re * re + im * im
-    minus, plus = match_step(re, im, square, t, spec_ref, weight_ref, back_ref, fold_ref)
+    minus, plus = match_step(re, im, square, 0, spec_ref, weight_ref, tab_ref)
     best_sc[0] = jnp.maximum(best_sc[0], minus)
     best_sc[1] = jnp.maximum(best_sc[1], plus)
 
@@ -271,8 +270,8 @@
     out_ref[HALF:] = total
 
 
-def vmem(count):
-    return [pl.BlockSpec(memory_space=pltpu.VMEM)] * count
+def full(*shape):
+    return pl.BlockSpec(shape, lambda i: (0,) * len(shape))
 
 
 def smem(count):
@@ -288,44 +287,54 @@
 
 
 def per_device(images, projections, ctf_row, defocus_term, astig_term, astig_cross, phase_shift):
-    tab = tables()
-    transform = (tab["real"], tab["pair"], tab["ahead"])
+    ahead, back, unfold = tables()
     groups = math.prod(lax.axis_size(a) for a in DEF)
     deep, wide = lax.axis_size("z"), lax.axis_size("xhi")
     core = lax.axis_index("core")
     swap = [(0, 1), (1, 0)]
-    spectrum = pltpu.VMEM((2, ROWS, N), F32)
+    plane = (2, ROWS, N)
     work = 2 * ROWS * 768 * 256 * 2
-
+    near_spec = pl.BlockSpec(memory_space=pltpu.HBM)
+
+    tile = images[0, 0]
+    received = lax.ppermute(tile, "xhi", swap)
+    mate = lax.ppermute(ctf_row, "xhi", swap)
     block = projections[0]
-    image = lax.all_to_all(
-        jnp.broadcast_to(block[None], (groups,) + block.shape), DEF, 0, 0, tiled=False
-    )
-
-    tile = images[0, 0]
-    received = lax.ppermute(tile, "core", swap)
-    own = pl.pallas_call(
+    copies = pl.pallas_call(
+        spread,
+        out_shape=pltpu.HBM((groups,) + block.shape, BF16),
+        in_specs=[near_spec],
+        out_specs=near_spec,
+        scratch_shapes=[pltpu.SemaphoreType.DMA((groups,))],
+        cost_estimate=cost(0, 1 << 20),
+        name="copies",
+    )(block)
+    image = lax.all_to_all(copies, DEF, 0, 0, tiled=False)
+
+    own, power = pl.pallas_call(
         own_kernel,
-        out_shape=spectrum,
-        in_specs=vmem(4),
-        out_specs=vmem(1)[0],
+        out_shape=[jax.ShapeDtypeStruct(plane, F32), jax.ShapeDtypeStruct((ROWS, N), BF16)],
+        grid=(1,),
+        in_specs=[full(N, N), full(*ahead.shape)],
+        out_specs=[full(*plane), full(ROWS, N)],
         compiler_params=params(16),
         cost_estimate=cost(work, 2 << 20),
         name="own_tile",
-    )(tile, *transform)
-    other, power = pl.pallas_call(
+    )(tile, ahead)
+    other = pl.pallas_call(
         other_kernel,
-        out_shape=[spectrum, pltpu.VMEM((ROWS, N), BF16)],
-        in_specs=vmem(5),
-        out_specs=vmem(2),
+        out_shape=jax.ShapeDtypeStruct(plane, F32),
+        grid=(1,),
+        in_specs=[full(N, N), full(*ahead.shape)] + smem(1),
+        out_specs=full(*plane),
         compiler_params=params(16),
         cost_estimate=cost(work, 2 << 20),
         name="other_tile",
-    )(received, own, *transform)
-
-    image, power = lax.optimization_barrier((image, power))
-
-    sums = jnp.where(core == 0, power.astype(F32), 0.0)
+    )(received, ahead, mate)
+
+    beside = lax.ppermute(power, "core", swap)
+    pair = (power.astype(F32) + beside.astype(F32)).astype(BF16)
+    sums = jnp.where(core == 0, pair.astype(F32), 0.0)
     for dz in range(deep):
         perm = [
             ((z * wide + x) * 2 + c, ((z + dz) % deep * wide + (x ^ c)) * 2 + c)
@@ -334,81 +343,82 @@
             for c in range(2)
             if dz or c
         ]
-        sums = sums + lax.ppermute(power, BLK, perm).astype(F32)
+        sums = sums + lax.ppermute(pair, BLK, perm).astype(F32)
     mine = sums.astype(BF16)
+
+    image, _ = lax.optimization_barrier((image, pair))
+    near_copies = pl.pallas_call(
+        library_kernel,
+        out_shape=pltpu.HBM((deep,) + plane, BF16),
+        grid=(1,),
+        in_specs=[full(groups, N // groups, N), full(*ahead.shape)],
+        out_specs=near_spec,
+        scratch_shapes=[pltpu.VMEM(plane, BF16), pltpu.SemaphoreType.DMA((deep,))],
+        compiler_params=params(16),
+        cost_estimate=cost(work, 4 << 20),
+        name="library",
+    )(image, ahead)
+    near_copies, mine, other = lax.optimization_barrier((near_copies, mine, other))
+    near_all = lax.all_to_all(near_copies, "z", 0, 0, tiled=False)
+
     theirs = lax.ppermute(mine, "core", swap)
-    mate = lax.ppermute(ctf_row, "core", swap)
     spec, weight = pl.pallas_call(
         whiten_kernel,
-        out_shape=[pltpu.VMEM((2, 2, ROWS, N), F32), pltpu.VMEM((2, ROWS, N), F32)],
-        in_specs=smem(6) + vmem(4),
-        out_specs=vmem(2),
-        compiler_params=params(16),
+        out_shape=[jax.ShapeDtypeStruct((2,) + plane, F32), jax.ShapeDtypeStruct(plane, F32)],
+        grid=(1,),
+        in_specs=smem(6) + [full(*plane)] * 2 + [full(ROWS, N)] * 2,
+        out_specs=[full(2, *plane), full(*plane)],
+        compiler_params=params(20),
         cost_estimate=cost(2 * ROWS * N * 60, 4 << 20),
         name="whiten",
     )(ctf_row, mate, defocus_term, astig_term, astig_cross, phase_shift, own, other, mine, theirs)
 
-    wide_shape = (deep, 2, ROWS, N)
-    near, near_copies = pl.pallas_call(
-        library_kernel,
-        out_shape=[pltpu.VMEM((2, ROWS, N), BF16), pltpu.HBM(wide_shape, BF16)],
-        in_specs=vmem(4),
-        out_specs=[vmem(1)[0], pl.BlockSpec(memory_space=pltpu.HBM)],
-        scratch_shapes=[pltpu.SemaphoreType.DMA((deep,))],
-        compiler_params=params(16),
-        cost_estimate=cost(work, 4 << 20),
-        name="library",
-    )(image, *transform)
-    far, _ = lax.optimization_barrier((lax.ppermute(near, "xhi", swap), mine))
-    near_all = lax.all_to_all(near_copies, "z", 0, 0, tiled=False)
-    far_copies = pl.pallas_call(
-        copy_kernel,
-        out_shape=pltpu.HBM(wide_shape, BF16),
-        in_specs=vmem(1),
-        out_specs=pl.BlockSpec(memory_space=pltpu.HBM),
-        scratch_shapes=[pltpu.SemaphoreType.DMA((deep,))],
-        compiler_params=params(4),
-        cost_estimate=cost(0, 3 << 20),
-        name="copies",
-    )(far)
-    far_all = lax.all_to_all(far_copies, "z", 0, 0, tiled=False)
-
+    near_all, spec, weight = lax.optimization_barrier((near_all, spec, weight))
+    far_all = lax.ppermute(near_all, "core", swap)
+    lib_spec = pl.BlockSpec((None,) + plane, lambda i: (i, 0, 0, 0))
     near_best = pl.pallas_call(
         near_kernel,
-        out_shape=pltpu.VMEM((2, 2, ROWS, N), F32),
+        out_shape=jax.ShapeDtypeStruct((2,) + plane, F32),
         grid=(deep,),
-        in_specs=vmem(5),
-        out_specs=vmem(1)[0],
-        compiler_params=params(16),
+        in_specs=[lib_spec, full(2, *plane), full(*plane), full(*back.shape)],
+        out_specs=full(2, *plane),
+        compiler_params=params(20),
         cost_estimate=cost(2 * deep * 2 * work, 8 << 20),
         name="near",
-    )(near_all, spec, weight, tab["back"], tab["fold"])
+    )(near_all, spec, weight, back)
     far_all, near_best = lax.optimization_barrier((far_all, near_best))
 
     def match(t, dtype, name):
         return pl.pallas_call(
-            functools.partial(far_kernel, t),
-            out_shape=pltpu.VMEM((2, ROWS, N), dtype),
+            far_kernel,
+            out_shape=jax.ShapeDtypeStruct(plane, dtype),
             grid=(deep,),
-            in_specs=vmem(6),
-            out_specs=vmem(1)[0],
-            scratch_shapes=[pltpu.VMEM((2, ROWS, N), F32)],
-            compiler_params=params(16),
+            in_specs=[
+                lib_spec,
+                pl.BlockSpec((1,) + plane, lambda i: (t, 0, 0, 0)),
+                pl.BlockSpec((1, ROWS, N), lambda i: (t, 0, 0)),
+                full(*back.shape),
+                pl.BlockSpec((1,) + plane, lambda i: (t, 0, 0, 0)),
+            ],
+            out_specs=full(*plane),
+            scratch_shapes=[pltpu.VMEM(plane, F32)],
+            compiler_params=params(20),
             cost_estimate=cost(deep * 2 * work, 4 << 20),
             name=name,
-        )(far_all, spec, weight, tab["back"], tab["fold"], near_best)
-
-    got = lax.ppermute(match(1, BF16, "far_other"), "core", swap)
+        )(far_all, spec, weight, back, near_best)
+
+    got = lax.ppermute(match(1, BF16, "far_other"), "xhi", swap)
     best = match(0, F32, "far_own")
     peak = pl.pallas_call(
         join_kernel,
         out_shape=jax.ShapeDtypeStruct((N, N), F32),
-        in_specs=vmem(3),
-        out_specs=vmem(1)[0],
+        grid=(1,),
+        in_specs=[full(*plane), full(*plane), full(*unfold.shape)],
+        out_specs=full(N, N),
         compiler_params=params(16),
         cost_estimate=cost(3 * 2 * HALF * 2 * ROWS * N, 2 << 20),
         name="join",
-    )(best, got, tab["unfold"])
+    )(best, got, unfold)
     return peak[None, None]
 
 

time: 75.6 us -> 81.6 us (1.079)
  local copies, waits for them, and re-layouts: 14.5 us -> 3 us
  Pallas kernels: 18 us -> 29.4 us
  waiting for transfers between devices: 8.72 us -> 16.7 us
  starting transfers between devices: 32.5 us -> 31 us
    pallas_call x8, Pallas kernels: 16.6 us -> 28.1 us  [the longest x1 10.1 us: per_device(): pl.pallas_call(spread, out_shape=pltpu.HBM((groups,) + block.shape, BF16)...]
    unnamed x52 -> x20, local copies, waits for them, and re-layouts: 13 us -> 3 us
    all_to_all x1, waiting for transfers between devices: 0.01 us -> 9.37 us  [per_device(): near_all = lax.all_to_all(near_copies, 'z', 0, 0, tiled=False)]
    ppermute x8 -> x9, starting transfers between devices: 15.1 us -> 21.3 us  [the longest x4 11.5 us: per_device(): sums = sums + lax.ppermute(pair, BLK, perm).astype(F32)]
    all_to_all x2 -> x1, starting transfers between devices: 8.73 us -> 4.22 us  [per_device(): image = lax.all_to_all(copies, DEF, 0, 0, tiled=False)]
    ppermute x1, starting transfers between devices: 3.62 us -> 1.06 us  [per_device(): theirs = lax.ppermute(mine, 'core', swap)]
    broadcast_in_dim x1 -> x0, local copies, waits for them, and re-layouts: 1.51 us -> none  [per_device(): jnp.broadcast_to(block[None], (groups,) + block.shape)]
    ppermute x8 -> x9, waiting for transfers between devices: 7.88 us -> 6.99 us  [the longest x1 6.03 us: per_device(): got = lax.ppermute(match(1, BF16, 'far_other'), 'xhi', swap)]
  transfers between devices with their start and end apart: 12 -> 12, of which waited for: 6 -> 5; matrix products, arithmetic and copies ran while one was open for 2% -> 0% of each run, Pallas kernels for 17% -> 30%
where the time goes in v4:
time: 81.6 us; the launch traced here: 81.1 us
  starting transfers between devices  31 us (38%)
  Pallas kernels  29.4 us (36%)
  waiting for transfers between devices  16.7 us (20%)
  local copies, waits for them, and re-layouts  3 us (4%)
  between operations  0.86 us (1%)
    ppermute x4, starting transfers between devices, per_device(): sums = sums + lax.ppermute(pair, BLK, perm).astype(F32)  11.5 us
    pallas_call x1, Pallas kernels, per_device(): pl.pallas_call(spread, out_shape=pltpu.HBM((groups,) + block.shape, BF16)...  10.1 us
    all_to_all x1, waiting for transfers between devices, per_device(): near_all = lax.all_to_all(near_copies, 'z', 0, 0, tiled=False)  9.37 us
    ppermute x1, waiting for transfers between devices, per_device(): got = lax.ppermute(match(1, BF16, 'far_other'), 'xhi', swap)  6.03 us
    pallas_call x2, Pallas kernels, match(): pl.pallas_call(far_kernel, out_shape=jax.ShapeDtypeStruct(plane, dtype),...  5.11 us
    pallas_call x1, Pallas kernels, per_device(): pl.pallas_call(near_kernel, out_shape=jax.ShapeDtypeStruct((2,) + plane,...  4.9 us
    all_to_all x1, starting transfers between devices, per_device(): near_all = lax.all_to_all(near_copies, 'z', 0, 0, tiled=False)  4.42 us
    all_to_all x1, starting transfers between devices, per_device(): image = lax.all_to_all(copies, DEF, 0, 0, tiled=False)  4.22 us
  transfers between devices with their start and end apart: 12, of which 5 were waited for; matrix products, arithmetic and copies ran while one was open for 0% of the time, Pallas kernels for 30%

profile of v4, /device:TPU:1, one launch (start us, length us, event | category | flops | bytes accessed | tf_op | source)
XLA Modules:
  0.0 81.1 jit_solution(8721677285682385987)
XLA Ops:
  0.0 0.0 copy-start
  0.0 1.1 %copy-done = bf16[1168,256]{1,0:T(8,128)(2,1)S(1)} copy-done((bf16[1168,256]{1,0:T(8,128)(2,1)S(1)}, bf16[1168,256]{1,0:T(8,128)(2,1)}, u32[]{:S(2)}) %copy-start) | copy-done | bytes 598040
  1.1 0.0 copy-start.1
  1.1 1.6 %own_tile.1 = (f32[2,200,384]{2,1,0:T(8,128)S(1)}, bf16[200,384]{1,0:T(8,128)(2,1)S(1)}) custom-call(bf16[384,384]{1,0:T(8,128)(2,1)} %bitcast.1.image_ref, bf16[1168,256]{1,0:T(8,128)(2,1)S(1)} %copy-done), custom_call_target="tpu_custom_call" | custom-call | flops 157286400 | bytes 2097152 | tf_op jit(solution)/shard_map/own_tile/pallas_call | solution.py:314
  2.6 0.0 copy-start.3
  2.7 0.8 %copy-done.3 = f32[2,200,384]{2,1,0:T(8,128)} copy-done((f32[2,200,384]{2,1,0:T(8,128)}, f32[2,200,384]{2,1,0:T(8,128)S(1)}, u32[]{:S(2)}) %copy-start.3) | copy-done | bytes 614424
  3.5 1.4 %collective-permute-start = (bf16[200,384]{1,0:T(8,128)(2,1)S(1)}, bf16[200,384]{1,0:T(8,128)(2,1)S(1)}, u32[]{:S(2)}, u32[]{:S(2)}) collective-permute-start(bf16[200,384]{1,0:T(8,128)(2,1)S(1)} %get-tuple-element.18), channel_id=1, source_target_pairs={{0,1},{1,0},{2,3},{3,2},{4,5},{5,4},{6,7},{7,6},{8,9},{9,8},{10,11... | collective-permute-start | bytes 460808 | tf_op jit(solution)/shard_map/ppermute | solution.py:335
  4.9 2.8 %collective-permute-start.5 = (bf16[384,384]{1,0:T(8,128)(2,1)}, bf16[384,384]{1,0:T(8,128)(2,1)S(1)}, u32[]{:S(2)}, u32[]{:S(2)}) collective-permute-start(bf16[384,384]{1,0:T(8,128)(2,1)} %bitcast.1.image_ref), channel_id=1, source_target_pairs={{0,2},{2,0},{1,3},{3,1},{4,6},{6,4},{5,7},{7,5},{8,10},{10,8},{9,1... | collective-permute-start | bytes 884744 | tf_op jit(solution)/shard_map/ppermute | solution.py:300
  7.7 10.1 %copies.1 = bf16[8,48,384]{2,1,0:T(8,128)(2,1)} custom-call(bf16[48,384]{1,0:T(8,128)(2,1)} %bitcast.3), custom_call_target="tpu_custom_call" | custom-call | bytes 1048576 | tf_op jit(solution)/shard_map/copies/pallas_call | solution.py:303
  17.8 4.2 %all-to-all-start = ((bf16[8,48,384]{2,1,0:T(8,128)(2,1)}), bf16[8,48,384]{2,1,0:T(8,128)(2,1)S(1)}, u32[]{:S(2)}, u32[]{:S(2)}) async-start(bf16[8,48,384]{2,1,0:T(8,128)(2,1)} %copies.1), calls=%async_computation | async-start | bytes 589824 | tf_op jit(solution)/shard_map/all_to_all | solution.py:312
  22.1 1.7 %collective-permute-start.6 = (s32[1,1]{1,0:T(1,128)}, s32[1,1]{1,0:T(1,128)}, u32[]{:S(2)}, u32[]{:S(2)}) collective-permute-start(s32[1,1]{1,0:T(1,128)} %param.12), channel_id=1, source_target_pairs={{0,2},{2,0},{1,3},{3,1},{4,6},{6,4},{5,7},{7,5},{8,10},{10,8},{9,1... | collective-permute-start | bytes 20 | tf_op jit(solution)/shard_map/ppermute | solution.py:301
  23.8 0.0 collective-permute-done
  23.8 4.8 %collective-permute-start.4 = (bf16[200,384]{1,0:T(8,128)(2,1)S(1)}, bf16[200,384]{1,0:T(8,128)(2,1)S(1)}, u32[]{:S(2)}, u32[]{:S(2)}) collective-permute-start(bf16[200,384]{1,0:T(8,128)(2,1)S(1)} %add_convert_fusion.1), channel_id=1, source_target_pairs={{0,12},{1,15},{2,14},{3,13},{4,0},{5,3},{6,2},{7,1},{8,4},{9,7},{1... | collective-permute-start | bytes 460808 | tf_op jit(solution)/shard_map/ppermute | solution.py:346
  28.6 1.1 %collective-permute-start.3 = (bf16[200,384]{1,0:T(8,128)(2,1)S(1)}, bf16[200,384]{1,0:T(8,128)(2,1)S(1)}, u32[]{:S(2)}, u32[]{:S(2)}) collective-permute-start(bf16[200,384]{1,0:T(8,128)(2,1)S(1)} %add_convert_fusion.1), channel_id=1, source_target_pairs={{0,8},{1,11},{2,10},{3,9},{4,12},{5,15},{6,14},{7,13},{8,0},{9,3},... | collective-permute-start | bytes 460808 | tf_op jit(solution)/shard_map/ppermute | solution.py:346
  29.7 2.0 %collective-permute-start.2 = (bf16[200,384]{1,0:T(8,128)(2,1)S(1)}, bf16[200,384]{1,0:T(8,128)(2,1)S(1)}, u32[]{:S(2)}, u32[]{:S(2)}) collective-permute-start(bf16[200,384]{1,0:T(8,128)(2,1)S(1)} %add_convert_fusion.1), channel_id=1, source_target_pairs={{0,4},{1,7},{2,6},{3,5},{4,8},{5,11},{6,10},{7,9},{8,12},{9,15},{1... | collective-permute-start | bytes 460808 | tf_op jit(solution)/shard_map/ppermute | solution.py:346
  31.7 0.0 collective-permute-done.6.mate_ref
  31.7 3.6 %collective-permute-start.1 = (bf16[200,384]{1,0:T(8,128)(2,1)S(1)}, bf16[200,384]{1,0:T(8,128)(2,1)S(1)}, u32[]{:S(2)}, u32[]{:S(2)}) collective-permute-start(bf16[200,384]{1,0:T(8,128)(2,1)S(1)} %add_convert_fusion.1), channel_id=1, source_target_pairs={{1,3},{3,1},{5,7},{7,5},{9,11},{11,9},{13,15},{15,13},{17,19},{19,... | collective-permute-start | bytes 460808 | tf_op jit(solution)/shard_map/ppermute | solution.py:346
  35.4 0.0 all-to-all-done.image_ref
  35.4 0.0 copy-done.1
  35.4 1.6 %library.1 = bf16[4,2,200,384]{3,2,1,0:T(8,128)(2,1)} custom-call(bf16[8,48,384]{2,1,0:T(8,128)(2,1)S(1)} %all-to-all-done.image_ref, bf16[1168,256]{1,0:T(8,128)(2,1)S(1)} %copy-done.1), custom_call_target="tpu_custom_call" | custom-call | flops 157286400 | bytes 4194304 | tf_op jit(solution)/shard_map/library/pallas_call | solution.py:350
  37.0 0.0 collective-permute-done.5.image_ref
  37.1 1.2 %other_tile.1.other_ref = f32[2,200,384]{2,1,0:T(8,128)S(1)} custom-call(bf16[384,384]{1,0:T(8,128)(2,1)S(1)} %collective-permute-done.5.image_ref, bf16[1168,256]{1,0:T(8,128)(2,1)S(1)} %copy-done.1, s32[1,1]{1,0:T(1,128)} %collective-permute-done.6.mate_ref), custom_call_target="tpu_custom_call" | custom-call | flops 157286400 | bytes 2097152 | tf_op jit(solution)/shard_map/other_tile/pallas_call | solution.py:324
  38.2 0.0 collective-permute-done.4
  38.2 0.0 collective-permute-done.3
  38.2 0.2 collective-permute-done.2
  38.4 0.8 collective-permute-done.1
  39.2 0.1 add_convert_fusion.mine_ref
  39.3 0.0 copy-start.6
  39.3 0.0 copy-start.7
  39.3 0.0 copy-start.8
  39.3 0.0 copy-start.9
  39.3 4.4 %all-to-all-start.1 = ((bf16[4,2,200,384]{3,2,1,0:T(8,128)(2,1)}), bf16[4,2,200,384]{3,2,1,0:T(8,128)(2,1)}, u32[]{:S(2)}, u32[]{:S(2)}) async-start(bf16[4,2,200,384]{3,2,1,0:T(8,128)(2,1)} %library.1), calls=%async_computation.1 | async-start | bytes 2457600 | tf_op jit(solution)/shard_map/all_to_all | solution.py:362
  43.8 0.0 copy-start.2
  43.8 1.1 %collective-permute-start.7 = (bf16[200,384]{1,0:T(8,128)(2,1)S(1)}, bf16[200,384]{1,0:T(8,128)(2,1)S(1)}, u32[]{:S(2)}, u32[]{:S(2)}) collective-permute-start(bf16[200,384]{1,0:T(8,128)(2,1)S(1)} %add_convert_fusion.mine_ref), channel_id=1, source_target_pairs={{0,1},{1,0},{2,3},{3,2},{4,5},{5,4},{6,7},{7,6},{8,9},{9,8},{10,11... | collective-permute-start | bytes 460808 | tf_op jit(solution)/shard_map/ppermute | solution.py:364
  45.5 0.4 collective-permute-done.7.theirs_ref
  45.9 0.0 copy-done.6
  45.9 0.0 copy-done.7
  45.9 0.0 copy-done.8
  45.9 0.0 copy-done.9
  45.9 0.0 copy-start.4
  45.9 1.1 %copy-done.4 = f32[2,200,384]{2,1,0:T(8,128)S(1)} copy-done((f32[2,200,384]{2,1,0:T(8,128)S(1)}, f32[2,200,384]{2,1,0:T(8,128)}, u32[]{:S(2)}) %copy-start.4) | copy-done | bytes 614424
  47.0 3.6 %whiten.1 = (f32[2,2,200,384]{3,2,1,0:T(8,128)S(1)}, f32[2,200,384]{2,1,0:T(8,128)S(1)}) custom-call(s32[1,1]{1,0:T(1,128)S(6)} %copy.11.row_ref, s32[1,1]{1,0:T(1,128)} %collective-permute-done.6.mate_ref, f32[64]{0:T(128)S(1)} %copy-done.6, f32[64]{0:T(128)S(1)} %copy-done.7, f32[64]{0:T(128)S(1)} %copy-done.8, f32[64]{0:T(128)S(1)} %copy-done.9, ...), custom_call_target="tpu_custom_call" | custom-call | flops 9216000 | bytes 4194304 | tf_op jit(solution)/shard_map/whiten/pallas_call | solution.py:365
  50.6 9.4 %all-to-all-done.1.lib_ref = bf16[4,2,200,384]{3,2,1,0:T(8,128)(2,1)} async-done(((bf16[4,2,200,384]{3,2,1,0:T(8,128)(2,1)}), bf16[4,2,200,384]{3,2,1,0:T(8,128)(2,1)}, u32[]{:S(2)}, u32[]{:S(2)}) %all-to-all-start.1) | async-done | bytes 1228832 | tf_op jit(solution)/shard_map/all_to_all | solution.py:362
  59.9 1.9 %collective-permute-start.8 = (bf16[4,2,200,384]{3,2,1,0:T(8,128)(2,1)}, bf16[4,2,200,384]{3,2,1,0:T(8,128)(2,1)S(1)}, u32[]{:S(2)}, u32[]{:S(2)}) collective-permute-start(bf16[4,2,200,384]{3,2,1,0:T(8,128)(2,1)} %all-to-all-done.1.lib_ref), channel_id=1, source_target_pairs={{0,1},{1,0},{2,3},{3,2},{4,5},{5,4},{6,7},{7,6},{8,9},{9,8},{10,11... | collective-permute-start | bytes 3686408 | tf_op jit(solution)/shard_map/ppermute | solution.py:377
  61.8 0.0 copy-done.2
  61.8 4.9 %near.1.start_ref = f32[2,2,200,384]{3,2,1,0:T(8,128)S(1)} custom-call(bf16[4,2,200,384]{3,2,1,0:T(8,128)(2,1)} %all-to-all-done.1.lib_ref, f32[2,2,200,384]{3,2,1,0:T(8,128)S(1)} %get-tuple-element.27.spec_ref, f32[2,200,384]{2,1,0:T(8,128)S(1)} %get-tuple-element.28.weight_ref, bf16[1184,256]{1,0:T(8,128)(2,1)S(1)} %copy-done.2), custom_call_target="tpu_custom_call" | custom-call | flops 2516582400 | bytes 8388608 | tf_op jit(solution)/shard_map/near/pallas_call | solution.py:379
  66.7 0.0 collective-permute-done.8.lib_ref
  66.7 2.6 %far_other.1 = bf16[2,200,384]{2,1,0:T(8,128)(2,1)S(1)} custom-call(bf16[4,2,200,384]{3,2,1,0:T(8,128)(2,1)S(1)} %collective-permute-done.8.lib_ref, f32[2,2,200,384]{3,2,1,0:T(8,128)S(1)} %get-tuple-element.27.spec_ref, f32[2,200,384]{2,1,0:T(8,128)S(1)} %get-tuple-element.28.weight_ref, bf16[1184,256]{1,0:T(8,128)(2,1)S(1)} %copy-done.2, ...), custom_call_target="tpu_custom_call" | custom-call | flops 1258291200 | bytes 4194304 | tf_op jit(solution)/shard_map/far_other/pallas_call | solution.py:392
  69.3 0.0 copy-start.5
  69.3 1.9 %collective-permute-start.9 = (bf16[2,200,384]{2,1,0:T(8,128)(2,1)S(1)}, bf16[2,200,384]{2,1,0:T(8,128)(2,1)S(1)}, u32[]{:S(2)}, u32[]{:S(2)}) collective-permute-start(bf16[2,200,384]{2,1,0:T(8,128)(2,1)S(1)} %far_other.1), channel_id=1, source_target_pairs={{0,2},{2,0},{1,3},{3,1},{4,6},{6,4},{5,7},{7,5},{8,10},{10,8},{9,1... | collective-permute-start | bytes 921608 | tf_op jit(solution)/shard_map/ppermute | solution.py:410
  71.2 2.5 %far_own.1.best_ref = f32[2,200,384]{2,1,0:T(8,128)S(1)} custom-call(bf16[4,2,200,384]{3,2,1,0:T(8,128)(2,1)S(1)} %collective-permute-done.8.lib_ref, f32[2,2,200,384]{3,2,1,0:T(8,128)S(1)} %get-tuple-element.27.spec_ref, f32[2,200,384]{2,1,0:T(8,128)S(1)} %get-tuple-element.28.weight_ref, bf16[1184,256]{1,0:T(8,128)(2,1)S(1)} %copy-done.2, ...), custom_call_target="tpu_custom_call" | custom-call | flops 1258291200 | bytes 4194304 | tf_op jit(solution)/shard_map/far_own/pallas_call | solution.py:392
  73.8 6.0 %collective-permute-done.9.got_ref = bf16[2,200,384]{2,1,0:T(8,128)(2,1)S(1)} collective-permute-done((bf16[2,200,384]{2,1,0:T(8,128)(2,1)S(1)}, bf16[2,200,384]{2,1,0:T(8,128)(2,1)S(1)}, u32[]{:S(2)}, u32[]{:S(2)}) %collective-permute-start.9) | collective-permute-done | bytes 307232 | tf_op jit(solution)/shard_map/ppermute | solution.py:410
  79.8 0.0 copy-done.5
  79.8 1.3 %join.1 = f32[384,384]{1,0:T(8,128)} custom-call(f32[2,200,384]{2,1,0:T(8,128)S(1)} %far_own.1.best_ref, bf16[2,200,384]{2,1,0:T(8,128)(2,1)S(1)} %collective-permute-done.9.got_ref, bf16[192,400]{1,0:T(8,128)(2,1)S(1)} %copy-done.5), custom_call_target="tpu_custom_call" | custom-call | flops 176947200 | bytes 2097152 | tf_op jit(solution)/shard_map/join/pallas_call | solution.py:412
  (1 shorter events, 0.0 us)
Async XLA Ops:
  0.0 1.1 %copy-start = (bf16[1168,256]{1,0:T(8,128)(2,1)S(1)}, bf16[1168,256]{1,0:T(8,128)(2,1)}, u32[]{:S(2)}) copy-start(bf16[1168,256]{1,0:T(8,128)(2,1)} %constant.14.clone.tab_ref) | copy-start | bytes 1794052
  1.1 34.3 %copy-start.1 = (bf16[1168,256]{1,0:T(8,128)(2,1)S(1)}, bf16[1168,256]{1,0:T(8,128)(2,1)}, u32[]{:S(2)}) copy-start(bf16[1168,256]{1,0:T(8,128)(2,1)} %constant.14.clone.tab_ref) | copy-start | bytes 1794052
  2.6 0.8 %copy-start.3 = (f32[2,200,384]{2,1,0:T(8,128)}, f32[2,200,384]{2,1,0:T(8,128)S(1)}, u32[]{:S(2)}) copy-start(f32[2,200,384]{2,1,0:T(8,128)S(1)} %get-tuple-element.21.own_ref) | copy-start | bytes 1843204
  3.5 20.3 %collective-permute-start = (bf16[200,384]{1,0:T(8,128)(2,1)S(1)}, bf16[200,384]{1,0:T(8,128)(2,1)S(1)}, u32[]{:S(2)}, u32[]{:S(2)}) collective-permute-start(bf16[200,384]{1,0:T(8,128)(2,1)S(1)} %get-tuple-element.18), channel_id=1, source_target_pairs={{0,1},{1,0},{2,3},{3,2},{4,5},{5,4},{6,7},{7,6},{8,9},{9,8},{10,11... | collective-permute-start | bytes 460808 | tf_op jit(solution)/shard_map/ppermute | solution.py:335
  4.9 32.1 %collective-permute-start.5 = (bf16[384,384]{1,0:T(8,128)(2,1)}, bf16[384,384]{1,0:T(8,128)(2,1)S(1)}, u32[]{:S(2)}, u32[]{:S(2)}) collective-permute-start(bf16[384,384]{1,0:T(8,128)(2,1)} %bitcast.1.image_ref), channel_id=1, source_target_pairs={{0,2},{2,0},{1,3},{3,1},{4,6},{6,4},{5,7},{7,5},{8,10},{10,8},{9,1... | collective-permute-start | bytes 884744 | tf_op jit(solution)/shard_map/ppermute | solution.py:300
  17.8 17.5 %all-to-all-start = ((bf16[8,48,384]{2,1,0:T(8,128)(2,1)}), bf16[8,48,384]{2,1,0:T(8,128)(2,1)S(1)}, u32[]{:S(2)}, u32[]{:S(2)}) async-start(bf16[8,48,384]{2,1,0:T(8,128)(2,1)} %copies.1), calls=%async_computation | async-start | bytes 589824 | tf_op jit(solution)/shard_map/all_to_all | solution.py:312
  22.1 9.7 %collective-permute-start.6 = (s32[1,1]{1,0:T(1,128)}, s32[1,1]{1,0:T(1,128)}, u32[]{:S(2)}, u32[]{:S(2)}) collective-permute-start(s32[1,1]{1,0:T(1,128)} %param.12), channel_id=1, source_target_pairs={{0,2},{2,0},{1,3},{3,1},{4,6},{6,4},{5,7},{7,5},{8,10},{10,8},{9,1... | collective-permute-start | bytes 20 | tf_op jit(solution)/shard_map/ppermute | solution.py:301
  23.8 14.4 %collective-permute-start.4 = (bf16[200,384]{1,0:T(8,128)(2,1)S(1)}, bf16[200,384]{1,0:T(8,128)(2,1)S(1)}, u32[]{:S(2)}, u32[]{:S(2)}) collective-permute-start(bf16[200,384]{1,0:T(8,128)(2,1)S(1)} %add_convert_fusion.1), channel_id=1, source_target_pairs={{0,12},{1,15},{2,14},{3,13},{4,0},{5,3},{6,2},{7,1},{8,4},{9,7},{1... | collective-permute-start | bytes 460808 | tf_op jit(solution)/shard_map/ppermute | solution.py:346
  28.6 9.6 %collective-permute-start.3 = (bf16[200,384]{1,0:T(8,128)(2,1)S(1)}, bf16[200,384]{1,0:T(8,128)(2,1)S(1)}, u32[]{:S(2)}, u32[]{:S(2)}) collective-permute-start(bf16[200,384]{1,0:T(8,128)(2,1)S(1)} %add_convert_fusion.1), channel_id=1, source_target_pairs={{0,8},{1,11},{2,10},{3,9},{4,12},{5,15},{6,14},{7,13},{8,0},{9,3},... | collective-permute-start | bytes 460808 | tf_op jit(solution)/shard_map/ppermute | solution.py:346
  29.7 8.7 %collective-permute-start.2 = (bf16[200,384]{1,0:T(8,128)(2,1)S(1)}, bf16[200,384]{1,0:T(8,128)(2,1)S(1)}, u32[]{:S(2)}, u32[]{:S(2)}) collective-permute-start(bf16[200,384]{1,0:T(8,128)(2,1)S(1)} %add_convert_fusion.1), channel_id=1, source_target_pairs={{0,4},{1,7},{2,6},{3,5},{4,8},{5,11},{6,10},{7,9},{8,12},{9,15},{1... | collective-permute-start | bytes 460808 | tf_op jit(solution)/shard_map/ppermute | solution.py:346
  31.7 7.4 %collective-permute-start.1 = (bf16[200,384]{1,0:T(8,128)(2,1)S(1)}, bf16[200,384]{1,0:T(8,128)(2,1)S(1)}, u32[]{:S(2)}, u32[]{:S(2)}) collective-permute-start(bf16[200,384]{1,0:T(8,128)(2,1)S(1)} %add_convert_fusion.1), channel_id=1, source_target_pairs={{1,3},{3,1},{5,7},{7,5},{9,11},{11,9},{13,15},{15,13},{17,19},{19,... | collective-permute-start | bytes 460808 | tf_op jit(solution)/shard_map/ppermute | solution.py:346
  39.3 6.6 %copy-start.6 = (f32[64]{0:T(128)S(1)}, f32[64]{0:T(128)}, u32[]{:S(2)}) copy-start(f32[64]{0:T(128)} %d_ref.1) | copy-start | bytes 772
  39.3 6.6 %copy-start.7 = (f32[64]{0:T(128)S(1)}, f32[64]{0:T(128)}, u32[]{:S(2)}) copy-start(f32[64]{0:T(128)} %a_ref.1) | copy-start | bytes 772
  39.3 6.5 %copy-start.8 = (f32[64]{0:T(128)S(1)}, f32[64]{0:T(128)}, u32[]{:S(2)}) copy-start(f32[64]{0:T(128)} %x_ref.1) | copy-start | bytes 772
  39.3 6.5 %copy-start.9 = (f32[64]{0:T(128)S(1)}, f32[64]{0:T(128)}, u32[]{:S(2)}) copy-start(f32[64]{0:T(128)} %p_ref.1) | copy-start | bytes 772
  39.3 20.6 %all-to-all-start.1 = ((bf16[4,2,200,384]{3,2,1,0:T(8,128)(2,1)}), bf16[4,2,200,384]{3,2,1,0:T(8,128)(2,1)}, u32[]{:S(2)}, u32[]{:S(2)}) async-start(bf16[4,2,200,384]{3,2,1,0:T(8,128)(2,1)} %library.1), calls=%async_computation.1 | async-start | bytes 2457600 | tf_op jit(solution)/shard_map/all_to_all | solution.py:362
  43.8 18.0 %copy-start.2 = (bf16[1184,256]{1,0:T(8,128)(2,1)S(1)}, bf16[1184,256]{1,0:T(8,128)(2,1)}, u32[]{:S(2)}) copy-start(bf16[1184,256]{1,0:T(8,128)(2,1)} %constant.15.clone.tab_ref) | copy-start | bytes 1818628
  43.8 2.1 %collective-permute-start.7 = (bf16[200,384]{1,0:T(8,128)(2,1)S(1)}, bf16[200,384]{1,0:T(8,128)(2,1)S(1)}, u32[]{:S(2)}, u32[]{:S(2)}) collective-permute-start(bf16[200,384]{1,0:T(8,128)(2,1)S(1)} %add_convert_fusion.mine_ref), channel_id=1, source_target_pairs={{0,1},{1,0},{2,3},{3,2},{4,5},{5,4},{6,7},{7,6},{8,9},{9,8},{10,11... | collective-permute-start | bytes 460808 | tf_op jit(solution)/shard_map/ppermute | solution.py:364
  45.9 1.1 %copy-start.4 = (f32[2,200,384]{2,1,0:T(8,128)S(1)}, f32[2,200,384]{2,1,0:T(8,128)}, u32[]{:S(2)}) copy-start(f32[2,200,384]{2,1,0:T(8,128)} %copy-done.3) | copy-start | bytes 1843204
  59.9 6.8 %collective-permute-start.8 = (bf16[4,2,200,384]{3,2,1,0:T(8,128)(2,1)}, bf16[4,2,200,384]{3,2,1,0:T(8,128)(2,1)S(1)}, u32[]{:S(2)}, u32[]{:S(2)}) collective-permute-start(bf16[4,2,200,384]{3,2,1,0:T(8,128)(2,1)} %all-to-all-done.1.lib_ref), channel_id=1, source_target_pairs={{0,1},{1,0},{2,3},{3,2},{4,5},{5,4},{6,7},{7,6},{8,9},{9,8},{10,11... | collective-permute-start | bytes 3686408 | tf_op jit(solution)/shard_map/ppermute | solution.py:377
  69.3 10.5 %copy-start.5 = (bf16[192,400]{1,0:T(8,128)(2,1)S(1)}, bf16[192,400]{1,0:T(8,128)(2,1)}, u32[]{:S(2)}) copy-start(bf16[192,400]{1,0:T(8,128)(2,1)} %constant.16.clone.unfold_ref) | copy-start | bytes 460804
  69.3 10.5 %collective-permute-start.9 = (bf16[2,200,384]{2,1,0:T(8,128)(2,1)S(1)}, bf16[2,200,384]{2,1,0:T(8,128)(2,1)S(1)}, u32[]{:S(2)}, u32[]{:S(2)}) collective-permute-start(bf16[2,200,384]{2,1,0:T(8,128)(2,1)S(1)} %far_other.1), channel_id=1, source_target_pairs={{0,2},{2,0},{1,3},{3,1},{4,6},{6,4},{5,7},{7,5},{8,10},{10,8},{9,1... | collective-permute-start | bytes 921608 | tf_op jit(solution)/shard_map/ppermute | solution.py:410

commit v5 on v4

--- a/solution.py
+++ b/solution.py
@@ -12,11 +12,13 @@
 
 DEF = ("xlo", "y")
 BLK = ("z", "xhi", "core")
+LIB = ("xlo", "y", "z")
 N = 384
 HALF = N // 2
 THIRD = N // 3
 BLOCKS = (64, 64, 72)
 ROWS = sum(BLOCKS)
+MARK = 16
 FOLD = 208
 ROOT = math.sqrt(3.0) / 2.0
 F32 = jnp.float32
@@ -140,41 +142,37 @@
         ref[1, :, at] = im.astype(ref.dtype)
 
 
-def own_kernel(image_ref, tab_ref, spec_ref, power_ref):
+def own_kernel(row_ref, image_ref, tab_ref, spec_ref, power_ref, sent_ref):
+    sent_ref[:N] = image_ref[...]
+    sent_ref[N:] = jnp.full((MARK, N), row_ref[0, 0], jnp.int32).astype(F32).astype(BF16)
     parts = half_spectrum(image_ref[...].reshape(N, N), tab_ref)
     store_spectrum(spec_ref, parts)
     for k, (re, im) in enumerate(parts):
         power_ref[:, k * THIRD : (k + 1) * THIRD] = (re * re + im * im).astype(BF16)
 
 
-def other_kernel(image_ref, tab_ref, mate_ref, spec_ref):
-    store_spectrum(spec_ref, half_spectrum(image_ref[...], tab_ref))
-
-
-def library_kernel(image_ref, tab_ref, out_ref, spec_sc, sems):
-    store_spectrum(spec_sc, half_spectrum(image_ref[...].reshape(N, N), tab_ref))
-    spread(spec_sc, out_ref, sems)
-
-
-def whiten_kernel(
+def other_kernel(image_ref, tab_ref, spec_ref):
+    store_spectrum(spec_ref, half_spectrum(image_ref[:N], tab_ref))
+
+
+def library_kernel(image_ref, tab_ref, out_ref):
+    store_spectrum(out_ref, half_spectrum(image_ref[...].reshape(N, N), tab_ref))
+
+
+def gain_kernel(
     row_ref,
-    mate_ref,
     d_ref,
     a_ref,
     x_ref,
     p_ref,
+    mark_ref,
     own_ref,
     other_ref,
-    mine_ref,
-    theirs_ref,
     spec_ref,
     weight_ref,
 ):
     u, v = row_numbers()
     scale = row_scale(u)
-    power = (mine_ref[...].astype(F32) + theirs_ref[...].astype(F32)) * (1.0 / 16.0)
-    mean = jnp.sum(power * scale) * (1.0 / (N * N))
-    inverse_noise = 1.0 / (jnp.where(u <= HALF, power, 1.0) + 0.05 * mean)
     row = jnp.where(u < HALF, u, u - N).astype(F32) * (1.0 / N)
     col = jnp.where(v < HALF, v, v - N).astype(F32) * (1.0 / N)
     radial = row * row + col * col
@@ -182,24 +180,36 @@
     skew = 2.0 * row * col
     inner = (u > 0) & (u < HALF)
     turn = 1.0 / (2.0 * math.pi)
-    for t, r in enumerate((row_ref[0, 0], mate_ref[0, 0])):
+    mate = jnp.max(mark_ref[...].astype(F32)).astype(jnp.int32)
+    for t, r in enumerate((row_ref[0, 0], mate)):
         base = (d_ref[r] * turn) * radial + (a_ref[r] * turn) * stretch + p_ref[r] * turn
         cross = (x_ref[r] * turn) * skew
         plus = -sine(base + cross)
         minus = -sine(base - cross)
         mirror = jnp.where(inner & (v == HALF), minus, plus)
-        gain = (0.5 * (plus + mirror)) * inverse_noise
+        gain = 0.5 * (plus + mirror)
         source = own_ref if t == 0 else other_ref
         spec_ref[t, 0] = source[0] * gain
         spec_ref[t, 1] = source[1] * gain
-        weight_ref[t] = (0.5 * scale) * (plus * plus + mirror * mirror) * inverse_noise
-
-
-def match_step(re, im, square, t, spec_ref, weight_ref, tab):
+        weight_ref[t] = (0.5 * scale) * (plus * plus + mirror * mirror)
+
+
+def whiten_kernel(spec_ref, weight_ref, mine_ref, theirs_ref, spec_out, weight_out):
+    u, _ = row_numbers()
+    power = (mine_ref[...].astype(F32) + theirs_ref[...].astype(F32)) * (1.0 / 16.0)
+    mean = jnp.sum(power * row_scale(u)) * (1.0 / (N * N))
+    inverse_noise = 1.0 / (jnp.where(u <= HALF, power, 1.0) + 0.05 * mean)
+    for t in range(2):
+        spec_out[t, 0] = spec_ref[t, 0] * inverse_noise
+        spec_out[t, 1] = spec_ref[t, 1] * inverse_noise
+        weight_out[t] = weight_ref[t] * inverse_noise
+
+
+def match_step(re, im, spec_ref, weight_ref, tab):
     wide = 2 * THIRD
-    norm = jnp.sum(square * weight_ref[t])
+    norm = jnp.sum((re * re + im * im) * weight_ref[...])
     scale = lax.rsqrt(jnp.full((1, THIRD), norm + 1e-06, F32))
-    s_re, s_im = spec_ref[t, 0], spec_ref[t, 1]
+    s_re, s_im = spec_ref[0], spec_ref[1]
     p_re = (s_re * re + s_im * im).astype(BF16)
     p_im = (s_im * re - s_re * im).astype(BF16)
     g = []
@@ -222,35 +232,19 @@
     return even - odd, even + odd
 
 
-def near_kernel(lib_ref, spec_ref, weight_ref, tab_ref, out_ref):
+def match_kernel(near_ref, far_ref, spec_ref, weight_ref, tab_ref, out_ref, best_sc):
     step = pl.program_id(0)
 
     @pl.when(step == 0)
     def _():
-        out_ref[...] = jnp.full_like(out_ref, -jnp.inf)
-
-    re = lib_ref[0].astype(F32)
-    im = lib_ref[1].astype(F32)
-    square = re * re + im * im
-    for t in range(2):
-        minus, plus = match_step(re, im, square, t, spec_ref, weight_ref, tab_ref)
-        out_ref[t, 0] = jnp.maximum(out_ref[t, 0], minus)
-        out_ref[t, 1] = jnp.maximum(out_ref[t, 1], plus)
-
-
-def far_kernel(lib_ref, spec_ref, weight_ref, tab_ref, start_ref, out_ref, best_sc):
-    step = pl.program_id(0)
-
-    @pl.when(step == 0)
-    def _():
-        best_sc[...] = start_ref[0]
-
-    re = lib_ref[0].astype(F32)
-    im = lib_ref[1].astype(F32)
-    square = re * re + im * im
-    minus, plus = match_step(re, im, square, 0, spec_ref, weight_ref, tab_ref)
-    best_sc[0] = jnp.maximum(best_sc[0], minus)
-    best_sc[1] = jnp.maximum(best_sc[1], plus)
+        best_sc[...] = jnp.full_like(best_sc, -jnp.inf)
+
+    pairs = [
+        match_step(ref[0].astype(F32), ref[1].astype(F32), spec_ref, weight_ref, tab_ref)
+        for ref in (near_ref, far_ref)
+    ]
+    for side in range(2):
+        best_sc[side] = jnp.maximum(best_sc[side], jnp.maximum(pairs[0][side], pairs[1][side]))
 
     @pl.when(step == pl.num_programs(0) - 1)
     def _():
@@ -289,48 +283,52 @@
 def per_device(images, projections, ctf_row, defocus_term, astig_term, astig_cross, phase_shift):
     ahead, back, unfold = tables()
     groups = math.prod(lax.axis_size(a) for a in DEF)
+    places = math.prod(lax.axis_size(a) for a in LIB)
     deep, wide = lax.axis_size("z"), lax.axis_size("xhi")
     core = lax.axis_index("core")
     swap = [(0, 1), (1, 0)]
     plane = (2, ROWS, N)
     work = 2 * ROWS * 768 * 256 * 2
-    near_spec = pl.BlockSpec(memory_space=pltpu.HBM)
 
     tile = images[0, 0]
-    received = lax.ppermute(tile, "xhi", swap)
-    mate = lax.ppermute(ctf_row, "xhi", swap)
     block = projections[0]
     copies = pl.pallas_call(
         spread,
-        out_shape=pltpu.HBM((groups,) + block.shape, BF16),
-        in_specs=[near_spec],
-        out_specs=near_spec,
-        scratch_shapes=[pltpu.SemaphoreType.DMA((groups,))],
+        out_shape=pltpu.HBM((places,) + block.shape, BF16),
+        grid=(1,),
+        in_specs=[full(*block.shape)],
+        out_specs=pl.BlockSpec(memory_space=pltpu.HBM),
+        scratch_shapes=[pltpu.SemaphoreType.DMA((places,))],
         cost_estimate=cost(0, 1 << 20),
         name="copies",
     )(block)
-    image = lax.all_to_all(copies, DEF, 0, 0, tiled=False)
-
-    own, power = pl.pallas_call(
+    images_all = lax.all_to_all(copies, LIB, 0, 0, tiled=False)
+
+    own, power, sent = pl.pallas_call(
         own_kernel,
-        out_shape=[jax.ShapeDtypeStruct(plane, F32), jax.ShapeDtypeStruct((ROWS, N), BF16)],
-        grid=(1,),
-        in_specs=[full(N, N), full(*ahead.shape)],
-        out_specs=[full(*plane), full(ROWS, N)],
+        out_shape=[
+            jax.ShapeDtypeStruct(plane, F32),
+            jax.ShapeDtypeStruct((ROWS, N), BF16),
+            jax.ShapeDtypeStruct((N + MARK, N), BF16),
+        ],
+        grid=(1,),
+        in_specs=smem(1) + [full(N, N), full(*ahead.shape)],
+        out_specs=[full(*plane), full(ROWS, N), full(N + MARK, N)],
         compiler_params=params(16),
         cost_estimate=cost(work, 2 << 20),
         name="own_tile",
-    )(tile, ahead)
+    )(ctf_row, tile, ahead)
+    received = lax.ppermute(sent, "xhi", swap)
     other = pl.pallas_call(
         other_kernel,
         out_shape=jax.ShapeDtypeStruct(plane, F32),
         grid=(1,),
-        in_specs=[full(N, N), full(*ahead.shape)] + smem(1),
+        in_specs=[full(N + MARK, N), full(*ahead.shape)],
         out_specs=full(*plane),
         compiler_params=params(16),
         cost_estimate=cost(work, 2 << 20),
         name="other_tile",
-    )(received, ahead, mate)
+    )(received, ahead)
 
     beside = lax.ppermute(power, "core", swap)
     pair = (power.astype(F32) + beside.astype(F32)).astype(BF16)
@@ -346,69 +344,70 @@
         sums = sums + lax.ppermute(pair, BLK, perm).astype(F32)
     mine = sums.astype(BF16)
 
-    image, _ = lax.optimization_barrier((image, pair))
-    near_copies = pl.pallas_call(
-        library_kernel,
-        out_shape=pltpu.HBM((deep,) + plane, BF16),
-        grid=(1,),
-        in_specs=[full(groups, N // groups, N), full(*ahead.shape)],
-        out_specs=near_spec,
-        scratch_shapes=[pltpu.VMEM(plane, BF16), pltpu.SemaphoreType.DMA((deep,))],
-        compiler_params=params(16),
-        cost_estimate=cost(work, 4 << 20),
-        name="library",
-    )(image, ahead)
-    near_copies, mine, other = lax.optimization_barrier((near_copies, mine, other))
-    near_all = lax.all_to_all(near_copies, "z", 0, 0, tiled=False)
-
-    theirs = lax.ppermute(mine, "core", swap)
     spec, weight = pl.pallas_call(
-        whiten_kernel,
+        gain_kernel,
         out_shape=[jax.ShapeDtypeStruct((2,) + plane, F32), jax.ShapeDtypeStruct(plane, F32)],
         grid=(1,),
-        in_specs=smem(6) + [full(*plane)] * 2 + [full(ROWS, N)] * 2,
+        in_specs=smem(5)
+        + [pl.BlockSpec((MARK, N), lambda i: (N // MARK, 0))]
+        + [full(*plane)] * 2,
         out_specs=[full(2, *plane), full(*plane)],
         compiler_params=params(20),
         cost_estimate=cost(2 * ROWS * N * 60, 4 << 20),
+        name="gain",
+    )(ctf_row, defocus_term, astig_term, astig_cross, phase_shift, received, own, other)
+
+    images_all, mine, spec = lax.optimization_barrier((images_all, mine, spec))
+
+    near_all = pl.pallas_call(
+        library_kernel,
+        out_shape=jax.ShapeDtypeStruct((deep,) + plane, BF16),
+        grid=(deep,),
+        in_specs=[
+            pl.BlockSpec((groups, None, N // groups, N), lambda i: (0, i, 0, 0)),
+            full(*ahead.shape),
+        ],
+        out_specs=pl.BlockSpec((None,) + plane, lambda i: (i, 0, 0, 0)),
+        compiler_params=params(16),
+        cost_estimate=cost(deep * work, 4 << 20),
+        name="library",
+    )(images_all.reshape(groups, deep, N // groups, N), ahead)
+    far_all = lax.ppermute(near_all, "core", swap)
+    theirs = lax.ppermute(mine, "core", swap)
+
+    white, white_weight = pl.pallas_call(
+        whiten_kernel,
+        out_shape=[jax.ShapeDtypeStruct((2,) + plane, F32), jax.ShapeDtypeStruct(plane, F32)],
+        grid=(1,),
+        in_specs=[full(2, *plane), full(*plane), full(ROWS, N), full(ROWS, N)],
+        out_specs=[full(2, *plane), full(*plane)],
+        compiler_params=params(20),
+        cost_estimate=cost(2 * ROWS * N * 4, 4 << 20),
         name="whiten",
-    )(ctf_row, mate, defocus_term, astig_term, astig_cross, phase_shift, own, other, mine, theirs)
-
-    near_all, spec, weight = lax.optimization_barrier((near_all, spec, weight))
-    far_all = lax.ppermute(near_all, "core", swap)
-    lib_spec = pl.BlockSpec((None,) + plane, lambda i: (i, 0, 0, 0))
-    near_best = pl.pallas_call(
-        near_kernel,
-        out_shape=jax.ShapeDtypeStruct((2,) + plane, F32),
-        grid=(deep,),
-        in_specs=[lib_spec, full(2, *plane), full(*plane), full(*back.shape)],
-        out_specs=full(2, *plane),
-        compiler_params=params(20),
-        cost_estimate=cost(2 * deep * 2 * work, 8 << 20),
-        name="near",
-    )(near_all, spec, weight, back)
-    far_all, near_best = lax.optimization_barrier((far_all, near_best))
+    )(spec, weight, mine, theirs)
 
     def match(t, dtype, name):
+        lib_spec = pl.BlockSpec((None,) + plane, lambda i: (i, 0, 0, 0))
         return pl.pallas_call(
-            far_kernel,
+            match_kernel,
             out_shape=jax.ShapeDtypeStruct(plane, dtype),
             grid=(deep,),
             in_specs=[
                 lib_spec,
-                pl.BlockSpec((1,) + plane, lambda i: (t, 0, 0, 0)),
-                pl.BlockSpec((1, ROWS, N), lambda i: (t, 0, 0)),
+                lib_spec,
+                pl.BlockSpec((None,) + plane, lambda i: (t, 0, 0, 0)),
+                pl.BlockSpec((None, ROWS, N), lambda i: (t, 0, 0)),
                 full(*back.shape),
-                pl.BlockSpec((1,) + plane, lambda i: (t, 0, 0, 0)),
             ],
             out_specs=full(*plane),
             scratch_shapes=[pltpu.VMEM(plane, F32)],
             compiler_params=params(20),
-            cost_estimate=cost(deep * 2 * work, 4 << 20),
+            cost_estimate=cost(2 * deep * 2 * work, 6 << 20),
             name=name,
-        )(far_all, spec, weight, back, near_best)
-
-    got = lax.ppermute(match(1, BF16, "far_other"), "xhi", swap)
-    best = match(0, F32, "far_own")
+        )(near_all, far_all, white, white_weight, back)
+
+    got = lax.ppermute(match(1, BF16, "match_other"), "xhi", swap)
+    best = match(0, F32, "match_own")
     peak = pl.pallas_call(
         join_kernel,
         out_shape=jax.ShapeDtypeStruct((N, N), F32),

time: 81.6 us -> 65.9 us (0.81)
  Pallas kernels: 29.4 us -> 18.1 us
  starting transfers between devices: 31 us -> 26.7 us
  local copies, waits for them, and re-layouts: 3 us -> 1.72 us
  other arithmetic: 0.16 us -> 1.29 us
    all_to_all x2 -> x1, waiting for transfers between devices: 9.37 us -> 0.01 us  [per_device(): images_all = lax.all_to_all(copies, LIB, 0, 0, tiled=False)]
    pallas_call x5, Pallas kernels: 21.7 us -> 15.2 us  [the longest x2 8.09 us: match(): pl.pallas_call(match_kernel, out_shape=jax.ShapeDtypeStruct(plane, dtype)...]
    ppermute x4, waiting for transfers between devices: 0.95 us -> 4.56 us  [per_device(): sums = sums + lax.ppermute(pair, BLK, perm).astype(F32)]
    ppermute x3 -> x2, waiting for transfers between devices: 6.04 us -> 9.63 us  [the longest x1 5.66 us: per_device(): got = lax.ppermute(match(1, BF16, 'match_other'), 'xhi', swap)]
    ppermute x3 -> x2, starting transfers between devices: 6.46 us -> 3.05 us  [the longest x1 2.45 us: per_device(): received = lax.ppermute(sent, 'xhi', swap)]
    pallas_call x1, Pallas kernels: 3.6 us -> 0.43 us  [per_device(): pl.pallas_call(whiten_kernel, out_shape=[jax.ShapeDtypeStruct((2,) + plan...]
    ppermute x1, waiting for transfers between devices: 0.36 us -> 2.63 us  [per_device(): theirs = lax.ppermute(mine, 'core', swap)]
    ppermute x1, starting transfers between devices: 1.89 us -> 0.09 us  [per_device(): far_all = lax.ppermute(near_all, 'core', swap)]
  transfers between devices with their start and end apart: 12 -> 10, of which waited for: 5 -> 6; matrix products, arithmetic and copies ran while one was open for 0% -> 2% of each run, Pallas kernels for 30% -> 13%
where the time goes in v5:
time: 65.9 us; the launch traced here: 65.5 us
  starting transfers between devices  26.7 us (41%)
  Pallas kernels  18.1 us (27%)
  waiting for transfers between devices  16.8 us (25%)
  local copies, waits for them, and re-layouts  1.72 us (3%)
  other arithmetic  1.29 us (2%)
  between operations  0.91 us (1%)
    ppermute x4, starting transfers between devices, per_device(): sums = sums + lax.ppermute(pair, BLK, perm).astype(F32)  12.2 us
    all_to_all x1, starting transfers between devices, per_device(): images_all = lax.all_to_all(copies, LIB, 0, 0, tiled=False)  9.96 us
    pallas_call x2, Pallas kernels, match(): pl.pallas_call(match_kernel, out_shape=jax.ShapeDtypeStruct(plane, dtype)...  8.09 us
    ppermute x1, waiting for transfers between devices, per_device(): got = lax.ppermute(match(1, BF16, 'match_other'), 'xhi', swap)  5.66 us
    ppermute x4, waiting for transfers between devices, per_device(): sums = sums + lax.ppermute(pair, BLK, perm).astype(F32)  4.56 us
    ppermute x1, waiting for transfers between devices, per_device(): received = lax.ppermute(sent, 'xhi', swap)  3.96 us
    pallas_call x1, Pallas kernels, per_device(): pl.pallas_call(gain_kernel, out_shape=[jax.ShapeDtypeStruct((2,) + plane,...  2.69 us
    ppermute x1, waiting for transfers between devices, per_device(): theirs = lax.ppermute(mine, 'core', swap)  2.63 us
  transfers between devices with their start and end apart: 10, of which 6 were waited for; matrix products, arithmetic and copies ran while one was open for 2% of the time, Pallas kernels for 13%

profile of v5, /device:TPU:1, one launch (start us, length us, event | category | flops | bytes accessed | tf_op | source)
XLA Modules:
  0.0 65.5 jit_solution(9898534760165230821)
XLA Ops:
  0.0 2.1 %copies.1 = bf16[32,48,384]{2,1,0:T(8,128)(2,1)} custom-call(bf16[48,384]{1,0:T(8,128)(2,1)} %bitcast.6), custom_call_target="tpu_custom_call" | custom-call | bytes 1048576 | tf_op jit(solution)/shard_map/copies/pallas_call | solution.py:295
  2.1 0.0 copy-start
  2.1 0.0 copy-start.5
  2.1 10.0 %all-to-all-start = ((bf16[32,48,384]{2,1,0:T(8,128)(2,1)}), bf16[32,48,384]{2,1,0:T(8,128)(2,1)S(1)}, u32[]{:S(2)}, u32[]{:S(2)}) async-start(bf16[32,48,384]{2,1,0:T(8,128)(2,1)} %copies.1), calls=%async_computation | async-start | bytes 2359296 | tf_op jit(solution)/shard_map/all_to_all | solution.py:305
  12.7 0.0 copy-done
  12.7 0.0 copy-done.5
  12.8 0.0 copy-start.7
  12.8 0.0 copy-start.8
  12.8 0.0 copy-start.9
  12.8 0.0 copy-start.10
  12.8 0.6 own_tile.1
  13.4 0.0 copy-start.1
  13.4 0.8 %copy-done.1 = f32[2,200,384]{2,1,0:T(8,128)} copy-done((f32[2,200,384]{2,1,0:T(8,128)}, f32[2,200,384]{2,1,0:T(8,128)S(1)}, u32[]{:S(2)}) %copy-start.1) | copy-done | bytes 614424
  14.2 1.0 %collective-permute-start = (bf16[200,384]{1,0:T(8,128)(2,1)S(1)}, bf16[200,384]{1,0:T(8,128)(2,1)S(1)}, u32[]{:S(2)}, u32[]{:S(2)}) collective-permute-start(bf16[200,384]{1,0:T(8,128)(2,1)S(1)} %get-tuple-element.15), channel_id=1, source_target_pairs={{0,1},{1,0},{2,3},{3,2},{4,5},{5,4},{6,7},{7,6},{8,9},{9,8},{10,11... | collective-permute-start | bytes 460808 | tf_op jit(solution)/shard_map/ppermute | solution.py:333
  15.2 2.5 %collective-permute-start.5 = (bf16[400,384]{1,0:T(8,128)(2,1)S(1)}, bf16[400,384]{1,0:T(8,128)(2,1)S(1)}, u32[]{:S(2)}, u32[]{:S(2)}) collective-permute-start(bf16[400,384]{1,0:T(8,128)(2,1)S(1)} %get-tuple-element.16), channel_id=1, source_target_pairs={{0,2},{2,0},{1,3},{3,1},{4,6},{6,4},{5,7},{7,5},{8,10},{10,8},{9,1... | collective-permute-start | bytes 921608 | tf_op jit(solution)/shard_map/ppermute | solution.py:321
  17.6 0.0 collective-permute-done
  17.7 2.9 %collective-permute-start.1 = (bf16[200,384]{1,0:T(8,128)(2,1)S(1)}, bf16[200,384]{1,0:T(8,128)(2,1)}, u32[]{:S(2)}, u32[]{:S(2)}) collective-permute-start(bf16[200,384]{1,0:T(8,128)(2,1)S(1)} %add_convert_fusion.1), channel_id=1, source_target_pairs={{1,3},{3,1},{5,7},{7,5},{9,11},{11,9},{13,15},{15,13},{17,19},{19,... | collective-permute-start | bytes 460808 | tf_op jit(solution)/shard_map/ppermute | solution.py:344
  20.6 3.3 %collective-permute-start.2 = (bf16[200,384]{1,0:T(8,128)(2,1)S(1)}, bf16[200,384]{1,0:T(8,128)(2,1)}, u32[]{:S(2)}, u32[]{:S(2)}) collective-permute-start(bf16[200,384]{1,0:T(8,128)(2,1)S(1)} %add_convert_fusion.1), channel_id=1, source_target_pairs={{0,4},{1,7},{2,6},{3,5},{4,8},{5,11},{6,10},{7,9},{8,12},{9,15},{1... | collective-permute-start | bytes 460808 | tf_op jit(solution)/shard_map/ppermute | solution.py:344
  23.9 3.1 %collective-permute-start.3 = (bf16[200,384]{1,0:T(8,128)(2,1)S(1)}, bf16[200,384]{1,0:T(8,128)(2,1)}, u32[]{:S(2)}, u32[]{:S(2)}) collective-permute-start(bf16[200,384]{1,0:T(8,128)(2,1)S(1)} %add_convert_fusion.1), channel_id=1, source_target_pairs={{0,8},{1,11},{2,10},{3,9},{4,12},{5,15},{6,14},{7,13},{8,0},{9,3},... | collective-permute-start | bytes 460808 | tf_op jit(solution)/shard_map/ppermute | solution.py:344
  27.0 2.9 %collective-permute-start.4 = (bf16[200,384]{1,0:T(8,128)(2,1)S(1)}, bf16[200,384]{1,0:T(8,128)(2,1)}, u32[]{:S(2)}, u32[]{:S(2)}) collective-permute-start(bf16[200,384]{1,0:T(8,128)(2,1)S(1)} %add_convert_fusion.1), channel_id=1, source_target_pairs={{0,12},{1,15},{2,14},{3,13},{4,0},{5,3},{6,2},{7,1},{8,4},{9,7},{1... | collective-permute-start | bytes 460808 | tf_op jit(solution)/shard_map/ppermute | solution.py:344
  29.9 0.0 copy-start.2
  29.9 4.0 %collective-permute-done.5.image_ref.mark_ref = bf16[400,384]{1,0:T(8,128)(2,1)S(1)} collective-permute-done((bf16[400,384]{1,0:T(8,128)(2,1)S(1)}, bf16[400,384]{1,0:T(8,128)(2,1)S(1)}, u32[]{:S(2)}, u32[]{:S(2)}) %collective-permute-start.5) | collective-permute-done | bytes 307232 | tf_op jit(solution)/shard_map/ppermute | solution.py:321
  33.8 0.5 other_tile.1.other_ref
  34.4 0.0 copy-done.7
  34.4 0.0 copy-done.8
  34.4 0.0 copy-done.9
  34.4 0.0 copy-done.10
  34.4 0.0 copy-done.2
  34.4 2.7 %gain.1 = (f32[2,2,200,384]{3,2,1,0:T(8,128)S(1)}, f32[2,200,384]{2,1,0:T(8,128)S(1)}) custom-call(s32[1,1]{1,0:T(1,128)S(6)} %copy.11.row_ref, f32[64]{0:T(128)S(1)} %copy-done.7, f32[64]{0:T(128)S(1)} %copy-done.8, f32[64]{0:T(128)S(1)} %copy-done.9, f32[64]{0:T(128)S(1)} %copy-done.10, bf16[400,384]{1,0:T(8,128)(2,1)S(1)} %collective-permute-done.5.image_ref.mark_ref, ...), custom_call_target="tpu_custom_call" | custom-call | flops 9216000 | bytes 4194304 | tf_op jit(solution)/shard_map/gain/pallas_call | solution.py:347
  37.1 0.0 copy-start.3
  37.1 0.8 %copy-done.3 = f32[2,200,384]{2,1,0:T(8,128)} copy-done((f32[2,200,384]{2,1,0:T(8,128)}, f32[2,200,384]{2,1,0:T(8,128)S(1)}, u32[]{:S(2)}) %copy-start.3) | copy-done | bytes 614424
  37.9 0.0 collective-permute-done.1
  37.9 2.5 %collective-permute-done.2 = bf16[200,384]{1,0:T(8,128)(2,1)} collective-permute-done((bf16[200,384]{1,0:T(8,128)(2,1)S(1)}, bf16[200,384]{1,0:T(8,128)(2,1)}, u32[]{:S(2)}, u32[]{:S(2)}) %collective-permute-start.2) | collective-permute-done | bytes 153632 | tf_op jit(solution)/shard_map/ppermute | solution.py:344
  40.4 1.9 %collective-permute-done.3 = bf16[200,384]{1,0:T(8,128)(2,1)} collective-permute-done((bf16[200,384]{1,0:T(8,128)(2,1)S(1)}, bf16[200,384]{1,0:T(8,128)(2,1)}, u32[]{:S(2)}, u32[]{:S(2)}) %collective-permute-start.3) | collective-permute-done | bytes 153632 | tf_op jit(solution)/shard_map/ppermute | solution.py:344
  42.3 0.2 collective-permute-done.4
  42.5 1.2 %add_convert_fusion.mine_ref = bf16[200,384]{1,0:T(8,128)(2,1)S(1)} fusion(bf16[200,384]{1,0:T(8,128)(2,1)} %collective-permute-done.4, bf16[200,384]{1,0:T(8,128)(2,1)} %collective-permute-done.3, bf16[200,384]{1,0:T(8,128)(2,1)} %collective-permute-done.2, bf16[200,384]{1,0:T(8,128)(2,1)} %collective-permute-done.1, ...), kind=kLoop, calls=%fused_computation | loop fusion | flops 844800 | bytes 921601 | tf_op jit(solution)/shard_map/convert_element_type | solution.py:345
  43.8 0.0 all-to-all-done
  43.8 0.0 copy-start.4
  43.8 2.3 %library.1.near_ref = bf16[4,2,200,384]{3,2,1,0:T(8,128)(2,1)S(1)} custom-call(bf16[8,4,48,384]{3,2,1,0:T(8,128)(2,1)S(1)} %bitcast.4, bf16[1168,256]{1,0:T(8,128)(2,1)S(1)} %copy-done), custom_call_target="tpu_custom_call" | custom-call | flops 629145600 | bytes 4194304 | tf_op jit(solution)/shard_map/library/pallas_call | solution.py:362
  46.1 0.0 copy-start.11
  46.1 0.1 collective-permute-start.6
  46.2 0.5 collective-permute-start.7
  46.7 2.6 %collective-permute-done.7.theirs_ref = bf16[200,384]{1,0:T(8,128)(2,1)S(1)} collective-permute-done((bf16[200,384]{1,0:T(8,128)(2,1)S(1)}, bf16[200,384]{1,0:T(8,128)(2,1)S(1)}, u32[]{:S(2)}, u32[]{:S(2)}) %collective-permute-start.7) | collective-permute-done | bytes 153632 | tf_op jit(solution)/shard_map/ppermute | solution.py:376
  49.4 0.0 copy-done.4
  49.4 0.4 whiten.1
  49.8 0.0 collective-permute-done.6.far_ref
  49.8 0.0 copy-done.11
  49.8 4.0 %match_other.1 = bf16[2,200,384]{2,1,0:T(8,128)(2,1)S(1)} custom-call(bf16[4,2,200,384]{3,2,1,0:T(8,128)(2,1)S(1)} %library.1.near_ref, bf16[4,2,200,384]{3,2,1,0:T(8,128)(2,1)S(1)} %collective-permute-done.6.far_ref, f32[2,2,200,384]{3,2,1,0:T(8,128)S(1)} %get-tuple-element.23.spec_ref, f32[2,200,384]{2,1,0:T(8,128)S(1)} %get-tuple-element.24.weight_ref, ...), custom_call_target="tpu_custom_call" | custom-call | flops 2516582400 | bytes 6291456 | tf_op jit(solution)/shard_map/match_other/pallas_call | solution.py:391
  53.9 0.0 copy-start.6
  53.9 0.6 collective-permute-start.8
  54.5 4.0 %match_own.1.best_ref = f32[2,200,384]{2,1,0:T(8,128)S(1)} custom-call(bf16[4,2,200,384]{3,2,1,0:T(8,128)(2,1)S(1)} %library.1.near_ref, bf16[4,2,200,384]{3,2,1,0:T(8,128)(2,1)S(1)} %collective-permute-done.6.far_ref, f32[2,2,200,384]{3,2,1,0:T(8,128)S(1)} %get-tuple-element.23.spec_ref, f32[2,200,384]{2,1,0:T(8,128)S(1)} %get-tuple-element.24.weight_ref, ...), custom_call_target="tpu_custom_call" | custom-call | flops 2516582400 | bytes 6291456 | tf_op jit(solution)/shard_map/match_own/pallas_call | solution.py:391
  58.5 5.7 %collective-permute-done.8.got_ref = bf16[2,200,384]{2,1,0:T(8,128)(2,1)S(1)} collective-permute-done((bf16[2,200,384]{2,1,0:T(8,128)(2,1)S(1)}, bf16[2,200,384]{2,1,0:T(8,128)(2,1)S(1)}, u32[]{:S(2)}, u32[]{:S(2)}) %collective-permute-start.8) | collective-permute-done | bytes 307232 | tf_op jit(solution)/shard_map/ppermute | solution.py:409
  64.2 0.0 copy-done.6
  64.2 1.3 %join.1 = f32[384,384]{1,0:T(8,128)} custom-call(f32[2,200,384]{2,1,0:T(8,128)S(1)} %match_own.1.best_ref, bf16[2,200,384]{2,1,0:T(8,128)(2,1)S(1)} %collective-permute-done.8.got_ref, bf16[192,400]{1,0:T(8,128)(2,1)S(1)} %copy-done.6), custom_call_target="tpu_custom_call" | custom-call | flops 176947200 | bytes 2097152 | tf_op jit(solution)/shard_map/join/pallas_call | solution.py:411
  (1 shorter events, 0.0 us)
Async XLA Ops:
  2.1 10.6 %copy-start = (bf16[1168,256]{1,0:T(8,128)(2,1)S(1)}, bf16[1168,256]{1,0:T(8,128)(2,1)}, u32[]{:S(2)}) copy-start(bf16[1168,256]{1,0:T(8,128)(2,1)} %constant.14.clone.tab_ref) | copy-start | bytes 1794052
  2.1 10.6 %copy-start.5 = (bf16[1,1,384,384]{3,2,1,0:T(8,128)(2,1)S(1)}, bf16[1,1,384,384]{3,2,1,0:T(8,128)(2,1)}, u32[]{:S(2)}) copy-start(bf16[1,1,384,384]{3,2,1,0:T(8,128)(2,1)} %param.10) | copy-start | bytes 884740
  2.1 41.6 %all-to-all-start = ((bf16[32,48,384]{2,1,0:T(8,128)(2,1)}), bf16[32,48,384]{2,1,0:T(8,128)(2,1)S(1)}, u32[]{:S(2)}, u32[]{:S(2)}) async-start(bf16[32,48,384]{2,1,0:T(8,128)(2,1)} %copies.1), calls=%async_computation | async-start | bytes 2359296 | tf_op jit(solution)/shard_map/all_to_all | solution.py:305
  12.8 21.6 %copy-start.7 = (f32[64]{0:T(128)S(1)}, f32[64]{0:T(128)}, u32[]{:S(2)}) copy-start(f32[64]{0:T(128)} %d_ref.1) | copy-start | bytes 772
  12.8 21.6 %copy-start.8 = (f32[64]{0:T(128)S(1)}, f32[64]{0:T(128)}, u32[]{:S(2)}) copy-start(f32[64]{0:T(128)} %a_ref.1) | copy-start | bytes 772
  12.8 21.6 %copy-start.9 = (f32[64]{0:T(128)S(1)}, f32[64]{0:T(128)}, u32[]{:S(2)}) copy-start(f32[64]{0:T(128)} %x_ref.1) | copy-start | bytes 772
  12.8 21.6 %copy-start.10 = (f32[64]{0:T(128)S(1)}, f32[64]{0:T(128)}, u32[]{:S(2)}) copy-start(f32[64]{0:T(128)} %p_ref.1) | copy-start | bytes 772
  13.4 0.8 %copy-start.1 = (f32[2,200,384]{2,1,0:T(8,128)}, f32[2,200,384]{2,1,0:T(8,128)S(1)}, u32[]{:S(2)}) copy-start(f32[2,200,384]{2,1,0:T(8,128)S(1)} %get-tuple-element.17.own_ref) | copy-start | bytes 1843204
  14.2 3.4 %collective-permute-start = (bf16[200,384]{1,0:T(8,128)(2,1)S(1)}, bf16[200,384]{1,0:T(8,128)(2,1)S(1)}, u32[]{:S(2)}, u32[]{:S(2)}) collective-permute-start(bf16[200,384]{1,0:T(8,128)(2,1)S(1)} %get-tuple-element.15), channel_id=1, source_target_pairs={{0,1},{1,0},{2,3},{3,2},{4,5},{5,4},{6,7},{7,6},{8,9},{9,8},{10,11... | collective-permute-start | bytes 460808 | tf_op jit(solution)/shard_map/ppermute | solution.py:333
  15.2 18.6 %collective-permute-start.5 = (bf16[400,384]{1,0:T(8,128)(2,1)S(1)}, bf16[400,384]{1,0:T(8,128)(2,1)S(1)}, u32[]{:S(2)}, u32[]{:S(2)}) collective-permute-start(bf16[400,384]{1,0:T(8,128)(2,1)S(1)} %get-tuple-element.16), channel_id=1, source_target_pairs={{0,2},{2,0},{1,3},{3,1},{4,6},{6,4},{5,7},{7,5},{8,10},{10,8},{9,1... | collective-permute-start | bytes 921608 | tf_op jit(solution)/shard_map/ppermute | solution.py:321
  17.7 20.3 %collective-permute-start.1 = (bf16[200,384]{1,0:T(8,128)(2,1)S(1)}, bf16[200,384]{1,0:T(8,128)(2,1)}, u32[]{:S(2)}, u32[]{:S(2)}) collective-permute-start(bf16[200,384]{1,0:T(8,128)(2,1)S(1)} %add_convert_fusion.1), channel_id=1, source_target_pairs={{1,3},{3,1},{5,7},{7,5},{9,11},{11,9},{13,15},{15,13},{17,19},{19,... | collective-permute-start | bytes 460808 | tf_op jit(solution)/shard_map/ppermute | solution.py:344
  20.6 19.8 %collective-permute-start.2 = (bf16[200,384]{1,0:T(8,128)(2,1)S(1)}, bf16[200,384]{1,0:T(8,128)(2,1)}, u32[]{:S(2)}, u32[]{:S(2)}) collective-permute-start(bf16[200,384]{1,0:T(8,128)(2,1)S(1)} %add_convert_fusion.1), channel_id=1, source_target_pairs={{0,4},{1,7},{2,6},{3,5},{4,8},{5,11},{6,10},{7,9},{8,12},{9,15},{1... | collective-permute-start | bytes 460808 | tf_op jit(solution)/shard_map/ppermute | solution.py:344
  23.9 18.5 %collective-permute-start.3 = (bf16[200,384]{1,0:T(8,128)(2,1)S(1)}, bf16[200,384]{1,0:T(8,128)(2,1)}, u32[]{:S(2)}, u32[]{:S(2)}) collective-permute-start(bf16[200,384]{1,0:T(8,128)(2,1)S(1)} %add_convert_fusion.1), channel_id=1, source_target_pairs={{0,8},{1,11},{2,10},{3,9},{4,12},{5,15},{6,14},{7,13},{8,0},{9,3},... | collective-permute-start | bytes 460808 | tf_op jit(solution)/shard_map/ppermute | solution.py:344
  27.0 15.5 %collective-permute-start.4 = (bf16[200,384]{1,0:T(8,128)(2,1)S(1)}, bf16[200,384]{1,0:T(8,128)(2,1)}, u32[]{:S(2)}, u32[]{:S(2)}) collective-permute-start(bf16[200,384]{1,0:T(8,128)(2,1)S(1)} %add_convert_fusion.1), channel_id=1, source_target_pairs={{0,12},{1,15},{2,14},{3,13},{4,0},{5,3},{6,2},{7,1},{8,4},{9,7},{1... | collective-permute-start | bytes 460808 | tf_op jit(solution)/shard_map/ppermute | solution.py:344
  29.9 4.5 %copy-start.2 = (f32[2,200,384]{2,1,0:T(8,128)S(1)}, f32[2,200,384]{2,1,0:T(8,128)}, u32[]{:S(2)}) copy-start(f32[2,200,384]{2,1,0:T(8,128)} %copy-done.1) | copy-start | bytes 1843204
  37.1 0.8 %copy-start.3 = (f32[2,200,384]{2,1,0:T(8,128)}, f32[2,200,384]{2,1,0:T(8,128)S(1)}, u32[]{:S(2)}) copy-start(f32[2,200,384]{2,1,0:T(8,128)S(1)} %get-tuple-element.21.weight_ref) | copy-start | bytes 1843204
  43.8 5.6 %copy-start.4 = (f32[2,200,384]{2,1,0:T(8,128)S(1)}, f32[2,200,384]{2,1,0:T(8,128)}, u32[]{:S(2)}) copy-start(f32[2,200,384]{2,1,0:T(8,128)} %copy-done.3) | copy-start | bytes 1843204
  46.1 3.7 %copy-start.11 = (bf16[1184,256]{1,0:T(8,128)(2,1)S(1)}, bf16[1184,256]{1,0:T(8,128)(2,1)}, u32[]{:S(2)}) copy-start(bf16[1184,256]{1,0:T(8,128)(2,1)} %constant.15.clone.tab_ref) | copy-start | bytes 1818628
  46.1 3.7 %collective-permute-start.6 = (bf16[4,2,200,384]{3,2,1,0:T(8,128)(2,1)S(1)}, bf16[4,2,200,384]{3,2,1,0:T(8,128)(2,1)S(1)}, u32[]{:S(2)}, u32[]{:S(2)}) collective-permute-start(bf16[4,2,200,384]{3,2,1,0:T(8,128)(2,1)S(1)} %library.1.near_ref), channel_id=1, source_target_pairs={{0,1},{1,0},{2,3},{3,2},{4,5},{5,4},{6,7},{7,6},{8,9},{9,8},{10,11... | collective-permute-start | bytes 3686408 | tf_op jit(solution)/shard_map/ppermute | solution.py:375
  46.2 3.1 %collective-permute-start.7 = (bf16[200,384]{1,0:T(8,128)(2,1)S(1)}, bf16[200,384]{1,0:T(8,128)(2,1)S(1)}, u32[]{:S(2)}, u32[]{:S(2)}) collective-permute-start(bf16[200,384]{1,0:T(8,128)(2,1)S(1)} %add_convert_fusion.mine_ref), channel_id=1, source_target_pairs={{0,1},{1,0},{2,3},{3,2},{4,5},{5,4},{6,7},{7,6},{8,9},{9,8},{10,11... | collective-permute-start | bytes 460808 | tf_op jit(solution)/shard_map/ppermute | solution.py:376
  53.9 10.3 %copy-start.6 = (bf16[192,400]{1,0:T(8,128)(2,1)S(1)}, bf16[192,400]{1,0:T(8,128)(2,1)}, u32[]{:S(2)}) copy-start(bf16[192,400]{1,0:T(8,128)(2,1)} %constant.16.clone.unfold_ref) | copy-start | bytes 460804
  53.9 10.3 %collective-permute-start.8 = (bf16[2,200,384]{2,1,0:T(8,128)(2,1)S(1)}, bf16[2,200,384]{2,1,0:T(8,128)(2,1)S(1)}, u32[]{:S(2)}, u32[]{:S(2)}) collective-permute-start(bf16[2,200,384]{2,1,0:T(8,128)(2,1)S(1)} %match_other.1), channel_id=1, source_target_pairs={{0,2},{2,0},{1,3},{3,1},{4,6},{6,4},{5,7},{7,5},{8,10},{10,8},{9,1... | collective-permute-start | bytes 921608 | tf_op jit(solution)/shard_map/ppermute | solution.py:409

commit v6 on v5

v6 whole, which is shorter than its diff:
```python
import math

import jax
import jax.numpy as jnp
import ml_dtypes
import numpy as np
from jax import lax
from jax.experimental import pallas as pl
from jax.experimental.pallas import tpu as pltpu
from jax.sharding import Mesh
from jax.sharding import PartitionSpec as P

DEF = ("xlo", "y")
BLK = ("z", "xhi", "core")
LIB = ("xlo", "y", "z")
N = 384
HALF = N // 2
THIRD = N // 3
BLOCKS = (64, 64, 72)
ROWS = sum(BLOCKS)
SPLIT = 96
PART = ROWS - SPLIT
FOLD = 208
ROOT = math.sqrt(3.0) / 2.0
F32 = jnp.float32
BF16 = jnp.bfloat16


def tables():
    j = np.arange(N)
    phase = (j[:, None] * j[None, :]) % N
    cos = np.cos(2.0 * np.pi * phase / N)
    sin = np.sin(2.0 * np.pi * phase / N)
    bf = ml_dtypes.bfloat16
    u = np.concatenate([3 * np.arange(b) + c for c, b in zip((1, 2, 0), BLOCKS)])
    keep = (u <= HALF)[:, None]
    u = np.minimum(u, HALF)
    r = np.arange(THIRD)
    b1, b2 = BLOCKS[0], BLOCKS[0] + BLOCKS[1]
    real = np.concatenate([(keep * cos[u])[b2:, r], (keep * -sin[u])[b2:, r]])
    c1, s1 = cos[u[:b1]][:, r], sin[u[:b1]][:, r]
    c2, s2 = cos[u[b1:b2]][:, r], sin[u[b1:b2]][:, r]
    pair = np.block([[c1, s1], [c2, -s2], [-s1, c1], [-s2, -c2]])
    ahead, back = [], []
    for k in range(3):
        ck = cos[r][:, 3 * r + k]
        sk = sin[r][:, 3 * r + k]
        ahead.append(np.block([[ck, -sk], [sk, ck]]))
        back.append(np.block([[ck.T, sk.T], [-sk.T, ck.T]]))
    ahead, back = np.stack(ahead), np.stack(back)
    weight = np.where((u == 0) | (u == HALF), 1.0, 2.0) * keep[:, 0]
    fold = np.zeros((2, ROWS, ROWS))
    fold[0, : HALF + 1] = cos[: HALF + 1][:, u].astype(bf).astype(float) * weight
    fold[1, : HALF + 1] = sin[: HALF + 1][:, u].astype(bf).astype(float) * weight
    unfold = np.zeros((HALF, 2 * ROWS))
    unfold[0, HALF] = 1.0
    for i in range(1, HALF):
        unfold[i, ROWS + HALF - i] = 1.0
    ahead_all = np.concatenate([ahead.reshape(-1, 2 * THIRD), pair, np.pad(real, ((0, 0), (0, THIRD)))])
    pad = ((0, 0), (0, FOLD - ROWS), (0, 2 * THIRD - ROWS))
    back_all = np.concatenate([back.reshape(-1, 2 * THIRD), np.pad(fold, pad).reshape(-1, 2 * THIRD)])
    return [jnp.asarray(a.astype(bf)) for a in (ahead_all, back_all, unfold)]


def dot(a, b):
    return jnp.dot(a, b, preferred_element_type=F32)


def row_numbers():
    i = lax.broadcasted_iota(jnp.int32, (ROWS, N), 0)
    k = lax.broadcasted_iota(jnp.int32, (ROWS, N), 1)
    b1, b2 = BLOCKS[0], BLOCKS[0] + BLOCKS[1]
    u = jnp.where(i < b1, 3 * i + 1, jnp.where(i < b2, 3 * (i - b1) + 2, 3 * (i - b2)))
    v = jnp.where(
        k < THIRD, 3 * k, jnp.where(k < 2 * THIRD, 3 * (k - THIRD) + 1, 3 * (k - 2 * THIRD) + 2)
    )
    return u, v


def row_scale(u):
    return jnp.where((u > 0) & (u < HALF), 2.0, jnp.where(u <= HALF, 1.0, 0.0))


def copy_kernel(block_ref, out_ref, wide_sc, sems):
    count = wide_sc.shape[0]
    wide_sc[...] = jnp.broadcast_to(block_ref[...][None], wide_sc.shape)
    moves = [
        pltpu.make_async_copy(wide_sc, out_ref.at[pl.ds(i * count, count)], sems.at[i])
        for i in range(out_ref.shape[0] // count)
    ]
    for move in moves:
        move.start()
    for move in moves:
        move.wait()


def sine(x):
    x = x - jnp.round(x)
    a = jnp.abs(x)
    a = jnp.minimum(a, 0.5 - a)
    s = a * a
    p = jnp.full_like(x, -15.0946425768229800)
    for c in (
        42.0586939448600400,
        -76.7058597530613900,
        81.6052492760750400,
        -41.3417022403997600,
        6.28318530717958648,
    ):
        p = p * s + c
    p = p * a
    return jnp.where(x < 0.0, -p, p)


def half_spectrum(image, tab):
    wide = 2 * THIRD
    pair, real = tab[3 * wide : 4 * wide, :], tab[4 * wide :, :THIRD]
    image = image.astype(F32)
    x0, x1, x2 = image[:THIRD], image[THIRD : 2 * THIRD], image[2 * THIRD :]
    plus, minus = x1 + x2, x1 - x2
    f0 = (x0 + plus).astype(BF16)
    f1 = jnp.concatenate([(x0 - 0.5 * plus).astype(BF16), (-ROOT * minus).astype(BF16)], axis=0)
    low = dot(real, f0)
    high = dot(pair, f1)
    b, c = BLOCKS[0] + BLOCKS[1], BLOCKS[2]
    re = jnp.concatenate([high[:b], low[:c]], axis=0)
    im = jnp.concatenate([high[b:], low[c:]], axis=0)
    r0, r1, r2 = re[:, :THIRD], re[:, THIRD : 2 * THIRD], re[:, 2 * THIRD :]
    i0, i1, i2 = im[:, :THIRD], im[:, THIRD : 2 * THIRD], im[:, 2 * THIRD :]
    rp, rm = r1 + r2, ROOT * (r1 - r2)
    ip, im_ = i1 + i2, ROOT * (i1 - i2)
    rh, ih = r0 - 0.5 * rp, i0 - 0.5 * ip
    parts = ((r0 + rp, i0 + ip), (rh + im_, ih - rm), (rh - im_, ih + rm))
    result = []
    for k, (a, b) in enumerate(parts):
        lhs = jnp.concatenate([a.astype(BF16), b.astype(BF16)], axis=1)
        out = dot(lhs, tab[k * wide : (k + 1) * wide, :])
        result.append((out[:, :THIRD], out[:, THIRD:]))
    return result


def store_spectrum(ref, parts):
    for k, (re, im) in enumerate(parts):
        at = slice(k * THIRD, (k + 1) * THIRD)
        ref[0, :, at] = re.astype(ref.dtype)
        ref[1, :, at] = im.astype(ref.dtype)


def ctf_factors(row, table):
    lane = lax.broadcasted_iota(jnp.int32, table.shape, 1).astype(F32)
    chosen = jnp.sum(jnp.where(lane == row, table, 0.0), axis=1, keepdims=True)
    chosen = chosen * (1.0 / (2.0 * math.pi))
    u, v = row_numbers()
    row = jnp.where(u < HALF, u, u - N).astype(F32) * (1.0 / N)
    col = jnp.where(v < HALF, v, v - N).astype(F32) * (1.0 / N)
    r2, c2 = row * row, col * col
    base = chosen[0:1] * (r2 + c2) + chosen[1:2] * (r2 - c2) + chosen[3:4]
    cross = chosen[2:3] * (2.0 * row * col)
    plus = -sine(base + cross)
    at = slice(0, THIRD)
    inner = (u[:, at] > 0) & (u[:, at] < HALF) & (v[:, at] == HALF)
    mirror = jnp.where(inner, -sine(base[:, at] - cross[:, at]), plus[:, at])
    gain = jnp.concatenate([0.5 * (plus[:, at] + mirror), plus[:, THIRD:]], axis=1)
    square = plus * plus
    square = jnp.concatenate(
        [0.5 * (square[:, at] + mirror * mirror), square[:, THIRD:]], axis=1
    )
    return gain, row_scale(u) * square


def tile_kernel(core_ref, mate_ref, own_ref, other_ref, tab_ref, spec_ref, keep_ref, send_ref, power_sc):
    parts = half_spectrum(own_ref[...], tab_ref)
    store_spectrum(spec_ref.at[0], parts)
    for k, (re, im) in enumerate(parts):
        power_sc[:, k * THIRD : (k + 1) * THIRD] = re * re + im * im
    low, high = power_sc[:PART], power_sc[SPLIT:]
    first = core_ref[...] == 0
    keep_ref[...] = jnp.where(first, low, high).astype(BF16)
    send_ref[...] = jnp.where(first, high, low).astype(BF16)
    store_spectrum(spec_ref.at[1], half_spectrum(other_ref[...], tab_ref))


def gain_kernel(row_ref, mate_ref, table_ref, tile_ref, spec_ref, weight_ref):
    for t, ref in enumerate((row_ref, mate_ref)):
        gain, weight_ref[t] = ctf_factors(ref[...].astype(F32), table_ref[...])
        spec_ref[t, 0] = tile_ref[t, 0] * gain
        spec_ref[t, 1] = tile_ref[t, 1] * gain


def library_kernel(image_ref, tab_ref, out_ref):
    store_spectrum(out_ref, half_spectrum(image_ref[...].reshape(N, N), tab_ref))


def match_step(re, im, spec_ref, weight_ref, tab):
    wide = 2 * THIRD
    norm = jnp.sum((re * re + im * im) * weight_ref[...])
    scale = lax.rsqrt(jnp.full((1, THIRD), norm + 1e-06, F32))
    s_re, s_im = spec_ref[0], spec_ref[1]
    p_re = (s_re * re + s_im * im).astype(BF16)
    p_im = (s_im * re - s_re * im).astype(BF16)
    g = []
    for k in range(3):
        at = slice(k * THIRD, (k + 1) * THIRD)
        lhs = jnp.concatenate([p_re[:, at], p_im[:, at]], axis=1)
        g.append(dot(lhs, tab[k * wide : (k + 1) * wide, :]))
    (r0, i0), (r1, i1), (r2, i2) = ((x[:, :THIRD], x[:, THIRD:]) for x in g)
    slant = scale * ROOT
    rp, rm = r1 + r2, slant * (r1 - r2)
    ip, im_ = i1 + i2, slant * (i1 - i2)
    rh, ih = scale * (r0 - 0.5 * rp), scale * (i0 - 0.5 * ip)
    h_re = [scale * (r0 + rp), rh - im_, rh + im_]
    h_im = [scale * (i0 + ip), ih + rm, ih - rm]
    h_re = jnp.concatenate([h.astype(BF16) for h in h_re], axis=1)
    h_im = jnp.concatenate([h.astype(BF16) for h in h_im], axis=1)
    first = 3 * wide
    even = dot(tab[first : first + ROWS, :ROWS], h_re)
    odd = dot(tab[first + FOLD : first + FOLD + ROWS, :ROWS], h_im)
    return even - odd, even + odd


def match_kernel(
    core_ref,
    near_ref,
    far_ref,
    spec_ref,
    weight_ref,
    mine_ref,
    theirs_ref,
    tab_ref,
    unfold_ref,
    out_ref,
    spec_sc,
    weight_sc,
    best_sc,
):
    step = pl.program_id(0)

    @pl.when(step == 0)
    def _():
        u, _ = row_numbers()
        mine, theirs = mine_ref[...].astype(F32), theirs_ref[...].astype(F32)
        first = core_ref[...] == 0
        low, high = jnp.where(first, mine, theirs), jnp.where(first, theirs, mine)
        power = jnp.concatenate([low[:SPLIT], high], axis=0) * (1.0 / 16.0)
        mean = jnp.sum(power * row_scale(u)) * (1.0 / (N * N))
        inverse_noise = 1.0 / (jnp.where(u <= HALF, power, 1.0) + 0.05 * mean)
        spec_sc[0] = spec_ref[0] * inverse_noise
        spec_sc[1] = spec_ref[1] * inverse_noise
        weight_sc[...] = weight_ref[...] * inverse_noise
        best_sc[...] = jnp.full_like(best_sc, -jnp.inf)

    pairs = [
        match_step(ref[0].astype(F32), ref[1].astype(F32), spec_sc, weight_sc, tab_ref)
        for ref in (near_ref, far_ref)
    ]
    for side in range(2):
        best_sc[side] = jnp.maximum(best_sc[side], jnp.maximum(pairs[0][side], pairs[1][side]))

    @pl.when(step == pl.num_programs(0) - 1)
    def _():
        out_ref[:HALF] = best_sc[0, :HALF].astype(out_ref.dtype)
        rest = best_sc[...].reshape(2 * ROWS, N)
        total = None
        for _ in range(3 if out_ref.dtype == F32 else 1):
            part = rest.astype(BF16)
            rest = rest - part.astype(F32)
            moved = dot(unfold_ref[...], part)
            total = moved if total is None else total + moved
        out_ref[HALF:] = total.astype(out_ref.dtype)


def join_kernel(best_ref, got_ref, out_ref):
    out_ref[...] = jnp.maximum(best_ref[...], got_ref[...].astype(F32))


def full(*shape):
    return pl.BlockSpec(shape, lambda i: (0,) * len(shape))


def cost(flops, size):
    return pl.CostEstimate(flops=flops, bytes_accessed=size, transcendentals=0)


def params(mib):
    return pltpu.CompilerParams(vmem_limit_bytes=mib << 20)


def per_device(images, projections, ctf_row, defocus_term, astig_term, astig_cross, phase_shift):
    ahead, back, unfold = tables()
    groups = math.prod(lax.axis_size(a) for a in DEF)
    places = math.prod(lax.axis_size(a) for a in LIB)
    deep, wide = lax.axis_size("z"), lax.axis_size("xhi")
    core = lax.axis_index("core").astype(jnp.int32).reshape(1, 1)
    swap = [(0, 1), (1, 0)]
    plane = (2, ROWS, N)
    work = 2 * ROWS * 768 * 256 * 2

    tile = images[0, 0]
    received = lax.ppermute(tile, "xhi", swap)
    mate = lax.ppermute(ctf_row, "xhi", swap)
    block = projections[0]
    copies = pl.pallas_call(
        copy_kernel,
        out_shape=pltpu.HBM((places,) + block.shape, BF16),
        grid=(1,),
        in_specs=[full(*block.shape)],
        out_specs=pl.BlockSpec(memory_space=pltpu.HBM),
        scratch_shapes=[
            pltpu.VMEM((groups,) + block.shape, BF16),
            pltpu.SemaphoreType.DMA((places // groups,)),
        ],
        cost_estimate=cost(0, 1 << 20),
        name="copies",
    )(block)
    images_all = lax.all_to_all(copies, LIB, 0, 0, tiled=False)

    tiles, keep, send = pl.pallas_call(
        tile_kernel,
        out_shape=[
            jax.ShapeDtypeStruct((2,) + plane, F32),
            jax.ShapeDtypeStruct((PART, N), BF16),
            jax.ShapeDtypeStruct((PART, N), BF16),
        ],
        grid=(1,),
        in_specs=[full(1, 1), full(1, 1), full(N, N), full(N, N), full(*ahead.shape)],
        out_specs=[full(2, *plane), full(PART, N), full(PART, N)],
        scratch_shapes=[pltpu.VMEM((ROWS, N), F32)],
        compiler_params=params(16),
        cost_estimate=cost(200 * work, 3 << 20),
        name="tile",
    )(core, mate, tile, received, ahead)

    pair = (keep.astype(F32) + lax.ppermute(send, "core", swap).astype(F32)).astype(BF16)
    sums = pair.astype(F32)
    for dz in range(1, deep):
        moved = lax.ppermute(pair, "z", [(z, (z + dz) % deep) for z in range(deep)])
        sums = sums + moved.astype(F32)
    sums = sums.astype(BF16)

    table = jnp.stack([defocus_term, astig_term, astig_cross, phase_shift])
    table = jnp.pad(table, ((0, 4), (0, 128 - table.shape[1])))
    spec, weight = pl.pallas_call(
        gain_kernel,
        out_shape=[
            jax.ShapeDtypeStruct((2,) + plane, F32),
            jax.ShapeDtypeStruct((2, ROWS, N), F32),
        ],
        grid=(1,),
        in_specs=[full(1, 1), full(1, 1), full(*table.shape), full(2, *plane)],
        out_specs=[full(2, *plane), full(2, ROWS, N)],
        compiler_params=params(20),
        cost_estimate=cost(2 * ROWS * N * 60, 4 << 20),
        name="gain",
    )(ctf_row, mate, table, tiles)

    images_all, sums, spec = lax.optimization_barrier((images_all, sums, spec))
    across = lax.ppermute(sums, "xhi", swap)
    mine = (sums.astype(F32) + across.astype(F32)).astype(BF16)
    theirs = lax.ppermute(mine, "core", swap)

    near_all = pl.pallas_call(
        library_kernel,
        out_shape=jax.ShapeDtypeStruct((deep,) + plane, BF16),
        grid=(deep,),
        in_specs=[
            pl.BlockSpec((groups, None, N // groups, N), lambda i: (0, i, 0, 0)),
            full(*ahead.shape),
        ],
        out_specs=pl.BlockSpec((None,) + plane, lambda i: (i, 0, 0, 0)),
        compiler_params=params(16),
        cost_estimate=cost(100 * deep * work, 4 << 20),
        name="library",
    )(images_all.reshape(groups, deep, N // groups, N), ahead)
    far_all = lax.ppermute(near_all, "core", swap)
    def match(t, dtype, name):
        lib_spec = pl.BlockSpec((None,) + plane, lambda i: (i, 0, 0, 0))
        return pl.pallas_call(
            match_kernel,
            out_shape=jax.ShapeDtypeStruct((N, N), dtype),
            grid=(deep,),
            in_specs=[
                full(1, 1),
                lib_spec,
                lib_spec,
                pl.BlockSpec((None,) + plane, lambda i: (t, 0, 0, 0)),
                pl.BlockSpec((None, ROWS, N), lambda i: (t, 0, 0)),
                full(PART, N),
                full(PART, N),
                full(*back.shape),
                full(*unfold.shape),
            ],
            out_specs=full(N, N),
            scratch_shapes=[
                pltpu.VMEM(plane, F32),
                pltpu.VMEM((ROWS, N), F32),
                pltpu.VMEM(plane, F32),
            ],
            compiler_params=params(20),
            cost_estimate=cost(2 * deep * 2 * work, 6 << 20),
            name=name,
        )(core, near_all, far_all, spec, weight, mine, theirs, back, unfold)

    got = lax.ppermute(match(1, BF16, "match_other"), "xhi", swap)
    best = match(0, F32, "match_own")
    peak = pl.pallas_call(
        join_kernel,
        out_shape=jax.ShapeDtypeStruct((N, N), F32),
        grid=(1,),
        in_specs=[full(N, N), full(N, N)],
        out_specs=full(N, N),
        cost_estimate=cost(N * N, 1 << 20),
        name="join",
    )(best, got)
    return peak[None, None]


def solution(mesh):
    fine = Mesh(mesh.devices.reshape(2, 4, 4, 2, 2), DEF + BLK)
    in_specs = (P(DEF, BLK, None, None), P(BLK, DEF, None), P(DEF, BLK), P(), P(), P(), P())
    out_specs = P(DEF, BLK, None, None)
    return jax.shard_map(
        per_device, mesh=fine, in_specs=in_specs, out_specs=out_specs, check_vma=False
    )
```

time: 65.9 us -> 65 us (0.986)
  starting transfers between devices: 26.7 us -> 25 us
  other arithmetic: 1.29 us -> 0.1 us
  Pallas kernels: 18.1 us -> 19.2 us
  local copies, waits for them, and re-layouts: 1.72 us -> 2.66 us
    ppermute x6 -> x7, waiting for transfers between devices: 8.53 us -> 14.3 us  [the longest x3 11 us: per_device(): moved = lax.ppermute(pair, 'z', [(z, (z + dz) % deep) for z in range(deep)])]
    ppermute x1, waiting for transfers between devices: 5.66 us -> 1.63 us  [per_device(): got = lax.ppermute(match(1, BF16, 'match_other'), 'xhi', swap)]
    ppermute x6 -> x7, starting transfers between devices: 15.6 us -> 11.6 us  [the longest x3 3.95 us: per_device(): moved = lax.ppermute(pair, 'z', [(z, (z + dz) % deep) for z in range(deep)])]
    ppermute x1, starting transfers between devices: 0.6 us -> 2.52 us  [per_device(): got = lax.ppermute(match(1, BF16, 'match_other'), 'xhi', swap)]
    ppermute x1, waiting for transfers between devices: 2.63 us -> 0.92 us  [per_device(): theirs = lax.ppermute(mine, 'core', swap)]
    convert_element_type x2 -> x3, other arithmetic: 1.29 us -> 0.09 us  [the longest x1 0.04 us: per_device(): sums = sums.astype(BF16)]
    pallas_call x6 -> x4, Pallas kernels: 11.7 us -> 12.8 us  [the longest x2 9.47 us: match(): pl.pallas_call(match_kernel, out_shape=jax.ShapeDtypeStruct((N, N), dtype...]
    unnamed x24 -> x22, local copies, waits for them, and re-layouts: 1.72 us -> 2.66 us
  transfers between devices with their start and end apart: 10 -> 11, of which waited for: 6 -> 7; matrix products, arithmetic and copies ran while one was open for 2% -> 0% of each run, Pallas kernels for 13% -> 16%
where the time goes in v6:
time: 65 us; the launch traced here: 64.7 us
  starting transfers between devices  25 us (38%)
  Pallas kernels  19.2 us (30%)
  waiting for transfers between devices  16.8 us (26%)
  local copies, waits for them, and re-layouts  2.66 us (4%)
  between operations  0.84 us (1%)
    ppermute x3, waiting for transfers between devices, per_device(): moved = lax.ppermute(pair, 'z', [(z, (z + dz) % deep) for z in range(deep)])  11 us
    pallas_call x2, Pallas kernels, match(): pl.pallas_call(match_kernel, out_shape=jax.ShapeDtypeStruct((N, N), dtype...  9.47 us
    all_to_all x1, starting transfers between devices, per_device(): images_all = lax.all_to_all(copies, LIB, 0, 0, tiled=False)  9.32 us
    ppermute x3, starting transfers between devices, per_device(): moved = lax.ppermute(pair, 'z', [(z, (z + dz) % deep) for z in range(deep)])  3.95 us
    ppermute x1, starting transfers between devices, per_device(): received = lax.ppermute(tile, 'xhi', swap)  3.57 us
    ppermute x1, waiting for transfers between devices, per_device(): across = lax.ppermute(sums, 'xhi', swap)  3 us
    unnamed x22, local copies, waits for them, and re-layouts  2.66 us
    ppermute x1, starting transfers between devices, per_device(): got = lax.ppermute(match(1, BF16, 'match_other'), 'xhi', swap)  2.52 us
  transfers between devices with their start and end apart: 11, of which 7 were waited for; matrix products, arithmetic and copies ran while one was open for 0% of the time, Pallas kernels for 16%

profile of v6, /device:TPU:1, one launch (start us, length us, event | category | flops | bytes accessed | tf_op | source)
XLA Modules:
  0.0 64.7 jit_solution(7391912745409585120)
XLA Ops:
  0.0 3.6 %collective-permute-start.1 = (bf16[384,384]{1,0:T(8,128)(2,1)}, bf16[384,384]{1,0:T(8,128)(2,1)S(1)}, u32[]{:S(2)}, u32[]{:S(2)}) collective-permute-start(bf16[384,384]{1,0:T(8,128)(2,1)} %bitcast.10), channel_id=1, source_target_pairs={{0,2},{2,0},{1,3},{3,1},{4,6},{6,4},{5,7},{7,5},{8,10},{10,8},{9,1... | collective-permute-start | bytes 884744 | tf_op jit(solution)/shard_map/ppermute | solution.py:299
  3.6 0.0 collective-permute-start
  3.6 1.9 %copies.1 = bf16[32,48,384]{2,1,0:T(8,128)(2,1)} custom-call(bf16[48,384]{1,0:T(8,128)(2,1)} %bitcast.12), custom_call_target="tpu_custom_call" | custom-call | bytes 1048576 | tf_op jit(solution)/shard_map/copies/pallas_call | solution.py:302
  5.5 0.0 copy-start.1
  5.5 0.0 copy-start.3
  5.5 9.3 %all-to-all-start = ((bf16[32,48,384]{2,1,0:T(8,128)(2,1)}), bf16[32,48,384]{2,1,0:T(8,128)(2,1)S(1)}, u32[]{:S(2)}, u32[]{:S(2)}) async-start(bf16[32,48,384]{2,1,0:T(8,128)(2,1)} %copies.1), calls=%async_computation | async-start | bytes 2359296 | tf_op jit(solution)/shard_map/all_to_all | solution.py:315
  14.8 0.0 collective-permute-done.mate_ref
  14.8 0.0 collective-permute-done.1.other_ref
  14.8 0.0 copy-done.1
  14.9 0.0 copy-done.3
  14.9 0.0 copy-start.7
  14.9 0.0 copy-start.8
  14.9 0.0 copy-start.9
  14.9 0.0 copy-start.10
  14.9 1.5 %tile.1 = (f32[2,2,200,384]{3,2,1,0:T(8,128)S(1)}, bf16[104,384]{1,0:T(8,128)(2,1)S(1)}, bf16[104,384]{1,0:T(8,128)(2,1)S(1)}) custom-call(s32[1,1]{1,0:T(1,128)} %bitcast.core_ref, s32[1,1]{1,0:T(1,128)} %collective-permute-done.mate_ref, bf16[384,384]{1,0:T(8,128)(2,1)S(1)} %bitcast.11, bf16[384,384]{1,0:T(8,128)(2,1)S(1)} %collective-permute-done.1.other_ref, ...), custom_call_target="tpu_custom_call" | custom-call | flops 31457280000 | bytes 3145728 | tf_op jit(solution)/shard_map/tile/pallas_call | solution.py:317
  16.4 1.6 %collective-permute-start.2 = (bf16[104,384]{1,0:T(8,128)(2,1)S(1)}, bf16[104,384]{1,0:T(8,128)(2,1)S(1)}, u32[]{:S(2)}, u32[]{:S(2)}) collective-permute-start(bf16[104,384]{1,0:T(8,128)(2,1)S(1)} %get-tuple-element.14), channel_id=1, source_target_pairs={{0,1},{1,0},{2,3},{3,2},{4,5},{5,4},{6,7},{7,6},{8,9},{9,8},{10,11... | collective-permute-start | bytes 239624 | tf_op jit(solution)/shard_map/ppermute | solution.py:333
  18.7 0.3 collective-permute-done.2
  19.0 2.8 %collective-permute-start.5 = (bf16[104,384]{1,0:T(8,128)(2,1)S(1)}, bf16[104,384]{1,0:T(8,128)(2,1)S(1)}, u32[]{:S(2)}, u32[]{:S(2)}) collective-permute-start(bf16[104,384]{1,0:T(8,128)(2,1)S(1)} %add_convert_fusion.2), channel_id=1, source_target_pairs={{0,12},{4,0},{8,4},{12,8},{1,13},{5,1},{9,5},{13,9},{2,14},{6,2},{... | collective-permute-start | bytes 239624 | tf_op jit(solution)/shard_map/ppermute | solution.py:336
  21.7 0.6 collective-permute-start.4
  22.3 0.6 collective-permute-start.3
  22.9 0.0 copy-done.7
  22.9 0.0 copy-done.8
  22.9 0.0 copy-done.9
  22.9 0.0 copy-done.10
  22.9 2.1 %gain.1 = (f32[2,2,200,384]{3,2,1,0:T(8,128)S(1)}, f32[2,200,384]{2,1,0:T(8,128)S(1)}) custom-call(s32[1,1]{1,0:T(1,128)S(6)} %copy.11.row_ref, s32[1,1]{1,0:T(1,128)} %collective-permute-done.mate_ref, f32[8,128]{1,0:T(8,128)S(1)} %select_maximum_fusion.table_ref, f32[2,2,200,384]{3,2,1,0:T(8,128)S(1)} %get-tuple-element.15.tile_ref), custom_call_target="tpu_custom_call" | custom-call | flops 9216000 | bytes 4194304 | tf_op jit(solution)/shard_map/gain/pallas_call | solution.py:342
  25.0 7.1 %collective-permute-done.5 = bf16[104,384]{1,0:T(8,128)(2,1)S(1)} collective-permute-done((bf16[104,384]{1,0:T(8,128)(2,1)S(1)}, bf16[104,384]{1,0:T(8,128)(2,1)S(1)}, u32[]{:S(2)}, u32[]{:S(2)}) %collective-permute-start.5) | collective-permute-done | bytes 79904 | tf_op jit(solution)/shard_map/ppermute | solution.py:336
  32.2 2.6 %collective-permute-done.4 = bf16[104,384]{1,0:T(8,128)(2,1)S(1)} collective-permute-done((bf16[104,384]{1,0:T(8,128)(2,1)S(1)}, bf16[104,384]{1,0:T(8,128)(2,1)S(1)}, u32[]{:S(2)}, u32[]{:S(2)}) %collective-permute-start.4) | collective-permute-done | bytes 79904 | tf_op jit(solution)/shard_map/ppermute | solution.py:336
  34.8 1.3 %collective-permute-done.3 = bf16[104,384]{1,0:T(8,128)(2,1)S(1)} collective-permute-done((bf16[104,384]{1,0:T(8,128)(2,1)S(1)}, bf16[104,384]{1,0:T(8,128)(2,1)S(1)}, u32[]{:S(2)}, u32[]{:S(2)}) %collective-permute-start.3) | collective-permute-done | bytes 79904 | tf_op jit(solution)/shard_map/ppermute | solution.py:336
  36.1 0.0 all-to-all-done
  36.1 0.0 copy-start.4
  36.1 1.1 %copy-done.4 = bf16[1168,256]{1,0:T(8,128)(2,1)S(1)} copy-done((bf16[1168,256]{1,0:T(8,128)(2,1)S(1)}, bf16[1168,256]{1,0:T(8,128)(2,1)}, u32[]{:S(2)}) %copy-start.4) | copy-done | bytes 598040
  37.2 0.0 copy-start.2
  37.2 0.0 copy-start.5
  37.2 2.3 %library.1.near_ref = bf16[4,2,200,384]{3,2,1,0:T(8,128)(2,1)S(1)} custom-call(bf16[8,4,48,384]{3,2,1,0:T(8,128)(2,1)S(1)} %bitcast.9, bf16[1168,256]{1,0:T(8,128)(2,1)S(1)} %copy-done.4), custom_call_target="tpu_custom_call" | custom-call | flops 62914560000 | bytes 4194304 | tf_op jit(solution)/shard_map/library/pallas_call | solution.py:361
  39.5 0.6 collective-permute-start.6
  40.1 2.5 %collective-permute-start.7 = (bf16[104,384]{1,0:T(8,128)(2,1)S(1)}, bf16[104,384]{1,0:T(8,128)(2,1)S(1)}, u32[]{:S(2)}, u32[]{:S(2)}) collective-permute-start(bf16[104,384]{1,0:T(8,128)(2,1)S(1)} %add_convert_fusion.1), channel_id=1, source_target_pairs={{0,2},{2,0},{1,3},{3,1},{4,6},{6,4},{5,7},{7,5},{8,10},{10,8},{9,1... | collective-permute-start | bytes 239624 | tf_op jit(solution)/shard_map/ppermute | solution.py:357
  42.6 3.0 %collective-permute-done.7 = bf16[104,384]{1,0:T(8,128)(2,1)S(1)} collective-permute-done((bf16[104,384]{1,0:T(8,128)(2,1)S(1)}, bf16[104,384]{1,0:T(8,128)(2,1)S(1)}, u32[]{:S(2)}, u32[]{:S(2)}) %collective-permute-start.7) | collective-permute-done | bytes 79904 | tf_op jit(solution)/shard_map/ppermute | solution.py:357
  45.6 1.0 %collective-permute-start.8 = (bf16[104,384]{1,0:T(8,128)(2,1)S(1)}, bf16[104,384]{1,0:T(8,128)(2,1)S(1)}, u32[]{:S(2)}, u32[]{:S(2)}) collective-permute-start(bf16[104,384]{1,0:T(8,128)(2,1)S(1)} %add_convert_fusion.mine_ref), channel_id=1, source_target_pairs={{0,1},{1,0},{2,3},{3,2},{4,5},{5,4},{6,7},{7,6},{8,9},{9,8},{10,11... | collective-permute-start | bytes 239624 | tf_op jit(solution)/shard_map/ppermute | solution.py:359
  46.5 0.9 %collective-permute-done.8.theirs_ref = bf16[104,384]{1,0:T(8,128)(2,1)S(1)} collective-permute-done((bf16[104,384]{1,0:T(8,128)(2,1)S(1)}, bf16[104,384]{1,0:T(8,128)(2,1)S(1)}, u32[]{:S(2)}, u32[]{:S(2)}) %collective-permute-start.8) | collective-permute-done | bytes 79904 | tf_op jit(solution)/shard_map/ppermute | solution.py:359
  47.5 0.0 collective-permute-done.6.far_ref
  47.5 0.0 copy-done.2
  47.5 0.0 copy-done.5
  47.5 4.6 %match_other.1 = bf16[384,384]{1,0:T(8,128)(2,1)S(1)} custom-call(s32[1,1]{1,0:T(1,128)} %bitcast.core_ref, bf16[4,2,200,384]{3,2,1,0:T(8,128)(2,1)S(1)} %library.1.near_ref, bf16[4,2,200,384]{3,2,1,0:T(8,128)(2,1)S(1)} %collective-permute-done.6.far_ref, f32[2,2,200,384]{3,2,1,0:T(8,128)S(1)} %get-tuple-element.18.spec_ref, ...), custom_call_target="tpu_custom_call" | custom-call | flops 2516582400 | bytes 6291456 | tf_op jit(solution)/shard_map/match_other/pallas_call | solution.py:377
  52.1 2.5 %collective-permute-start.9 = (bf16[384,384]{1,0:T(8,128)(2,1)S(1)}, bf16[384,384]{1,0:T(8,128)(2,1)S(1)}, u32[]{:S(2)}, u32[]{:S(2)}) collective-permute-start(bf16[384,384]{1,0:T(8,128)(2,1)S(1)} %match_other.1), channel_id=1, source_target_pairs={{0,2},{2,0},{1,3},{3,1},{4,6},{6,4},{5,7},{7,5},{8,10},{10,8},{9,1... | collective-permute-start | bytes 884744 | tf_op jit(solution)/shard_map/ppermute | solution.py:403
  54.6 4.8 %match_own.1.best_ref = f32[384,384]{1,0:T(8,128)S(1)} custom-call(s32[1,1]{1,0:T(1,128)} %bitcast.core_ref, bf16[4,2,200,384]{3,2,1,0:T(8,128)(2,1)S(1)} %library.1.near_ref, bf16[4,2,200,384]{3,2,1,0:T(8,128)(2,1)S(1)} %collective-permute-done.6.far_ref, f32[2,2,200,384]{3,2,1,0:T(8,128)S(1)} %get-tuple-element.18.spec_ref, ...), custom_call_target="tpu_custom_call" | custom-call | flops 2516582400 | bytes 6291456 | tf_op jit(solution)/shard_map/match_own/pallas_call | solution.py:377
  59.5 0.0 copy-start
  59.5 0.8 %copy-done = f32[384,384]{1,0:T(8,128)} copy-done((f32[384,384]{1,0:T(8,128)}, f32[384,384]{1,0:T(8,128)S(1)}, u32[]{:S(2)}) %copy-start) | copy-done | bytes 589848
  60.3 1.6 %collective-permute-done.9.got_ref = bf16[384,384]{1,0:T(8,128)(2,1)S(1)} collective-permute-done((bf16[384,384]{1,0:T(8,128)(2,1)S(1)}, bf16[384,384]{1,0:T(8,128)(2,1)S(1)}, u32[]{:S(2)}, u32[]{:S(2)}) %collective-permute-start.9) | collective-permute-done | bytes 294944 | tf_op jit(solution)/shard_map/ppermute | solution.py:403
  61.9 0.0 copy-start.6
  61.9 0.7 %copy-done.6 = bf16[384,384]{1,0:T(8,128)(2,1)} copy-done((bf16[384,384]{1,0:T(8,128)(2,1)}, bf16[384,384]{1,0:T(8,128)(2,1)S(1)}, u32[]{:S(2)}) %copy-start.6) | copy-done | bytes 294936
  62.7 2.0 %join.1 = f32[384,384]{1,0:T(8,128)} custom-call(f32[384,384]{1,0:T(8,128)} %copy-done, bf16[384,384]{1,0:T(8,128)(2,1)} %copy-done.6), custom_call_target="tpu_custom_call" | custom-call | flops 147456 | bytes 1048576 | tf_op jit(solution)/shard_map/join/pallas_call | solution.py:405
  (4 shorter events, 0.1 us)
Async XLA Ops:
  0.0 14.8 %collective-permute-start.1 = (bf16[384,384]{1,0:T(8,128)(2,1)}, bf16[384,384]{1,0:T(8,128)(2,1)S(1)}, u32[]{:S(2)}, u32[]{:S(2)}) collective-permute-start(bf16[384,384]{1,0:T(8,128)(2,1)} %bitcast.10), channel_id=1, source_target_pairs={{0,2},{2,0},{1,3},{3,1},{4,6},{6,4},{5,7},{7,5},{8,10},{10,8},{9,1... | collective-permute-start | bytes 884744 | tf_op jit(solution)/shard_map/ppermute | solution.py:299
  3.6 11.3 %collective-permute-start = (s32[1,1]{1,0:T(1,128)}, s32[1,1]{1,0:T(1,128)}, u32[]{:S(2)}, u32[]{:S(2)}) collective-permute-start(s32[1,1]{1,0:T(1,128)} %param.12), channel_id=1, source_target_pairs={{0,2},{2,0},{1,3},{3,1},{4,6},{6,4},{5,7},{7,5},{8,10},{10,8},{9,1... | collective-permute-start | bytes 20 | tf_op jit(solution)/shard_map/ppermute | solution.py:300
  5.5 9.4 %copy-start.1 = (bf16[1,1,384,384]{3,2,1,0:T(8,128)(2,1)S(1)}, bf16[1,1,384,384]{3,2,1,0:T(8,128)(2,1)}, u32[]{:S(2)}) copy-start(bf16[1,1,384,384]{3,2,1,0:T(8,128)(2,1)} %param.10) | copy-start | bytes 884740
  5.5 9.4 %copy-start.3 = (bf16[1168,256]{1,0:T(8,128)(2,1)S(1)}, bf16[1168,256]{1,0:T(8,128)(2,1)}, u32[]{:S(2)}) copy-start(bf16[1168,256]{1,0:T(8,128)(2,1)} %constant.13.clone.tab_ref) | copy-start | bytes 1794052
  5.5 30.6 %all-to-all-start = ((bf16[32,48,384]{2,1,0:T(8,128)(2,1)}), bf16[32,48,384]{2,1,0:T(8,128)(2,1)S(1)}, u32[]{:S(2)}, u32[]{:S(2)}) async-start(bf16[32,48,384]{2,1,0:T(8,128)(2,1)} %copies.1), calls=%async_computation | async-start | bytes 2359296 | tf_op jit(solution)/shard_map/all_to_all | solution.py:315
  14.9 8.0 %copy-start.7 = (f32[64]{0:T(128)S(1)}, f32[64]{0:T(128)}, u32[]{:S(2)}) copy-start(f32[64]{0:T(128)} %param.16) | copy-start | bytes 772
  14.9 8.0 %copy-start.8 = (f32[64]{0:T(128)S(1)}, f32[64]{0:T(128)}, u32[]{:S(2)}) copy-start(f32[64]{0:T(128)} %param.15) | copy-start | bytes 772
  14.9 8.0 %copy-start.9 = (f32[64]{0:T(128)S(1)}, f32[64]{0:T(128)}, u32[]{:S(2)}) copy-start(f32[64]{0:T(128)} %param.14) | copy-start | bytes 772
  14.9 8.0 %copy-start.10 = (f32[64]{0:T(128)S(1)}, f32[64]{0:T(128)}, u32[]{:S(2)}) copy-start(f32[64]{0:T(128)} %param.13) | copy-start | bytes 772
  16.4 2.5 %collective-permute-start.2 = (bf16[104,384]{1,0:T(8,128)(2,1)S(1)}, bf16[104,384]{1,0:T(8,128)(2,1)S(1)}, u32[]{:S(2)}, u32[]{:S(2)}) collective-permute-start(bf16[104,384]{1,0:T(8,128)(2,1)S(1)} %get-tuple-element.14), channel_id=1, source_target_pairs={{0,1},{1,0},{2,3},{3,2},{4,5},{5,4},{6,7},{7,6},{8,9},{9,8},{10,11... | collective-permute-start | bytes 239624 | tf_op jit(solution)/shard_map/ppermute | solution.py:333
  19.0 13.2 %collective-permute-start.5 = (bf16[104,384]{1,0:T(8,128)(2,1)S(1)}, bf16[104,384]{1,0:T(8,128)(2,1)S(1)}, u32[]{:S(2)}, u32[]{:S(2)}) collective-permute-start(bf16[104,384]{1,0:T(8,128)(2,1)S(1)} %add_convert_fusion.2), channel_id=1, source_target_pairs={{0,12},{4,0},{8,4},{12,8},{1,13},{5,1},{9,5},{13,9},{2,14},{6,2},{... | collective-permute-start | bytes 239624 | tf_op jit(solution)/shard_map/ppermute | solution.py:336
  21.7 13.0 %collective-permute-start.4 = (bf16[104,384]{1,0:T(8,128)(2,1)S(1)}, bf16[104,384]{1,0:T(8,128)(2,1)S(1)}, u32[]{:S(2)}, u32[]{:S(2)}) collective-permute-start(bf16[104,384]{1,0:T(8,128)(2,1)S(1)} %add_convert_fusion.2), channel_id=1, source_target_pairs={{0,8},{4,12},{8,0},{12,4},{1,9},{5,13},{9,1},{13,5},{2,10},{6,14},... | collective-permute-start | bytes 239624 | tf_op jit(solution)/shard_map/ppermute | solution.py:336
  22.3 13.7 %collective-permute-start.3 = (bf16[104,384]{1,0:T(8,128)(2,1)S(1)}, bf16[104,384]{1,0:T(8,128)(2,1)S(1)}, u32[]{:S(2)}, u32[]{:S(2)}) collective-permute-start(bf16[104,384]{1,0:T(8,128)(2,1)S(1)} %add_convert_fusion.2), channel_id=1, source_target_pairs={{0,4},{4,8},{8,12},{12,0},{1,5},{5,9},{9,13},{13,1},{2,6},{6,10},{... | collective-permute-start | bytes 239624 | tf_op jit(solution)/shard_map/ppermute | solution.py:336
  36.1 1.1 %copy-start.4 = (bf16[1168,256]{1,0:T(8,128)(2,1)S(1)}, bf16[1168,256]{1,0:T(8,128)(2,1)}, u32[]{:S(2)}) copy-start(bf16[1168,256]{1,0:T(8,128)(2,1)} %constant.13.clone.tab_ref) | copy-start | bytes 1794052
  37.2 10.3 %copy-start.2 = (bf16[1184,256]{1,0:T(8,128)(2,1)S(1)}, bf16[1184,256]{1,0:T(8,128)(2,1)}, u32[]{:S(2)}) copy-start(bf16[1184,256]{1,0:T(8,128)(2,1)} %constant.14.clone.tab_ref) | copy-start | bytes 1818628
  37.2 10.3 %copy-start.5 = (bf16[192,400]{1,0:T(8,128)(2,1)S(1)}, bf16[192,400]{1,0:T(8,128)(2,1)}, u32[]{:S(2)}) copy-start(bf16[192,400]{1,0:T(8,128)(2,1)} %constant.15.clone.unfold_ref) | copy-start | bytes 460804
  39.5 7.9 %collective-permute-start.6 = (bf16[4,2,200,384]{3,2,1,0:T(8,128)(2,1)S(1)}, bf16[4,2,200,384]{3,2,1,0:T(8,128)(2,1)S(1)}, u32[]{:S(2)}, u32[]{:S(2)}) collective-permute-start(bf16[4,2,200,384]{3,2,1,0:T(8,128)(2,1)S(1)} %library.1.near_ref), channel_id=1, source_target_pairs={{0,1},{1,0},{2,3},{3,2},{4,5},{5,4},{6,7},{7,6},{8,9},{9,8},{10,11... | collective-permute-start | bytes 3686408 | tf_op jit(solution)/shard_map/ppermute | solution.py:374
  40.1 5.5 %collective-permute-start.7 = (bf16[104,384]{1,0:T(8,128)(2,1)S(1)}, bf16[104,384]{1,0:T(8,128)(2,1)S(1)}, u32[]{:S(2)}, u32[]{:S(2)}) collective-permute-start(bf16[104,384]{1,0:T(8,128)(2,1)S(1)} %add_convert_fusion.1), channel_id=1, source_target_pairs={{0,2},{2,0},{1,3},{3,1},{4,6},{6,4},{5,7},{7,5},{8,10},{10,8},{9,1... | collective-permute-start | bytes 239624 | tf_op jit(solution)/shard_map/ppermute | solution.py:357
  45.6 1.9 %collective-permute-start.8 = (bf16[104,384]{1,0:T(8,128)(2,1)S(1)}, bf16[104,384]{1,0:T(8,128)(2,1)S(1)}, u32[]{:S(2)}, u32[]{:S(2)}) collective-permute-start(bf16[104,384]{1,0:T(8,128)(2,1)S(1)} %add_convert_fusion.mine_ref), channel_id=1, source_target_pairs={{0,1},{1,0},{2,3},{3,2},{4,5},{5,4},{6,7},{7,6},{8,9},{9,8},{10,11... | collective-permute-start | bytes 239624 | tf_op jit(solution)/shard_map/ppermute | solution.py:359
  52.1 9.8 %collective-permute-start.9 = (bf16[384,384]{1,0:T(8,128)(2,1)S(1)}, bf16[384,384]{1,0:T(8,128)(2,1)S(1)}, u32[]{:S(2)}, u32[]{:S(2)}) collective-permute-start(bf16[384,384]{1,0:T(8,128)(2,1)S(1)} %match_other.1), channel_id=1, source_target_pairs={{0,2},{2,0},{1,3},{3,1},{4,6},{6,4},{5,7},{7,5},{8,10},{10,8},{9,1... | collective-permute-start | bytes 884744 | tf_op jit(solution)/shard_map/ppermute | solution.py:403
  59.5 0.8 %copy-start = (f32[384,384]{1,0:T(8,128)}, f32[384,384]{1,0:T(8,128)S(1)}, u32[]{:S(2)}) copy-start(f32[384,384]{1,0:T(8,128)S(1)} %match_own.1.best_ref) | copy-start | bytes 1769476
  61.9 0.7 %copy-start.6 = (bf16[384,384]{1,0:T(8,128)(2,1)}, bf16[384,384]{1,0:T(8,128)(2,1)S(1)}, u32[]{:S(2)}) copy-start(bf16[384,384]{1,0:T(8,128)(2,1)S(1)} %collective-permute-done.9.got_ref) | copy-start | bytes 884740

commit v7 on v6

--- a/solution.py
+++ b/solution.py
@@ -168,19 +168,23 @@
     return gain, row_scale(u) * square
 
 
-def tile_kernel(core_ref, mate_ref, own_ref, other_ref, tab_ref, spec_ref, keep_ref, send_ref, power_sc):
-    parts = half_spectrum(own_ref[...], tab_ref)
-    store_spectrum(spec_ref.at[0], parts)
-    for k, (re, im) in enumerate(parts):
-        power_sc[:, k * THIRD : (k + 1) * THIRD] = re * re + im * im
+def tile_kernel(
+    core_ref, mate_ref, own_ref, other_ref, tab_ref, spec_ref, keep_ref, send_ref, power_sc
+):
+    for t, ref in enumerate((own_ref, other_ref)):
+        parts = half_spectrum(ref[...], tab_ref)
+        store_spectrum(spec_ref.at[t], parts)
+        for k, (re, im) in enumerate(parts):
+            at = slice(k * THIRD, (k + 1) * THIRD)
+            square = re * re + im * im
+            power_sc[:, at] = square if t == 0 else power_sc[:, at] + square
     low, high = power_sc[:PART], power_sc[SPLIT:]
     first = core_ref[...] == 0
     keep_ref[...] = jnp.where(first, low, high).astype(BF16)
     send_ref[...] = jnp.where(first, high, low).astype(BF16)
-    store_spectrum(spec_ref.at[1], half_spectrum(other_ref[...], tab_ref))
-
-
-def gain_kernel(row_ref, mate_ref, table_ref, tile_ref, spec_ref, weight_ref):
+
+
+def gain_kernel(row_ref, mate_ref, table_ref, tile_ref, tab_ref, spec_ref, weight_ref):
     for t, ref in enumerate((row_ref, mate_ref)):
         gain, weight_ref[t] = ctf_factors(ref[...].astype(F32), table_ref[...])
         spec_ref[t, 0] = tile_ref[t, 0] * gain
@@ -218,40 +222,44 @@
     return even - odd, even + odd
 
 
-def match_kernel(
-    core_ref,
-    near_ref,
-    far_ref,
-    spec_ref,
-    weight_ref,
-    mine_ref,
-    theirs_ref,
-    tab_ref,
-    unfold_ref,
-    out_ref,
-    spec_sc,
-    weight_sc,
-    best_sc,
-):
+def whiten_kernel(core_ref, spec_ref, weight_ref, mine_ref, theirs_ref, spec_out, weight_out):
+    mine, theirs = mine_ref[...].astype(F32), theirs_ref[...].astype(F32)
+    first = core_ref[...] == 0
+    low, high = jnp.where(first, mine, theirs), jnp.where(first, theirs, mine)
+    power = jnp.concatenate([low[:SPLIT], high], axis=0) * (1.0 / 16.0)
+    u, _ = row_numbers()
+    mean = jnp.sum(power * row_scale(u)) * (1.0 / (N * N))
+    inverse_noise = 1.0 / (jnp.where(u <= HALF, power, 1.0) + 0.05 * mean)
+    for t in range(2):
+        spec_out[t, 0] = spec_ref[t, 0] * inverse_noise
+        spec_out[t, 1] = spec_ref[t, 1] * inverse_noise
+        weight_out[t] = weight_ref[t] * inverse_noise
+
+
+def near_kernel(lib_ref, spec_ref, weight_ref, tab_ref, out_ref):
     step = pl.program_id(0)
 
     @pl.when(step == 0)
     def _():
-        u, _ = row_numbers()
-        mine, theirs = mine_ref[...].astype(F32), theirs_ref[...].astype(F32)
-        first = core_ref[...] == 0
-        low, high = jnp.where(first, mine, theirs), jnp.where(first, theirs, mine)
-        power = jnp.concatenate([low[:SPLIT], high], axis=0) * (1.0 / 16.0)
-        mean = jnp.sum(power * row_scale(u)) * (1.0 / (N * N))
-        inverse_noise = 1.0 / (jnp.where(u <= HALF, power, 1.0) + 0.05 * mean)
-        spec_sc[0] = spec_ref[0] * inverse_noise
-        spec_sc[1] = spec_ref[1] * inverse_noise
-        weight_sc[...] = weight_ref[...] * inverse_noise
-        best_sc[...] = jnp.full_like(best_sc, -jnp.inf)
+        out_ref[...] = jnp.full_like(out_ref, -jnp.inf)
+
+    re, im = lib_ref[0].astype(F32), lib_ref[1].astype(F32)
+    for t in range(2):
+        sides = match_step(re, im, spec_ref.at[t], weight_ref.at[t], tab_ref)
+        for k in range(2):
+            out_ref[t, k] = jnp.maximum(out_ref[t, k], sides[k])
+
+
+def far_kernel(lib_ref, spec_ref, weight_ref, tab_ref, start_ref, unfold_ref, out_ref, best_sc):
+    step = pl.program_id(0)
+
+    @pl.when(step == 0)
+    def _():
+        best_sc[...] = start_ref[...]
 
     pairs = [
-        match_step(ref[0].astype(F32), ref[1].astype(F32), spec_sc, weight_sc, tab_ref)
-        for ref in (near_ref, far_ref)
+        match_step(lib_ref[i, 0].astype(F32), lib_ref[i, 1].astype(F32), spec_ref, weight_ref, tab_ref)
+        for i in range(2)
     ]
     for side in range(2):
         best_sc[side] = jnp.maximum(best_sc[side], jnp.maximum(pairs[0][side], pairs[1][side]))
@@ -267,10 +275,6 @@
             moved = dot(unfold_ref[...], part)
             total = moved if total is None else total + moved
         out_ref[HALF:] = total.astype(out_ref.dtype)
-
-
-def join_kernel(best_ref, got_ref, out_ref):
-    out_ref[...] = jnp.maximum(best_ref[...], got_ref[...].astype(F32))
 
 
 def full(*shape):
@@ -325,7 +329,7 @@
         in_specs=[full(1, 1), full(1, 1), full(N, N), full(N, N), full(*ahead.shape)],
         out_specs=[full(2, *plane), full(PART, N), full(PART, N)],
         scratch_shapes=[pltpu.VMEM((ROWS, N), F32)],
-        compiler_params=params(16),
+        compiler_params=params(12),
         cost_estimate=cost(200 * work, 3 << 20),
         name="tile",
     )(core, mate, tile, received, ahead)
@@ -335,7 +339,7 @@
     for dz in range(1, deep):
         moved = lax.ppermute(pair, "z", [(z, (z + dz) % deep) for z in range(deep)])
         sums = sums + moved.astype(F32)
-    sums = sums.astype(BF16)
+    mine = sums.astype(BF16)
 
     table = jnp.stack([defocus_term, astig_term, astig_cross, phase_shift])
     table = jnp.pad(table, ((0, 4), (0, 128 - table.shape[1])))
@@ -346,17 +350,28 @@
             jax.ShapeDtypeStruct((2, ROWS, N), F32),
         ],
         grid=(1,),
-        in_specs=[full(1, 1), full(1, 1), full(*table.shape), full(2, *plane)],
+        in_specs=[full(1, 1), full(1, 1), full(*table.shape), full(2, *plane), full(*ahead.shape)],
         out_specs=[full(2, *plane), full(2, ROWS, N)],
-        compiler_params=params(20),
+        compiler_params=params(12),
         cost_estimate=cost(2 * ROWS * N * 60, 4 << 20),
         name="gain",
-    )(ctf_row, mate, table, tiles)
-
-    images_all, sums, spec = lax.optimization_barrier((images_all, sums, spec))
-    across = lax.ppermute(sums, "xhi", swap)
-    mine = (sums.astype(F32) + across.astype(F32)).astype(BF16)
+    )(ctf_row, mate, table, tiles, ahead)
+
+    images_all, mine, spec = lax.optimization_barrier((images_all, mine, spec))
     theirs = lax.ppermute(mine, "core", swap)
+    white, white_weight = pl.pallas_call(
+        whiten_kernel,
+        out_shape=[
+            jax.ShapeDtypeStruct((2,) + plane, F32),
+            jax.ShapeDtypeStruct((2, ROWS, N), F32),
+        ],
+        grid=(1,),
+        in_specs=[full(1, 1), full(2, *plane), full(2, ROWS, N), full(PART, N), full(PART, N)],
+        out_specs=[full(2, *plane), full(2, ROWS, N)],
+        compiler_params=params(12),
+        cost_estimate=cost(2 * ROWS * N * 4, 4 << 20),
+        name="whiten",
+    )(core, spec, weight, mine, theirs)
 
     near_all = pl.pallas_call(
         library_kernel,
@@ -367,51 +382,51 @@
             full(*ahead.shape),
         ],
         out_specs=pl.BlockSpec((None,) + plane, lambda i: (i, 0, 0, 0)),
-        compiler_params=params(16),
-        cost_estimate=cost(100 * deep * work, 4 << 20),
+        compiler_params=params(12),
+        cost_estimate=cost(deep * work, 4 << 20),
         name="library",
     )(images_all.reshape(groups, deep, N // groups, N), ahead)
     far_all = lax.ppermute(near_all, "core", swap)
+    near_best = pl.pallas_call(
+        near_kernel,
+        out_shape=jax.ShapeDtypeStruct((2,) + plane, F32),
+        grid=(deep,),
+        in_specs=[
+            pl.BlockSpec((None,) + plane, lambda i: (i, 0, 0, 0)),
+            full(2, *plane),
+            full(2, ROWS, N),
+            full(*back.shape),
+        ],
+        out_specs=full(2, *plane),
+        compiler_params=params(12),
+        cost_estimate=cost(2 * deep * 2 * work, 8 << 20),
+        name="near",
+    )(near_all, white, white_weight, back)
+    far_all, near_best = lax.optimization_barrier((far_all, near_best))
+
     def match(t, dtype, name):
-        lib_spec = pl.BlockSpec((None,) + plane, lambda i: (i, 0, 0, 0))
         return pl.pallas_call(
-            match_kernel,
+            far_kernel,
             out_shape=jax.ShapeDtypeStruct((N, N), dtype),
-            grid=(deep,),
+            grid=(deep // 2,),
             in_specs=[
-                full(1, 1),
-                lib_spec,
-                lib_spec,
+                pl.BlockSpec((2,) + plane, lambda i: (i, 0, 0, 0)),
                 pl.BlockSpec((None,) + plane, lambda i: (t, 0, 0, 0)),
                 pl.BlockSpec((None, ROWS, N), lambda i: (t, 0, 0)),
-                full(PART, N),
-                full(PART, N),
                 full(*back.shape),
+                pl.BlockSpec((None,) + plane, lambda i: (t, 0, 0, 0)),
                 full(*unfold.shape),
             ],
             out_specs=full(N, N),
-            scratch_shapes=[
-                pltpu.VMEM(plane, F32),
-                pltpu.VMEM((ROWS, N), F32),
-                pltpu.VMEM(plane, F32),
-            ],
-            compiler_params=params(20),
-            cost_estimate=cost(2 * deep * 2 * work, 6 << 20),
+            scratch_shapes=[pltpu.VMEM(plane, F32)],
+            compiler_params=params(12),
+            cost_estimate=cost(deep * 2 * work, 5 << 20),
             name=name,
-        )(core, near_all, far_all, spec, weight, mine, theirs, back, unfold)
-
-    got = lax.ppermute(match(1, BF16, "match_other"), "xhi", swap)
-    best = match(0, F32, "match_own")
-    peak = pl.pallas_call(
-        join_kernel,
-        out_shape=jax.ShapeDtypeStruct((N, N), F32),
-        grid=(1,),
-        in_specs=[full(N, N), full(N, N)],
-        out_specs=full(N, N),
-        cost_estimate=cost(N * N, 1 << 20),
-        name="join",
-    )(best, got)
-    return peak[None, None]
+        )(far_all, white, white_weight, back, near_best, unfold)
+
+    got = lax.ppermute(match(1, BF16, "far_other"), "xhi", swap)
+    best = match(0, F32, "far_own")
+    return jnp.maximum(best, got.astype(F32))[None, None]
 
 
 def solution(mesh):

time: 65 us -> 59.6 us (0.917)
  starting transfers between devices: 25 us -> 21.7 us
  Pallas kernels: 19.2 us -> 17.2 us
  local copies, waits for them, and re-layouts: 2.66 us -> 0.87 us
  waiting for transfers between devices: 16.8 us -> 17.7 us
  other arithmetic: 0.1 us -> 0.95 us
    ppermute x2 -> x1, starting transfers between devices: 4.98 us -> 2.53 us  [per_device(): got = lax.ppermute(match(1, BF16, 'far_other'), 'xhi', swap)]
    pallas_call x3 -> x4, Pallas kernels: 11.5 us -> 9.43 us  [the longest x2 4.89 us: match(): pl.pallas_call(far_kernel, out_shape=jax.ShapeDtypeStruct((N, N), dtype),...]
    unnamed x22 -> x20, local copies, waits for them, and re-layouts: 2.66 us -> 0.87 us
    ppermute x1, waiting for transfers between devices: 0.92 us -> 2.57 us  [per_device(): theirs = lax.ppermute(mine, 'core', swap)]
    broadcast_in_dim x0 -> x1, other arithmetic: none -> 0.86 us  [per_device(): return jnp.maximum(best, got.astype(F32))[None, None]]
    ppermute x1, starting transfers between devices: 0.95 us -> 0.09 us  [per_device(): theirs = lax.ppermute(mine, 'core', swap)]
    ppermute x3, waiting for transfers between devices: 11 us -> 10.2 us  [per_device(): moved = lax.ppermute(pair, 'z', [(z, (z + dz) % deep) for z in range(deep)])]
    ppermute x2 -> x1, waiting for transfers between devices: 4.63 us -> 4.7 us  [per_device(): got = lax.ppermute(match(1, BF16, 'far_other'), 'xhi', swap)]
  transfers between devices with their start and end apart: 11 -> 10, of which waited for: 7 -> 6; matrix products, arithmetic and copies ran while one was open for 0% -> 0% of each run, Pallas kernels for 16% -> 21%
where the time goes in v7:
time: 59.6 us; the launch traced here: 59.3 us
  starting transfers between devices  21.7 us (36%)
  waiting for transfers between devices  17.7 us (30%)
  Pallas kernels  17.2 us (29%)
  other arithmetic  0.95 us (2%)
  between operations  0.89 us (1%)
  local copies, waits for them, and re-layouts  0.87 us (1%)
    ppermute x3, waiting for transfers between devices, per_device(): moved = lax.ppermute(pair, 'z', [(z, (z + dz) % deep) for z in range(deep)])  10.2 us
    all_to_all x1, starting transfers between devices, per_device(): images_all = lax.all_to_all(copies, LIB, 0, 0, tiled=False)  9.32 us
    pallas_call x2, Pallas kernels, match(): pl.pallas_call(far_kernel, out_shape=jax.ShapeDtypeStruct((N, N), dtype),...  4.89 us
    ppermute x1, waiting for transfers between devices, per_device(): got = lax.ppermute(match(1, BF16, 'far_other'), 'xhi', swap)  4.7 us
    pallas_call x1, Pallas kernels, per_device(): pl.pallas_call(near_kernel, out_shape=jax.ShapeDtypeStruct((2,) + plane,...  4.04 us
    ppermute x3, starting transfers between devices, per_device(): moved = lax.ppermute(pair, 'z', [(z, (z + dz) % deep) for z in range(deep)])  3.95 us
    ppermute x1, starting transfers between devices, per_device(): received = lax.ppermute(tile, 'xhi', swap)  3.57 us
    ppermute x1, waiting for transfers between devices, per_device(): theirs = lax.ppermute(mine, 'core', swap)  2.57 us
  transfers between devices with their start and end apart: 10, of which 6 were waited for; matrix products, arithmetic and copies ran while one was open for 0% of the time, Pallas kernels for 21%

profile of v7, /device:TPU:1, one launch (start us, length us, event | category | flops | bytes accessed | tf_op | source)
XLA Modules:
  0.0 59.3 jit_solution(10462140149237110357)
XLA Ops:
  0.0 3.6 %collective-permute-start.1 = (bf16[384,384]{1,0:T(8,128)(2,1)}, bf16[384,384]{1,0:T(8,128)(2,1)S(1)}, u32[]{:S(2)}, u32[]{:S(2)}) collective-permute-start(bf16[384,384]{1,0:T(8,128)(2,1)} %bitcast.11), channel_id=1, source_target_pairs={{0,2},{2,0},{1,3},{3,1},{4,6},{6,4},{5,7},{7,5},{8,10},{10,8},{9,1... | collective-permute-start | bytes 884744 | tf_op jit(solution)/shard_map/ppermute | solution.py:303
  3.6 0.0 collective-permute-start
  3.6 1.9 %copies.1 = bf16[32,48,384]{2,1,0:T(8,128)(2,1)} custom-call(bf16[48,384]{1,0:T(8,128)(2,1)} %bitcast.13), custom_call_target="tpu_custom_call" | custom-call | bytes 1048576 | tf_op jit(solution)/shard_map/copies/pallas_call | solution.py:306
  5.5 0.0 copy-start.1
  5.5 0.0 copy-start.5
  5.5 9.3 %all-to-all-start = ((bf16[32,48,384]{2,1,0:T(8,128)(2,1)}), bf16[32,48,384]{2,1,0:T(8,128)(2,1)S(1)}, u32[]{:S(2)}, u32[]{:S(2)}) async-start(bf16[32,48,384]{2,1,0:T(8,128)(2,1)} %copies.1), calls=%async_computation | async-start | bytes 2359296 | tf_op jit(solution)/shard_map/all_to_all | solution.py:319
  14.8 0.0 collective-permute-done.mate_ref
  14.8 0.0 collective-permute-done.1.other_ref
  14.8 0.0 copy-done.1
  14.9 0.0 copy-done.5
  14.9 0.0 copy-start.6
  14.9 0.0 copy-start.7
  14.9 0.0 copy-start.8
  14.9 0.0 copy-start.9
  14.9 1.5 %tile.1 = (f32[2,2,200,384]{3,2,1,0:T(8,128)S(1)}, bf16[104,384]{1,0:T(8,128)(2,1)S(1)}, bf16[104,384]{1,0:T(8,128)(2,1)S(1)}) custom-call(s32[1,1]{1,0:T(1,128)} %bitcast.1.core_ref, s32[1,1]{1,0:T(1,128)} %collective-permute-done.mate_ref, bf16[384,384]{1,0:T(8,128)(2,1)S(1)} %bitcast.12, bf16[384,384]{1,0:T(8,128)(2,1)S(1)} %collective-permute-done.1.other_ref, ...), custom_call_target="tpu_custom_call" | custom-call | flops 31457280000 | bytes 3145728 | tf_op jit(solution)/shard_map/tile/pallas_call | solution.py:321
  16.4 1.6 %collective-permute-start.2 = (bf16[104,384]{1,0:T(8,128)(2,1)S(1)}, bf16[104,384]{1,0:T(8,128)(2,1)S(1)}, u32[]{:S(2)}, u32[]{:S(2)}) collective-permute-start(bf16[104,384]{1,0:T(8,128)(2,1)S(1)} %get-tuple-element.18), channel_id=1, source_target_pairs={{0,1},{1,0},{2,3},{3,2},{4,5},{5,4},{6,7},{7,6},{8,9},{9,8},{10,11... | collective-permute-start | bytes 239624 | tf_op jit(solution)/shard_map/ppermute | solution.py:337
  18.6 0.3 collective-permute-done.2
  18.9 2.8 %collective-permute-start.5 = (bf16[104,384]{1,0:T(8,128)(2,1)S(1)}, bf16[104,384]{1,0:T(8,128)(2,1)S(1)}, u32[]{:S(2)}, u32[]{:S(2)}) collective-permute-start(bf16[104,384]{1,0:T(8,128)(2,1)S(1)} %add_convert_fusion.1), channel_id=1, source_target_pairs={{0,12},{4,0},{8,4},{12,8},{1,13},{5,1},{9,5},{13,9},{2,14},{6,2},{... | collective-permute-start | bytes 239624 | tf_op jit(solution)/shard_map/ppermute | solution.py:340
  21.7 0.6 collective-permute-start.4
  22.3 0.6 collective-permute-start.3
  22.9 0.0 copy-done.6
  22.9 0.0 copy-done.7
  22.9 0.0 copy-done.8
  22.9 0.0 copy-done.9
  22.9 2.1 %gain.1 = (f32[2,2,200,384]{3,2,1,0:T(8,128)S(1)}, f32[2,200,384]{2,1,0:T(8,128)S(1)}) custom-call(s32[1,1]{1,0:T(1,128)S(6)} %copy.11.row_ref, s32[1,1]{1,0:T(1,128)} %collective-permute-done.mate_ref, f32[8,128]{1,0:T(8,128)S(1)} %select_maximum_fusion.table_ref, f32[2,2,200,384]{3,2,1,0:T(8,128)S(1)} %get-tuple-element.19.tile_ref, ...), custom_call_target="tpu_custom_call" | custom-call | flops 9216000 | bytes 4194304 | tf_op jit(solution)/shard_map/gain/pallas_call | solution.py:346
  25.0 0.0 copy-start.3
  25.0 0.8 %copy-done.3 = f32[2,200,384]{2,1,0:T(8,128)} copy-done((f32[2,200,384]{2,1,0:T(8,128)}, f32[2,200,384]{2,1,0:T(8,128)S(1)}, u32[]{:S(2)}) %copy-start.3) | copy-done | bytes 614424
  25.8 6.3 %collective-permute-done.5 = bf16[104,384]{1,0:T(8,128)(2,1)S(1)} collective-permute-done((bf16[104,384]{1,0:T(8,128)(2,1)S(1)}, bf16[104,384]{1,0:T(8,128)(2,1)S(1)}, u32[]{:S(2)}, u32[]{:S(2)}) %collective-permute-start.5) | collective-permute-done | bytes 79904 | tf_op jit(solution)/shard_map/ppermute | solution.py:340
  32.2 2.6 %collective-permute-done.4 = bf16[104,384]{1,0:T(8,128)(2,1)S(1)} collective-permute-done((bf16[104,384]{1,0:T(8,128)(2,1)S(1)}, bf16[104,384]{1,0:T(8,128)(2,1)S(1)}, u32[]{:S(2)}, u32[]{:S(2)}) %collective-permute-start.4) | collective-permute-done | bytes 79904 | tf_op jit(solution)/shard_map/ppermute | solution.py:340
  34.7 1.3 %collective-permute-done.3 = bf16[104,384]{1,0:T(8,128)(2,1)S(1)} collective-permute-done((bf16[104,384]{1,0:T(8,128)(2,1)S(1)}, bf16[104,384]{1,0:T(8,128)(2,1)S(1)}, u32[]{:S(2)}, u32[]{:S(2)}) %collective-permute-start.3) | collective-permute-done | bytes 79904 | tf_op jit(solution)/shard_map/ppermute | solution.py:340
  36.1 0.0 all-to-all-done
  36.1 0.0 copy-start.4
  36.1 2.4 %library.1.lib_ref = bf16[4,2,200,384]{3,2,1,0:T(8,128)(2,1)S(1)} custom-call(bf16[8,4,48,384]{3,2,1,0:T(8,128)(2,1)S(1)} %bitcast.10, bf16[1168,256]{1,0:T(8,128)(2,1)S(1)} %copy-done.1), custom_call_target="tpu_custom_call" | custom-call | flops 629145600 | bytes 4194304 | tf_op jit(solution)/shard_map/library/pallas_call | solution.py:376
  38.5 0.0 copy-start
  38.5 0.6 collective-permute-start.6
  39.1 0.1 collective-permute-start.7
  39.2 2.6 %collective-permute-done.7.theirs_ref = bf16[104,384]{1,0:T(8,128)(2,1)S(1)} collective-permute-done((bf16[104,384]{1,0:T(8,128)(2,1)S(1)}, bf16[104,384]{1,0:T(8,128)(2,1)S(1)}, u32[]{:S(2)}, u32[]{:S(2)}) %collective-permute-start.7) | collective-permute-done | bytes 79904 | tf_op jit(solution)/shard_map/ppermute | solution.py:361
  41.7 0.0 copy-done.4
  41.7 0.5 whiten.1
  42.2 0.0 copy-done
  42.2 0.0 copy-start.2
  42.3 4.0 %near.1.start_ref = f32[2,2,200,384]{3,2,1,0:T(8,128)S(1)} custom-call(bf16[4,2,200,384]{3,2,1,0:T(8,128)(2,1)S(1)} %library.1.lib_ref, f32[2,2,200,384]{3,2,1,0:T(8,128)S(1)} %get-tuple-element.25.spec_ref, f32[2,200,384]{2,1,0:T(8,128)S(1)} %get-tuple-element.26.weight_ref, bf16[1184,256]{1,0:T(8,128)(2,1)S(1)} %copy-done), custom_call_target="tpu_custom_call" | custom-call | flops 2516582400 | bytes 8388608 | tf_op jit(solution)/shard_map/near/pallas_call | solution.py:390
  46.3 0.0 collective-permute-done.6.lib_ref
  46.3 0.0 copy-done.2
  46.3 2.3 %far_other.1 = bf16[384,384]{1,0:T(8,128)(2,1)S(1)} custom-call(bf16[4,2,200,384]{3,2,1,0:T(8,128)(2,1)S(1)} %collective-permute-done.6.lib_ref, f32[2,2,200,384]{3,2,1,0:T(8,128)S(1)} %get-tuple-element.25.spec_ref, f32[2,200,384]{2,1,0:T(8,128)S(1)} %get-tuple-element.26.weight_ref, bf16[1184,256]{1,0:T(8,128)(2,1)S(1)} %copy-done, ...), custom_call_target="tpu_custom_call" | custom-call | flops 1258291200 | bytes 5242880 | tf_op jit(solution)/shard_map/far_other/pallas_call | solution.py:408
  48.7 2.5 %collective-permute-start.8 = (bf16[384,384]{1,0:T(8,128)(2,1)S(1)}, bf16[384,384]{1,0:T(8,128)(2,1)S(1)}, u32[]{:S(2)}, u32[]{:S(2)}) collective-permute-start(bf16[384,384]{1,0:T(8,128)(2,1)S(1)} %far_other.1), channel_id=1, source_target_pairs={{0,2},{2,0},{1,3},{3,1},{4,6},{6,4},{5,7},{7,5},{8,10},{10,8},{9,1... | collective-permute-start | bytes 884744 | tf_op jit(solution)/shard_map/ppermute | solution.py:427
  51.2 2.6 %far_own.1 = f32[384,384]{1,0:T(8,128)S(1)} custom-call(bf16[4,2,200,384]{3,2,1,0:T(8,128)(2,1)S(1)} %collective-permute-done.6.lib_ref, f32[2,2,200,384]{3,2,1,0:T(8,128)S(1)} %get-tuple-element.25.spec_ref, f32[2,200,384]{2,1,0:T(8,128)S(1)} %get-tuple-element.26.weight_ref, bf16[1184,256]{1,0:T(8,128)(2,1)S(1)} %copy-done, ...), custom_call_target="tpu_custom_call" | custom-call | flops 1258291200 | bytes 5242880 | tf_op jit(solution)/shard_map/far_own/pallas_call | solution.py:408
  53.8 4.7 %collective-permute-done.8 = bf16[384,384]{1,0:T(8,128)(2,1)S(1)} collective-permute-done((bf16[384,384]{1,0:T(8,128)(2,1)S(1)}, bf16[384,384]{1,0:T(8,128)(2,1)S(1)}, u32[]{:S(2)}, u32[]{:S(2)}) %collective-permute-start.8) | collective-permute-done | bytes 294944 | tf_op jit(solution)/shard_map/ppermute | solution.py:427
  58.5 0.9 %maximum_bitcast_fusion = f32[1,1,384,384]{3,2,1,0:T(8,128)} fusion(f32[384,384]{1,0:T(8,128)S(1)} %far_own.1, bf16[384,384]{1,0:T(8,128)(2,1)S(1)} %collective-permute-done.8), kind=kLoop, calls=%fused_computation | loop fusion | flops 294912 | bytes 1474560 | tf_op jit(solution)/shard_map/broadcast_in_dim | solution.py:429
  (3 shorter events, 0.1 us)
Async XLA Ops:
  0.0 14.8 %collective-permute-start.1 = (bf16[384,384]{1,0:T(8,128)(2,1)}, bf16[384,384]{1,0:T(8,128)(2,1)S(1)}, u32[]{:S(2)}, u32[]{:S(2)}) collective-permute-start(bf16[384,384]{1,0:T(8,128)(2,1)} %bitcast.11), channel_id=1, source_target_pairs={{0,2},{2,0},{1,3},{3,1},{4,6},{6,4},{5,7},{7,5},{8,10},{10,8},{9,1... | collective-permute-start | bytes 884744 | tf_op jit(solution)/shard_map/ppermute | solution.py:303
  3.6 11.3 %collective-permute-start = (s32[1,1]{1,0:T(1,128)}, s32[1,1]{1,0:T(1,128)}, u32[]{:S(2)}, u32[]{:S(2)}) collective-permute-start(s32[1,1]{1,0:T(1,128)} %param.12), channel_id=1, source_target_pairs={{0,2},{2,0},{1,3},{3,1},{4,6},{6,4},{5,7},{7,5},{8,10},{10,8},{9,1... | collective-permute-start | bytes 20 | tf_op jit(solution)/shard_map/ppermute | solution.py:304
  5.5 9.4 %copy-start.1 = (bf16[1168,256]{1,0:T(8,128)(2,1)S(1)}, bf16[1168,256]{1,0:T(8,128)(2,1)}, u32[]{:S(2)}) copy-start(bf16[1168,256]{1,0:T(8,128)(2,1)} %constant.13.clone.tab_ref) | copy-start | bytes 1794052
  5.5 9.4 %copy-start.5 = (bf16[1,1,384,384]{3,2,1,0:T(8,128)(2,1)S(1)}, bf16[1,1,384,384]{3,2,1,0:T(8,128)(2,1)}, u32[]{:S(2)}) copy-start(bf16[1,1,384,384]{3,2,1,0:T(8,128)(2,1)} %param.10) | copy-start | bytes 884740
  5.5 30.6 %all-to-all-start = ((bf16[32,48,384]{2,1,0:T(8,128)(2,1)}), bf16[32,48,384]{2,1,0:T(8,128)(2,1)S(1)}, u32[]{:S(2)}, u32[]{:S(2)}) async-start(bf16[32,48,384]{2,1,0:T(8,128)(2,1)} %copies.1), calls=%async_computation | async-start | bytes 2359296 | tf_op jit(solution)/shard_map/all_to_all | solution.py:319
  14.9 8.0 %copy-start.6 = (f32[64]{0:T(128)S(1)}, f32[64]{0:T(128)}, u32[]{:S(2)}) copy-start(f32[64]{0:T(128)} %param.16) | copy-start | bytes 772
  14.9 8.0 %copy-start.7 = (f32[64]{0:T(128)S(1)}, f32[64]{0:T(128)}, u32[]{:S(2)}) copy-start(f32[64]{0:T(128)} %param.15) | copy-start | bytes 772
  14.9 8.0 %copy-start.8 = (f32[64]{0:T(128)S(1)}, f32[64]{0:T(128)}, u32[]{:S(2)}) copy-start(f32[64]{0:T(128)} %param.14) | copy-start | bytes 772
  14.9 8.0 %copy-start.9 = (f32[64]{0:T(128)S(1)}, f32[64]{0:T(128)}, u32[]{:S(2)}) copy-start(f32[64]{0:T(128)} %param.13) | copy-start | bytes 772
  16.4 2.5 %collective-permute-start.2 = (bf16[104,384]{1,0:T(8,128)(2,1)S(1)}, bf16[104,384]{1,0:T(8,128)(2,1)S(1)}, u32[]{:S(2)}, u32[]{:S(2)}) collective-permute-start(bf16[104,384]{1,0:T(8,128)(2,1)S(1)} %get-tuple-element.18), channel_id=1, source_target_pairs={{0,1},{1,0},{2,3},{3,2},{4,5},{5,4},{6,7},{7,6},{8,9},{9,8},{10,11... | collective-permute-start | bytes 239624 | tf_op jit(solution)/shard_map/ppermute | solution.py:337
  18.9 13.2 %collective-permute-start.5 = (bf16[104,384]{1,0:T(8,128)(2,1)S(1)}, bf16[104,384]{1,0:T(8,128)(2,1)S(1)}, u32[]{:S(2)}, u32[]{:S(2)}) collective-permute-start(bf16[104,384]{1,0:T(8,128)(2,1)S(1)} %add_convert_fusion.1), channel_id=1, source_target_pairs={{0,12},{4,0},{8,4},{12,8},{1,13},{5,1},{9,5},{13,9},{2,14},{6,2},{... | collective-permute-start | bytes 239624 | tf_op jit(solution)/shard_map/ppermute | solution.py:340
  21.7 13.0 %collective-permute-start.4 = (bf16[104,384]{1,0:T(8,128)(2,1)S(1)}, bf16[104,384]{1,0:T(8,128)(2,1)S(1)}, u32[]{:S(2)}, u32[]{:S(2)}) collective-permute-start(bf16[104,384]{1,0:T(8,128)(2,1)S(1)} %add_convert_fusion.1), channel_id=1, source_target_pairs={{0,8},{4,12},{8,0},{12,4},{1,9},{5,13},{9,1},{13,5},{2,10},{6,14},... | collective-permute-start | bytes 239624 | tf_op jit(solution)/shard_map/ppermute | solution.py:340
  22.3 13.8 %collective-permute-start.3 = (bf16[104,384]{1,0:T(8,128)(2,1)S(1)}, bf16[104,384]{1,0:T(8,128)(2,1)S(1)}, u32[]{:S(2)}, u32[]{:S(2)}) collective-permute-start(bf16[104,384]{1,0:T(8,128)(2,1)S(1)} %add_convert_fusion.1), channel_id=1, source_target_pairs={{0,4},{4,8},{8,12},{12,0},{1,5},{5,9},{9,13},{13,1},{2,6},{6,10},{... | collective-permute-start | bytes 239624 | tf_op jit(solution)/shard_map/ppermute | solution.py:340
  25.0 0.8 %copy-start.3 = (f32[2,200,384]{2,1,0:T(8,128)}, f32[2,200,384]{2,1,0:T(8,128)S(1)}, u32[]{:S(2)}) copy-start(f32[2,200,384]{2,1,0:T(8,128)S(1)} %get-tuple-element.23.weight_ref) | copy-start | bytes 1843204
  36.1 5.6 %copy-start.4 = (f32[2,200,384]{2,1,0:T(8,128)S(1)}, f32[2,200,384]{2,1,0:T(8,128)}, u32[]{:S(2)}) copy-start(f32[2,200,384]{2,1,0:T(8,128)} %copy-done.3) | copy-start | bytes 1843204
  38.5 3.8 %copy-start = (bf16[1184,256]{1,0:T(8,128)(2,1)S(1)}, bf16[1184,256]{1,0:T(8,128)(2,1)}, u32[]{:S(2)}) copy-start(bf16[1184,256]{1,0:T(8,128)(2,1)} %constant.14.clone.tab_ref) | copy-start | bytes 1818628
  38.5 7.8 %collective-permute-start.6 = (bf16[4,2,200,384]{3,2,1,0:T(8,128)(2,1)S(1)}, bf16[4,2,200,384]{3,2,1,0:T(8,128)(2,1)S(1)}, u32[]{:S(2)}, u32[]{:S(2)}) collective-permute-start(bf16[4,2,200,384]{3,2,1,0:T(8,128)(2,1)S(1)} %library.1.lib_ref), channel_id=1, source_target_pairs={{0,1},{1,0},{2,3},{3,2},{4,5},{5,4},{6,7},{7,6},{8,9},{9,8},{10,11... | collective-permute-start | bytes 3686408 | tf_op jit(solution)/shard_map/ppermute | solution.py:389
  39.1 2.7 %collective-permute-start.7 = (bf16[104,384]{1,0:T(8,128)(2,1)S(1)}, bf16[104,384]{1,0:T(8,128)(2,1)S(1)}, u32[]{:S(2)}, u32[]{:S(2)}) collective-permute-start(bf16[104,384]{1,0:T(8,128)(2,1)S(1)} %add_convert_fusion.mine_ref), channel_id=1, source_target_pairs={{0,1},{1,0},{2,3},{3,2},{4,5},{5,4},{6,7},{7,6},{8,9},{9,8},{10,11... | collective-permute-start | bytes 239624 | tf_op jit(solution)/shard_map/ppermute | solution.py:361
  42.2 4.1 %copy-start.2 = (bf16[192,400]{1,0:T(8,128)(2,1)S(1)}, bf16[192,400]{1,0:T(8,128)(2,1)}, u32[]{:S(2)}) copy-start(bf16[192,400]{1,0:T(8,128)(2,1)} %constant.15.clone.unfold_ref) | copy-start | bytes 460804
  48.7 9.8 %collective-permute-start.8 = (bf16[384,384]{1,0:T(8,128)(2,1)S(1)}, bf16[384,384]{1,0:T(8,128)(2,1)S(1)}, u32[]{:S(2)}, u32[]{:S(2)}) collective-permute-start(bf16[384,384]{1,0:T(8,128)(2,1)S(1)} %far_other.1), channel_id=1, source_target_pairs={{0,2},{2,0},{1,3},{3,1},{4,6},{6,4},{5,7},{7,5},{8,10},{10,8},{9,1... | collective-permute-start | bytes 884744 | tf_op jit(solution)/shard_map/ppermute | solution.py:427

commit v8 on v7

--- a/solution.py
+++ b/solution.py
@@ -236,30 +236,16 @@
         weight_out[t] = weight_ref[t] * inverse_noise
 
 
-def near_kernel(lib_ref, spec_ref, weight_ref, tab_ref, out_ref):
+def match_kernel(near_ref, far_ref, spec_ref, weight_ref, tab_ref, unfold_ref, out_ref, best_sc):
     step = pl.program_id(0)
 
     @pl.when(step == 0)
     def _():
-        out_ref[...] = jnp.full_like(out_ref, -jnp.inf)
-
-    re, im = lib_ref[0].astype(F32), lib_ref[1].astype(F32)
-    for t in range(2):
-        sides = match_step(re, im, spec_ref.at[t], weight_ref.at[t], tab_ref)
-        for k in range(2):
-            out_ref[t, k] = jnp.maximum(out_ref[t, k], sides[k])
-
-
-def far_kernel(lib_ref, spec_ref, weight_ref, tab_ref, start_ref, unfold_ref, out_ref, best_sc):
-    step = pl.program_id(0)
-
-    @pl.when(step == 0)
-    def _():
-        best_sc[...] = start_ref[...]
+        best_sc[...] = jnp.full_like(best_sc, -jnp.inf)
 
     pairs = [
-        match_step(lib_ref[i, 0].astype(F32), lib_ref[i, 1].astype(F32), spec_ref, weight_ref, tab_ref)
-        for i in range(2)
+        match_step(ref[0].astype(F32), ref[1].astype(F32), spec_ref, weight_ref, tab_ref)
+        for ref in (near_ref, far_ref)
     ]
     for side in range(2):
         best_sc[side] = jnp.maximum(best_sc[side], jnp.maximum(pairs[0][side], pairs[1][side]))
@@ -335,11 +321,10 @@
     )(core, mate, tile, received, ahead)
 
     pair = (keep.astype(F32) + lax.ppermute(send, "core", swap).astype(F32)).astype(BF16)
-    sums = pair.astype(F32)
-    for dz in range(1, deep):
-        moved = lax.ppermute(pair, "z", [(z, (z + dz) % deep) for z in range(deep)])
-        sums = sums + moved.astype(F32)
-    mine = sums.astype(BF16)
+    moves = [
+        lax.ppermute(pair, "z", [(z, (z + dz) % deep) for z in range(deep)])
+        for dz in range(1, deep)
+    ]
 
     table = jnp.stack([defocus_term, astig_term, astig_cross, phase_shift])
     table = jnp.pad(table, ((0, 4), (0, 128 - table.shape[1])))
@@ -357,21 +342,7 @@
         name="gain",
     )(ctf_row, mate, table, tiles, ahead)
 
-    images_all, mine, spec = lax.optimization_barrier((images_all, mine, spec))
-    theirs = lax.ppermute(mine, "core", swap)
-    white, white_weight = pl.pallas_call(
-        whiten_kernel,
-        out_shape=[
-            jax.ShapeDtypeStruct((2,) + plane, F32),
-            jax.ShapeDtypeStruct((2, ROWS, N), F32),
-        ],
-        grid=(1,),
-        in_specs=[full(1, 1), full(2, *plane), full(2, ROWS, N), full(PART, N), full(PART, N)],
-        out_specs=[full(2, *plane), full(2, ROWS, N)],
-        compiler_params=params(12),
-        cost_estimate=cost(2 * ROWS * N * 4, 4 << 20),
-        name="whiten",
-    )(core, spec, weight, mine, theirs)
+    images_all, pair, spec = lax.optimization_barrier((images_all, pair, spec))
 
     near_all = pl.pallas_call(
         library_kernel,
@@ -387,45 +358,46 @@
         name="library",
     )(images_all.reshape(groups, deep, N // groups, N), ahead)
     far_all = lax.ppermute(near_all, "core", swap)
-    near_best = pl.pallas_call(
-        near_kernel,
-        out_shape=jax.ShapeDtypeStruct((2,) + plane, F32),
-        grid=(deep,),
-        in_specs=[
-            pl.BlockSpec((None,) + plane, lambda i: (i, 0, 0, 0)),
-            full(2, *plane),
-            full(2, ROWS, N),
-            full(*back.shape),
+    moves, near_all = lax.optimization_barrier((moves, near_all))
+    mine = sum((m.astype(F32) for m in moves), pair.astype(F32)).astype(BF16)
+    theirs = lax.ppermute(mine, "core", swap)
+    white, white_weight = pl.pallas_call(
+        whiten_kernel,
+        out_shape=[
+            jax.ShapeDtypeStruct((2,) + plane, F32),
+            jax.ShapeDtypeStruct((2, ROWS, N), F32),
         ],
-        out_specs=full(2, *plane),
+        grid=(1,),
+        in_specs=[full(1, 1), full(2, *plane), full(2, ROWS, N), full(PART, N), full(PART, N)],
+        out_specs=[full(2, *plane), full(2, ROWS, N)],
         compiler_params=params(12),
-        cost_estimate=cost(2 * deep * 2 * work, 8 << 20),
-        name="near",
-    )(near_all, white, white_weight, back)
-    far_all, near_best = lax.optimization_barrier((far_all, near_best))
+        cost_estimate=cost(60 * work, 4 << 20),
+        name="whiten",
+    )(core, spec, weight, mine, theirs)
 
     def match(t, dtype, name):
+        lib_spec = pl.BlockSpec((None,) + plane, lambda i: (i, 0, 0, 0))
         return pl.pallas_call(
-            far_kernel,
+            match_kernel,
             out_shape=jax.ShapeDtypeStruct((N, N), dtype),
-            grid=(deep // 2,),
+            grid=(deep,),
             in_specs=[
-                pl.BlockSpec((2,) + plane, lambda i: (i, 0, 0, 0)),
+                lib_spec,
+                lib_spec,
                 pl.BlockSpec((None,) + plane, lambda i: (t, 0, 0, 0)),
                 pl.BlockSpec((None, ROWS, N), lambda i: (t, 0, 0)),
                 full(*back.shape),
-                pl.BlockSpec((None,) + plane, lambda i: (t, 0, 0, 0)),
                 full(*unfold.shape),
             ],
             out_specs=full(N, N),
             scratch_shapes=[pltpu.VMEM(plane, F32)],
             compiler_params=params(12),
-            cost_estimate=cost(deep * 2 * work, 5 << 20),
+            cost_estimate=cost(2 * deep * 2 * work, 6 << 20),
             name=name,
-        )(far_all, white, white_weight, back, near_best, unfold)
-
-    got = lax.ppermute(match(1, BF16, "far_other"), "xhi", swap)
-    best = match(0, F32, "far_own")
+        )(near_all, far_all, white, white_weight, back, unfold)
+
+    got = lax.ppermute(match(1, BF16, "match_other"), "xhi", swap)
+    best = match(0, F32, "match_own")
     return jnp.maximum(best, got.astype(F32))[None, None]
 
 

time: 59.6 us -> 55.3 us (0.928)
  waiting for transfers between devices: 17.7 us -> 9.44 us
  starting transfers between devices: 21.7 us -> 24.9 us
    ppermute x4, waiting for transfers between devices: 14.9 us -> 2.69 us  [the longest x1 2.63 us: per_device(): got = lax.ppermute(match(1, BF16, 'match_other'), 'xhi', swap)]
    all_to_all x1, waiting for transfers between devices: 0.01 us -> 4.76 us  [per_device(): images_all = lax.all_to_all(copies, LIB, 0, 0, tiled=False)]
    ppermute x1, starting transfers between devices: 0.58 us -> 3.36 us  [per_device(): far_all = lax.ppermute(near_all, 'core', swap)]
    pallas_call x3 -> x2, Pallas kernels: 8.93 us -> 8.97 us  [match(): pl.pallas_call(match_kernel, out_shape=jax.ShapeDtypeStruct((N, N), dtype...]
  transfers between devices with their start and end apart: 10 -> 10, of which waited for: 6 -> 3; matrix products, arithmetic and copies ran while one was open for 0% -> 0% of each run, Pallas kernels for 21% -> 23%
where the time goes in v8:
time: 55.3 us; the launch traced here: 54.8 us
  starting transfers between devices  24.9 us (45%)
  Pallas kernels  17.2 us (31%)
  waiting for transfers between devices  9.44 us (17%)
  local copies, waits for them, and re-layouts  1.44 us (3%)
  other arithmetic  0.95 us (2%)
  between operations  0.83 us (2%)
    all_to_all x1, starting transfers between devices, per_device(): images_all = lax.all_to_all(copies, LIB, 0, 0, tiled=False)  9.32 us
    pallas_call x2, Pallas kernels, match(): pl.pallas_call(match_kernel, out_shape=jax.ShapeDtypeStruct((N, N), dtype...  8.97 us
    all_to_all x1, waiting for transfers between devices, per_device(): images_all = lax.all_to_all(copies, LIB, 0, 0, tiled=False)  4.76 us
    ppermute x3, starting transfers between devices, per_device(): lax.ppermute(pair, 'z', [(z, (z + dz) % deep) for z in range(deep)])  3.95 us
    ppermute x1, starting transfers between devices, per_device(): received = lax.ppermute(tile, 'xhi', swap)  3.57 us
    ppermute x1, starting transfers between devices, per_device(): far_all = lax.ppermute(near_all, 'core', swap)  3.36 us
    ppermute x1, waiting for transfers between devices, per_device(): got = lax.ppermute(match(1, BF16, 'match_other'), 'xhi', swap)  2.63 us
    ppermute x1, starting transfers between devices, per_device(): got = lax.ppermute(match(1, BF16, 'match_other'), 'xhi', swap)  2.53 us
  transfers between devices with their start and end apart: 10, of which 3 were waited for; matrix products, arithmetic and copies ran while one was open for 0% of the time, Pallas kernels for 23%

profile of v8, /device:TPU:1, one launch (start us, length us, event | category | flops | bytes accessed | tf_op | source)
XLA Modules:
  0.0 54.8 jit_solution(4728891450211253316)
XLA Ops:
  0.0 3.6 %collective-permute-start.1 = (bf16[384,384]{1,0:T(8,128)(2,1)}, bf16[384,384]{1,0:T(8,128)(2,1)S(1)}, u32[]{:S(2)}, u32[]{:S(2)}) collective-permute-start(bf16[384,384]{1,0:T(8,128)(2,1)} %bitcast.11), channel_id=1, source_target_pairs={{0,2},{2,0},{1,3},{3,1},{4,6},{6,4},{5,7},{7,5},{8,10},{10,8},{9,1... | collective-permute-start | bytes 884744 | tf_op jit(solution)/shard_map/ppermute | solution.py:289
  3.6 0.0 collective-permute-start
  3.6 1.9 %copies.1 = bf16[32,48,384]{2,1,0:T(8,128)(2,1)} custom-call(bf16[48,384]{1,0:T(8,128)(2,1)} %bitcast.13), custom_call_target="tpu_custom_call" | custom-call | bytes 1048576 | tf_op jit(solution)/shard_map/copies/pallas_call | solution.py:292
  5.5 0.0 copy-start
  5.5 0.0 copy-start.3
  5.5 9.3 %all-to-all-start = ((bf16[32,48,384]{2,1,0:T(8,128)(2,1)}), bf16[32,48,384]{2,1,0:T(8,128)(2,1)S(1)}, u32[]{:S(2)}, u32[]{:S(2)}) async-start(bf16[32,48,384]{2,1,0:T(8,128)(2,1)} %copies.1), calls=%async_computation | async-start | bytes 2359296 | tf_op jit(solution)/shard_map/all_to_all | solution.py:305
  15.5 0.0 collective-permute-done.mate_ref
  15.5 0.0 collective-permute-done.1.other_ref
  15.5 0.0 copy-done
  15.5 0.0 copy-done.3
  15.5 0.0 copy-start.6
  15.5 0.0 copy-start.7
  15.5 0.0 copy-start.8
  15.6 0.0 copy-start.9
  15.6 1.5 %tile.1 = (f32[2,2,200,384]{3,2,1,0:T(8,128)S(1)}, bf16[104,384]{1,0:T(8,128)(2,1)S(1)}, bf16[104,384]{1,0:T(8,128)(2,1)S(1)}) custom-call(s32[1,1]{1,0:T(1,128)} %bitcast.core_ref, s32[1,1]{1,0:T(1,128)} %collective-permute-done.mate_ref, bf16[384,384]{1,0:T(8,128)(2,1)S(1)} %bitcast.12, bf16[384,384]{1,0:T(8,128)(2,1)S(1)} %collective-permute-done.1.other_ref, ...), custom_call_target="tpu_custom_call" | custom-call | flops 31457280000 | bytes 3145728 | tf_op jit(solution)/shard_map/tile/pallas_call | solution.py:307
  17.0 1.6 %collective-permute-start.2 = (bf16[104,384]{1,0:T(8,128)(2,1)S(1)}, bf16[104,384]{1,0:T(8,128)(2,1)S(1)}, u32[]{:S(2)}, u32[]{:S(2)}) collective-permute-start(bf16[104,384]{1,0:T(8,128)(2,1)S(1)} %get-tuple-element.20), channel_id=1, source_target_pairs={{0,1},{1,0},{2,3},{3,2},{4,5},{5,4},{6,7},{7,6},{8,9},{9,8},{10,11... | collective-permute-start | bytes 239624 | tf_op jit(solution)/shard_map/ppermute | solution.py:323
  18.6 0.0 copy-done.6
  18.6 0.0 copy-done.7
  18.6 0.0 copy-done.8
  18.6 0.0 copy-done.9
  18.7 2.1 %gain.1 = (f32[2,2,200,384]{3,2,1,0:T(8,128)S(1)}, f32[2,200,384]{2,1,0:T(8,128)S(1)}) custom-call(s32[1,1]{1,0:T(1,128)S(6)} %copy.11.row_ref, s32[1,1]{1,0:T(1,128)} %collective-permute-done.mate_ref, f32[8,128]{1,0:T(8,128)S(1)} %select_maximum_fusion.table_ref, f32[2,2,200,384]{3,2,1,0:T(8,128)S(1)} %get-tuple-element.21.tile_ref, ...), custom_call_target="tpu_custom_call" | custom-call | flops 9216000 | bytes 4194304 | tf_op jit(solution)/shard_map/gain/pallas_call | solution.py:331
  20.7 0.0 copy-start.1
  20.7 0.8 %copy-done.1 = f32[2,200,384]{2,1,0:T(8,128)} copy-done((f32[2,200,384]{2,1,0:T(8,128)}, f32[2,200,384]{2,1,0:T(8,128)S(1)}, u32[]{:S(2)}) %copy-start.1) | copy-done | bytes 614424
  21.5 0.0 collective-permute-done.2
  21.6 2.8 %collective-permute-start.5 = (bf16[104,384]{1,0:T(8,128)(2,1)S(1)}, bf16[104,384]{1,0:T(8,128)(2,1)S(1)}, u32[]{:S(2)}, u32[]{:S(2)}) collective-permute-start(bf16[104,384]{1,0:T(8,128)(2,1)S(1)} %add_convert_fusion.1), channel_id=1, source_target_pairs={{0,12},{4,0},{8,4},{12,8},{1,13},{5,1},{9,5},{13,9},{2,14},{6,2},{... | collective-permute-start | bytes 239624 | tf_op jit(solution)/shard_map/ppermute | solution.py:325
  24.4 0.6 %collective-permute-start.4 = (bf16[104,384]{1,0:T(8,128)(2,1)S(1)}, bf16[104,384]{1,0:T(8,128)(2,1)S(1)}, u32[]{:S(2)}, u32[]{:S(2)}) collective-permute-start(bf16[104,384]{1,0:T(8,128)(2,1)S(1)} %add_convert_fusion.1), channel_id=1, source_target_pairs={{0,8},{4,12},{8,0},{12,4},{1,9},{5,13},{9,1},{13,5},{2,10},{6,14},... | collective-permute-start | bytes 239624 | tf_op jit(solution)/shard_map/ppermute | solution.py:325
  24.9 0.6 %collective-permute-start.3 = (bf16[104,384]{1,0:T(8,128)(2,1)S(1)}, bf16[104,384]{1,0:T(8,128)(2,1)S(1)}, u32[]{:S(2)}, u32[]{:S(2)}) collective-permute-start(bf16[104,384]{1,0:T(8,128)(2,1)S(1)} %add_convert_fusion.1), channel_id=1, source_target_pairs={{0,4},{4,8},{8,12},{12,0},{1,5},{5,9},{9,13},{13,1},{2,6},{6,10},{... | collective-permute-start | bytes 239624 | tf_op jit(solution)/shard_map/ppermute | solution.py:325
  25.5 4.8 %all-to-all-done = bf16[32,48,384]{2,1,0:T(8,128)(2,1)S(1)} async-done(((bf16[32,48,384]{2,1,0:T(8,128)(2,1)}), bf16[32,48,384]{2,1,0:T(8,128)(2,1)S(1)}, u32[]{:S(2)}, u32[]{:S(2)}) %all-to-all-start) | async-done | bytes 1179680 | tf_op jit(solution)/shard_map/all_to_all | solution.py:305
  30.3 0.0 copy-start.2
  30.3 2.3 %library.1.near_ref = bf16[4,2,200,384]{3,2,1,0:T(8,128)(2,1)S(1)} custom-call(bf16[8,4,48,384]{3,2,1,0:T(8,128)(2,1)S(1)} %bitcast.10, bf16[1168,256]{1,0:T(8,128)(2,1)S(1)} %copy-done), custom_call_target="tpu_custom_call" | custom-call | flops 629145600 | bytes 4194304 | tf_op jit(solution)/shard_map/library/pallas_call | solution.py:347
  32.6 3.4 %collective-permute-start.6 = (bf16[4,2,200,384]{3,2,1,0:T(8,128)(2,1)S(1)}, bf16[4,2,200,384]{3,2,1,0:T(8,128)(2,1)S(1)}, u32[]{:S(2)}, u32[]{:S(2)}) collective-permute-start(bf16[4,2,200,384]{3,2,1,0:T(8,128)(2,1)S(1)} %library.1.near_ref), channel_id=1, source_target_pairs={{0,1},{1,0},{2,3},{3,2},{4,5},{5,4},{6,7},{7,6},{8,9},{9,8},{10,11... | collective-permute-start | bytes 3686408 | tf_op jit(solution)/shard_map/ppermute | solution.py:360
  36.0 0.0 collective-permute-done.5
  36.0 0.0 collective-permute-done.4
  36.0 0.0 collective-permute-done.3
  36.1 0.6 %collective-permute-start.7 = (bf16[104,384]{1,0:T(8,128)(2,1)S(1)}, bf16[104,384]{1,0:T(8,128)(2,1)S(1)}, u32[]{:S(2)}, u32[]{:S(2)}) collective-permute-start(bf16[104,384]{1,0:T(8,128)(2,1)S(1)} %add_convert_fusion.mine_ref), channel_id=1, source_target_pairs={{0,1},{1,0},{2,3},{3,2},{4,5},{5,4},{6,7},{7,6},{8,9},{9,8},{10,11... | collective-permute-start | bytes 239624 | tf_op jit(solution)/shard_map/ppermute | solution.py:363
  36.7 2.0 %collective-permute-done.7.theirs_ref = bf16[104,384]{1,0:T(8,128)(2,1)S(1)} collective-permute-done((bf16[104,384]{1,0:T(8,128)(2,1)S(1)}, bf16[104,384]{1,0:T(8,128)(2,1)S(1)}, u32[]{:S(2)}, u32[]{:S(2)}) %collective-permute-start.7) | collective-permute-done | bytes 79904 | tf_op jit(solution)/shard_map/ppermute | solution.py:363
  38.7 0.0 copy-done.2
  38.7 0.0 copy-start.4
  38.7 0.0 copy-start.5
  38.7 0.5 whiten.1
  39.2 0.0 collective-permute-done.6.far_ref
  39.2 0.5 copy-done.4
  39.7 0.0 copy-done.5
  39.8 4.3 %match_other.1 = bf16[384,384]{1,0:T(8,128)(2,1)S(1)} custom-call(bf16[4,2,200,384]{3,2,1,0:T(8,128)(2,1)S(1)} %library.1.near_ref, bf16[4,2,200,384]{3,2,1,0:T(8,128)(2,1)S(1)} %collective-permute-done.6.far_ref, f32[2,2,200,384]{3,2,1,0:T(8,128)S(1)} %get-tuple-element.31.spec_ref, f32[2,200,384]{2,1,0:T(8,128)S(1)} %get-tuple-element.32.weight_ref, ...), custom_call_target="tpu_custom_call" | custom-call | flops 2516582400 | bytes 6291456 | tf_op jit(solution)/shard_map/match_other/pallas_call | solution.py:380
  44.1 2.5 %collective-permute-start.8 = (bf16[384,384]{1,0:T(8,128)(2,1)S(1)}, bf16[384,384]{1,0:T(8,128)(2,1)S(1)}, u32[]{:S(2)}, u32[]{:S(2)}) collective-permute-start(bf16[384,384]{1,0:T(8,128)(2,1)S(1)} %match_other.1), channel_id=1, source_target_pairs={{0,2},{2,0},{1,3},{3,1},{4,6},{6,4},{5,7},{7,5},{8,10},{10,8},{9,1... | collective-permute-start | bytes 884744 | tf_op jit(solution)/shard_map/ppermute | solution.py:399
  46.6 4.6 %match_own.1 = f32[384,384]{1,0:T(8,128)S(1)} custom-call(bf16[4,2,200,384]{3,2,1,0:T(8,128)(2,1)S(1)} %library.1.near_ref, bf16[4,2,200,384]{3,2,1,0:T(8,128)(2,1)S(1)} %collective-permute-done.6.far_ref, f32[2,2,200,384]{3,2,1,0:T(8,128)S(1)} %get-tuple-element.31.spec_ref, f32[2,200,384]{2,1,0:T(8,128)S(1)} %get-tuple-element.32.weight_ref, ...), custom_call_target="tpu_custom_call" | custom-call | flops 2516582400 | bytes 6291456 | tf_op jit(solution)/shard_map/match_own/pallas_call | solution.py:380
  51.3 2.6 %collective-permute-done.8 = bf16[384,384]{1,0:T(8,128)(2,1)S(1)} collective-permute-done((bf16[384,384]{1,0:T(8,128)(2,1)S(1)}, bf16[384,384]{1,0:T(8,128)(2,1)S(1)}, u32[]{:S(2)}, u32[]{:S(2)}) %collective-permute-start.8) | collective-permute-done | bytes 294944 | tf_op jit(solution)/shard_map/ppermute | solution.py:399
  53.9 0.9 %maximum_bitcast_fusion = f32[1,1,384,384]{3,2,1,0:T(8,128)} fusion(f32[384,384]{1,0:T(8,128)S(1)} %match_own.1, bf16[384,384]{1,0:T(8,128)(2,1)S(1)} %collective-permute-done.8), kind=kLoop, calls=%fused_computation | loop fusion | flops 294912 | bytes 1474560 | tf_op jit(solution)/shard_map/broadcast_in_dim | solution.py:401
  (3 shorter events, 0.1 us)
Async XLA Ops:
  0.0 15.5 %collective-permute-start.1 = (bf16[384,384]{1,0:T(8,128)(2,1)}, bf16[384,384]{1,0:T(8,128)(2,1)S(1)}, u32[]{:S(2)}, u32[]{:S(2)}) collective-permute-start(bf16[384,384]{1,0:T(8,128)(2,1)} %bitcast.11), channel_id=1, source_target_pairs={{0,2},{2,0},{1,3},{3,1},{4,6},{6,4},{5,7},{7,5},{8,10},{10,8},{9,1... | collective-permute-start | bytes 884744 | tf_op jit(solution)/shard_map/ppermute | solution.py:289
  3.6 11.9 %collective-permute-start = (s32[1,1]{1,0:T(1,128)}, s32[1,1]{1,0:T(1,128)}, u32[]{:S(2)}, u32[]{:S(2)}) collective-permute-start(s32[1,1]{1,0:T(1,128)} %param.12), channel_id=1, source_target_pairs={{0,2},{2,0},{1,3},{3,1},{4,6},{6,4},{5,7},{7,5},{8,10},{10,8},{9,1... | collective-permute-start | bytes 20 | tf_op jit(solution)/shard_map/ppermute | solution.py:290
  5.5 10.0 %copy-start = (bf16[1168,256]{1,0:T(8,128)(2,1)S(1)}, bf16[1168,256]{1,0:T(8,128)(2,1)}, u32[]{:S(2)}) copy-start(bf16[1168,256]{1,0:T(8,128)(2,1)} %constant.13.clone.tab_ref) | copy-start | bytes 1794052
  5.5 10.0 %copy-start.3 = (bf16[1,1,384,384]{3,2,1,0:T(8,128)(2,1)S(1)}, bf16[1,1,384,384]{3,2,1,0:T(8,128)(2,1)}, u32[]{:S(2)}) copy-start(bf16[1,1,384,384]{3,2,1,0:T(8,128)(2,1)} %param.10) | copy-start | bytes 884740
  5.5 24.8 %all-to-all-start = ((bf16[32,48,384]{2,1,0:T(8,128)(2,1)}), bf16[32,48,384]{2,1,0:T(8,128)(2,1)S(1)}, u32[]{:S(2)}, u32[]{:S(2)}) async-start(bf16[32,48,384]{2,1,0:T(8,128)(2,1)} %copies.1), calls=%async_computation | async-start | bytes 2359296 | tf_op jit(solution)/shard_map/all_to_all | solution.py:305
  15.5 3.1 %copy-start.6 = (f32[64]{0:T(128)S(1)}, f32[64]{0:T(128)}, u32[]{:S(2)}) copy-start(f32[64]{0:T(128)} %param.16) | copy-start | bytes 772
  15.5 3.1 %copy-start.7 = (f32[64]{0:T(128)S(1)}, f32[64]{0:T(128)}, u32[]{:S(2)}) copy-start(f32[64]{0:T(128)} %param.15) | copy-start | bytes 772
  15.5 3.1 %copy-start.8 = (f32[64]{0:T(128)S(1)}, f32[64]{0:T(128)}, u32[]{:S(2)}) copy-start(f32[64]{0:T(128)} %param.14) | copy-start | bytes 772
  15.6 3.1 %copy-start.9 = (f32[64]{0:T(128)S(1)}, f32[64]{0:T(128)}, u32[]{:S(2)}) copy-start(f32[64]{0:T(128)} %param.13) | copy-start | bytes 772
  17.0 4.5 %collective-permute-start.2 = (bf16[104,384]{1,0:T(8,128)(2,1)S(1)}, bf16[104,384]{1,0:T(8,128)(2,1)S(1)}, u32[]{:S(2)}, u32[]{:S(2)}) collective-permute-start(bf16[104,384]{1,0:T(8,128)(2,1)S(1)} %get-tuple-element.20), channel_id=1, source_target_pairs={{0,1},{1,0},{2,3},{3,2},{4,5},{5,4},{6,7},{7,6},{8,9},{9,8},{10,11... | collective-permute-start | bytes 239624 | tf_op jit(solution)/shard_map/ppermute | solution.py:323
  20.7 0.8 %copy-start.1 = (f32[2,200,384]{2,1,0:T(8,128)}, f32[2,200,384]{2,1,0:T(8,128)S(1)}, u32[]{:S(2)}) copy-start(f32[2,200,384]{2,1,0:T(8,128)S(1)} %get-tuple-element.26.weight_ref) | copy-start | bytes 1843204
  21.6 14.4 %collective-permute-start.5 = (bf16[104,384]{1,0:T(8,128)(2,1)S(1)}, bf16[104,384]{1,0:T(8,128)(2,1)S(1)}, u32[]{:S(2)}, u32[]{:S(2)}) collective-permute-start(bf16[104,384]{1,0:T(8,128)(2,1)S(1)} %add_convert_fusion.1), channel_id=1, source_target_pairs={{0,12},{4,0},{8,4},{12,8},{1,13},{5,1},{9,5},{13,9},{2,14},{6,2},{... | collective-permute-start | bytes 239624 | tf_op jit(solution)/shard_map/ppermute | solution.py:325
  24.4 11.6 %collective-permute-start.4 = (bf16[104,384]{1,0:T(8,128)(2,1)S(1)}, bf16[104,384]{1,0:T(8,128)(2,1)S(1)}, u32[]{:S(2)}, u32[]{:S(2)}) collective-permute-start(bf16[104,384]{1,0:T(8,128)(2,1)S(1)} %add_convert_fusion.1), channel_id=1, source_target_pairs={{0,8},{4,12},{8,0},{12,4},{1,9},{5,13},{9,1},{13,5},{2,10},{6,14},... | collective-permute-start | bytes 239624 | tf_op jit(solution)/shard_map/ppermute | solution.py:325
  24.9 11.1 %collective-permute-start.3 = (bf16[104,384]{1,0:T(8,128)(2,1)S(1)}, bf16[104,384]{1,0:T(8,128)(2,1)S(1)}, u32[]{:S(2)}, u32[]{:S(2)}) collective-permute-start(bf16[104,384]{1,0:T(8,128)(2,1)S(1)} %add_convert_fusion.1), channel_id=1, source_target_pairs={{0,4},{4,8},{8,12},{12,0},{1,5},{5,9},{9,13},{13,1},{2,6},{6,10},{... | collective-permute-start | bytes 239624 | tf_op jit(solution)/shard_map/ppermute | solution.py:325
  30.3 8.4 %copy-start.2 = (f32[2,200,384]{2,1,0:T(8,128)S(1)}, f32[2,200,384]{2,1,0:T(8,128)}, u32[]{:S(2)}) copy-start(f32[2,200,384]{2,1,0:T(8,128)} %copy-done.1) | copy-start | bytes 1843204
  32.6 6.5 %collective-permute-start.6 = (bf16[4,2,200,384]{3,2,1,0:T(8,128)(2,1)S(1)}, bf16[4,2,200,384]{3,2,1,0:T(8,128)(2,1)S(1)}, u32[]{:S(2)}, u32[]{:S(2)}) collective-permute-start(bf16[4,2,200,384]{3,2,1,0:T(8,128)(2,1)S(1)} %library.1.near_ref), channel_id=1, source_target_pairs={{0,1},{1,0},{2,3},{3,2},{4,5},{5,4},{6,7},{7,6},{8,9},{9,8},{10,11... | collective-permute-start | bytes 3686408 | tf_op jit(solution)/shard_map/ppermute | solution.py:360
  36.1 2.6 %collective-permute-start.7 = (bf16[104,384]{1,0:T(8,128)(2,1)S(1)}, bf16[104,384]{1,0:T(8,128)(2,1)S(1)}, u32[]{:S(2)}, u32[]{:S(2)}) collective-permute-start(bf16[104,384]{1,0:T(8,128)(2,1)S(1)} %add_convert_fusion.mine_ref), channel_id=1, source_target_pairs={{0,1},{1,0},{2,3},{3,2},{4,5},{5,4},{6,7},{7,6},{8,9},{9,8},{10,11... | collective-permute-start | bytes 239624 | tf_op jit(solution)/shard_map/ppermute | solution.py:363
  38.7 1.1 %copy-start.4 = (bf16[1184,256]{1,0:T(8,128)(2,1)S(1)}, bf16[1184,256]{1,0:T(8,128)(2,1)}, u32[]{:S(2)}) copy-start(bf16[1184,256]{1,0:T(8,128)(2,1)} %constant.14.clone.tab_ref) | copy-start | bytes 1818628
  38.7 1.1 %copy-start.5 = (bf16[192,400]{1,0:T(8,128)(2,1)S(1)}, bf16[192,400]{1,0:T(8,128)(2,1)}, u32[]{:S(2)}) copy-start(bf16[192,400]{1,0:T(8,128)(2,1)} %constant.15.clone.unfold_ref) | copy-start | bytes 460804
  44.1 9.8 %collective-permute-start.8 = (bf16[384,384]{1,0:T(8,128)(2,1)S(1)}, bf16[384,384]{1,0:T(8,128)(2,1)S(1)}, u32[]{:S(2)}, u32[]{:S(2)}) collective-permute-start(bf16[384,384]{1,0:T(8,128)(2,1)S(1)} %match_other.1), channel_id=1, source_target_pairs={{0,2},{2,0},{1,3},{3,1},{4,6},{6,4},{5,7},{7,5},{8,10},{10,8},{9,1... | collective-permute-start | bytes 884744 | tf_op jit(solution)/shard_map/ppermute | solution.py:399

commit v9 on v8

--- a/solution.py
+++ b/solution.py
@@ -18,6 +18,7 @@
 THIRD = N // 3
 BLOCKS = (64, 64, 72)
 ROWS = sum(BLOCKS)
+MARK = 16
 SPLIT = 96
 PART = ROWS - SPLIT
 FOLD = 208
@@ -81,7 +82,7 @@
     return jnp.where((u > 0) & (u < HALF), 2.0, jnp.where(u <= HALF, 1.0, 0.0))
 
 
-def copy_kernel(block_ref, out_ref, wide_sc, sems):
+def copy_kernel(row_ref, tile_ref, block_ref, out_ref, sent_ref, wide_sc, sems):
     count = wide_sc.shape[0]
     wide_sc[...] = jnp.broadcast_to(block_ref[...][None], wide_sc.shape)
     moves = [
@@ -90,6 +91,8 @@
     ]
     for move in moves:
         move.start()
+    sent_ref[:N] = tile_ref[...]
+    sent_ref[N:] = jnp.broadcast_to(row_ref[...].astype(F32), (MARK, N)).astype(BF16)
     for move in moves:
         move.wait()
 
@@ -168,11 +171,9 @@
     return gain, row_scale(u) * square
 
 
-def tile_kernel(
-    core_ref, mate_ref, own_ref, other_ref, tab_ref, spec_ref, keep_ref, send_ref, power_sc
-):
+def tile_kernel(core_ref, own_ref, other_ref, tab_ref, spec_ref, keep_ref, send_ref, power_sc):
     for t, ref in enumerate((own_ref, other_ref)):
-        parts = half_spectrum(ref[...], tab_ref)
+        parts = half_spectrum(ref[:N], tab_ref)
         store_spectrum(spec_ref.at[t], parts)
         for k, (re, im) in enumerate(parts):
             at = slice(k * THIRD, (k + 1) * THIRD)
@@ -184,9 +185,10 @@
     send_ref[...] = jnp.where(first, high, low).astype(BF16)
 
 
-def gain_kernel(row_ref, mate_ref, table_ref, tile_ref, tab_ref, spec_ref, weight_ref):
-    for t, ref in enumerate((row_ref, mate_ref)):
-        gain, weight_ref[t] = ctf_factors(ref[...].astype(F32), table_ref[...])
+def gain_kernel(row_ref, mark_ref, table_ref, tile_ref, *refs):
+    spec_ref, weight_ref = refs[-2:]
+    for t, row in enumerate((row_ref[...], mark_ref[0:1, 0:1])):
+        gain, weight_ref[t] = ctf_factors(row.astype(F32), table_ref[...])
         spec_ref[t, 0] = tile_ref[t, 0] * gain
         spec_ref[t, 1] = tile_ref[t, 1] * gain
 
@@ -222,7 +224,8 @@
     return even - odd, even + odd
 
 
-def whiten_kernel(core_ref, spec_ref, weight_ref, mine_ref, theirs_ref, spec_out, weight_out):
+def whiten_kernel(core_ref, spec_ref, weight_ref, mine_ref, theirs_ref, *refs):
+    spec_out, weight_out = refs[-2:]
     mine, theirs = mine_ref[...].astype(F32), theirs_ref[...].astype(F32)
     first = core_ref[...] == 0
     low, high = jnp.where(first, mine, theirs), jnp.where(first, theirs, mine)
@@ -243,12 +246,13 @@
     def _():
         best_sc[...] = jnp.full_like(best_sc, -jnp.inf)
 
-    pairs = [
-        match_step(ref[0].astype(F32), ref[1].astype(F32), spec_ref, weight_ref, tab_ref)
-        for ref in (near_ref, far_ref)
-    ]
-    for side in range(2):
-        best_sc[side] = jnp.maximum(best_sc[side], jnp.maximum(pairs[0][side], pairs[1][side]))
+    for i in range(near_ref.shape[0]):
+        pairs = [
+            match_step(ref[i, 0].astype(F32), ref[i, 1].astype(F32), spec_ref, weight_ref, tab_ref)
+            for ref in (near_ref, far_ref)
+        ]
+        for k in range(2):
+            best_sc[k] = jnp.maximum(best_sc[k], jnp.maximum(pairs[0][k], pairs[1][k]))
 
     @pl.when(step == pl.num_programs(0) - 1)
     def _():
@@ -282,26 +286,29 @@
     deep, wide = lax.axis_size("z"), lax.axis_size("xhi")
     core = lax.axis_index("core").astype(jnp.int32).reshape(1, 1)
     swap = [(0, 1), (1, 0)]
+    kept = [pl.BlockSpec(memory_space=pltpu.VMEM)]
     plane = (2, ROWS, N)
     work = 2 * ROWS * 768 * 256 * 2
 
     tile = images[0, 0]
-    received = lax.ppermute(tile, "xhi", swap)
-    mate = lax.ppermute(ctf_row, "xhi", swap)
     block = projections[0]
-    copies = pl.pallas_call(
+    copies, sent = pl.pallas_call(
         copy_kernel,
-        out_shape=pltpu.HBM((places,) + block.shape, BF16),
+        out_shape=[
+            pltpu.HBM((places,) + block.shape, BF16),
+            jax.ShapeDtypeStruct((N + MARK, N), BF16),
+        ],
         grid=(1,),
-        in_specs=[full(*block.shape)],
-        out_specs=pl.BlockSpec(memory_space=pltpu.HBM),
+        in_specs=[full(1, 1), full(N, N), full(*block.shape)],
+        out_specs=[pl.BlockSpec(memory_space=pltpu.HBM), full(N + MARK, N)],
         scratch_shapes=[
             pltpu.VMEM((groups,) + block.shape, BF16),
             pltpu.SemaphoreType.DMA((places // groups,)),
         ],
         cost_estimate=cost(0, 1 << 20),
         name="copies",
-    )(block)
+    )(ctf_row, tile, block)
+    received = lax.ppermute(sent, "xhi", swap)
     images_all = lax.all_to_all(copies, LIB, 0, 0, tiled=False)
 
     tiles, keep, send = pl.pallas_call(
@@ -312,13 +319,13 @@
             jax.ShapeDtypeStruct((PART, N), BF16),
         ],
         grid=(1,),
-        in_specs=[full(1, 1), full(1, 1), full(N, N), full(N, N), full(*ahead.shape)],
+        in_specs=[full(1, 1), full(N, N), full(N + MARK, N), full(*ahead.shape)],
         out_specs=[full(2, *plane), full(PART, N), full(PART, N)],
         scratch_shapes=[pltpu.VMEM((ROWS, N), F32)],
         compiler_params=params(12),
         cost_estimate=cost(200 * work, 3 << 20),
         name="tile",
-    )(core, mate, tile, received, ahead)
+    )(core, tile, received, ahead)
 
     pair = (keep.astype(F32) + lax.ppermute(send, "core", swap).astype(F32)).astype(BF16)
     moves = [
@@ -335,12 +342,18 @@
             jax.ShapeDtypeStruct((2, ROWS, N), F32),
         ],
         grid=(1,),
-        in_specs=[full(1, 1), full(1, 1), full(*table.shape), full(2, *plane), full(*ahead.shape)],
+        in_specs=[
+            full(1, 1),
+            pl.BlockSpec((MARK, N), lambda i: (N // MARK, 0)),
+            full(*table.shape),
+            full(2, *plane),
+        ]
+        + kept * 3,
         out_specs=[full(2, *plane), full(2, ROWS, N)],
         compiler_params=params(12),
         cost_estimate=cost(2 * ROWS * N * 60, 4 << 20),
         name="gain",
-    )(ctf_row, mate, table, tiles, ahead)
+    )(ctf_row, received, table, tiles, ahead, back, unfold)
 
     images_all, pair, spec = lax.optimization_barrier((images_all, pair, spec))
 
@@ -368,19 +381,20 @@
             jax.ShapeDtypeStruct((2, ROWS, N), F32),
         ],
         grid=(1,),
-        in_specs=[full(1, 1), full(2, *plane), full(2, ROWS, N), full(PART, N), full(PART, N)],
+        in_specs=[full(1, 1), full(2, *plane), full(2, ROWS, N), full(PART, N), full(PART, N)]
+        + kept * 2,
         out_specs=[full(2, *plane), full(2, ROWS, N)],
         compiler_params=params(12),
         cost_estimate=cost(60 * work, 4 << 20),
         name="whiten",
-    )(core, spec, weight, mine, theirs)
+    )(core, spec, weight, mine, theirs, back, unfold)
 
     def match(t, dtype, name):
-        lib_spec = pl.BlockSpec((None,) + plane, lambda i: (i, 0, 0, 0))
+        lib_spec = pl.BlockSpec((2,) + plane, lambda i: (i, 0, 0, 0))
         return pl.pallas_call(
             match_kernel,
             out_shape=jax.ShapeDtypeStruct((N, N), dtype),
-            grid=(deep,),
+            grid=(deep // 2,),
             in_specs=[
                 lib_spec,
                 lib_spec,

time: 55.3 us -> 54.6 us (0.987)
  starting transfers between devices: 24.9 us -> 22.4 us
  waiting for transfers between devices: 9.44 us -> 11.9 us
  Pallas kernels: 17.2 us -> 16.4 us
    all_to_all x1, waiting for transfers between devices: 4.76 us -> 6.04 us  [per_device(): images_all = lax.all_to_all(copies, LIB, 0, 0, tiled=False)]
    all_to_all x1, starting transfers between devices: 9.32 us -> 8.08 us  [per_device(): images_all = lax.all_to_all(copies, LIB, 0, 0, tiled=False)]
    ppermute x1, waiting for transfers between devices: 2.63 us -> 3.68 us  [per_device(): got = lax.ppermute(match(1, BF16, 'match_other'), 'xhi', swap)]
    pallas_call x1, Pallas kernels: 1.86 us -> 2.79 us  [per_device(): pl.pallas_call(copy_kernel, out_shape=[pltpu.HBM((places,) + block.shape,...]
    ppermute x1, starting transfers between devices: 2.53 us -> 1.81 us  [per_device(): got = lax.ppermute(match(1, BF16, 'match_other'), 'xhi', swap)]
    pallas_call x1, Pallas kernels: 1.47 us -> 0.86 us  [per_device(): pl.pallas_call(tile_kernel, out_shape=[jax.ShapeDtypeStruct((2,) + plane,...]
    pallas_call x1, Pallas kernels: 2.06 us -> 1.47 us  [per_device(): pl.pallas_call(gain_kernel, out_shape=[jax.ShapeDtypeStruct((2,) + plane,...]
    pallas_call x2, Pallas kernels: 8.97 us -> 8.4 us  [match(): pl.pallas_call(match_kernel, out_shape=jax.ShapeDtypeStruct((N, N), dtype...]
  transfers between devices with their start and end apart: 10 -> 9, of which waited for: 3 -> 3; matrix products, arithmetic and copies ran while one was open for 0% -> 0% of each run, Pallas kernels for 23% -> 17%
where the time goes in v9:
time: 54.6 us; the launch traced here: 54.3 us
  starting transfers between devices  22.4 us (41%)
  Pallas kernels  16.4 us (30%)
  waiting for transfers between devices  11.9 us (22%)
  local copies, waits for them, and re-layouts  1.94 us (4%)
  other arithmetic  0.95 us (2%)
  between operations  0.86 us (2%)
    pallas_call x2, Pallas kernels, match(): pl.pallas_call(match_kernel, out_shape=jax.ShapeDtypeStruct((N, N), dtype...  8.4 us
    all_to_all x1, starting transfers between devices, per_device(): images_all = lax.all_to_all(copies, LIB, 0, 0, tiled=False)  8.08 us
    all_to_all x1, waiting for transfers between devices, per_device(): images_all = lax.all_to_all(copies, LIB, 0, 0, tiled=False)  6.04 us
    ppermute x3, starting transfers between devices, per_device(): lax.ppermute(pair, 'z', [(z, (z + dz) % deep) for z in range(deep)])  3.97 us
    ppermute x1, waiting for transfers between devices, per_device(): got = lax.ppermute(match(1, BF16, 'match_other'), 'xhi', swap)  3.68 us
    ppermute x1, starting transfers between devices, per_device(): received = lax.ppermute(sent, 'xhi', swap)  3.65 us
    ppermute x1, starting transfers between devices, per_device(): far_all = lax.ppermute(near_all, 'core', swap)  3.06 us
    pallas_call x1, Pallas kernels, per_device(): pl.pallas_call(copy_kernel, out_shape=[pltpu.HBM((places,) + block.shape,...  2.79 us
  transfers between devices with their start and end apart: 9, of which 3 were waited for; matrix products, arithmetic and copies ran while one was open for 0% of the time, Pallas kernels for 17%

profile of v9, /device:TPU:1, one launch (start us, length us, event | category | flops | bytes accessed | tf_op | source)
XLA Modules:
  0.0 54.3 jit_solution(13197261877947528536)
XLA Ops:
  0.7 2.8 %copies.1 = (bf16[32,48,384]{2,1,0:T(8,128)(2,1)}, bf16[400,384]{1,0:T(8,128)(2,1)}) custom-call(s32[1,1]{1,0:T(1,128)S(6)} %copy.11.row_ref, bf16[384,384]{1,0:T(8,128)(2,1)} %bitcast.11, bf16[48,384]{1,0:T(8,128)(2,1)} %bitcast.13), custom_call_target="tpu_custom_call" | custom-call | bytes 1048576 | tf_op jit(solution)/shard_map/copies/pallas_call | solution.py:295
  3.5 0.0 copy-start
  3.5 0.0 copy-start.2
  3.5 3.7 %collective-permute-start = (bf16[400,384]{1,0:T(8,128)(2,1)}, bf16[400,384]{1,0:T(8,128)(2,1)S(1)}, u32[]{:S(2)}, u32[]{:S(2)}) collective-permute-start(bf16[400,384]{1,0:T(8,128)(2,1)} %get-tuple-element.21), channel_id=1, source_target_pairs={{0,2},{2,0},{1,3},{3,1},{4,6},{6,4},{5,7},{7,5},{8,10},{10,8},{9,1... | collective-permute-start | bytes 921608 | tf_op jit(solution)/shard_map/ppermute | solution.py:311
  7.1 8.1 %all-to-all-start = ((bf16[32,48,384]{2,1,0:T(8,128)(2,1)}), bf16[32,48,384]{2,1,0:T(8,128)(2,1)S(1)}, u32[]{:S(2)}, u32[]{:S(2)}) async-start(bf16[32,48,384]{2,1,0:T(8,128)(2,1)} %get-tuple-element.24), calls=%async_computation | async-start | bytes 2359296 | tf_op jit(solution)/shard_map/all_to_all | solution.py:312
  15.2 0.0 collective-permute-done.other_ref.mark_ref
  15.2 0.0 copy-done
  15.2 0.0 copy-done.2
  15.3 0.0 copy-start.8
  15.3 0.0 copy-start.9
  15.3 0.0 copy-start.10
  15.3 0.0 copy-start.11
  15.3 0.0 copy-start.1
  15.3 0.0 copy-start.3
  15.3 0.9 %tile.1 = (f32[2,2,200,384]{3,2,1,0:T(8,128)S(1)}, bf16[104,384]{1,0:T(8,128)(2,1)S(1)}, bf16[104,384]{1,0:T(8,128)(2,1)S(1)}) custom-call(s32[1,1]{1,0:T(1,128)} %bitcast.core_ref, bf16[384,384]{1,0:T(8,128)(2,1)S(1)} %bitcast.12, bf16[400,384]{1,0:T(8,128)(2,1)S(1)} %collective-permute-done.other_ref.mark_ref, bf16[1168,256]{1,0:T(8,128)(2,1)S(1)} %copy-done), custom_call_target="tpu_custom_call" | custom-call | flops 31457280000 | bytes 3145728 | tf_op jit(solution)/shard_map/tile/pallas_call | solution.py:314
  16.2 1.3 %collective-permute-start.1 = (bf16[104,384]{1,0:T(8,128)(2,1)S(1)}, bf16[104,384]{1,0:T(8,128)(2,1)S(1)}, u32[]{:S(2)}, u32[]{:S(2)}) collective-permute-start(bf16[104,384]{1,0:T(8,128)(2,1)S(1)} %get-tuple-element.23), channel_id=1, source_target_pairs={{0,1},{1,0},{2,3},{3,2},{4,5},{5,4},{6,7},{7,6},{8,9},{9,8},{10,11... | collective-permute-start | bytes 239624 | tf_op jit(solution)/shard_map/ppermute | solution.py:330
  17.5 0.0 copy-done.8
  17.5 0.0 copy-done.9
  17.5 0.0 copy-done.10
  17.5 0.0 copy-done.11
  17.5 0.0 copy-done.1
  17.5 0.0 copy-done.3
  17.6 1.5 %gain.1 = (f32[2,2,200,384]{3,2,1,0:T(8,128)S(1)}, f32[2,200,384]{2,1,0:T(8,128)S(1)}) custom-call(s32[1,1]{1,0:T(1,128)S(6)} %copy.11.row_ref, bf16[400,384]{1,0:T(8,128)(2,1)S(1)} %collective-permute-done.other_ref.mark_ref, f32[8,128]{1,0:T(8,128)S(1)} %select_maximum_fusion.table_ref, f32[2,2,200,384]{3,2,1,0:T(8,128)S(1)} %get-tuple-element.25.tile_ref, ...), custom_call_target="tpu_custom_call" | custom-call | flops 9216000 | bytes 4194304 | tf_op jit(solution)/shard_map/gain/pallas_call | solution.py:338
  19.0 0.0 copy-start.4
  19.0 1.0 %copy-done.4 = f32[2,2,200,384]{3,2,1,0:T(8,128)} copy-done((f32[2,2,200,384]{3,2,1,0:T(8,128)}, f32[2,2,200,384]{3,2,1,0:T(8,128)S(1)}, u32[]{:S(2)}) %copy-start.4) | copy-done | bytes 1228824
  20.1 0.0 copy-start.6
  20.1 0.8 %copy-done.6 = f32[2,200,384]{2,1,0:T(8,128)} copy-done((f32[2,200,384]{2,1,0:T(8,128)}, f32[2,200,384]{2,1,0:T(8,128)S(1)}, u32[]{:S(2)}) %copy-start.6) | copy-done | bytes 614424
  20.9 0.0 collective-permute-done.1
  20.9 3.1 %collective-permute-start.4 = (bf16[104,384]{1,0:T(8,128)(2,1)S(1)}, bf16[104,384]{1,0:T(8,128)(2,1)S(1)}, u32[]{:S(2)}, u32[]{:S(2)}) collective-permute-start(bf16[104,384]{1,0:T(8,128)(2,1)S(1)} %add_convert_fusion.1), channel_id=1, source_target_pairs={{0,12},{4,0},{8,4},{12,8},{1,13},{5,1},{9,5},{13,9},{2,14},{6,2},{... | collective-permute-start | bytes 239624 | tf_op jit(solution)/shard_map/ppermute | solution.py:332
  24.1 0.3 collective-permute-start.3
  24.3 0.6 %collective-permute-start.2 = (bf16[104,384]{1,0:T(8,128)(2,1)S(1)}, bf16[104,384]{1,0:T(8,128)(2,1)S(1)}, u32[]{:S(2)}, u32[]{:S(2)}) collective-permute-start(bf16[104,384]{1,0:T(8,128)(2,1)S(1)} %add_convert_fusion.1), channel_id=1, source_target_pairs={{0,4},{4,8},{8,12},{12,0},{1,5},{5,9},{9,13},{13,1},{2,6},{6,10},{... | collective-permute-start | bytes 239624 | tf_op jit(solution)/shard_map/ppermute | solution.py:332
  24.9 6.0 %all-to-all-done = bf16[32,48,384]{2,1,0:T(8,128)(2,1)S(1)} async-done(((bf16[32,48,384]{2,1,0:T(8,128)(2,1)}), bf16[32,48,384]{2,1,0:T(8,128)(2,1)S(1)}, u32[]{:S(2)}, u32[]{:S(2)}) %all-to-all-start) | async-done | bytes 1179680 | tf_op jit(solution)/shard_map/all_to_all | solution.py:312
  31.0 0.0 copy-start.5
  31.0 0.0 copy-start.7
  31.0 2.4 %library.1.near_ref = bf16[4,2,200,384]{3,2,1,0:T(8,128)(2,1)S(1)} custom-call(bf16[8,4,48,384]{3,2,1,0:T(8,128)(2,1)S(1)} %bitcast.10, bf16[1168,256]{1,0:T(8,128)(2,1)S(1)} %copy-done), custom_call_target="tpu_custom_call" | custom-call | flops 629145600 | bytes 4194304 | tf_op jit(solution)/shard_map/library/pallas_call | solution.py:360
  33.3 3.1 %collective-permute-start.5 = (bf16[4,2,200,384]{3,2,1,0:T(8,128)(2,1)S(1)}, bf16[4,2,200,384]{3,2,1,0:T(8,128)(2,1)S(1)}, u32[]{:S(2)}, u32[]{:S(2)}) collective-permute-start(bf16[4,2,200,384]{3,2,1,0:T(8,128)(2,1)S(1)} %library.1.near_ref), channel_id=1, source_target_pairs={{0,1},{1,0},{2,3},{3,2},{4,5},{5,4},{6,7},{7,6},{8,9},{9,8},{10,11... | collective-permute-start | bytes 3686408 | tf_op jit(solution)/shard_map/ppermute | solution.py:373
  36.4 0.0 collective-permute-done.4
  36.4 0.0 collective-permute-done.3
  36.4 0.0 collective-permute-done.2
  36.5 0.5 collective-permute-start.6
  37.0 2.1 %collective-permute-done.6.theirs_ref = bf16[104,384]{1,0:T(8,128)(2,1)S(1)} collective-permute-done((bf16[104,384]{1,0:T(8,128)(2,1)S(1)}, bf16[104,384]{1,0:T(8,128)(2,1)S(1)}, u32[]{:S(2)}, u32[]{:S(2)}) %collective-permute-start.6) | collective-permute-done | bytes 79904 | tf_op jit(solution)/shard_map/ppermute | solution.py:376
  39.0 0.0 copy-done.5
  39.0 0.0 copy-done.7
  39.1 0.5 whiten.1
  39.6 0.0 collective-permute-done.5.far_ref
  39.6 4.1 %match_other.1 = bf16[384,384]{1,0:T(8,128)(2,1)S(1)} custom-call(bf16[4,2,200,384]{3,2,1,0:T(8,128)(2,1)S(1)} %library.1.near_ref, bf16[4,2,200,384]{3,2,1,0:T(8,128)(2,1)S(1)} %collective-permute-done.5.far_ref, f32[2,2,200,384]{3,2,1,0:T(8,128)S(1)} %get-tuple-element.35.spec_ref, f32[2,200,384]{2,1,0:T(8,128)S(1)} %get-tuple-element.36.weight_ref, ...), custom_call_target="tpu_custom_call" | custom-call | flops 2516582400 | bytes 6291456 | tf_op jit(solution)/shard_map/match_other/pallas_call | solution.py:394
  43.7 1.8 %collective-permute-start.7 = (bf16[384,384]{1,0:T(8,128)(2,1)S(1)}, bf16[384,384]{1,0:T(8,128)(2,1)S(1)}, u32[]{:S(2)}, u32[]{:S(2)}) collective-permute-start(bf16[384,384]{1,0:T(8,128)(2,1)S(1)} %match_other.1), channel_id=1, source_target_pairs={{0,2},{2,0},{1,3},{3,1},{4,6},{6,4},{5,7},{7,5},{8,10},{10,8},{9,1... | collective-permute-start | bytes 884744 | tf_op jit(solution)/shard_map/ppermute | solution.py:413
  45.5 4.3 %match_own.1 = f32[384,384]{1,0:T(8,128)S(1)} custom-call(bf16[4,2,200,384]{3,2,1,0:T(8,128)(2,1)S(1)} %library.1.near_ref, bf16[4,2,200,384]{3,2,1,0:T(8,128)(2,1)S(1)} %collective-permute-done.5.far_ref, f32[2,2,200,384]{3,2,1,0:T(8,128)S(1)} %get-tuple-element.35.spec_ref, f32[2,200,384]{2,1,0:T(8,128)S(1)} %get-tuple-element.36.weight_ref, ...), custom_call_target="tpu_custom_call" | custom-call | flops 2516582400 | bytes 6291456 | tf_op jit(solution)/shard_map/match_own/pallas_call | solution.py:394
  49.8 3.7 %collective-permute-done.7 = bf16[384,384]{1,0:T(8,128)(2,1)S(1)} collective-permute-done((bf16[384,384]{1,0:T(8,128)(2,1)S(1)}, bf16[384,384]{1,0:T(8,128)(2,1)S(1)}, u32[]{:S(2)}, u32[]{:S(2)}) %collective-permute-start.7) | collective-permute-done | bytes 294944 | tf_op jit(solution)/shard_map/ppermute | solution.py:413
  53.5 0.9 %maximum_bitcast_fusion = f32[1,1,384,384]{3,2,1,0:T(8,128)} fusion(f32[384,384]{1,0:T(8,128)S(1)} %match_own.1, bf16[384,384]{1,0:T(8,128)(2,1)S(1)} %collective-permute-done.7), kind=kLoop, calls=%fused_computation | loop fusion | flops 294912 | bytes 1474560 | tf_op jit(solution)/shard_map/broadcast_in_dim | solution.py:415
  (3 shorter events, 0.1 us)
Async XLA Ops:
  3.5 11.8 %copy-start = (bf16[1168,256]{1,0:T(8,128)(2,1)S(1)}, bf16[1168,256]{1,0:T(8,128)(2,1)}, u32[]{:S(2)}) copy-start(bf16[1168,256]{1,0:T(8,128)(2,1)} %constant.13.clone.tab_ref.refs_0_) | copy-start | bytes 1794052
  3.5 11.8 %copy-start.2 = (bf16[1,1,384,384]{3,2,1,0:T(8,128)(2,1)S(1)}, bf16[1,1,384,384]{3,2,1,0:T(8,128)(2,1)}, u32[]{:S(2)}) copy-start(bf16[1,1,384,384]{3,2,1,0:T(8,128)(2,1)} %param.10) | copy-start | bytes 884740
  3.5 11.8 %collective-permute-start = (bf16[400,384]{1,0:T(8,128)(2,1)}, bf16[400,384]{1,0:T(8,128)(2,1)S(1)}, u32[]{:S(2)}, u32[]{:S(2)}) collective-permute-start(bf16[400,384]{1,0:T(8,128)(2,1)} %get-tuple-element.21), channel_id=1, source_target_pairs={{0,2},{2,0},{1,3},{3,1},{4,6},{6,4},{5,7},{7,5},{8,10},{10,8},{9,1... | collective-permute-start | bytes 921608 | tf_op jit(solution)/shard_map/ppermute | solution.py:311
  7.1 23.8 %all-to-all-start = ((bf16[32,48,384]{2,1,0:T(8,128)(2,1)}), bf16[32,48,384]{2,1,0:T(8,128)(2,1)S(1)}, u32[]{:S(2)}, u32[]{:S(2)}) async-start(bf16[32,48,384]{2,1,0:T(8,128)(2,1)} %get-tuple-element.24), calls=%async_computation | async-start | bytes 2359296 | tf_op jit(solution)/shard_map/all_to_all | solution.py:312
  15.3 2.2 %copy-start.8 = (f32[64]{0:T(128)S(1)}, f32[64]{0:T(128)}, u32[]{:S(2)}) copy-start(f32[64]{0:T(128)} %param.16) | copy-start | bytes 772
  15.3 2.2 %copy-start.9 = (f32[64]{0:T(128)S(1)}, f32[64]{0:T(128)}, u32[]{:S(2)}) copy-start(f32[64]{0:T(128)} %param.15) | copy-start | bytes 772
  15.3 2.2 %copy-start.10 = (f32[64]{0:T(128)S(1)}, f32[64]{0:T(128)}, u32[]{:S(2)}) copy-start(f32[64]{0:T(128)} %param.14) | copy-start | bytes 772
  15.3 2.2 %copy-start.11 = (f32[64]{0:T(128)S(1)}, f32[64]{0:T(128)}, u32[]{:S(2)}) copy-start(f32[64]{0:T(128)} %param.13) | copy-start | bytes 772
  15.3 2.2 %copy-start.1 = (bf16[1184,256]{1,0:T(8,128)(2,1)S(1)}, bf16[1184,256]{1,0:T(8,128)(2,1)}, u32[]{:S(2)}) copy-start(bf16[1184,256]{1,0:T(8,128)(2,1)} %constant.14.clone.refs_1_.refs_0_.tab_ref) | copy-start | bytes 1818628
  15.3 2.2 %copy-start.3 = (bf16[192,400]{1,0:T(8,128)(2,1)S(1)}, bf16[192,400]{1,0:T(8,128)(2,1)}, u32[]{:S(2)}) copy-start(bf16[192,400]{1,0:T(8,128)(2,1)} %constant.15.clone.refs_2_.refs_1_.unfold_ref) | copy-start | bytes 460804
  16.2 4.7 %collective-permute-start.1 = (bf16[104,384]{1,0:T(8,128)(2,1)S(1)}, bf16[104,384]{1,0:T(8,128)(2,1)S(1)}, u32[]{:S(2)}, u32[]{:S(2)}) collective-permute-start(bf16[104,384]{1,0:T(8,128)(2,1)S(1)} %get-tuple-element.23), channel_id=1, source_target_pairs={{0,1},{1,0},{2,3},{3,2},{4,5},{5,4},{6,7},{7,6},{8,9},{9,8},{10,11... | collective-permute-start | bytes 239624 | tf_op jit(solution)/shard_map/ppermute | solution.py:330
  19.0 1.1 %copy-start.4 = (f32[2,2,200,384]{3,2,1,0:T(8,128)}, f32[2,2,200,384]{3,2,1,0:T(8,128)S(1)}, u32[]{:S(2)}) copy-start(f32[2,2,200,384]{3,2,1,0:T(8,128)S(1)} %get-tuple-element.29.spec_ref) | copy-start | bytes 3686404
  20.1 0.8 %copy-start.6 = (f32[2,200,384]{2,1,0:T(8,128)}, f32[2,200,384]{2,1,0:T(8,128)S(1)}, u32[]{:S(2)}) copy-start(f32[2,200,384]{2,1,0:T(8,128)S(1)} %get-tuple-element.30.weight_ref) | copy-start | bytes 1843204
  20.9 15.4 %collective-permute-start.4 = (bf16[104,384]{1,0:T(8,128)(2,1)S(1)}, bf16[104,384]{1,0:T(8,128)(2,1)S(1)}, u32[]{:S(2)}, u32[]{:S(2)}) collective-permute-start(bf16[104,384]{1,0:T(8,128)(2,1)S(1)} %add_convert_fusion.1), channel_id=1, source_target_pairs={{0,12},{4,0},{8,4},{12,8},{1,13},{5,1},{9,5},{13,9},{2,14},{6,2},{... | collective-permute-start | bytes 239624 | tf_op jit(solution)/shard_map/ppermute | solution.py:332
  24.1 12.3 %collective-permute-start.3 = (bf16[104,384]{1,0:T(8,128)(2,1)S(1)}, bf16[104,384]{1,0:T(8,128)(2,1)S(1)}, u32[]{:S(2)}, u32[]{:S(2)}) collective-permute-start(bf16[104,384]{1,0:T(8,128)(2,1)S(1)} %add_convert_fusion.1), channel_id=1, source_target_pairs={{0,8},{4,12},{8,0},{12,4},{1,9},{5,13},{9,1},{13,5},{2,10},{6,14},... | collective-permute-start | bytes 239624 | tf_op jit(solution)/shard_map/ppermute | solution.py:332
  24.3 12.1 %collective-permute-start.2 = (bf16[104,384]{1,0:T(8,128)(2,1)S(1)}, bf16[104,384]{1,0:T(8,128)(2,1)S(1)}, u32[]{:S(2)}, u32[]{:S(2)}) collective-permute-start(bf16[104,384]{1,0:T(8,128)(2,1)S(1)} %add_convert_fusion.1), channel_id=1, source_target_pairs={{0,4},{4,8},{8,12},{12,0},{1,5},{5,9},{9,13},{13,1},{2,6},{6,10},{... | collective-permute-start | bytes 239624 | tf_op jit(solution)/shard_map/ppermute | solution.py:332
  31.0 8.1 %copy-start.5 = (f32[2,2,200,384]{3,2,1,0:T(8,128)S(1)}, f32[2,2,200,384]{3,2,1,0:T(8,128)}, u32[]{:S(2)}) copy-start(f32[2,2,200,384]{3,2,1,0:T(8,128)} %copy-done.4) | copy-start | bytes 3686404
  31.0 8.1 %copy-start.7 = (f32[2,200,384]{2,1,0:T(8,128)S(1)}, f32[2,200,384]{2,1,0:T(8,128)}, u32[]{:S(2)}) copy-start(f32[2,200,384]{2,1,0:T(8,128)} %copy-done.6) | copy-start | bytes 1843204
  33.3 6.2 %collective-permute-start.5 = (bf16[4,2,200,384]{3,2,1,0:T(8,128)(2,1)S(1)}, bf16[4,2,200,384]{3,2,1,0:T(8,128)(2,1)S(1)}, u32[]{:S(2)}, u32[]{:S(2)}) collective-permute-start(bf16[4,2,200,384]{3,2,1,0:T(8,128)(2,1)S(1)} %library.1.near_ref), channel_id=1, source_target_pairs={{0,1},{1,0},{2,3},{3,2},{4,5},{5,4},{6,7},{7,6},{8,9},{9,8},{10,11... | collective-permute-start | bytes 3686408 | tf_op jit(solution)/shard_map/ppermute | solution.py:373
  36.5 2.6 %collective-permute-start.6 = (bf16[104,384]{1,0:T(8,128)(2,1)S(1)}, bf16[104,384]{1,0:T(8,128)(2,1)S(1)}, u32[]{:S(2)}, u32[]{:S(2)}) collective-permute-start(bf16[104,384]{1,0:T(8,128)(2,1)S(1)} %add_convert_fusion.mine_ref), channel_id=1, source_target_pairs={{0,1},{1,0},{2,3},{3,2},{4,5},{5,4},{6,7},{7,6},{8,9},{9,8},{10,11... | collective-permute-start | bytes 239624 | tf_op jit(solution)/shard_map/ppermute | solution.py:376
  43.7 9.8 %collective-permute-start.7 = (bf16[384,384]{1,0:T(8,128)(2,1)S(1)}, bf16[384,384]{1,0:T(8,128)(2,1)S(1)}, u32[]{:S(2)}, u32[]{:S(2)}) collective-permute-start(bf16[384,384]{1,0:T(8,128)(2,1)S(1)} %match_other.1), channel_id=1, source_target_pairs={{0,2},{2,0},{1,3},{3,1},{4,6},{6,4},{5,7},{7,5},{8,10},{10,8},{9,1... | collective-permute-start | bytes 884744 | tf_op jit(solution)/shard_map/ppermute | solution.py:413

commit v10 on v9

--- a/solution.py
+++ b/solution.py
@@ -18,7 +18,6 @@
 THIRD = N // 3
 BLOCKS = (64, 64, 72)
 ROWS = sum(BLOCKS)
-MARK = 16
 SPLIT = 96
 PART = ROWS - SPLIT
 FOLD = 208
@@ -82,7 +81,10 @@
     return jnp.where((u > 0) & (u < HALF), 2.0, jnp.where(u <= HALF, 1.0, 0.0))
 
 
-def copy_kernel(row_ref, tile_ref, block_ref, out_ref, sent_ref, wide_sc, sems):
+def copy_kernel(block_in, out_ref, block_ref, wide_sc, sem, sems):
+    fetch = pltpu.make_async_copy(block_in, block_ref, sem)
+    fetch.start()
+    fetch.wait()
     count = wide_sc.shape[0]
     wide_sc[...] = jnp.broadcast_to(block_ref[...][None], wide_sc.shape)
     moves = [
@@ -91,8 +93,6 @@
     ]
     for move in moves:
         move.start()
-    sent_ref[:N] = tile_ref[...]
-    sent_ref[N:] = jnp.broadcast_to(row_ref[...].astype(F32), (MARK, N)).astype(BF16)
     for move in moves:
         move.wait()
 
@@ -173,7 +173,7 @@
 
 def tile_kernel(core_ref, own_ref, other_ref, tab_ref, spec_ref, keep_ref, send_ref, power_sc):
     for t, ref in enumerate((own_ref, other_ref)):
-        parts = half_spectrum(ref[:N], tab_ref)
+        parts = half_spectrum(ref[...], tab_ref)
         store_spectrum(spec_ref.at[t], parts)
         for k, (re, im) in enumerate(parts):
             at = slice(k * THIRD, (k + 1) * THIRD)
@@ -185,12 +185,11 @@
     send_ref[...] = jnp.where(first, high, low).astype(BF16)
 
 
-def gain_kernel(row_ref, mark_ref, table_ref, tile_ref, *refs):
+def gain_kernel(row_ref, table_ref, tile_ref, *refs):
     spec_ref, weight_ref = refs[-2:]
-    for t, row in enumerate((row_ref[...], mark_ref[0:1, 0:1])):
-        gain, weight_ref[t] = ctf_factors(row.astype(F32), table_ref[...])
-        spec_ref[t, 0] = tile_ref[t, 0] * gain
-        spec_ref[t, 1] = tile_ref[t, 1] * gain
+    gain, weight_ref[...] = ctf_factors(row_ref[...].astype(F32), table_ref[...])
+    spec_ref[0] = tile_ref[0] * gain
+    spec_ref[1] = tile_ref[1] * gain
 
 
 def library_kernel(image_ref, tab_ref, out_ref):
@@ -224,7 +223,9 @@
     return even - odd, even + odd
 
 
-def whiten_kernel(core_ref, spec_ref, weight_ref, mine_ref, theirs_ref, *refs):
+def whiten_kernel(
+    core_ref, own_ref, own_weight_ref, spec_ref, weight_ref, mine_ref, theirs_ref, *refs
+):
     spec_out, weight_out = refs[-2:]
     mine, theirs = mine_ref[...].astype(F32), theirs_ref[...].astype(F32)
     first = core_ref[...] == 0
@@ -233,10 +234,10 @@
     u, _ = row_numbers()
     mean = jnp.sum(power * row_scale(u)) * (1.0 / (N * N))
     inverse_noise = 1.0 / (jnp.where(u <= HALF, power, 1.0) + 0.05 * mean)
-    for t in range(2):
-        spec_out[t, 0] = spec_ref[t, 0] * inverse_noise
-        spec_out[t, 1] = spec_ref[t, 1] * inverse_noise
-        weight_out[t] = weight_ref[t] * inverse_noise
+    for t, (spec, weight) in enumerate(((own_ref, own_weight_ref), (spec_ref, weight_ref))):
+        spec_out[t, 0] = spec[0] * inverse_noise
+        spec_out[t, 1] = spec[1] * inverse_noise
+        weight_out[t] = weight[...] * inverse_noise
 
 
 def match_kernel(near_ref, far_ref, spec_ref, weight_ref, tab_ref, unfold_ref, out_ref, best_sc):
@@ -292,23 +293,21 @@
 
     tile = images[0, 0]
     block = projections[0]
-    copies, sent = pl.pallas_call(
+    received = lax.ppermute(tile, "xhi", swap)
+    copies = pl.pallas_call(
         copy_kernel,
-        out_shape=[
-            pltpu.HBM((places,) + block.shape, BF16),
-            jax.ShapeDtypeStruct((N + MARK, N), BF16),
-        ],
-        grid=(1,),
-        in_specs=[full(1, 1), full(N, N), full(*block.shape)],
-        out_specs=[pl.BlockSpec(memory_space=pltpu.HBM), full(N + MARK, N)],
+        out_shape=pltpu.HBM((places,) + block.shape, BF16),
+        in_specs=[pl.BlockSpec(memory_space=pltpu.HBM)],
+        out_specs=pl.BlockSpec(memory_space=pltpu.HBM),
         scratch_shapes=[
+            pltpu.VMEM(block.shape, BF16),
             pltpu.VMEM((groups,) + block.shape, BF16),
+            pltpu.SemaphoreType.DMA,
             pltpu.SemaphoreType.DMA((places // groups,)),
         ],
         cost_estimate=cost(0, 1 << 20),
         name="copies",
-    )(ctf_row, tile, block)
-    received = lax.ppermute(sent, "xhi", swap)
+    )(block)
     images_all = lax.all_to_all(copies, LIB, 0, 0, tiled=False)
 
     tiles, keep, send = pl.pallas_call(
@@ -319,7 +318,7 @@
             jax.ShapeDtypeStruct((PART, N), BF16),
         ],
         grid=(1,),
-        in_specs=[full(1, 1), full(N, N), full(N + MARK, N), full(*ahead.shape)],
+        in_specs=[full(1, 1), full(N, N), full(N, N), full(*ahead.shape)],
         out_specs=[full(2, *plane), full(PART, N), full(PART, N)],
         scratch_shapes=[pltpu.VMEM((ROWS, N), F32)],
         compiler_params=params(12),
@@ -335,27 +334,31 @@
 
     table = jnp.stack([defocus_term, astig_term, astig_cross, phase_shift])
     table = jnp.pad(table, ((0, 4), (0, 128 - table.shape[1])))
-    spec, weight = pl.pallas_call(
-        gain_kernel,
-        out_shape=[
-            jax.ShapeDtypeStruct((2,) + plane, F32),
-            jax.ShapeDtypeStruct((2, ROWS, N), F32),
-        ],
-        grid=(1,),
-        in_specs=[
-            full(1, 1),
-            pl.BlockSpec((MARK, N), lambda i: (N // MARK, 0)),
-            full(*table.shape),
-            full(2, *plane),
-        ]
-        + kept * 3,
-        out_specs=[full(2, *plane), full(2, ROWS, N)],
-        compiler_params=params(12),
-        cost_estimate=cost(2 * ROWS * N * 60, 4 << 20),
-        name="gain",
-    )(ctf_row, received, table, tiles, ahead, back, unfold)
-
-    images_all, pair, spec = lax.optimization_barrier((images_all, pair, spec))
+    row, _ = lax.optimization_barrier((ctf_row, pair))
+    mate = lax.ppermute(row, "xhi", swap)
+
+    def gain(t, row, tables, name):
+        return pl.pallas_call(
+            gain_kernel,
+            out_shape=[
+                jax.ShapeDtypeStruct(plane, F32),
+                jax.ShapeDtypeStruct((ROWS, N), F32),
+            ],
+            grid=(1,),
+            in_specs=[
+                full(1, 1),
+                full(*table.shape),
+                pl.BlockSpec((None,) + plane, lambda i: (t, 0, 0, 0)),
+            ]
+            + kept * len(tables),
+            out_specs=[full(*plane), full(ROWS, N)],
+            compiler_params=params(12),
+            cost_estimate=cost(8 * work, 3 << 20),
+            name=name,
+        )(row, table, tiles, *tables)
+
+    own = gain(0, ctf_row, (ahead, back, unfold), "gain_own")
+    images_all, pair, own = lax.optimization_barrier((images_all, pair, own))
 
     near_all = pl.pallas_call(
         library_kernel,
@@ -371,7 +374,8 @@
         name="library",
     )(images_all.reshape(groups, deep, N // groups, N), ahead)
     far_all = lax.ppermute(near_all, "core", swap)
-    moves, near_all = lax.optimization_barrier((moves, near_all))
+    moves, near_all, mate = lax.optimization_barrier((moves, near_all, mate))
+    other = gain(1, mate, (), "gain_other")
     mine = sum((m.astype(F32) for m in moves), pair.astype(F32)).astype(BF16)
     theirs = lax.ppermute(mine, "core", swap)
     white, white_weight = pl.pallas_call(
@@ -381,13 +385,15 @@
             jax.ShapeDtypeStruct((2, ROWS, N), F32),
         ],
         grid=(1,),
-        in_specs=[full(1, 1), full(2, *plane), full(2, ROWS, N), full(PART, N), full(PART, N)]
+        in_specs=[full(1, 1)]
+        + [full(*plane), full(ROWS, N)] * 2
+        + [full(PART, N)] * 2
         + kept * 2,
         out_specs=[full(2, *plane), full(2, ROWS, N)],
         compiler_params=params(12),
         cost_estimate=cost(60 * work, 4 << 20),
         name="whiten",
-    )(core, spec, weight, mine, theirs, back, unfold)
+    )(core, *own, *other, mine, theirs, back, unfold)
 
     def match(t, dtype, name):
         lib_spec = pl.BlockSpec((2,) + plane, lambda i: (i, 0, 0, 0))

time: 54.6 us -> 53.2 us (0.974)
  starting transfers between devices: 22.4 us -> 24.2 us
  waiting for transfers between devices: 11.9 us -> 10.1 us
  local copies, waits for them, and re-layouts: 1.94 us -> 0.88 us
  Pallas kernels: 16.4 us -> 15.8 us
    ppermute x1 -> x2, starting transfers between devices: 3.65 us -> 5.3 us  [the longest x1 3.57 us: per_device(): received = lax.ppermute(tile, 'xhi', swap)]
    all_to_all x1, waiting for transfers between devices: 6.04 us -> 4.51 us  [per_device(): images_all = lax.all_to_all(copies, LIB, 0, 0, tiled=False)]
    ppermute x1, waiting for transfers between devices: 2.08 us -> 0.9 us  [per_device(): theirs = lax.ppermute(mine, 'core', swap)]
    unnamed x24, local copies, waits for them, and re-layouts: 1.94 us -> 0.88 us
    ppermute x1, waiting for transfers between devices: 0.01 us -> 0.89 us  [per_device(): lax.ppermute(send, 'core', swap).astype(F32)]
    pallas_call x2 -> x3, Pallas kernels: 4.26 us -> 4.05 us  [the longest x2 2.2 us: gain(): pl.pallas_call(gain_kernel, out_shape=[jax.ShapeDtypeStruct(plane, F32),...]
  transfers between devices with their start and end apart: 9 -> 10, of which waited for: 3 -> 4; matrix products, arithmetic and copies ran while one was open for 0% -> 0% of each run, Pallas kernels for 17% -> 22%
where the time goes in v10:
time: 53.2 us; the launch traced here: 52.9 us
  starting transfers between devices  24.2 us (45%)
  Pallas kernels  15.8 us (30%)
  waiting for transfers between devices  10.1 us (19%)
  other arithmetic  0.95 us (2%)
  local copies, waits for them, and re-layouts  0.88 us (2%)
  between operations  0.88 us (2%)
    all_to_all x1, starting transfers between devices, per_device(): images_all = lax.all_to_all(copies, LIB, 0, 0, tiled=False)  8.22 us
    pallas_call x2, Pallas kernels, match(): pl.pallas_call(match_kernel, out_shape=jax.ShapeDtypeStruct((N, N), dtype...  8.11 us
    all_to_all x1, waiting for transfers between devices, per_device(): images_all = lax.all_to_all(copies, LIB, 0, 0, tiled=False)  4.51 us
    ppermute x3, starting transfers between devices, per_device(): lax.ppermute(pair, 'z', [(z, (z + dz) % deep) for z in range(deep)])  3.94 us
    ppermute x1, waiting for transfers between devices, per_device(): got = lax.ppermute(match(1, BF16, 'match_other'), 'xhi', swap)  3.82 us
    ppermute x1, starting transfers between devices, per_device(): received = lax.ppermute(tile, 'xhi', swap)  3.57 us
    ppermute x1, starting transfers between devices, per_device(): far_all = lax.ppermute(near_all, 'core', swap)  3.29 us
    pallas_call x1, Pallas kernels, per_device(): pl.pallas_call(library_kernel, out_shape=jax.ShapeDtypeStruct((deep,) + p...  2.34 us
  transfers between devices with their start and end apart: 10, of which 4 were waited for; matrix products, arithmetic and copies ran while one was open for 0% of the time, Pallas kernels for 22%

profile of v10, /device:TPU:1, one launch (start us, length us, event | category | flops | bytes accessed | tf_op | source)
XLA Modules:
  0.0 52.9 jit_solution(4574655405315867577)
XLA Ops:
  0.0 3.6 %collective-permute-start = (bf16[384,384]{1,0:T(8,128)(2,1)}, bf16[384,384]{1,0:T(8,128)(2,1)S(1)}, u32[]{:S(2)}, u32[]{:S(2)}) collective-permute-start(bf16[384,384]{1,0:T(8,128)(2,1)} %bitcast.11), channel_id=1, source_target_pairs={{0,2},{2,0},{1,3},{3,1},{4,6},{6,4},{5,7},{7,5},{8,10},{10,8},{9,1... | collective-permute-start | bytes 884744 | tf_op jit(solution)/shard_map/ppermute | solution.py:296
  3.6 1.9 %copies.1 = bf16[32,48,384]{2,1,0:T(8,128)(2,1)} custom-call(bf16[48,384]{1,0:T(8,128)(2,1)} %bitcast.13), custom_call_target="tpu_custom_call" | custom-call | bytes 1048576 | tf_op jit(solution)/shard_map/copies/pallas_call | solution.py:297
  5.4 0.0 copy-start
  5.4 0.0 copy-start.1
  5.5 8.2 %all-to-all-start = ((bf16[32,48,384]{2,1,0:T(8,128)(2,1)}), bf16[32,48,384]{2,1,0:T(8,128)(2,1)S(1)}, u32[]{:S(2)}, u32[]{:S(2)}) async-start(bf16[32,48,384]{2,1,0:T(8,128)(2,1)} %copies.1), calls=%async_computation | async-start | bytes 2359296 | tf_op jit(solution)/shard_map/all_to_all | solution.py:311
  14.3 0.0 collective-permute-done.other_ref
  14.4 0.0 copy-done
  14.4 0.0 copy-done.1
  14.4 0.0 copy-start.8
  14.4 0.0 copy-start.9
  14.4 0.0 copy-start.10
  14.4 0.0 copy-start.11
  14.4 0.0 copy-start.2
  14.4 0.0 copy-start.3
  14.4 0.8 %tile.1 = (f32[2,2,200,384]{3,2,1,0:T(8,128)S(1)}, bf16[104,384]{1,0:T(8,128)(2,1)S(1)}, bf16[104,384]{1,0:T(8,128)(2,1)S(1)}) custom-call(s32[1,1]{1,0:T(1,128)} %bitcast.core_ref, bf16[384,384]{1,0:T(8,128)(2,1)S(1)} %bitcast.12, bf16[384,384]{1,0:T(8,128)(2,1)S(1)} %collective-permute-done.other_ref, bf16[1168,256]{1,0:T(8,128)(2,1)S(1)} %copy-done), custom_call_target="tpu_custom_call" | custom-call | flops 31457280000 | bytes 3145728 | tf_op jit(solution)/shard_map/tile/pallas_call | solution.py:313
  15.3 0.0 copy-start.4
  15.3 1.3 %collective-permute-start.1 = (bf16[104,384]{1,0:T(8,128)(2,1)S(1)}, bf16[104,384]{1,0:T(8,128)(2,1)S(1)}, u32[]{:S(2)}, u32[]{:S(2)}) collective-permute-start(bf16[104,384]{1,0:T(8,128)(2,1)S(1)} %get-tuple-element.25), channel_id=1, source_target_pairs={{0,1},{1,0},{2,3},{3,2},{4,5},{5,4},{6,7},{7,6},{8,9},{9,8},{10,11... | collective-permute-start | bytes 239624 | tf_op jit(solution)/shard_map/ppermute | solution.py:329
  16.6 0.0 copy-done.8
  16.6 0.0 copy-done.9
  16.6 0.0 copy-done.10
  16.6 0.0 copy-done.11
  16.7 0.9 %collective-permute-done.1 = bf16[104,384]{1,0:T(8,128)(2,1)S(1)} collective-permute-done((bf16[104,384]{1,0:T(8,128)(2,1)S(1)}, bf16[104,384]{1,0:T(8,128)(2,1)S(1)}, u32[]{:S(2)}, u32[]{:S(2)}) %collective-permute-start.1) | collective-permute-done | bytes 79904 | tf_op jit(solution)/shard_map/ppermute | solution.py:329
  17.6 2.8 %collective-permute-start.4 = (bf16[104,384]{1,0:T(8,128)(2,1)S(1)}, bf16[104,384]{1,0:T(8,128)(2,1)S(1)}, u32[]{:S(2)}, u32[]{:S(2)}) collective-permute-start(bf16[104,384]{1,0:T(8,128)(2,1)S(1)} %add_convert_fusion.1), channel_id=1, source_target_pairs={{0,12},{4,0},{8,4},{12,8},{1,13},{5,1},{9,5},{13,9},{2,14},{6,2},{... | collective-permute-start | bytes 239624 | tf_op jit(solution)/shard_map/ppermute | solution.py:331
  20.4 0.6 %collective-permute-start.3 = (bf16[104,384]{1,0:T(8,128)(2,1)S(1)}, bf16[104,384]{1,0:T(8,128)(2,1)S(1)}, u32[]{:S(2)}, u32[]{:S(2)}) collective-permute-start(bf16[104,384]{1,0:T(8,128)(2,1)S(1)} %add_convert_fusion.1), channel_id=1, source_target_pairs={{0,8},{4,12},{8,0},{12,4},{1,9},{5,13},{9,1},{13,5},{2,10},{6,14},... | collective-permute-start | bytes 239624 | tf_op jit(solution)/shard_map/ppermute | solution.py:331
  20.9 0.6 %collective-permute-start.2 = (bf16[104,384]{1,0:T(8,128)(2,1)S(1)}, bf16[104,384]{1,0:T(8,128)(2,1)S(1)}, u32[]{:S(2)}, u32[]{:S(2)}) collective-permute-start(bf16[104,384]{1,0:T(8,128)(2,1)S(1)} %add_convert_fusion.1), channel_id=1, source_target_pairs={{0,4},{4,8},{8,12},{12,0},{1,5},{5,9},{9,13},{13,1},{2,6},{6,10},{... | collective-permute-start | bytes 239624 | tf_op jit(solution)/shard_map/ppermute | solution.py:331
  21.5 0.0 copy-done.2
  21.5 0.0 copy-done.3
  21.5 0.8 %gain_own.1 = (f32[2,200,384]{2,1,0:T(8,128)S(1)}, f32[200,384]{1,0:T(8,128)S(1)}) custom-call(s32[1,1]{1,0:T(1,128)S(6)} %copy.11.row_ref, f32[8,128]{1,0:T(8,128)S(1)} %select_maximum_fusion.table_ref, f32[2,2,200,384]{3,2,1,0:T(8,128)S(1)} %get-tuple-element.26.tile_ref, bf16[1168,256]{1,0:T(8,128)(2,1)S(1)} %copy-done, bf16[1184,256]{1,0:T(8,128)(2,1)S(1)} %copy-done.2, ...), custom_call_target="tpu_custom_call" | custom-call | flops 1258291200 | bytes 3145728 | tf_op jit(solution)/shard_map/gain_own/pallas_call | solution.py:341
  22.4 0.0 copy-done.4
  22.4 0.0 copy-start.6
  22.4 0.8 %copy-done.6 = f32[2,200,384]{2,1,0:T(8,128)} copy-done((f32[2,200,384]{2,1,0:T(8,128)}, f32[2,200,384]{2,1,0:T(8,128)S(1)}, u32[]{:S(2)}) %copy-start.6) | copy-done | bytes 614424
  23.2 1.7 %collective-permute-start.5 = (s32[1,1]{1,0:T(1,128)}, s32[1,1]{1,0:T(1,128)}, u32[]{:S(2)}, u32[]{:S(2)}) collective-permute-start(s32[1,1]{1,0:T(1,128)} %param.12), channel_id=1, source_target_pairs={{0,2},{2,0},{1,3},{3,1},{4,6},{6,4},{5,7},{7,5},{8,10},{10,8},{9,1... | collective-permute-start | bytes 20 | tf_op jit(solution)/shard_map/ppermute | solution.py:338
  24.9 4.5 %all-to-all-done = bf16[32,48,384]{2,1,0:T(8,128)(2,1)S(1)} async-done(((bf16[32,48,384]{2,1,0:T(8,128)(2,1)}), bf16[32,48,384]{2,1,0:T(8,128)(2,1)S(1)}, u32[]{:S(2)}, u32[]{:S(2)}) %all-to-all-start) | async-done | bytes 1179680 | tf_op jit(solution)/shard_map/all_to_all | solution.py:311
  29.4 0.0 copy-start.5
  29.4 2.3 %library.1.near_ref = bf16[4,2,200,384]{3,2,1,0:T(8,128)(2,1)S(1)} custom-call(bf16[8,4,48,384]{3,2,1,0:T(8,128)(2,1)S(1)} %bitcast.10, bf16[1168,256]{1,0:T(8,128)(2,1)S(1)} %copy-done), custom_call_target="tpu_custom_call" | custom-call | flops 629145600 | bytes 4194304 | tf_op jit(solution)/shard_map/library/pallas_call | solution.py:363
  31.8 3.3 %collective-permute-start.6 = (bf16[4,2,200,384]{3,2,1,0:T(8,128)(2,1)S(1)}, bf16[4,2,200,384]{3,2,1,0:T(8,128)(2,1)S(1)}, u32[]{:S(2)}, u32[]{:S(2)}) collective-permute-start(bf16[4,2,200,384]{3,2,1,0:T(8,128)(2,1)S(1)} %library.1.near_ref), channel_id=1, source_target_pairs={{0,1},{1,0},{2,3},{3,2},{4,5},{5,4},{6,7},{7,6},{8,9},{9,8},{10,11... | collective-permute-start | bytes 3686408 | tf_op jit(solution)/shard_map/ppermute | solution.py:376
  35.1 0.0 collective-permute-done.5.row_ref
  35.1 0.0 collective-permute-done.4
  35.1 0.0 collective-permute-done.3
  35.1 0.0 collective-permute-done.2
  35.1 0.0 copy-start.7
  35.2 0.3 collective-permute-start.7
  35.4 0.0 copy-done.5
  35.4 1.4 %gain_other.1 = (f32[2,200,384]{2,1,0:T(8,128)S(1)}, f32[200,384]{1,0:T(8,128)S(1)}) custom-call(s32[1,1]{1,0:T(1,128)} %collective-permute-done.5.row_ref, f32[8,128]{1,0:T(8,128)S(1)} %select_maximum_fusion.table_ref, f32[2,2,200,384]{3,2,1,0:T(8,128)S(1)} %copy-done.5), custom_call_target="tpu_custom_call" | custom-call | flops 1258291200 | bytes 3145728 | tf_op jit(solution)/shard_map/gain_other/pallas_call | solution.py:341
  36.8 0.9 %collective-permute-done.7.theirs_ref = bf16[104,384]{1,0:T(8,128)(2,1)S(1)} collective-permute-done((bf16[104,384]{1,0:T(8,128)(2,1)S(1)}, bf16[104,384]{1,0:T(8,128)(2,1)S(1)}, u32[]{:S(2)}, u32[]{:S(2)}) %collective-permute-start.7) | collective-permute-done | bytes 79904 | tf_op jit(solution)/shard_map/ppermute | solution.py:380
  37.7 0.0 copy-done.7
  37.7 0.5 whiten.1
  38.2 0.0 collective-permute-done.6.far_ref
  38.2 3.9 %match_other.1 = bf16[384,384]{1,0:T(8,128)(2,1)S(1)} custom-call(bf16[4,2,200,384]{3,2,1,0:T(8,128)(2,1)S(1)} %library.1.near_ref, bf16[4,2,200,384]{3,2,1,0:T(8,128)(2,1)S(1)} %collective-permute-done.6.far_ref, f32[2,2,200,384]{3,2,1,0:T(8,128)S(1)} %get-tuple-element.41.spec_ref, f32[2,200,384]{2,1,0:T(8,128)S(1)} %get-tuple-element.42.weight_ref, ...), custom_call_target="tpu_custom_call" | custom-call | flops 2516582400 | bytes 6291456 | tf_op jit(solution)/shard_map/match_other/pallas_call | solution.py:400
  42.2 1.8 %collective-permute-start.8 = (bf16[384,384]{1,0:T(8,128)(2,1)S(1)}, bf16[384,384]{1,0:T(8,128)(2,1)S(1)}, u32[]{:S(2)}, u32[]{:S(2)}) collective-permute-start(bf16[384,384]{1,0:T(8,128)(2,1)S(1)} %match_other.1), channel_id=1, source_target_pairs={{0,2},{2,0},{1,3},{3,1},{4,6},{6,4},{5,7},{7,5},{8,10},{10,8},{9,1... | collective-permute-start | bytes 884744 | tf_op jit(solution)/shard_map/ppermute | solution.py:419
  44.0 4.2 %match_own.1 = f32[384,384]{1,0:T(8,128)S(1)} custom-call(bf16[4,2,200,384]{3,2,1,0:T(8,128)(2,1)S(1)} %library.1.near_ref, bf16[4,2,200,384]{3,2,1,0:T(8,128)(2,1)S(1)} %collective-permute-done.6.far_ref, f32[2,2,200,384]{3,2,1,0:T(8,128)S(1)} %get-tuple-element.41.spec_ref, f32[2,200,384]{2,1,0:T(8,128)S(1)} %get-tuple-element.42.weight_ref, ...), custom_call_target="tpu_custom_call" | custom-call | flops 2516582400 | bytes 6291456 | tf_op jit(solution)/shard_map/match_own/pallas_call | solution.py:400
  48.2 3.8 %collective-permute-done.8 = bf16[384,384]{1,0:T(8,128)(2,1)S(1)} collective-permute-done((bf16[384,384]{1,0:T(8,128)(2,1)S(1)}, bf16[384,384]{1,0:T(8,128)(2,1)S(1)}, u32[]{:S(2)}, u32[]{:S(2)}) %collective-permute-start.8) | collective-permute-done | bytes 294944 | tf_op jit(solution)/shard_map/ppermute | solution.py:419
  52.0 0.9 %maximum_bitcast_fusion = f32[1,1,384,384]{3,2,1,0:T(8,128)} fusion(f32[384,384]{1,0:T(8,128)S(1)} %match_own.1, bf16[384,384]{1,0:T(8,128)(2,1)S(1)} %collective-permute-done.8), kind=kLoop, calls=%fused_computation | loop fusion | flops 294912 | bytes 1474560 | tf_op jit(solution)/shard_map/broadcast_in_dim | solution.py:421
  (3 shorter events, 0.1 us)
Async XLA Ops:
  0.0 14.3 %collective-permute-start = (bf16[384,384]{1,0:T(8,128)(2,1)}, bf16[384,384]{1,0:T(8,128)(2,1)S(1)}, u32[]{:S(2)}, u32[]{:S(2)}) collective-permute-start(bf16[384,384]{1,0:T(8,128)(2,1)} %bitcast.11), channel_id=1, source_target_pairs={{0,2},{2,0},{1,3},{3,1},{4,6},{6,4},{5,7},{7,5},{8,10},{10,8},{9,1... | collective-permute-start | bytes 884744 | tf_op jit(solution)/shard_map/ppermute | solution.py:296
  5.4 8.9 %copy-start = (bf16[1168,256]{1,0:T(8,128)(2,1)S(1)}, bf16[1168,256]{1,0:T(8,128)(2,1)}, u32[]{:S(2)}) copy-start(bf16[1168,256]{1,0:T(8,128)(2,1)} %constant.13.clone.tab_ref.refs_0_) | copy-start | bytes 1794052
  5.4 8.9 %copy-start.1 = (bf16[1,1,384,384]{3,2,1,0:T(8,128)(2,1)S(1)}, bf16[1,1,384,384]{3,2,1,0:T(8,128)(2,1)}, u32[]{:S(2)}) copy-start(bf16[1,1,384,384]{3,2,1,0:T(8,128)(2,1)} %param.10) | copy-start | bytes 884740
  5.5 24.0 %all-to-all-start = ((bf16[32,48,384]{2,1,0:T(8,128)(2,1)}), bf16[32,48,384]{2,1,0:T(8,128)(2,1)S(1)}, u32[]{:S(2)}, u32[]{:S(2)}) async-start(bf16[32,48,384]{2,1,0:T(8,128)(2,1)} %copies.1), calls=%async_computation | async-start | bytes 2359296 | tf_op jit(solution)/shard_map/all_to_all | solution.py:311
  14.4 2.3 %copy-start.8 = (f32[64]{0:T(128)S(1)}, f32[64]{0:T(128)}, u32[]{:S(2)}) copy-start(f32[64]{0:T(128)} %param.16) | copy-start | bytes 772
  14.4 2.3 %copy-start.9 = (f32[64]{0:T(128)S(1)}, f32[64]{0:T(128)}, u32[]{:S(2)}) copy-start(f32[64]{0:T(128)} %param.15) | copy-start | bytes 772
  14.4 2.2 %copy-start.10 = (f32[64]{0:T(128)S(1)}, f32[64]{0:T(128)}, u32[]{:S(2)}) copy-start(f32[64]{0:T(128)} %param.14) | copy-start | bytes 772
  14.4 2.2 %copy-start.11 = (f32[64]{0:T(128)S(1)}, f32[64]{0:T(128)}, u32[]{:S(2)}) copy-start(f32[64]{0:T(128)} %param.13) | copy-start | bytes 772
  14.4 7.1 %copy-start.2 = (bf16[1184,256]{1,0:T(8,128)(2,1)S(1)}, bf16[1184,256]{1,0:T(8,128)(2,1)}, u32[]{:S(2)}) copy-start(bf16[1184,256]{1,0:T(8,128)(2,1)} %constant.14.clone.refs_1_.refs_0_.tab_ref) | copy-start | bytes 1818628
  14.4 7.1 %copy-start.3 = (bf16[192,400]{1,0:T(8,128)(2,1)S(1)}, bf16[192,400]{1,0:T(8,128)(2,1)}, u32[]{:S(2)}) copy-start(bf16[192,400]{1,0:T(8,128)(2,1)} %constant.15.clone.refs_2_.refs_1_.unfold_ref) | copy-start | bytes 460804
  15.3 7.1 %copy-start.4 = (f32[2,2,200,384]{3,2,1,0:T(8,128)}, f32[2,2,200,384]{3,2,1,0:T(8,128)S(1)}, u32[]{:S(2)}) copy-start(f32[2,2,200,384]{3,2,1,0:T(8,128)S(1)} %get-tuple-element.26.tile_ref) | copy-start | bytes 3686404
  15.3 2.2 %collective-permute-start.1 = (bf16[104,384]{1,0:T(8,128)(2,1)S(1)}, bf16[104,384]{1,0:T(8,128)(2,1)S(1)}, u32[]{:S(2)}, u32[]{:S(2)}) collective-permute-start(bf16[104,384]{1,0:T(8,128)(2,1)S(1)} %get-tuple-element.25), channel_id=1, source_target_pairs={{0,1},{1,0},{2,3},{3,2},{4,5},{5,4},{6,7},{7,6},{8,9},{9,8},{10,11... | collective-permute-start | bytes 239624 | tf_op jit(solution)/shard_map/ppermute | solution.py:329
  17.6 17.5 %collective-permute-start.4 = (bf16[104,384]{1,0:T(8,128)(2,1)S(1)}, bf16[104,384]{1,0:T(8,128)(2,1)S(1)}, u32[]{:S(2)}, u32[]{:S(2)}) collective-permute-start(bf16[104,384]{1,0:T(8,128)(2,1)S(1)} %add_convert_fusion.1), channel_id=1, source_target_pairs={{0,12},{4,0},{8,4},{12,8},{1,13},{5,1},{9,5},{13,9},{2,14},{6,2},{... | collective-permute-start | bytes 239624 | tf_op jit(solution)/shard_map/ppermute | solution.py:331
  20.4 14.7 %collective-permute-start.3 = (bf16[104,384]{1,0:T(8,128)(2,1)S(1)}, bf16[104,384]{1,0:T(8,128)(2,1)S(1)}, u32[]{:S(2)}, u32[]{:S(2)}) collective-permute-start(bf16[104,384]{1,0:T(8,128)(2,1)S(1)} %add_convert_fusion.1), channel_id=1, source_target_pairs={{0,8},{4,12},{8,0},{12,4},{1,9},{5,13},{9,1},{13,5},{2,10},{6,14},... | collective-permute-start | bytes 239624 | tf_op jit(solution)/shard_map/ppermute | solution.py:331
  20.9 14.1 %collective-permute-start.2 = (bf16[104,384]{1,0:T(8,128)(2,1)S(1)}, bf16[104,384]{1,0:T(8,128)(2,1)S(1)}, u32[]{:S(2)}, u32[]{:S(2)}) collective-permute-start(bf16[104,384]{1,0:T(8,128)(2,1)S(1)} %add_convert_fusion.1), channel_id=1, source_target_pairs={{0,4},{4,8},{8,12},{12,0},{1,5},{5,9},{9,13},{13,1},{2,6},{6,10},{... | collective-permute-start | bytes 239624 | tf_op jit(solution)/shard_map/ppermute | solution.py:331
  22.4 0.8 %copy-start.6 = (f32[2,200,384]{2,1,0:T(8,128)}, f32[2,200,384]{2,1,0:T(8,128)S(1)}, u32[]{:S(2)}) copy-start(f32[2,200,384]{2,1,0:T(8,128)S(1)} %get-tuple-element.32.own_ref) | copy-start | bytes 1843204
  23.2 11.9 %collective-permute-start.5 = (s32[1,1]{1,0:T(1,128)}, s32[1,1]{1,0:T(1,128)}, u32[]{:S(2)}, u32[]{:S(2)}) collective-permute-start(s32[1,1]{1,0:T(1,128)} %param.12), channel_id=1, source_target_pairs={{0,2},{2,0},{1,3},{3,1},{4,6},{6,4},{5,7},{7,5},{8,10},{10,8},{9,1... | collective-permute-start | bytes 20 | tf_op jit(solution)/shard_map/ppermute | solution.py:338
  29.4 6.0 %copy-start.5 = (f32[2,2,200,384]{3,2,1,0:T(8,128)S(1)}, f32[2,2,200,384]{3,2,1,0:T(8,128)}, u32[]{:S(2)}) copy-start(f32[2,2,200,384]{3,2,1,0:T(8,128)} %copy-done.4) | copy-start | bytes 3686404
  31.8 6.5 %collective-permute-start.6 = (bf16[4,2,200,384]{3,2,1,0:T(8,128)(2,1)S(1)}, bf16[4,2,200,384]{3,2,1,0:T(8,128)(2,1)S(1)}, u32[]{:S(2)}, u32[]{:S(2)}) collective-permute-start(bf16[4,2,200,384]{3,2,1,0:T(8,128)(2,1)S(1)} %library.1.near_ref), channel_id=1, source_target_pairs={{0,1},{1,0},{2,3},{3,2},{4,5},{5,4},{6,7},{7,6},{8,9},{9,8},{10,11... | collective-permute-start | bytes 3686408 | tf_op jit(solution)/shard_map/ppermute | solution.py:376
  35.1 2.6 %copy-start.7 = (f32[2,200,384]{2,1,0:T(8,128)S(1)}, f32[2,200,384]{2,1,0:T(8,128)}, u32[]{:S(2)}) copy-start(f32[2,200,384]{2,1,0:T(8,128)} %copy-done.6) | copy-start | bytes 1843204
  35.2 2.6 %collective-permute-start.7 = (bf16[104,384]{1,0:T(8,128)(2,1)S(1)}, bf16[104,384]{1,0:T(8,128)(2,1)S(1)}, u32[]{:S(2)}, u32[]{:S(2)}) collective-permute-start(bf16[104,384]{1,0:T(8,128)(2,1)S(1)} %add_convert_fusion.mine_ref), channel_id=1, source_target_pairs={{0,1},{1,0},{2,3},{3,2},{4,5},{5,4},{6,7},{7,6},{8,9},{9,8},{10,11... | collective-permute-start | bytes 239624 | tf_op jit(solution)/shard_map/ppermute | solution.py:380
  42.2 9.8 %collective-permute-start.8 = (bf16[384,384]{1,0:T(8,128)(2,1)S(1)}, bf16[384,384]{1,0:T(8,128)(2,1)S(1)}, u32[]{:S(2)}, u32[]{:S(2)}) collective-permute-start(bf16[384,384]{1,0:T(8,128)(2,1)S(1)} %match_other.1), channel_id=1, source_target_pairs={{0,2},{2,0},{1,3},{3,1},{4,6},{6,4},{5,7},{7,5},{8,10},{10,8},{9,1... | collective-permute-start | bytes 884744 | tf_op jit(solution)/shard_map/ppermute | solution.py:419

commit v11 on v10

--- a/solution.py
+++ b/solution.py
@@ -1,3 +1,4 @@
+import functools
 import math
 
 import jax
@@ -193,7 +194,10 @@
 
 
 def library_kernel(image_ref, tab_ref, out_ref):
-    store_spectrum(out_ref, half_spectrum(image_ref[...].reshape(N, N), tab_ref))
+    step = pl.program_id(0)
+    for i in range(2):
+        image = image_ref[:, 2 * step + i].reshape(N, N)
+        store_spectrum(out_ref.at[2 * step + i], half_spectrum(image, tab_ref))
 
 
 def match_step(re, im, spec_ref, weight_ref, tab):
@@ -240,16 +244,24 @@
         weight_out[t] = weight[...] * inverse_noise
 
 
-def match_kernel(near_ref, far_ref, spec_ref, weight_ref, tab_ref, unfold_ref, out_ref, best_sc):
+def match_kernel(
+    t, near_ref, far_ref, spec_ref, weight_ref, tab_ref, unfold_ref, out_ref, best_sc
+):
     step = pl.program_id(0)
 
     @pl.when(step == 0)
     def _():
         best_sc[...] = jnp.full_like(best_sc, -jnp.inf)
 
-    for i in range(near_ref.shape[0]):
+    for i in range(2):
         pairs = [
-            match_step(ref[i, 0].astype(F32), ref[i, 1].astype(F32), spec_ref, weight_ref, tab_ref)
+            match_step(
+                ref[2 * step + i, 0].astype(F32),
+                ref[2 * step + i, 1].astype(F32),
+                spec_ref.at[t],
+                weight_ref.at[t],
+                tab_ref,
+            )
             for ref in (near_ref, far_ref)
         ]
         for k in range(2):
@@ -362,13 +374,10 @@
 
     near_all = pl.pallas_call(
         library_kernel,
-        out_shape=jax.ShapeDtypeStruct((deep,) + plane, BF16),
-        grid=(deep,),
-        in_specs=[
-            pl.BlockSpec((groups, None, N // groups, N), lambda i: (0, i, 0, 0)),
-            full(*ahead.shape),
-        ],
-        out_specs=pl.BlockSpec((None,) + plane, lambda i: (i, 0, 0, 0)),
+        out_shape=pltpu.VMEM((deep,) + plane, BF16),
+        grid=(deep // 2,),
+        in_specs=kept * 2,
+        out_specs=kept[0],
         compiler_params=params(12),
         cost_estimate=cost(deep * work, 4 << 20),
         name="library",
@@ -381,35 +390,23 @@
     white, white_weight = pl.pallas_call(
         whiten_kernel,
         out_shape=[
-            jax.ShapeDtypeStruct((2,) + plane, F32),
-            jax.ShapeDtypeStruct((2, ROWS, N), F32),
+            pltpu.VMEM((2,) + plane, F32),
+            pltpu.VMEM((2, ROWS, N), F32),
         ],
-        grid=(1,),
-        in_specs=[full(1, 1)]
-        + [full(*plane), full(ROWS, N)] * 2
-        + [full(PART, N)] * 2
-        + kept * 2,
-        out_specs=[full(2, *plane), full(2, ROWS, N)],
+        in_specs=kept * 9,
+        out_specs=kept * 2,
         compiler_params=params(12),
         cost_estimate=cost(60 * work, 4 << 20),
         name="whiten",
     )(core, *own, *other, mine, theirs, back, unfold)
 
     def match(t, dtype, name):
-        lib_spec = pl.BlockSpec((2,) + plane, lambda i: (i, 0, 0, 0))
         return pl.pallas_call(
-            match_kernel,
-            out_shape=jax.ShapeDtypeStruct((N, N), dtype),
+            functools.partial(match_kernel, t),
+            out_shape=pltpu.VMEM((N, N), dtype),
             grid=(deep // 2,),
-            in_specs=[
-                lib_spec,
-                lib_spec,
-                pl.BlockSpec((None,) + plane, lambda i: (t, 0, 0, 0)),
-                pl.BlockSpec((None, ROWS, N), lambda i: (t, 0, 0)),
-                full(*back.shape),
-                full(*unfold.shape),
-            ],
-            out_specs=full(N, N),
+            in_specs=kept * 6,
+            out_specs=kept[0],
             scratch_shapes=[pltpu.VMEM(plane, F32)],
             compiler_params=params(12),
             cost_estimate=cost(2 * deep * 2 * work, 6 << 20),

time: 53.2 us -> 52.6 us (0.989)
  Pallas kernels: 15.8 us -> 15.2 us
    pallas_call x4, Pallas kernels: 10.9 us -> 10.3 us  [the longest x2 8.11 us: match(): pl.pallas_call(functools.partial(match_kernel, t), out_shape=pltpu.VMEM((...]
    ppermute x1, waiting for transfers between devices: 0.9 us -> 0.29 us  [per_device(): theirs = lax.ppermute(mine, 'core', swap)]
  transfers between devices with their start and end apart: 10 -> 10, of which waited for: 4 -> 5; matrix products, arithmetic and copies ran while one was open for 0% -> 0% of each run, Pallas kernels for 22% -> 22%
where the time goes in v11:
time: 52.6 us; the launch traced here: 52.2 us
  starting transfers between devices  24.4 us (46%)
  Pallas kernels  15.2 us (29%)
  waiting for transfers between devices  9.94 us (19%)
  other arithmetic  0.95 us (2%)
  local copies, waits for them, and re-layouts  0.88 us (2%)
  between operations  0.87 us (2%)
    all_to_all x1, starting transfers between devices, per_device(): images_all = lax.all_to_all(copies, LIB, 0, 0, tiled=False)  8.22 us
    pallas_call x2, Pallas kernels, match(): pl.pallas_call(functools.partial(match_kernel, t), out_shape=pltpu.VMEM((...  8.11 us
    all_to_all x1, waiting for transfers between devices, per_device(): images_all = lax.all_to_all(copies, LIB, 0, 0, tiled=False)  4.51 us
    ppermute x3, starting transfers between devices, per_device(): lax.ppermute(pair, 'z', [(z, (z + dz) % deep) for z in range(deep)])  3.94 us
    ppermute x1, waiting for transfers between devices, per_device(): got = lax.ppermute(match(1, BF16, 'match_other'), 'xhi', swap)  3.8 us
    ppermute x1, starting transfers between devices, per_device(): received = lax.ppermute(tile, 'xhi', swap)  3.57 us
    ppermute x1, starting transfers between devices, per_device(): far_all = lax.ppermute(near_all, 'core', swap)  3.3 us
    pallas_call x2, Pallas kernels, gain(): pl.pallas_call(gain_kernel, out_shape=[jax.ShapeDtypeStruct(plane, F32),...  2.2 us
  transfers between devices with their start and end apart: 10, of which 5 were waited for; matrix products, arithmetic and copies ran while one was open for 0% of the time, Pallas kernels for 22%

profile of v11, /device:TPU:1, one launch (start us, length us, event | category | flops | bytes accessed | tf_op | source)
XLA Modules:
  0.0 52.2 jit_solution(1115648418859009556)
XLA Ops:
  0.0 3.6 %collective-permute-start = (bf16[384,384]{1,0:T(8,128)(2,1)}, bf16[384,384]{1,0:T(8,128)(2,1)S(1)}, u32[]{:S(2)}, u32[]{:S(2)}) collective-permute-start(bf16[384,384]{1,0:T(8,128)(2,1)} %bitcast.11), channel_id=1, source_target_pairs={{0,2},{2,0},{1,3},{3,1},{4,6},{6,4},{5,7},{7,5},{8,10},{10,8},{9,1... | collective-permute-start | bytes 884744 | tf_op jit(solution)/shard_map/ppermute | solution.py:308
  3.6 1.9 %copies.1 = bf16[32,48,384]{2,1,0:T(8,128)(2,1)} custom-call(bf16[48,384]{1,0:T(8,128)(2,1)} %bitcast.13), custom_call_target="tpu_custom_call" | custom-call | bytes 1048576 | tf_op jit(solution)/shard_map/copies/pallas_call | solution.py:309
  5.4 0.0 copy-start
  5.4 0.0 copy-start.1
  5.5 8.2 %all-to-all-start = ((bf16[32,48,384]{2,1,0:T(8,128)(2,1)}), bf16[32,48,384]{2,1,0:T(8,128)(2,1)S(1)}, u32[]{:S(2)}, u32[]{:S(2)}) async-start(bf16[32,48,384]{2,1,0:T(8,128)(2,1)} %copies.1), calls=%async_computation | async-start | bytes 2359296 | tf_op jit(solution)/shard_map/all_to_all | solution.py:323
  14.3 0.0 collective-permute-done.other_ref
  14.4 0.0 copy-done
  14.4 0.0 copy-done.1
  14.4 0.0 copy-start.8
  14.4 0.0 copy-start.9
  14.4 0.0 copy-start.10
  14.4 0.0 copy-start.11
  14.4 0.0 copy-start.2
  14.4 0.0 copy-start.3
  14.4 0.8 %tile.1 = (f32[2,2,200,384]{3,2,1,0:T(8,128)S(1)}, bf16[104,384]{1,0:T(8,128)(2,1)S(1)}, bf16[104,384]{1,0:T(8,128)(2,1)S(1)}) custom-call(s32[1,1]{1,0:T(1,128)} %bitcast.core_ref, bf16[384,384]{1,0:T(8,128)(2,1)S(1)} %bitcast.12, bf16[384,384]{1,0:T(8,128)(2,1)S(1)} %collective-permute-done.other_ref, bf16[1168,256]{1,0:T(8,128)(2,1)S(1)} %copy-done), custom_call_target="tpu_custom_call" | custom-call | flops 31457280000 | bytes 3145728 | tf_op jit(solution)/shard_map/tile/pallas_call | solution.py:325
  15.3 0.0 copy-start.4
  15.3 1.3 %collective-permute-start.1 = (bf16[104,384]{1,0:T(8,128)(2,1)S(1)}, bf16[104,384]{1,0:T(8,128)(2,1)S(1)}, u32[]{:S(2)}, u32[]{:S(2)}) collective-permute-start(bf16[104,384]{1,0:T(8,128)(2,1)S(1)} %get-tuple-element.25), channel_id=1, source_target_pairs={{0,1},{1,0},{2,3},{3,2},{4,5},{5,4},{6,7},{7,6},{8,9},{9,8},{10,11... | collective-permute-start | bytes 239624 | tf_op jit(solution)/shard_map/ppermute | solution.py:341
  16.6 0.0 copy-done.8
  16.6 0.0 copy-done.9
  16.6 0.0 copy-done.10
  16.6 0.0 copy-done.11
  16.7 0.9 %collective-permute-done.1 = bf16[104,384]{1,0:T(8,128)(2,1)S(1)} collective-permute-done((bf16[104,384]{1,0:T(8,128)(2,1)S(1)}, bf16[104,384]{1,0:T(8,128)(2,1)S(1)}, u32[]{:S(2)}, u32[]{:S(2)}) %collective-permute-start.1) | collective-permute-done | bytes 79904 | tf_op jit(solution)/shard_map/ppermute | solution.py:341
  17.6 2.8 %collective-permute-start.4 = (bf16[104,384]{1,0:T(8,128)(2,1)S(1)}, bf16[104,384]{1,0:T(8,128)(2,1)S(1)}, u32[]{:S(2)}, u32[]{:S(2)}) collective-permute-start(bf16[104,384]{1,0:T(8,128)(2,1)S(1)} %add_convert_fusion.1), channel_id=1, source_target_pairs={{0,12},{4,0},{8,4},{12,8},{1,13},{5,1},{9,5},{13,9},{2,14},{6,2},{... | collective-permute-start | bytes 239624 | tf_op jit(solution)/shard_map/ppermute | solution.py:343
  20.4 0.6 %collective-permute-start.3 = (bf16[104,384]{1,0:T(8,128)(2,1)S(1)}, bf16[104,384]{1,0:T(8,128)(2,1)S(1)}, u32[]{:S(2)}, u32[]{:S(2)}) collective-permute-start(bf16[104,384]{1,0:T(8,128)(2,1)S(1)} %add_convert_fusion.1), channel_id=1, source_target_pairs={{0,8},{4,12},{8,0},{12,4},{1,9},{5,13},{9,1},{13,5},{2,10},{6,14},... | collective-permute-start | bytes 239624 | tf_op jit(solution)/shard_map/ppermute | solution.py:343
  20.9 0.6 %collective-permute-start.2 = (bf16[104,384]{1,0:T(8,128)(2,1)S(1)}, bf16[104,384]{1,0:T(8,128)(2,1)S(1)}, u32[]{:S(2)}, u32[]{:S(2)}) collective-permute-start(bf16[104,384]{1,0:T(8,128)(2,1)S(1)} %add_convert_fusion.1), channel_id=1, source_target_pairs={{0,4},{4,8},{8,12},{12,0},{1,5},{5,9},{9,13},{13,1},{2,6},{6,10},{... | collective-permute-start | bytes 239624 | tf_op jit(solution)/shard_map/ppermute | solution.py:343
  21.5 0.0 copy-done.2
  21.5 0.0 copy-done.3
  21.5 0.8 %gain_own.1 = (f32[2,200,384]{2,1,0:T(8,128)S(1)}, f32[200,384]{1,0:T(8,128)S(1)}) custom-call(s32[1,1]{1,0:T(1,128)S(6)} %copy.11.row_ref, f32[8,128]{1,0:T(8,128)S(1)} %select_maximum_fusion.table_ref, f32[2,2,200,384]{3,2,1,0:T(8,128)S(1)} %get-tuple-element.26.tile_ref, bf16[1168,256]{1,0:T(8,128)(2,1)S(1)} %copy-done, bf16[1184,256]{1,0:T(8,128)(2,1)S(1)} %copy-done.2, ...), custom_call_target="tpu_custom_call" | custom-call | flops 1258291200 | bytes 3145728 | tf_op jit(solution)/shard_map/gain_own/pallas_call | solution.py:353
  22.4 0.0 copy-done.4
  22.4 0.0 copy-start.6
  22.4 0.8 %copy-done.6 = f32[2,200,384]{2,1,0:T(8,128)} copy-done((f32[2,200,384]{2,1,0:T(8,128)}, f32[2,200,384]{2,1,0:T(8,128)S(1)}, u32[]{:S(2)}) %copy-start.6) | copy-done | bytes 614424
  23.2 1.7 %collective-permute-start.5 = (s32[1,1]{1,0:T(1,128)}, s32[1,1]{1,0:T(1,128)}, u32[]{:S(2)}, u32[]{:S(2)}) collective-permute-start(s32[1,1]{1,0:T(1,128)} %param.12), channel_id=1, source_target_pairs={{0,2},{2,0},{1,3},{3,1},{4,6},{6,4},{5,7},{7,5},{8,10},{10,8},{9,1... | collective-permute-start | bytes 20 | tf_op jit(solution)/shard_map/ppermute | solution.py:350
  24.9 4.5 %all-to-all-done = bf16[32,48,384]{2,1,0:T(8,128)(2,1)S(1)} async-done(((bf16[32,48,384]{2,1,0:T(8,128)(2,1)}), bf16[32,48,384]{2,1,0:T(8,128)(2,1)S(1)}, u32[]{:S(2)}, u32[]{:S(2)}) %all-to-all-start) | async-done | bytes 1179680 | tf_op jit(solution)/shard_map/all_to_all | solution.py:323
  29.4 0.0 copy-start.5
  29.4 1.7 %library.1.near_ref = bf16[4,2,200,384]{3,2,1,0:T(8,128)(2,1)S(1)} custom-call(bf16[8,4,48,384]{3,2,1,0:T(8,128)(2,1)S(1)} %bitcast.10, bf16[1168,256]{1,0:T(8,128)(2,1)S(1)} %copy-done), custom_call_target="tpu_custom_call" | custom-call | flops 629145600 | bytes 4194304 | tf_op jit(solution)/shard_map/library/pallas_call | solution.py:375
  31.2 3.3 %collective-permute-start.6 = (bf16[4,2,200,384]{3,2,1,0:T(8,128)(2,1)S(1)}, bf16[4,2,200,384]{3,2,1,0:T(8,128)(2,1)S(1)}, u32[]{:S(2)}, u32[]{:S(2)}) collective-permute-start(bf16[4,2,200,384]{3,2,1,0:T(8,128)(2,1)S(1)} %library.1.near_ref), channel_id=1, source_target_pairs={{0,1},{1,0},{2,3},{3,2},{4,5},{5,4},{6,7},{7,6},{8,9},{9,8},{10,11... | collective-permute-start | bytes 3686408 | tf_op jit(solution)/shard_map/ppermute | solution.py:385
  34.5 0.0 collective-permute-done.5.row_ref
  34.5 0.0 collective-permute-done.4
  34.5 0.0 collective-permute-done.3
  34.5 0.4 collective-permute-done.2
  35.0 0.0 copy-start.7
  35.0 0.5 collective-permute-start.7
  35.4 0.0 copy-done.5
  35.4 1.4 %gain_other.1 = (f32[2,200,384]{2,1,0:T(8,128)S(1)}, f32[200,384]{1,0:T(8,128)S(1)}) custom-call(s32[1,1]{1,0:T(1,128)} %collective-permute-done.5.row_ref, f32[8,128]{1,0:T(8,128)S(1)} %select_maximum_fusion.table_ref, f32[2,2,200,384]{3,2,1,0:T(8,128)S(1)} %copy-done.5), custom_call_target="tpu_custom_call" | custom-call | flops 1258291200 | bytes 3145728 | tf_op jit(solution)/shard_map/gain_other/pallas_call | solution.py:353
  36.8 0.3 collective-permute-done.7.theirs_ref
  37.1 0.0 copy-done.7
  37.1 0.5 whiten.1
  37.6 0.0 collective-permute-done.6.far_ref
  37.6 3.9 %match_other.1 = bf16[384,384]{1,0:T(8,128)(2,1)S(1)} custom-call(bf16[4,2,200,384]{3,2,1,0:T(8,128)(2,1)S(1)} %library.1.near_ref, bf16[4,2,200,384]{3,2,1,0:T(8,128)(2,1)S(1)} %collective-permute-done.6.far_ref, f32[2,2,200,384]{3,2,1,0:T(8,128)S(1)} %get-tuple-element.41.spec_ref, f32[2,200,384]{2,1,0:T(8,128)S(1)} %get-tuple-element.42.weight_ref, ...), custom_call_target="tpu_custom_call" | custom-call | flops 2516582400 | bytes 6291456 | tf_op jit(solution)/shard_map/match_other/pallas_call | solution.py:404
  41.6 1.8 %collective-permute-start.8 = (bf16[384,384]{1,0:T(8,128)(2,1)S(1)}, bf16[384,384]{1,0:T(8,128)(2,1)S(1)}, u32[]{:S(2)}, u32[]{:S(2)}) collective-permute-start(bf16[384,384]{1,0:T(8,128)(2,1)S(1)} %match_other.1), channel_id=1, source_target_pairs={{0,2},{2,0},{1,3},{3,1},{4,6},{6,4},{5,7},{7,5},{8,10},{10,8},{9,1... | collective-permute-start | bytes 884744 | tf_op jit(solution)/shard_map/ppermute | solution.py:416
  43.4 4.2 %match_own.1 = f32[384,384]{1,0:T(8,128)S(1)} custom-call(bf16[4,2,200,384]{3,2,1,0:T(8,128)(2,1)S(1)} %library.1.near_ref, bf16[4,2,200,384]{3,2,1,0:T(8,128)(2,1)S(1)} %collective-permute-done.6.far_ref, f32[2,2,200,384]{3,2,1,0:T(8,128)S(1)} %get-tuple-element.41.spec_ref, f32[2,200,384]{2,1,0:T(8,128)S(1)} %get-tuple-element.42.weight_ref, ...), custom_call_target="tpu_custom_call" | custom-call | flops 2516582400 | bytes 6291456 | tf_op jit(solution)/shard_map/match_own/pallas_call | solution.py:404
  47.6 3.8 %collective-permute-done.8 = bf16[384,384]{1,0:T(8,128)(2,1)S(1)} collective-permute-done((bf16[384,384]{1,0:T(8,128)(2,1)S(1)}, bf16[384,384]{1,0:T(8,128)(2,1)S(1)}, u32[]{:S(2)}, u32[]{:S(2)}) %collective-permute-start.8) | collective-permute-done | bytes 294944 | tf_op jit(solution)/shard_map/ppermute | solution.py:416
  51.4 0.9 %maximum_bitcast_fusion = f32[1,1,384,384]{3,2,1,0:T(8,128)} fusion(f32[384,384]{1,0:T(8,128)S(1)} %match_own.1, bf16[384,384]{1,0:T(8,128)(2,1)S(1)} %collective-permute-done.8), kind=kLoop, calls=%fused_computation | loop fusion | flops 294912 | bytes 1474560 | tf_op jit(solution)/shard_map/broadcast_in_dim | solution.py:418
  (3 shorter events, 0.1 us)
Async XLA Ops:
  0.0 14.3 %collective-permute-start = (bf16[384,384]{1,0:T(8,128)(2,1)}, bf16[384,384]{1,0:T(8,128)(2,1)S(1)}, u32[]{:S(2)}, u32[]{:S(2)}) collective-permute-start(bf16[384,384]{1,0:T(8,128)(2,1)} %bitcast.11), channel_id=1, source_target_pairs={{0,2},{2,0},{1,3},{3,1},{4,6},{6,4},{5,7},{7,5},{8,10},{10,8},{9,1... | collective-permute-start | bytes 884744 | tf_op jit(solution)/shard_map/ppermute | solution.py:308
  5.4 8.9 %copy-start = (bf16[1168,256]{1,0:T(8,128)(2,1)S(1)}, bf16[1168,256]{1,0:T(8,128)(2,1)}, u32[]{:S(2)}) copy-start(bf16[1168,256]{1,0:T(8,128)(2,1)} %constant.13.clone.tab_ref.refs_0_) | copy-start | bytes 1794052
  5.4 8.9 %copy-start.1 = (bf16[1,1,384,384]{3,2,1,0:T(8,128)(2,1)S(1)}, bf16[1,1,384,384]{3,2,1,0:T(8,128)(2,1)}, u32[]{:S(2)}) copy-start(bf16[1,1,384,384]{3,2,1,0:T(8,128)(2,1)} %param.10) | copy-start | bytes 884740
  5.5 24.0 %all-to-all-start = ((bf16[32,48,384]{2,1,0:T(8,128)(2,1)}), bf16[32,48,384]{2,1,0:T(8,128)(2,1)S(1)}, u32[]{:S(2)}, u32[]{:S(2)}) async-start(bf16[32,48,384]{2,1,0:T(8,128)(2,1)} %copies.1), calls=%async_computation | async-start | bytes 2359296 | tf_op jit(solution)/shard_map/all_to_all | solution.py:323
  14.4 2.3 %copy-start.8 = (f32[64]{0:T(128)S(1)}, f32[64]{0:T(128)}, u32[]{:S(2)}) copy-start(f32[64]{0:T(128)} %param.16) | copy-start | bytes 772
  14.4 2.3 %copy-start.9 = (f32[64]{0:T(128)S(1)}, f32[64]{0:T(128)}, u32[]{:S(2)}) copy-start(f32[64]{0:T(128)} %param.15) | copy-start | bytes 772
  14.4 2.2 %copy-start.10 = (f32[64]{0:T(128)S(1)}, f32[64]{0:T(128)}, u32[]{:S(2)}) copy-start(f32[64]{0:T(128)} %param.14) | copy-start | bytes 772
  14.4 2.2 %copy-start.11 = (f32[64]{0:T(128)S(1)}, f32[64]{0:T(128)}, u32[]{:S(2)}) copy-start(f32[64]{0:T(128)} %param.13) | copy-start | bytes 772
  14.4 7.1 %copy-start.2 = (bf16[1184,256]{1,0:T(8,128)(2,1)S(1)}, bf16[1184,256]{1,0:T(8,128)(2,1)}, u32[]{:S(2)}) copy-start(bf16[1184,256]{1,0:T(8,128)(2,1)} %constant.14.clone.refs_1_.refs_0_.tab_ref) | copy-start | bytes 1818628
  14.4 7.1 %copy-start.3 = (bf16[192,400]{1,0:T(8,128)(2,1)S(1)}, bf16[192,400]{1,0:T(8,128)(2,1)}, u32[]{:S(2)}) copy-start(bf16[192,400]{1,0:T(8,128)(2,1)} %constant.15.clone.refs_2_.refs_1_.unfold_ref) | copy-start | bytes 460804
  15.3 7.1 %copy-start.4 = (f32[2,2,200,384]{3,2,1,0:T(8,128)}, f32[2,2,200,384]{3,2,1,0:T(8,128)S(1)}, u32[]{:S(2)}) copy-start(f32[2,2,200,384]{3,2,1,0:T(8,128)S(1)} %get-tuple-element.26.tile_ref) | copy-start | bytes 3686404
  15.3 2.2 %collective-permute-start.1 = (bf16[104,384]{1,0:T(8,128)(2,1)S(1)}, bf16[104,384]{1,0:T(8,128)(2,1)S(1)}, u32[]{:S(2)}, u32[]{:S(2)}) collective-permute-start(bf16[104,384]{1,0:T(8,128)(2,1)S(1)} %get-tuple-element.25), channel_id=1, source_target_pairs={{0,1},{1,0},{2,3},{3,2},{4,5},{5,4},{6,7},{7,6},{8,9},{9,8},{10,11... | collective-permute-start | bytes 239624 | tf_op jit(solution)/shard_map/ppermute | solution.py:341
  17.6 16.9 %collective-permute-start.4 = (bf16[104,384]{1,0:T(8,128)(2,1)S(1)}, bf16[104,384]{1,0:T(8,128)(2,1)S(1)}, u32[]{:S(2)}, u32[]{:S(2)}) collective-permute-start(bf16[104,384]{1,0:T(8,128)(2,1)S(1)} %add_convert_fusion.1), channel_id=1, source_target_pairs={{0,12},{4,0},{8,4},{12,8},{1,13},{5,1},{9,5},{13,9},{2,14},{6,2},{... | collective-permute-start | bytes 239624 | tf_op jit(solution)/shard_map/ppermute | solution.py:343
  20.4 14.1 %collective-permute-start.3 = (bf16[104,384]{1,0:T(8,128)(2,1)S(1)}, bf16[104,384]{1,0:T(8,128)(2,1)S(1)}, u32[]{:S(2)}, u32[]{:S(2)}) collective-permute-start(bf16[104,384]{1,0:T(8,128)(2,1)S(1)} %add_convert_fusion.1), channel_id=1, source_target_pairs={{0,8},{4,12},{8,0},{12,4},{1,9},{5,13},{9,1},{13,5},{2,10},{6,14},... | collective-permute-start | bytes 239624 | tf_op jit(solution)/shard_map/ppermute | solution.py:343
  20.9 14.0 %collective-permute-start.2 = (bf16[104,384]{1,0:T(8,128)(2,1)S(1)}, bf16[104,384]{1,0:T(8,128)(2,1)S(1)}, u32[]{:S(2)}, u32[]{:S(2)}) collective-permute-start(bf16[104,384]{1,0:T(8,128)(2,1)S(1)} %add_convert_fusion.1), channel_id=1, source_target_pairs={{0,4},{4,8},{8,12},{12,0},{1,5},{5,9},{9,13},{13,1},{2,6},{6,10},{... | collective-permute-start | bytes 239624 | tf_op jit(solution)/shard_map/ppermute | solution.py:343
  22.4 0.8 %copy-start.6 = (f32[2,200,384]{2,1,0:T(8,128)}, f32[2,200,384]{2,1,0:T(8,128)S(1)}, u32[]{:S(2)}) copy-start(f32[2,200,384]{2,1,0:T(8,128)S(1)} %get-tuple-element.32.own_ref) | copy-start | bytes 1843204
  23.2 11.3 %collective-permute-start.5 = (s32[1,1]{1,0:T(1,128)}, s32[1,1]{1,0:T(1,128)}, u32[]{:S(2)}, u32[]{:S(2)}) collective-permute-start(s32[1,1]{1,0:T(1,128)} %param.12), channel_id=1, source_target_pairs={{0,2},{2,0},{1,3},{3,1},{4,6},{6,4},{5,7},{7,5},{8,10},{10,8},{9,1... | collective-permute-start | bytes 20 | tf_op jit(solution)/shard_map/ppermute | solution.py:350
  29.4 6.0 %copy-start.5 = (f32[2,2,200,384]{3,2,1,0:T(8,128)S(1)}, f32[2,2,200,384]{3,2,1,0:T(8,128)}, u32[]{:S(2)}) copy-start(f32[2,2,200,384]{3,2,1,0:T(8,128)} %copy-done.4) | copy-start | bytes 3686404
  31.2 6.5 %collective-permute-start.6 = (bf16[4,2,200,384]{3,2,1,0:T(8,128)(2,1)S(1)}, bf16[4,2,200,384]{3,2,1,0:T(8,128)(2,1)S(1)}, u32[]{:S(2)}, u32[]{:S(2)}) collective-permute-start(bf16[4,2,200,384]{3,2,1,0:T(8,128)(2,1)S(1)} %library.1.near_ref), channel_id=1, source_target_pairs={{0,1},{1,0},{2,3},{3,2},{4,5},{5,4},{6,7},{7,6},{8,9},{9,8},{10,11... | collective-permute-start | bytes 3686408 | tf_op jit(solution)/shard_map/ppermute | solution.py:385
  35.0 2.2 %copy-start.7 = (f32[2,200,384]{2,1,0:T(8,128)S(1)}, f32[2,200,384]{2,1,0:T(8,128)}, u32[]{:S(2)}) copy-start(f32[2,200,384]{2,1,0:T(8,128)} %copy-done.6) | copy-start | bytes 1843204
  35.0 2.2 %collective-permute-start.7 = (bf16[104,384]{1,0:T(8,128)(2,1)S(1)}, bf16[104,384]{1,0:T(8,128)(2,1)S(1)}, u32[]{:S(2)}, u32[]{:S(2)}) collective-permute-start(bf16[104,384]{1,0:T(8,128)(2,1)S(1)} %add_convert_fusion.mine_ref), channel_id=1, source_target_pairs={{0,1},{1,0},{2,3},{3,2},{4,5},{5,4},{6,7},{7,6},{8,9},{9,8},{10,11... | collective-permute-start | bytes 239624 | tf_op jit(solution)/shard_map/ppermute | solution.py:389
  41.6 9.8 %collective-permute-start.8 = (bf16[384,384]{1,0:T(8,128)(2,1)S(1)}, bf16[384,384]{1,0:T(8,128)(2,1)S(1)}, u32[]{:S(2)}, u32[]{:S(2)}) collective-permute-start(bf16[384,384]{1,0:T(8,128)(2,1)S(1)} %match_other.1), channel_id=1, source_target_pairs={{0,2},{2,0},{1,3},{3,1},{4,6},{6,4},{5,7},{7,5},{8,10},{10,8},{9,1... | collective-permute-start | bytes 884744 | tf_op jit(solution)/shard_map/ppermute | solution.py:416

commit v12 on v11

--- a/solution.py
+++ b/solution.py
@@ -186,11 +186,11 @@
     send_ref[...] = jnp.where(first, high, low).astype(BF16)
 
 
-def gain_kernel(row_ref, table_ref, tile_ref, *refs):
+def gain_kernel(t, row_ref, table_ref, tile_ref, *refs):
     spec_ref, weight_ref = refs[-2:]
     gain, weight_ref[...] = ctf_factors(row_ref[...].astype(F32), table_ref[...])
-    spec_ref[0] = tile_ref[0] * gain
-    spec_ref[1] = tile_ref[1] * gain
+    spec_ref[0] = tile_ref[t, 0] * gain
+    spec_ref[1] = tile_ref[t, 1] * gain
 
 
 def library_kernel(image_ref, tab_ref, out_ref):
@@ -198,33 +198,6 @@
     for i in range(2):
         image = image_ref[:, 2 * step + i].reshape(N, N)
         store_spectrum(out_ref.at[2 * step + i], half_spectrum(image, tab_ref))
-
-
-def match_step(re, im, spec_ref, weight_ref, tab):
-    wide = 2 * THIRD
-    norm = jnp.sum((re * re + im * im) * weight_ref[...])
-    scale = lax.rsqrt(jnp.full((1, THIRD), norm + 1e-06, F32))
-    s_re, s_im = spec_ref[0], spec_ref[1]
-    p_re = (s_re * re + s_im * im).astype(BF16)
-    p_im = (s_im * re - s_re * im).astype(BF16)
-    g = []
-    for k in range(3):
-        at = slice(k * THIRD, (k + 1) * THIRD)
-        lhs = jnp.concatenate([p_re[:, at], p_im[:, at]], axis=1)
-        g.append(dot(lhs, tab[k * wide : (k + 1) * wide, :]))
-    (r0, i0), (r1, i1), (r2, i2) = ((x[:, :THIRD], x[:, THIRD:]) for x in g)
-    slant = scale * ROOT
-    rp, rm = r1 + r2, slant * (r1 - r2)
-    ip, im_ = i1 + i2, slant * (i1 - i2)
-    rh, ih = scale * (r0 - 0.5 * rp), scale * (i0 - 0.5 * ip)
-    h_re = [scale * (r0 + rp), rh - im_, rh + im_]
-    h_im = [scale * (i0 + ip), ih + rm, ih - rm]
-    h_re = jnp.concatenate([h.astype(BF16) for h in h_re], axis=1)
-    h_im = jnp.concatenate([h.astype(BF16) for h in h_im], axis=1)
-    first = 3 * wide
-    even = dot(tab[first : first + ROWS, :ROWS], h_re)
-    odd = dot(tab[first + FOLD : first + FOLD + ROWS, :ROWS], h_im)
-    return even - odd, even + odd
 
 
 def whiten_kernel(
@@ -245,39 +218,57 @@
 
 
 def match_kernel(
-    t, near_ref, far_ref, spec_ref, weight_ref, tab_ref, unfold_ref, out_ref, best_sc
+    t, near_ref, far_ref, spec_ref, weight_ref, tab_ref, unfold_ref, out_ref, p_sc, h_sc, best_sc
 ):
-    step = pl.program_id(0)
-
-    @pl.when(step == 0)
-    def _():
-        best_sc[...] = jnp.full_like(best_sc, -jnp.inf)
-
-    for i in range(2):
-        pairs = [
-            match_step(
-                ref[2 * step + i, 0].astype(F32),
-                ref[2 * step + i, 1].astype(F32),
-                spec_ref.at[t],
-                weight_ref.at[t],
-                tab_ref,
-            )
-            for ref in (near_ref, far_ref)
-        ]
-        for k in range(2):
-            best_sc[k] = jnp.maximum(best_sc[k], jnp.maximum(pairs[0][k], pairs[1][k]))
-
-    @pl.when(step == pl.num_programs(0) - 1)
-    def _():
-        out_ref[:HALF] = best_sc[0, :HALF].astype(out_ref.dtype)
-        rest = best_sc[...].reshape(2 * ROWS, N)
-        total = None
-        for _ in range(3 if out_ref.dtype == F32 else 1):
-            part = rest.astype(BF16)
-            rest = rest - part.astype(F32)
-            moved = dot(unfold_ref[...], part)
-            total = moved if total is None else total + moved
-        out_ref[HALF:] = total.astype(out_ref.dtype)
+    wide = 2 * THIRD
+    count = 2 * near_ref.shape[0]
+    s_re, s_im = spec_ref[t, 0], spec_ref[t, 1]
+    scales = []
+    for j in range(count):
+        ref = (near_ref, far_ref)[j % 2]
+        re, im = ref[j // 2, 0].astype(F32), ref[j // 2, 1].astype(F32)
+        norm = jnp.sum((re * re + im * im) * weight_ref[t])
+        scales.append(lax.rsqrt(jnp.full((1, THIRD), norm + 1e-06, F32)))
+        p_re = (s_re * re + s_im * im).astype(BF16)
+        p_im = (s_im * re - s_re * im).astype(BF16)
+        rows = slice(j * FOLD, j * FOLD + ROWS)
+        for k in range(3):
+            at = slice(k * THIRD, (k + 1) * THIRD)
+            p_sc[k, rows, :THIRD] = p_re[:, at]
+            p_sc[k, rows, THIRD:] = p_im[:, at]
+    g = [dot(p_sc[k], tab_ref[k * wide : (k + 1) * wide, :]) for k in range(3)]
+    for j, scale in enumerate(scales):
+        rows = slice(j * FOLD, j * FOLD + ROWS)
+        (r0, i0), (r1, i1), (r2, i2) = ((x[rows, :THIRD], x[rows, THIRD:]) for x in g)
+        slant = scale * ROOT
+        rp, rm = r1 + r2, slant * (r1 - r2)
+        ip, im_ = i1 + i2, slant * (i1 - i2)
+        rh, ih = scale * (r0 - 0.5 * rp), scale * (i0 - 0.5 * ip)
+        h_re = (scale * (r0 + rp), rh - im_, rh + im_)
+        h_im = (scale * (i0 + ip), ih + rm, ih - rm)
+        for k in range(3):
+            at = slice(j * N + k * THIRD, j * N + (k + 1) * THIRD)
+            h_sc[0, :, at] = h_re[k].astype(BF16)
+            h_sc[1, :, at] = h_im[k].astype(BF16)
+    first = 3 * wide
+    even = dot(tab_ref[first : first + ROWS, :ROWS], h_sc[0])
+    odd = dot(tab_ref[first + FOLD : first + FOLD + ROWS, :ROWS], h_sc[1])
+    minus, plus = even[:, :N] - odd[:, :N], even[:, :N] + odd[:, :N]
+    for j in range(1, count):
+        at = slice(j * N, (j + 1) * N)
+        minus = jnp.maximum(minus, even[:, at] - odd[:, at])
+        plus = jnp.maximum(plus, even[:, at] + odd[:, at])
+    best_sc[0] = minus
+    best_sc[1] = plus
+    out_ref[:HALF] = best_sc[0, :HALF].astype(out_ref.dtype)
+    rest = best_sc[...].reshape(2 * ROWS, N)
+    total = None
+    for _ in range(3 if out_ref.dtype == F32 else 1):
+        part = rest.astype(BF16)
+        rest = rest - part.astype(F32)
+        moved = dot(unfold_ref[...], part)
+        total = moved if total is None else total + moved
+    out_ref[HALF:] = total.astype(out_ref.dtype)
 
 
 def full(*shape):
@@ -351,19 +342,14 @@
 
     def gain(t, row, tables, name):
         return pl.pallas_call(
-            gain_kernel,
+            functools.partial(gain_kernel, t),
             out_shape=[
-                jax.ShapeDtypeStruct(plane, F32),
-                jax.ShapeDtypeStruct((ROWS, N), F32),
+                pltpu.VMEM(plane, F32),
+                pltpu.VMEM((ROWS, N), F32),
             ],
+            in_specs=[full(1, 1)] + kept * (2 + len(tables)),
+            out_specs=kept * 2,
             grid=(1,),
-            in_specs=[
-                full(1, 1),
-                full(*table.shape),
-                pl.BlockSpec((None,) + plane, lambda i: (t, 0, 0, 0)),
-            ]
-            + kept * len(tables),
-            out_specs=[full(*plane), full(ROWS, N)],
             compiler_params=params(12),
             cost_estimate=cost(8 * work, 3 << 20),
             name=name,
@@ -404,11 +390,14 @@
         return pl.pallas_call(
             functools.partial(match_kernel, t),
             out_shape=pltpu.VMEM((N, N), dtype),
-            grid=(deep // 2,),
             in_specs=kept * 6,
             out_specs=kept[0],
-            scratch_shapes=[pltpu.VMEM(plane, F32)],
-            compiler_params=params(12),
+            scratch_shapes=[
+                pltpu.VMEM((3, 2 * deep * FOLD, 2 * THIRD), BF16),
+                pltpu.VMEM((2, ROWS, 2 * deep * N), BF16),
+                pltpu.VMEM(plane, F32),
+            ],
+            compiler_params=params(24),
             cost_estimate=cost(2 * deep * 2 * work, 6 << 20),
             name=name,
         )(near_all, far_all, white, white_weight, back, unfold)

time: 52.6 us -> 52.2 us (level)
  Pallas kernels: 15.2 us -> 14.2 us
  waiting for transfers between devices: 9.94 us -> 10.5 us
    pallas_call x2, Pallas kernels: 8.11 us -> 7.12 us  [match(): pl.pallas_call(functools.partial(match_kernel, t), out_shape=pltpu.VMEM((...]
  transfers between devices with their start and end apart: 10 -> 10, of which waited for: 5 -> 5; matrix products, arithmetic and copies ran while one was open for 0% -> 0% of each run, Pallas kernels for 22% -> 21%
where the time goes in v12:
time: 52.2 us; the launch traced here: 51.9 us
  starting transfers between devices  24.5 us (47%)
  Pallas kernels  14.2 us (27%)
  waiting for transfers between devices  10.5 us (20%)
  other arithmetic  0.95 us (2%)
  local copies, waits for them, and re-layouts  0.88 us (2%)
  between operations  0.87 us (2%)
    all_to_all x1, starting transfers between devices, per_device(): images_all = lax.all_to_all(copies, LIB, 0, 0, tiled=False)  8.22 us
    pallas_call x2, Pallas kernels, match(): pl.pallas_call(functools.partial(match_kernel, t), out_shape=pltpu.VMEM((...  7.12 us
    all_to_all x1, waiting for transfers between devices, per_device(): images_all = lax.all_to_all(copies, LIB, 0, 0, tiled=False)  4.51 us
    ppermute x1, waiting for transfers between devices, per_device(): got = lax.ppermute(match(1, BF16, 'match_other'), 'xhi', swap)  4.32 us
    ppermute x3, starting transfers between devices, per_device(): lax.ppermute(pair, 'z', [(z, (z + dz) % deep) for z in range(deep)])  3.95 us
    ppermute x1, starting transfers between devices, per_device(): received = lax.ppermute(tile, 'xhi', swap)  3.57 us
    ppermute x1, starting transfers between devices, per_device(): far_all = lax.ppermute(near_all, 'core', swap)  3.29 us
    pallas_call x2, Pallas kernels, gain(): pl.pallas_call(functools.partial(gain_kernel, t), out_shape=[pltpu.VMEM(p...  2.2 us
  transfers between devices with their start and end apart: 10, of which 5 were waited for; matrix products, arithmetic and copies ran while one was open for 0% of the time, Pallas kernels for 21%

profile of v12, /device:TPU:1, one launch (start us, length us, event | category | flops | bytes accessed | tf_op | source)
XLA Modules:
  0.0 51.9 jit_solution(10762245747649244947)
XLA Ops:
  0.0 3.6 %collective-permute-start = (bf16[384,384]{1,0:T(8,128)(2,1)}, bf16[384,384]{1,0:T(8,128)(2,1)S(1)}, u32[]{:S(2)}, u32[]{:S(2)}) collective-permute-start(bf16[384,384]{1,0:T(8,128)(2,1)} %bitcast.11), channel_id=1, source_target_pairs={{0,2},{2,0},{1,3},{3,1},{4,6},{6,4},{5,7},{7,5},{8,10},{10,8},{9,1... | collective-permute-start | bytes 884744 | tf_op jit(solution)/shard_map/ppermute | solution.py:299
  3.6 1.9 %copies.1 = bf16[32,48,384]{2,1,0:T(8,128)(2,1)} custom-call(bf16[48,384]{1,0:T(8,128)(2,1)} %bitcast.13), custom_call_target="tpu_custom_call" | custom-call | bytes 1048576 | tf_op jit(solution)/shard_map/copies/pallas_call | solution.py:300
  5.4 0.0 copy-start
  5.4 0.0 copy-start.1
  5.5 8.2 %all-to-all-start = ((bf16[32,48,384]{2,1,0:T(8,128)(2,1)}), bf16[32,48,384]{2,1,0:T(8,128)(2,1)S(1)}, u32[]{:S(2)}, u32[]{:S(2)}) async-start(bf16[32,48,384]{2,1,0:T(8,128)(2,1)} %copies.1), calls=%async_computation | async-start | bytes 2359296 | tf_op jit(solution)/shard_map/all_to_all | solution.py:314
  14.3 0.0 collective-permute-done.other_ref
  14.4 0.0 copy-done
  14.4 0.0 copy-done.1
  14.4 0.0 copy-start.8
  14.4 0.0 copy-start.9
  14.4 0.0 copy-start.10
  14.4 0.0 copy-start.11
  14.4 0.0 copy-start.2
  14.4 0.0 copy-start.3
  14.4 0.9 %tile.1 = (f32[2,2,200,384]{3,2,1,0:T(8,128)S(1)}, bf16[104,384]{1,0:T(8,128)(2,1)S(1)}, bf16[104,384]{1,0:T(8,128)(2,1)S(1)}) custom-call(s32[1,1]{1,0:T(1,128)} %bitcast.core_ref, bf16[384,384]{1,0:T(8,128)(2,1)S(1)} %bitcast.12, bf16[384,384]{1,0:T(8,128)(2,1)S(1)} %collective-permute-done.other_ref, bf16[1168,256]{1,0:T(8,128)(2,1)S(1)} %copy-done), custom_call_target="tpu_custom_call" | custom-call | flops 31457280000 | bytes 3145728 | tf_op jit(solution)/shard_map/tile/pallas_call | solution.py:316
  15.3 0.0 copy-start.4
  15.3 1.3 %collective-permute-start.1 = (bf16[104,384]{1,0:T(8,128)(2,1)S(1)}, bf16[104,384]{1,0:T(8,128)(2,1)S(1)}, u32[]{:S(2)}, u32[]{:S(2)}) collective-permute-start(bf16[104,384]{1,0:T(8,128)(2,1)S(1)} %get-tuple-element.25), channel_id=1, source_target_pairs={{0,1},{1,0},{2,3},{3,2},{4,5},{5,4},{6,7},{7,6},{8,9},{9,8},{10,11... | collective-permute-start | bytes 239624 | tf_op jit(solution)/shard_map/ppermute | solution.py:332
  16.6 0.0 copy-done.8
  16.6 0.0 copy-done.9
  16.6 0.0 copy-done.10
  16.6 0.0 copy-done.11
  16.7 0.9 %collective-permute-done.1 = bf16[104,384]{1,0:T(8,128)(2,1)S(1)} collective-permute-done((bf16[104,384]{1,0:T(8,128)(2,1)S(1)}, bf16[104,384]{1,0:T(8,128)(2,1)S(1)}, u32[]{:S(2)}, u32[]{:S(2)}) %collective-permute-start.1) | collective-permute-done | bytes 79904 | tf_op jit(solution)/shard_map/ppermute | solution.py:332
  17.6 2.8 %collective-permute-start.4 = (bf16[104,384]{1,0:T(8,128)(2,1)S(1)}, bf16[104,384]{1,0:T(8,128)(2,1)S(1)}, u32[]{:S(2)}, u32[]{:S(2)}) collective-permute-start(bf16[104,384]{1,0:T(8,128)(2,1)S(1)} %add_convert_fusion.1), channel_id=1, source_target_pairs={{0,12},{4,0},{8,4},{12,8},{1,13},{5,1},{9,5},{13,9},{2,14},{6,2},{... | collective-permute-start | bytes 239624 | tf_op jit(solution)/shard_map/ppermute | solution.py:334
  20.4 0.6 %collective-permute-start.3 = (bf16[104,384]{1,0:T(8,128)(2,1)S(1)}, bf16[104,384]{1,0:T(8,128)(2,1)S(1)}, u32[]{:S(2)}, u32[]{:S(2)}) collective-permute-start(bf16[104,384]{1,0:T(8,128)(2,1)S(1)} %add_convert_fusion.1), channel_id=1, source_target_pairs={{0,8},{4,12},{8,0},{12,4},{1,9},{5,13},{9,1},{13,5},{2,10},{6,14},... | collective-permute-start | bytes 239624 | tf_op jit(solution)/shard_map/ppermute | solution.py:334
  20.9 0.6 %collective-permute-start.2 = (bf16[104,384]{1,0:T(8,128)(2,1)S(1)}, bf16[104,384]{1,0:T(8,128)(2,1)S(1)}, u32[]{:S(2)}, u32[]{:S(2)}) collective-permute-start(bf16[104,384]{1,0:T(8,128)(2,1)S(1)} %add_convert_fusion.1), channel_id=1, source_target_pairs={{0,4},{4,8},{8,12},{12,0},{1,5},{5,9},{9,13},{13,1},{2,6},{6,10},{... | collective-permute-start | bytes 239624 | tf_op jit(solution)/shard_map/ppermute | solution.py:334
  21.5 0.0 copy-done.2
  21.5 0.0 copy-done.3
  21.5 0.8 %gain_own.1 = (f32[2,200,384]{2,1,0:T(8,128)S(1)}, f32[200,384]{1,0:T(8,128)S(1)}) custom-call(s32[1,1]{1,0:T(1,128)S(6)} %copy.11.row_ref, f32[8,128]{1,0:T(8,128)S(1)} %select_maximum_fusion.table_ref, f32[2,2,200,384]{3,2,1,0:T(8,128)S(1)} %get-tuple-element.26.tile_ref, bf16[1168,256]{1,0:T(8,128)(2,1)S(1)} %copy-done, bf16[1184,256]{1,0:T(8,128)(2,1)S(1)} %copy-done.2, ...), custom_call_target="tpu_custom_call" | custom-call | flops 1258291200 | bytes 3145728 | tf_op jit(solution)/shard_map/gain_own/pallas_call | solution.py:344
  22.4 0.0 copy-done.4
  22.4 0.0 copy-start.6
  22.4 0.8 %copy-done.6 = f32[2,200,384]{2,1,0:T(8,128)} copy-done((f32[2,200,384]{2,1,0:T(8,128)}, f32[2,200,384]{2,1,0:T(8,128)S(1)}, u32[]{:S(2)}) %copy-start.6) | copy-done | bytes 614424
  23.2 1.7 %collective-permute-start.5 = (s32[1,1]{1,0:T(1,128)}, s32[1,1]{1,0:T(1,128)}, u32[]{:S(2)}, u32[]{:S(2)}) collective-permute-start(s32[1,1]{1,0:T(1,128)} %param.12), channel_id=1, source_target_pairs={{0,2},{2,0},{1,3},{3,1},{4,6},{6,4},{5,7},{7,5},{8,10},{10,8},{9,1... | collective-permute-start | bytes 20 | tf_op jit(solution)/shard_map/ppermute | solution.py:341
  24.9 4.5 %all-to-all-done = bf16[32,48,384]{2,1,0:T(8,128)(2,1)S(1)} async-done(((bf16[32,48,384]{2,1,0:T(8,128)(2,1)}), bf16[32,48,384]{2,1,0:T(8,128)(2,1)S(1)}, u32[]{:S(2)}, u32[]{:S(2)}) %all-to-all-start) | async-done | bytes 1179680 | tf_op jit(solution)/shard_map/all_to_all | solution.py:314
  29.4 0.0 copy-start.5
  29.4 1.7 %library.1.near_ref = bf16[4,2,200,384]{3,2,1,0:T(8,128)(2,1)S(1)} custom-call(bf16[8,4,48,384]{3,2,1,0:T(8,128)(2,1)S(1)} %bitcast.10, bf16[1168,256]{1,0:T(8,128)(2,1)S(1)} %copy-done), custom_call_target="tpu_custom_call" | custom-call | flops 629145600 | bytes 4194304 | tf_op jit(solution)/shard_map/library/pallas_call | solution.py:361
  31.2 3.3 %collective-permute-start.6 = (bf16[4,2,200,384]{3,2,1,0:T(8,128)(2,1)S(1)}, bf16[4,2,200,384]{3,2,1,0:T(8,128)(2,1)S(1)}, u32[]{:S(2)}, u32[]{:S(2)}) collective-permute-start(bf16[4,2,200,384]{3,2,1,0:T(8,128)(2,1)S(1)} %library.1.near_ref), channel_id=1, source_target_pairs={{0,1},{1,0},{2,3},{3,2},{4,5},{5,4},{6,7},{7,6},{8,9},{9,8},{10,11... | collective-permute-start | bytes 3686408 | tf_op jit(solution)/shard_map/ppermute | solution.py:371
  34.5 0.0 collective-permute-done.5.row_ref
  34.5 0.0 collective-permute-done.4
  34.5 0.0 collective-permute-done.3
  34.5 0.4 collective-permute-done.2
  35.0 0.0 copy-start.7
  35.0 0.5 collective-permute-start.7
  35.4 0.0 copy-done.5
  35.4 1.4 %gain_other.1 = (f32[2,200,384]{2,1,0:T(8,128)S(1)}, f32[200,384]{1,0:T(8,128)S(1)}) custom-call(s32[1,1]{1,0:T(1,128)} %collective-permute-done.5.row_ref, f32[8,128]{1,0:T(8,128)S(1)} %select_maximum_fusion.table_ref, f32[2,2,200,384]{3,2,1,0:T(8,128)S(1)} %copy-done.5), custom_call_target="tpu_custom_call" | custom-call | flops 1258291200 | bytes 3145728 | tf_op jit(solution)/shard_map/gain_other/pallas_call | solution.py:344
  36.8 0.3 collective-permute-done.7.theirs_ref
  37.1 0.0 copy-done.7
  37.1 0.5 whiten.1
  37.6 0.0 collective-permute-done.6.far_ref
  37.6 3.4 %match_other.1 = bf16[384,384]{1,0:T(8,128)(2,1)S(1)} custom-call(bf16[4,2,200,384]{3,2,1,0:T(8,128)(2,1)S(1)} %library.1.near_ref, bf16[4,2,200,384]{3,2,1,0:T(8,128)(2,1)S(1)} %collective-permute-done.6.far_ref, f32[2,2,200,384]{3,2,1,0:T(8,128)S(1)} %get-tuple-element.41.spec_ref, f32[2,200,384]{2,1,0:T(8,128)S(1)} %get-tuple-element.42.weight_ref, ...), custom_call_target="tpu_custom_call" | custom-call | flops 2516582400 | bytes 6291456 | tf_op jit(solution)/shard_map/match_other/pallas_call | solution.py:390
  41.1 2.0 %collective-permute-start.8 = (bf16[384,384]{1,0:T(8,128)(2,1)S(1)}, bf16[384,384]{1,0:T(8,128)(2,1)S(1)}, u32[]{:S(2)}, u32[]{:S(2)}) collective-permute-start(bf16[384,384]{1,0:T(8,128)(2,1)S(1)} %match_other.1), channel_id=1, source_target_pairs={{0,2},{2,0},{1,3},{3,1},{4,6},{6,4},{5,7},{7,5},{8,10},{10,8},{9,1... | collective-permute-start | bytes 884744 | tf_op jit(solution)/shard_map/ppermute | solution.py:405
  43.1 3.7 %match_own.1 = f32[384,384]{1,0:T(8,128)S(1)} custom-call(bf16[4,2,200,384]{3,2,1,0:T(8,128)(2,1)S(1)} %library.1.near_ref, bf16[4,2,200,384]{3,2,1,0:T(8,128)(2,1)S(1)} %collective-permute-done.6.far_ref, f32[2,2,200,384]{3,2,1,0:T(8,128)S(1)} %get-tuple-element.41.spec_ref, f32[2,200,384]{2,1,0:T(8,128)S(1)} %get-tuple-element.42.weight_ref, ...), custom_call_target="tpu_custom_call" | custom-call | flops 2516582400 | bytes 6291456 | tf_op jit(solution)/shard_map/match_own/pallas_call | solution.py:390
  46.8 4.3 %collective-permute-done.8 = bf16[384,384]{1,0:T(8,128)(2,1)S(1)} collective-permute-done((bf16[384,384]{1,0:T(8,128)(2,1)S(1)}, bf16[384,384]{1,0:T(8,128)(2,1)S(1)}, u32[]{:S(2)}, u32[]{:S(2)}) %collective-permute-start.8) | collective-permute-done | bytes 294944 | tf_op jit(solution)/shard_map/ppermute | solution.py:405
  51.1 0.9 %maximum_bitcast_fusion = f32[1,1,384,384]{3,2,1,0:T(8,128)} fusion(f32[384,384]{1,0:T(8,128)S(1)} %match_own.1, bf16[384,384]{1,0:T(8,128)(2,1)S(1)} %collective-permute-done.8), kind=kLoop, calls=%fused_computation | loop fusion | flops 294912 | bytes 1474560 | tf_op jit(solution)/shard_map/broadcast_in_dim | solution.py:407
  (3 shorter events, 0.1 us)
Async XLA Ops:
  0.0 14.3 %collective-permute-start = (bf16[384,384]{1,0:T(8,128)(2,1)}, bf16[384,384]{1,0:T(8,128)(2,1)S(1)}, u32[]{:S(2)}, u32[]{:S(2)}) collective-permute-start(bf16[384,384]{1,0:T(8,128)(2,1)} %bitcast.11), channel_id=1, source_target_pairs={{0,2},{2,0},{1,3},{3,1},{4,6},{6,4},{5,7},{7,5},{8,10},{10,8},{9,1... | collective-permute-start | bytes 884744 | tf_op jit(solution)/shard_map/ppermute | solution.py:299
  5.4 8.9 %copy-start = (bf16[1168,256]{1,0:T(8,128)(2,1)S(1)}, bf16[1168,256]{1,0:T(8,128)(2,1)}, u32[]{:S(2)}) copy-start(bf16[1168,256]{1,0:T(8,128)(2,1)} %constant.13.clone.tab_ref.refs_0_) | copy-start | bytes 1794052
  5.4 8.9 %copy-start.1 = (bf16[1,1,384,384]{3,2,1,0:T(8,128)(2,1)S(1)}, bf16[1,1,384,384]{3,2,1,0:T(8,128)(2,1)}, u32[]{:S(2)}) copy-start(bf16[1,1,384,384]{3,2,1,0:T(8,128)(2,1)} %param.10) | copy-start | bytes 884740
  5.5 24.0 %all-to-all-start = ((bf16[32,48,384]{2,1,0:T(8,128)(2,1)}), bf16[32,48,384]{2,1,0:T(8,128)(2,1)S(1)}, u32[]{:S(2)}, u32[]{:S(2)}) async-start(bf16[32,48,384]{2,1,0:T(8,128)(2,1)} %copies.1), calls=%async_computation | async-start | bytes 2359296 | tf_op jit(solution)/shard_map/all_to_all | solution.py:314
  14.4 2.3 %copy-start.8 = (f32[64]{0:T(128)S(1)}, f32[64]{0:T(128)}, u32[]{:S(2)}) copy-start(f32[64]{0:T(128)} %param.16) | copy-start | bytes 772
  14.4 2.2 %copy-start.9 = (f32[64]{0:T(128)S(1)}, f32[64]{0:T(128)}, u32[]{:S(2)}) copy-start(f32[64]{0:T(128)} %param.15) | copy-start | bytes 772
  14.4 2.2 %copy-start.10 = (f32[64]{0:T(128)S(1)}, f32[64]{0:T(128)}, u32[]{:S(2)}) copy-start(f32[64]{0:T(128)} %param.14) | copy-start | bytes 772
  14.4 2.2 %copy-start.11 = (f32[64]{0:T(128)S(1)}, f32[64]{0:T(128)}, u32[]{:S(2)}) copy-start(f32[64]{0:T(128)} %param.13) | copy-start | bytes 772
  14.4 7.1 %copy-start.2 = (bf16[1184,256]{1,0:T(8,128)(2,1)S(1)}, bf16[1184,256]{1,0:T(8,128)(2,1)}, u32[]{:S(2)}) copy-start(bf16[1184,256]{1,0:T(8,128)(2,1)} %constant.14.clone.refs_1_.refs_0_.tab_ref) | copy-start | bytes 1818628
  14.4 7.1 %copy-start.3 = (bf16[192,400]{1,0:T(8,128)(2,1)S(1)}, bf16[192,400]{1,0:T(8,128)(2,1)}, u32[]{:S(2)}) copy-start(bf16[192,400]{1,0:T(8,128)(2,1)} %constant.15.clone.refs_2_.refs_1_.unfold_ref) | copy-start | bytes 460804
  15.3 7.1 %copy-start.4 = (f32[2,2,200,384]{3,2,1,0:T(8,128)}, f32[2,2,200,384]{3,2,1,0:T(8,128)S(1)}, u32[]{:S(2)}) copy-start(f32[2,2,200,384]{3,2,1,0:T(8,128)S(1)} %get-tuple-element.26.tile_ref) | copy-start | bytes 3686404
  15.3 2.2 %collective-permute-start.1 = (bf16[104,384]{1,0:T(8,128)(2,1)S(1)}, bf16[104,384]{1,0:T(8,128)(2,1)S(1)}, u32[]{:S(2)}, u32[]{:S(2)}) collective-permute-start(bf16[104,384]{1,0:T(8,128)(2,1)S(1)} %get-tuple-element.25), channel_id=1, source_target_pairs={{0,1},{1,0},{2,3},{3,2},{4,5},{5,4},{6,7},{7,6},{8,9},{9,8},{10,11... | collective-permute-start | bytes 239624 | tf_op jit(solution)/shard_map/ppermute | solution.py:332
  17.6 16.9 %collective-permute-start.4 = (bf16[104,384]{1,0:T(8,128)(2,1)S(1)}, bf16[104,384]{1,0:T(8,128)(2,1)S(1)}, u32[]{:S(2)}, u32[]{:S(2)}) collective-permute-start(bf16[104,384]{1,0:T(8,128)(2,1)S(1)} %add_convert_fusion.1), channel_id=1, source_target_pairs={{0,12},{4,0},{8,4},{12,8},{1,13},{5,1},{9,5},{13,9},{2,14},{6,2},{... | collective-permute-start | bytes 239624 | tf_op jit(solution)/shard_map/ppermute | solution.py:334
  20.4 14.1 %collective-permute-start.3 = (bf16[104,384]{1,0:T(8,128)(2,1)S(1)}, bf16[104,384]{1,0:T(8,128)(2,1)S(1)}, u32[]{:S(2)}, u32[]{:S(2)}) collective-permute-start(bf16[104,384]{1,0:T(8,128)(2,1)S(1)} %add_convert_fusion.1), channel_id=1, source_target_pairs={{0,8},{4,12},{8,0},{12,4},{1,9},{5,13},{9,1},{13,5},{2,10},{6,14},... | collective-permute-start | bytes 239624 | tf_op jit(solution)/shard_map/ppermute | solution.py:334
  20.9 14.0 %collective-permute-start.2 = (bf16[104,384]{1,0:T(8,128)(2,1)S(1)}, bf16[104,384]{1,0:T(8,128)(2,1)S(1)}, u32[]{:S(2)}, u32[]{:S(2)}) collective-permute-start(bf16[104,384]{1,0:T(8,128)(2,1)S(1)} %add_convert_fusion.1), channel_id=1, source_target_pairs={{0,4},{4,8},{8,12},{12,0},{1,5},{5,9},{9,13},{13,1},{2,6},{6,10},{... | collective-permute-start | bytes 239624 | tf_op jit(solution)/shard_map/ppermute | solution.py:334
  22.4 0.8 %copy-start.6 = (f32[2,200,384]{2,1,0:T(8,128)}, f32[2,200,384]{2,1,0:T(8,128)S(1)}, u32[]{:S(2)}) copy-start(f32[2,200,384]{2,1,0:T(8,128)S(1)} %get-tuple-element.32.own_ref) | copy-start | bytes 1843204
  23.2 11.3 %collective-permute-start.5 = (s32[1,1]{1,0:T(1,128)}, s32[1,1]{1,0:T(1,128)}, u32[]{:S(2)}, u32[]{:S(2)}) collective-permute-start(s32[1,1]{1,0:T(1,128)} %param.12), channel_id=1, source_target_pairs={{0,2},{2,0},{1,3},{3,1},{4,6},{6,4},{5,7},{7,5},{8,10},{10,8},{9,1... | collective-permute-start | bytes 20 | tf_op jit(solution)/shard_map/ppermute | solution.py:341
  29.4 6.0 %copy-start.5 = (f32[2,2,200,384]{3,2,1,0:T(8,128)S(1)}, f32[2,2,200,384]{3,2,1,0:T(8,128)}, u32[]{:S(2)}) copy-start(f32[2,2,200,384]{3,2,1,0:T(8,128)} %copy-done.4) | copy-start | bytes 3686404
  31.2 6.5 %collective-permute-start.6 = (bf16[4,2,200,384]{3,2,1,0:T(8,128)(2,1)S(1)}, bf16[4,2,200,384]{3,2,1,0:T(8,128)(2,1)S(1)}, u32[]{:S(2)}, u32[]{:S(2)}) collective-permute-start(bf16[4,2,200,384]{3,2,1,0:T(8,128)(2,1)S(1)} %library.1.near_ref), channel_id=1, source_target_pairs={{0,1},{1,0},{2,3},{3,2},{4,5},{5,4},{6,7},{7,6},{8,9},{9,8},{10,11... | collective-permute-start | bytes 3686408 | tf_op jit(solution)/shard_map/ppermute | solution.py:371
  35.0 2.2 %copy-start.7 = (f32[2,200,384]{2,1,0:T(8,128)S(1)}, f32[2,200,384]{2,1,0:T(8,128)}, u32[]{:S(2)}) copy-start(f32[2,200,384]{2,1,0:T(8,128)} %copy-done.6) | copy-start | bytes 1843204
  35.0 2.1 %collective-permute-start.7 = (bf16[104,384]{1,0:T(8,128)(2,1)S(1)}, bf16[104,384]{1,0:T(8,128)(2,1)S(1)}, u32[]{:S(2)}, u32[]{:S(2)}) collective-permute-start(bf16[104,384]{1,0:T(8,128)(2,1)S(1)} %add_convert_fusion.mine_ref), channel_id=1, source_target_pairs={{0,1},{1,0},{2,3},{3,2},{4,5},{5,4},{6,7},{7,6},{8,9},{9,8},{10,11... | collective-permute-start | bytes 239624 | tf_op jit(solution)/shard_map/ppermute | solution.py:375
  41.1 10.0 %collective-permute-start.8 = (bf16[384,384]{1,0:T(8,128)(2,1)S(1)}, bf16[384,384]{1,0:T(8,128)(2,1)S(1)}, u32[]{:S(2)}, u32[]{:S(2)}) collective-permute-start(bf16[384,384]{1,0:T(8,128)(2,1)S(1)} %match_other.1), channel_id=1, source_target_pairs={{0,2},{2,0},{1,3},{3,1},{4,6},{6,4},{5,7},{7,5},{8,10},{10,8},{9,1... | collective-permute-start | bytes 884744 | tf_op jit(solution)/shard_map/ppermute | solution.py:405

commit v13 on v12

--- a/solution.py
+++ b/solution.py
@@ -193,11 +193,10 @@
     spec_ref[1] = tile_ref[t, 1] * gain
 
 
-def library_kernel(image_ref, tab_ref, out_ref):
-    step = pl.program_id(0)
-    for i in range(2):
-        image = image_ref[:, 2 * step + i].reshape(N, N)
-        store_spectrum(out_ref.at[2 * step + i], half_spectrum(image, tab_ref))
+def library_kernel(first, image_ref, tab_ref, out_ref):
+    for i in range(out_ref.shape[0]):
+        image = image_ref[:, first + i].reshape(N, N)
+        store_spectrum(out_ref.at[i], half_spectrum(image, tab_ref))
 
 
 def whiten_kernel(
@@ -217,16 +216,16 @@
         weight_out[t] = weight[...] * inverse_noise
 
 
-def match_kernel(
-    t, near_ref, far_ref, spec_ref, weight_ref, tab_ref, unfold_ref, out_ref, p_sc, h_sc, best_sc
-):
+def match_kernel(t, *refs):
+    libs, refs = refs[:4], refs[4:]
+    spec_ref, weight_ref, tab_ref, unfold_ref, out_ref, p_sc, h_sc, best_sc = refs
     wide = 2 * THIRD
-    count = 2 * near_ref.shape[0]
+    count = 4 * libs[0].shape[0]
     s_re, s_im = spec_ref[t, 0], spec_ref[t, 1]
     scales = []
     for j in range(count):
-        ref = (near_ref, far_ref)[j % 2]
-        re, im = ref[j // 2, 0].astype(F32), ref[j // 2, 1].astype(F32)
+        ref = libs[j % 4]
+        re, im = ref[j // 4, 0].astype(F32), ref[j // 4, 1].astype(F32)
         norm = jnp.sum((re * re + im * im) * weight_ref[t])
         scales.append(lax.rsqrt(jnp.full((1, THIRD), norm + 1e-06, F32)))
         p_re = (s_re * re + s_im * im).astype(BF16)
@@ -358,18 +357,22 @@
     own = gain(0, ctf_row, (ahead, back, unfold), "gain_own")
     images_all, pair, own = lax.optimization_barrier((images_all, pair, own))
 
-    near_all = pl.pallas_call(
-        library_kernel,
-        out_shape=pltpu.VMEM((deep,) + plane, BF16),
-        grid=(deep // 2,),
-        in_specs=kept * 2,
-        out_specs=kept[0],
-        compiler_params=params(12),
-        cost_estimate=cost(deep * work, 4 << 20),
-        name="library",
-    )(images_all.reshape(groups, deep, N // groups, N), ahead)
-    far_all = lax.ppermute(near_all, "core", swap)
-    moves, near_all, mate = lax.optimization_barrier((moves, near_all, mate))
+    images_all = images_all.reshape(groups, deep, N // groups, N)
+    near = [
+        pl.pallas_call(
+            functools.partial(library_kernel, first),
+            out_shape=pltpu.VMEM((deep // 2,) + plane, BF16),
+            in_specs=kept * 2,
+            out_specs=kept[0],
+            compiler_params=params(12),
+            cost_estimate=cost(deep // 2 * work, 3 << 20),
+            name="library",
+        )(images_all, ahead)
+        for first in (0, deep // 2)
+    ]
+    far = [lax.ppermute(part, "core", swap) for part in near]
+
+    moves, near, mate = lax.optimization_barrier((moves, near, mate))
     other = gain(1, mate, (), "gain_other")
     mine = sum((m.astype(F32) for m in moves), pair.astype(F32)).astype(BF16)
     theirs = lax.ppermute(mine, "core", swap)
@@ -390,7 +393,7 @@
         return pl.pallas_call(
             functools.partial(match_kernel, t),
             out_shape=pltpu.VMEM((N, N), dtype),
-            in_specs=kept * 6,
+            in_specs=kept * 8,
             out_specs=kept[0],
             scratch_shapes=[
                 pltpu.VMEM((3, 2 * deep * FOLD, 2 * THIRD), BF16),
@@ -400,7 +403,7 @@
             compiler_params=params(24),
             cost_estimate=cost(2 * deep * 2 * work, 6 << 20),
             name=name,
-        )(near_all, far_all, white, white_weight, back, unfold)
+        )(*near, *far, white, white_weight, back, unfold)
 
     got = lax.ppermute(match(1, BF16, "match_other"), "xhi", swap)
     best = match(0, F32, "match_own")

time: 52.2 us -> 52.4 us (level)
    ppermute x1 -> x2, starting transfers between devices: 3.29 us -> 3.38 us  [per_device(): far = [lax.ppermute(part, 'core', swap) for part in near]]
    pallas_call x1 -> x2, Pallas kernels: 1.73 us -> 1.69 us  [per_device(): pl.pallas_call(functools.partial(library_kernel, first), out_shape=pltpu....]
  transfers between devices with their start and end apart: 10 -> 11, of which waited for: 5 -> 4; matrix products, arithmetic and copies ran while one was open for 0% -> 0% of each run, Pallas kernels for 21% -> 21%
where the time goes in v13:
time: 52.4 us; the launch traced here: 52.1 us
  starting transfers between devices  24.6 us (47%)
  Pallas kernels  14.4 us (27%)
  waiting for transfers between devices  10.3 us (20%)
  other arithmetic  0.95 us (2%)
  between operations  0.93 us (2%)
  local copies, waits for them, and re-layouts  0.88 us (2%)
    all_to_all x1, starting transfers between devices, per_device(): images_all = lax.all_to_all(copies, LIB, 0, 0, tiled=False)  8.22 us
    pallas_call x2, Pallas kernels, match(): pl.pallas_call(functools.partial(match_kernel, t), out_shape=pltpu.VMEM((...  7.21 us
    ppermute x1, waiting for transfers between devices, per_device(): got = lax.ppermute(match(1, BF16, 'match_other'), 'xhi', swap)  4.51 us
    all_to_all x1, waiting for transfers between devices, per_device(): images_all = lax.all_to_all(copies, LIB, 0, 0, tiled=False)  4.51 us
    ppermute x3, starting transfers between devices, per_device(): lax.ppermute(pair, 'z', [(z, (z + dz) % deep) for z in range(deep)])  3.95 us
    ppermute x1, starting transfers between devices, per_device(): received = lax.ppermute(tile, 'xhi', swap)  3.57 us
    ppermute x2, starting transfers between devices, per_device(): far = [lax.ppermute(part, 'core', swap) for part in near]  3.38 us
    pallas_call x2, Pallas kernels, gain(): pl.pallas_call(functools.partial(gain_kernel, t), out_shape=[pltpu.VMEM(p...  2.33 us
  transfers between devices with their start and end apart: 11, of which 4 were waited for; matrix products, arithmetic and copies ran while one was open for 0% of the time, Pallas kernels for 21%

profile of v13, /device:TPU:1, one launch (start us, length us, event | category | flops | bytes accessed | tf_op | source)
XLA Modules:
  0.0 52.1 jit_solution(14774179413889770953)
XLA Ops:
  0.0 3.6 %collective-permute-start = (bf16[384,384]{1,0:T(8,128)(2,1)}, bf16[384,384]{1,0:T(8,128)(2,1)S(1)}, u32[]{:S(2)}, u32[]{:S(2)}) collective-permute-start(bf16[384,384]{1,0:T(8,128)(2,1)} %bitcast.12), channel_id=1, source_target_pairs={{0,2},{2,0},{1,3},{3,1},{4,6},{6,4},{5,7},{7,5},{8,10},{10,8},{9,1... | collective-permute-start | bytes 884744 | tf_op jit(solution)/shard_map/ppermute | solution.py:298
  3.6 1.8 %copies.1 = bf16[32,48,384]{2,1,0:T(8,128)(2,1)} custom-call(bf16[48,384]{1,0:T(8,128)(2,1)} %bitcast.14), custom_call_target="tpu_custom_call" | custom-call | bytes 1048576 | tf_op jit(solution)/shard_map/copies/pallas_call | solution.py:299
  5.4 0.0 copy-start
  5.4 0.0 copy-start.1
  5.5 8.2 %all-to-all-start = ((bf16[32,48,384]{2,1,0:T(8,128)(2,1)}), bf16[32,48,384]{2,1,0:T(8,128)(2,1)S(1)}, u32[]{:S(2)}, u32[]{:S(2)}) async-start(bf16[32,48,384]{2,1,0:T(8,128)(2,1)} %copies.1), calls=%async_computation | async-start | bytes 2359296 | tf_op jit(solution)/shard_map/all_to_all | solution.py:313
  14.3 0.0 collective-permute-done.other_ref
  14.4 0.0 copy-done
  14.4 0.0 copy-done.1
  14.4 0.0 copy-start.8
  14.4 0.0 copy-start.9
  14.4 0.0 copy-start.10
  14.4 0.0 copy-start.11
  14.4 0.0 copy-start.2
  14.4 0.0 copy-start.3
  14.4 0.9 %tile.1 = (f32[2,2,200,384]{3,2,1,0:T(8,128)S(1)}, bf16[104,384]{1,0:T(8,128)(2,1)S(1)}, bf16[104,384]{1,0:T(8,128)(2,1)S(1)}) custom-call(s32[1,1]{1,0:T(1,128)} %bitcast.core_ref, bf16[384,384]{1,0:T(8,128)(2,1)S(1)} %bitcast.13, bf16[384,384]{1,0:T(8,128)(2,1)S(1)} %collective-permute-done.other_ref, bf16[1168,256]{1,0:T(8,128)(2,1)S(1)} %copy-done), custom_call_target="tpu_custom_call" | custom-call | flops 31457280000 | bytes 3145728 | tf_op jit(solution)/shard_map/tile/pallas_call | solution.py:315
  15.3 0.0 copy-start.4
  15.3 1.3 %collective-permute-start.1 = (bf16[104,384]{1,0:T(8,128)(2,1)S(1)}, bf16[104,384]{1,0:T(8,128)(2,1)S(1)}, u32[]{:S(2)}, u32[]{:S(2)}) collective-permute-start(bf16[104,384]{1,0:T(8,128)(2,1)S(1)} %get-tuple-element.26), channel_id=1, source_target_pairs={{0,1},{1,0},{2,3},{3,2},{4,5},{5,4},{6,7},{7,6},{8,9},{9,8},{10,11... | collective-permute-start | bytes 239624 | tf_op jit(solution)/shard_map/ppermute | solution.py:331
  16.6 0.0 copy-done.8
  16.6 0.0 copy-done.9
  16.6 0.0 copy-done.10
  16.6 0.0 copy-done.11
  16.7 0.9 %collective-permute-done.1 = bf16[104,384]{1,0:T(8,128)(2,1)S(1)} collective-permute-done((bf16[104,384]{1,0:T(8,128)(2,1)S(1)}, bf16[104,384]{1,0:T(8,128)(2,1)S(1)}, u32[]{:S(2)}, u32[]{:S(2)}) %collective-permute-start.1) | collective-permute-done | bytes 79904 | tf_op jit(solution)/shard_map/ppermute | solution.py:331
  17.6 2.8 %collective-permute-start.4 = (bf16[104,384]{1,0:T(8,128)(2,1)S(1)}, bf16[104,384]{1,0:T(8,128)(2,1)S(1)}, u32[]{:S(2)}, u32[]{:S(2)}) collective-permute-start(bf16[104,384]{1,0:T(8,128)(2,1)S(1)} %add_convert_fusion.1), channel_id=1, source_target_pairs={{0,12},{4,0},{8,4},{12,8},{1,13},{5,1},{9,5},{13,9},{2,14},{6,2},{... | collective-permute-start | bytes 239624 | tf_op jit(solution)/shard_map/ppermute | solution.py:333
  20.4 0.6 %collective-permute-start.3 = (bf16[104,384]{1,0:T(8,128)(2,1)S(1)}, bf16[104,384]{1,0:T(8,128)(2,1)S(1)}, u32[]{:S(2)}, u32[]{:S(2)}) collective-permute-start(bf16[104,384]{1,0:T(8,128)(2,1)S(1)} %add_convert_fusion.1), channel_id=1, source_target_pairs={{0,8},{4,12},{8,0},{12,4},{1,9},{5,13},{9,1},{13,5},{2,10},{6,14},... | collective-permute-start | bytes 239624 | tf_op jit(solution)/shard_map/ppermute | solution.py:333
  20.9 0.6 %collective-permute-start.2 = (bf16[104,384]{1,0:T(8,128)(2,1)S(1)}, bf16[104,384]{1,0:T(8,128)(2,1)S(1)}, u32[]{:S(2)}, u32[]{:S(2)}) collective-permute-start(bf16[104,384]{1,0:T(8,128)(2,1)S(1)} %add_convert_fusion.1), channel_id=1, source_target_pairs={{0,4},{4,8},{8,12},{12,0},{1,5},{5,9},{9,13},{13,1},{2,6},{6,10},{... | collective-permute-start | bytes 239624 | tf_op jit(solution)/shard_map/ppermute | solution.py:333
  21.5 0.0 copy-done.2
  21.5 0.0 copy-done.3
  21.5 0.8 %gain_own.1 = (f32[2,200,384]{2,1,0:T(8,128)S(1)}, f32[200,384]{1,0:T(8,128)S(1)}) custom-call(s32[1,1]{1,0:T(1,128)S(6)} %copy.11.row_ref, f32[8,128]{1,0:T(8,128)S(1)} %select_maximum_fusion.table_ref, f32[2,2,200,384]{3,2,1,0:T(8,128)S(1)} %get-tuple-element.27.tile_ref, bf16[1168,256]{1,0:T(8,128)(2,1)S(1)} %copy-done, bf16[1184,256]{1,0:T(8,128)(2,1)S(1)} %copy-done.2, ...), custom_call_target="tpu_custom_call" | custom-call | flops 1258291200 | bytes 3145728 | tf_op jit(solution)/shard_map/gain_own/pallas_call | solution.py:343
  22.4 0.0 copy-done.4
  22.4 0.0 copy-start.6
  22.4 0.8 %copy-done.6 = f32[2,200,384]{2,1,0:T(8,128)} copy-done((f32[2,200,384]{2,1,0:T(8,128)}, f32[2,200,384]{2,1,0:T(8,128)S(1)}, u32[]{:S(2)}) %copy-start.6) | copy-done | bytes 614424
  23.2 1.7 %collective-permute-start.5 = (s32[1,1]{1,0:T(1,128)}, s32[1,1]{1,0:T(1,128)}, u32[]{:S(2)}, u32[]{:S(2)}) collective-permute-start(s32[1,1]{1,0:T(1,128)} %param.12), channel_id=1, source_target_pairs={{0,2},{2,0},{1,3},{3,1},{4,6},{6,4},{5,7},{7,5},{8,10},{10,8},{9,1... | collective-permute-start | bytes 20 | tf_op jit(solution)/shard_map/ppermute | solution.py:340
  24.9 4.5 %all-to-all-done = bf16[32,48,384]{2,1,0:T(8,128)(2,1)S(1)} async-done(((bf16[32,48,384]{2,1,0:T(8,128)(2,1)}), bf16[32,48,384]{2,1,0:T(8,128)(2,1)S(1)}, u32[]{:S(2)}, u32[]{:S(2)}) %all-to-all-start) | async-done | bytes 1179680 | tf_op jit(solution)/shard_map/all_to_all | solution.py:313
  29.4 0.8 %library.2.refs_0_ = bf16[2,2,200,384]{3,2,1,0:T(8,128)(2,1)S(1)} custom-call(bf16[8,4,48,384]{3,2,1,0:T(8,128)(2,1)S(1)} %bitcast.10, bf16[1168,256]{1,0:T(8,128)(2,1)S(1)} %copy-done), custom_call_target="tpu_custom_call" | custom-call | flops 314572800 | bytes 3145728 | tf_op jit(solution)/shard_map/library/pallas_call | solution.py:362
  30.3 0.0 copy-start.5
  30.3 3.3 %collective-permute-start.6 = (bf16[2,2,200,384]{3,2,1,0:T(8,128)(2,1)S(1)}, bf16[2,2,200,384]{3,2,1,0:T(8,128)(2,1)S(1)}, u32[]{:S(2)}, u32[]{:S(2)}) collective-permute-start(bf16[2,2,200,384]{3,2,1,0:T(8,128)(2,1)S(1)} %library.2.refs_0_), channel_id=1, source_target_pairs={{0,1},{1,0},{2,3},{3,2},{4,5},{5,4},{6,7},{7,6},{8,9},{9,8},{10,11... | collective-permute-start | bytes 1843208 | tf_op jit(solution)/shard_map/ppermute | solution.py:373
  33.6 0.8 %library.3.refs_1_ = bf16[2,2,200,384]{3,2,1,0:T(8,128)(2,1)S(1)} custom-call(bf16[8,4,48,384]{3,2,1,0:T(8,128)(2,1)S(1)} %bitcast.11, bf16[1168,256]{1,0:T(8,128)(2,1)S(1)} %copy-done), custom_call_target="tpu_custom_call" | custom-call | flops 314572800 | bytes 3145728 | tf_op jit(solution)/shard_map/library/pallas_call | solution.py:362
  34.4 0.0 collective-permute-done.5.row_ref
  34.4 0.1 collective-permute-start.7
  34.5 0.0 collective-permute-done.4
  34.5 0.0 collective-permute-done.3
  34.6 0.4 collective-permute-done.2
  35.0 0.0 copy-start.7
  35.0 0.5 collective-permute-start.8
  35.4 0.0 copy-done.5
  35.4 1.5 %gain_other.1 = (f32[2,200,384]{2,1,0:T(8,128)S(1)}, f32[200,384]{1,0:T(8,128)S(1)}) custom-call(s32[1,1]{1,0:T(1,128)} %collective-permute-done.5.row_ref, f32[8,128]{1,0:T(8,128)S(1)} %select_maximum_fusion.table_ref, f32[2,2,200,384]{3,2,1,0:T(8,128)S(1)} %copy-done.5), custom_call_target="tpu_custom_call" | custom-call | flops 1258291200 | bytes 3145728 | tf_op jit(solution)/shard_map/gain_other/pallas_call | solution.py:343
  37.0 0.0 collective-permute-done.8.theirs_ref
  37.0 0.0 copy-done.7
  37.0 0.5 whiten.1
  37.5 0.0 collective-permute-done.6.refs_2_
  37.5 0.0 collective-permute-done.7.refs_3_
  37.5 3.5 %match_other.1 = bf16[384,384]{1,0:T(8,128)(2,1)S(1)} custom-call(bf16[2,2,200,384]{3,2,1,0:T(8,128)(2,1)S(1)} %library.2.refs_0_, bf16[2,2,200,384]{3,2,1,0:T(8,128)(2,1)S(1)} %library.3.refs_1_, bf16[2,2,200,384]{3,2,1,0:T(8,128)(2,1)S(1)} %collective-permute-done.6.refs_2_, bf16[2,2,200,384]{3,2,1,0:T(8,128)(2,1)S(1)} %collective-permute-done.7.refs_3_, ...), custom_call_target="tpu_custom_call" | custom-call | flops 2516582400 | bytes 6291456 | tf_op jit(solution)/shard_map/match_other/pallas_call | solution.py:393
  41.0 2.0 %collective-permute-start.9 = (bf16[384,384]{1,0:T(8,128)(2,1)S(1)}, bf16[384,384]{1,0:T(8,128)(2,1)S(1)}, u32[]{:S(2)}, u32[]{:S(2)}) collective-permute-start(bf16[384,384]{1,0:T(8,128)(2,1)S(1)} %match_other.1), channel_id=1, source_target_pairs={{0,2},{2,0},{1,3},{3,1},{4,6},{6,4},{5,7},{7,5},{8,10},{10,8},{9,1... | collective-permute-start | bytes 884744 | tf_op jit(solution)/shard_map/ppermute | solution.py:408
  43.0 3.7 %match_own.1 = f32[384,384]{1,0:T(8,128)S(1)} custom-call(bf16[2,2,200,384]{3,2,1,0:T(8,128)(2,1)S(1)} %library.2.refs_0_, bf16[2,2,200,384]{3,2,1,0:T(8,128)(2,1)S(1)} %library.3.refs_1_, bf16[2,2,200,384]{3,2,1,0:T(8,128)(2,1)S(1)} %collective-permute-done.6.refs_2_, bf16[2,2,200,384]{3,2,1,0:T(8,128)(2,1)S(1)} %collective-permute-done.7.refs_3_, ...), custom_call_target="tpu_custom_call" | custom-call | flops 2516582400 | bytes 6291456 | tf_op jit(solution)/shard_map/match_own/pallas_call | solution.py:393
  46.7 4.5 %collective-permute-done.9 = bf16[384,384]{1,0:T(8,128)(2,1)S(1)} collective-permute-done((bf16[384,384]{1,0:T(8,128)(2,1)S(1)}, bf16[384,384]{1,0:T(8,128)(2,1)S(1)}, u32[]{:S(2)}, u32[]{:S(2)}) %collective-permute-start.9) | collective-permute-done | bytes 294944 | tf_op jit(solution)/shard_map/ppermute | solution.py:408
  51.2 0.9 %maximum_bitcast_fusion = f32[1,1,384,384]{3,2,1,0:T(8,128)} fusion(f32[384,384]{1,0:T(8,128)S(1)} %match_own.1, bf16[384,384]{1,0:T(8,128)(2,1)S(1)} %collective-permute-done.9), kind=kLoop, calls=%fused_computation | loop fusion | flops 294912 | bytes 1474560 | tf_op jit(solution)/shard_map/broadcast_in_dim | solution.py:410
  (3 shorter events, 0.1 us)
Async XLA Ops:
  0.0 14.3 %collective-permute-start = (bf16[384,384]{1,0:T(8,128)(2,1)}, bf16[384,384]{1,0:T(8,128)(2,1)S(1)}, u32[]{:S(2)}, u32[]{:S(2)}) collective-permute-start(bf16[384,384]{1,0:T(8,128)(2,1)} %bitcast.12), channel_id=1, source_target_pairs={{0,2},{2,0},{1,3},{3,1},{4,6},{6,4},{5,7},{7,5},{8,10},{10,8},{9,1... | collective-permute-start | bytes 884744 | tf_op jit(solution)/shard_map/ppermute | solution.py:298
  5.4 8.9 %copy-start = (bf16[1168,256]{1,0:T(8,128)(2,1)S(1)}, bf16[1168,256]{1,0:T(8,128)(2,1)}, u32[]{:S(2)}) copy-start(bf16[1168,256]{1,0:T(8,128)(2,1)} %constant.13.clone.tab_ref.refs_0_) | copy-start | bytes 1794052
  5.4 8.9 %copy-start.1 = (bf16[1,1,384,384]{3,2,1,0:T(8,128)(2,1)S(1)}, bf16[1,1,384,384]{3,2,1,0:T(8,128)(2,1)}, u32[]{:S(2)}) copy-start(bf16[1,1,384,384]{3,2,1,0:T(8,128)(2,1)} %param.10) | copy-start | bytes 884740
  5.5 24.0 %all-to-all-start = ((bf16[32,48,384]{2,1,0:T(8,128)(2,1)}), bf16[32,48,384]{2,1,0:T(8,128)(2,1)S(1)}, u32[]{:S(2)}, u32[]{:S(2)}) async-start(bf16[32,48,384]{2,1,0:T(8,128)(2,1)} %copies.1), calls=%async_computation | async-start | bytes 2359296 | tf_op jit(solution)/shard_map/all_to_all | solution.py:313
  14.4 2.3 %copy-start.8 = (f32[64]{0:T(128)S(1)}, f32[64]{0:T(128)}, u32[]{:S(2)}) copy-start(f32[64]{0:T(128)} %param.16) | copy-start | bytes 772
  14.4 2.2 %copy-start.9 = (f32[64]{0:T(128)S(1)}, f32[64]{0:T(128)}, u32[]{:S(2)}) copy-start(f32[64]{0:T(128)} %param.15) | copy-start | bytes 772
  14.4 2.2 %copy-start.10 = (f32[64]{0:T(128)S(1)}, f32[64]{0:T(128)}, u32[]{:S(2)}) copy-start(f32[64]{0:T(128)} %param.14) | copy-start | bytes 772
  14.4 2.2 %copy-start.11 = (f32[64]{0:T(128)S(1)}, f32[64]{0:T(128)}, u32[]{:S(2)}) copy-start(f32[64]{0:T(128)} %param.13) | copy-start | bytes 772
  14.4 7.1 %copy-start.2 = (bf16[1184,256]{1,0:T(8,128)(2,1)S(1)}, bf16[1184,256]{1,0:T(8,128)(2,1)}, u32[]{:S(2)}) copy-start(bf16[1184,256]{1,0:T(8,128)(2,1)} %constant.14.clone.refs_1_.refs_0_.refs_6_) | copy-start | bytes 1818628
  14.4 7.1 %copy-start.3 = (bf16[192,400]{1,0:T(8,128)(2,1)S(1)}, bf16[192,400]{1,0:T(8,128)(2,1)}, u32[]{:S(2)}) copy-start(bf16[192,400]{1,0:T(8,128)(2,1)} %constant.15.clone.refs_2_.refs_1_.refs_7_) | copy-start | bytes 460804
  15.3 7.1 %copy-start.4 = (f32[2,2,200,384]{3,2,1,0:T(8,128)}, f32[2,2,200,384]{3,2,1,0:T(8,128)S(1)}, u32[]{:S(2)}) copy-start(f32[2,2,200,384]{3,2,1,0:T(8,128)S(1)} %get-tuple-element.27.tile_ref) | copy-start | bytes 3686404
  15.3 2.2 %collective-permute-start.1 = (bf16[104,384]{1,0:T(8,128)(2,1)S(1)}, bf16[104,384]{1,0:T(8,128)(2,1)S(1)}, u32[]{:S(2)}, u32[]{:S(2)}) collective-permute-start(bf16[104,384]{1,0:T(8,128)(2,1)S(1)} %get-tuple-element.26), channel_id=1, source_target_pairs={{0,1},{1,0},{2,3},{3,2},{4,5},{5,4},{6,7},{7,6},{8,9},{9,8},{10,11... | collective-permute-start | bytes 239624 | tf_op jit(solution)/shard_map/ppermute | solution.py:331
  17.6 17.0 %collective-permute-start.4 = (bf16[104,384]{1,0:T(8,128)(2,1)S(1)}, bf16[104,384]{1,0:T(8,128)(2,1)S(1)}, u32[]{:S(2)}, u32[]{:S(2)}) collective-permute-start(bf16[104,384]{1,0:T(8,128)(2,1)S(1)} %add_convert_fusion.1), channel_id=1, source_target_pairs={{0,12},{4,0},{8,4},{12,8},{1,13},{5,1},{9,5},{13,9},{2,14},{6,2},{... | collective-permute-start | bytes 239624 | tf_op jit(solution)/shard_map/ppermute | solution.py:333
  20.4 14.2 %collective-permute-start.3 = (bf16[104,384]{1,0:T(8,128)(2,1)S(1)}, bf16[104,384]{1,0:T(8,128)(2,1)S(1)}, u32[]{:S(2)}, u32[]{:S(2)}) collective-permute-start(bf16[104,384]{1,0:T(8,128)(2,1)S(1)} %add_convert_fusion.1), channel_id=1, source_target_pairs={{0,8},{4,12},{8,0},{12,4},{1,9},{5,13},{9,1},{13,5},{2,10},{6,14},... | collective-permute-start | bytes 239624 | tf_op jit(solution)/shard_map/ppermute | solution.py:333
  20.9 14.0 %collective-permute-start.2 = (bf16[104,384]{1,0:T(8,128)(2,1)S(1)}, bf16[104,384]{1,0:T(8,128)(2,1)S(1)}, u32[]{:S(2)}, u32[]{:S(2)}) collective-permute-start(bf16[104,384]{1,0:T(8,128)(2,1)S(1)} %add_convert_fusion.1), channel_id=1, source_target_pairs={{0,4},{4,8},{8,12},{12,0},{1,5},{5,9},{9,13},{13,1},{2,6},{6,10},{... | collective-permute-start | bytes 239624 | tf_op jit(solution)/shard_map/ppermute | solution.py:333
  22.4 0.8 %copy-start.6 = (f32[2,200,384]{2,1,0:T(8,128)}, f32[2,200,384]{2,1,0:T(8,128)S(1)}, u32[]{:S(2)}) copy-start(f32[2,200,384]{2,1,0:T(8,128)S(1)} %get-tuple-element.34.own_ref) | copy-start | bytes 1843204
  23.2 11.2 %collective-permute-start.5 = (s32[1,1]{1,0:T(1,128)}, s32[1,1]{1,0:T(1,128)}, u32[]{:S(2)}, u32[]{:S(2)}) collective-permute-start(s32[1,1]{1,0:T(1,128)} %param.12), channel_id=1, source_target_pairs={{0,2},{2,0},{1,3},{3,1},{4,6},{6,4},{5,7},{7,5},{8,10},{10,8},{9,1... | collective-permute-start | bytes 20 | tf_op jit(solution)/shard_map/ppermute | solution.py:340
  30.3 5.2 %copy-start.5 = (f32[2,2,200,384]{3,2,1,0:T(8,128)S(1)}, f32[2,2,200,384]{3,2,1,0:T(8,128)}, u32[]{:S(2)}) copy-start(f32[2,2,200,384]{3,2,1,0:T(8,128)} %copy-done.4) | copy-start | bytes 3686404
  30.3 7.2 %collective-permute-start.6 = (bf16[2,2,200,384]{3,2,1,0:T(8,128)(2,1)S(1)}, bf16[2,2,200,384]{3,2,1,0:T(8,128)(2,1)S(1)}, u32[]{:S(2)}, u32[]{:S(2)}) collective-permute-start(bf16[2,2,200,384]{3,2,1,0:T(8,128)(2,1)S(1)} %library.2.refs_0_), channel_id=1, source_target_pairs={{0,1},{1,0},{2,3},{3,2},{4,5},{5,4},{6,7},{7,6},{8,9},{9,8},{10,11... | collective-permute-start | bytes 1843208 | tf_op jit(solution)/shard_map/ppermute | solution.py:373
  34.4 3.1 %collective-permute-start.7 = (bf16[2,2,200,384]{3,2,1,0:T(8,128)(2,1)S(1)}, bf16[2,2,200,384]{3,2,1,0:T(8,128)(2,1)S(1)}, u32[]{:S(2)}, u32[]{:S(2)}) collective-permute-start(bf16[2,2,200,384]{3,2,1,0:T(8,128)(2,1)S(1)} %library.3.refs_1_), channel_id=1, source_target_pairs={{0,1},{1,0},{2,3},{3,2},{4,5},{5,4},{6,7},{7,6},{8,9},{9,8},{10,11... | collective-permute-start | bytes 1843208 | tf_op jit(solution)/shard_map/ppermute | solution.py:373
  35.0 2.0 %copy-start.7 = (f32[2,200,384]{2,1,0:T(8,128)S(1)}, f32[2,200,384]{2,1,0:T(8,128)}, u32[]{:S(2)}) copy-start(f32[2,200,384]{2,1,0:T(8,128)} %copy-done.6) | copy-start | bytes 1843204
  35.0 2.0 %collective-permute-start.8 = (bf16[104,384]{1,0:T(8,128)(2,1)S(1)}, bf16[104,384]{1,0:T(8,128)(2,1)S(1)}, u32[]{:S(2)}, u32[]{:S(2)}) collective-permute-start(bf16[104,384]{1,0:T(8,128)(2,1)S(1)} %add_convert_fusion.mine_ref), channel_id=1, source_target_pairs={{0,1},{1,0},{2,3},{3,2},{4,5},{5,4},{6,7},{7,6},{8,9},{9,8},{10,11... | collective-permute-start | bytes 239624 | tf_op jit(solution)/shard_map/ppermute | solution.py:378
  41.0 10.2 %collective-permute-start.9 = (bf16[384,384]{1,0:T(8,128)(2,1)S(1)}, bf16[384,384]{1,0:T(8,128)(2,1)S(1)}, u32[]{:S(2)}, u32[]{:S(2)}) collective-permute-start(bf16[384,384]{1,0:T(8,128)(2,1)S(1)} %match_other.1), channel_id=1, source_target_pairs={{0,2},{2,0},{1,3},{3,1},{4,6},{6,4},{5,7},{7,5},{8,10},{10,8},{9,1... | collective-permute-start | bytes 884744 | tf_op jit(solution)/shard_map/ppermute | solution.py:408

commit v14 on v13

--- a/solution.py
+++ b/solution.py
@@ -187,8 +187,10 @@
 
 
 def gain_kernel(t, row_ref, table_ref, tile_ref, *refs):
-    spec_ref, weight_ref = refs[-2:]
-    gain, weight_ref[...] = ctf_factors(row_ref[...].astype(F32), table_ref[...])
+    spec_ref, weight_ref, sent_ref = refs[-3:]
+    row = row_ref[0:1, 0:1].astype(F32)
+    sent_ref[...] = jnp.broadcast_to(row, sent_ref.shape)
+    gain, weight_ref[...] = ctf_factors(row, table_ref[...])
     spec_ref[0] = tile_ref[t, 0] * gain
     spec_ref[1] = tile_ref[t, 1] * gain
 
@@ -336,25 +338,24 @@
 
     table = jnp.stack([defocus_term, astig_term, astig_cross, phase_shift])
     table = jnp.pad(table, ((0, 4), (0, 128 - table.shape[1])))
-    row, _ = lax.optimization_barrier((ctf_row, pair))
-    mate = lax.ppermute(row, "xhi", swap)
-
     def gain(t, row, tables, name):
         return pl.pallas_call(
             functools.partial(gain_kernel, t),
             out_shape=[
                 pltpu.VMEM(plane, F32),
                 pltpu.VMEM((ROWS, N), F32),
+                pltpu.VMEM((8, 128), F32),
             ],
-            in_specs=[full(1, 1)] + kept * (2 + len(tables)),
-            out_specs=kept * 2,
+            in_specs=([full(1, 1)] if t == 0 else kept) + kept * (2 + len(tables)),
+            out_specs=kept * 3,
             grid=(1,),
             compiler_params=params(12),
             cost_estimate=cost(8 * work, 3 << 20),
             name=name,
         )(row, table, tiles, *tables)
 
-    own = gain(0, ctf_row, (ahead, back, unfold), "gain_own")
+    *own, sent = gain(0, ctf_row, (ahead, back, unfold), "gain_own")
+    mate = lax.ppermute(sent, "xhi", swap)
     images_all, pair, own = lax.optimization_barrier((images_all, pair, own))
 
     images_all = images_all.reshape(groups, deep, N // groups, N)
@@ -365,7 +366,7 @@
             in_specs=kept * 2,
             out_specs=kept[0],
             compiler_params=params(12),
-            cost_estimate=cost(deep // 2 * work, 3 << 20),
+            cost_estimate=cost(deep // 2 * work * (1 + 5 * first), 3 << 20),
             name="library",
         )(images_all, ahead)
         for first in (0, deep // 2)
@@ -373,7 +374,7 @@
     far = [lax.ppermute(part, "core", swap) for part in near]
 
     moves, near, mate = lax.optimization_barrier((moves, near, mate))
-    other = gain(1, mate, (), "gain_other")
+    *other, _ = gain(1, mate, (), "gain_other")
     mine = sum((m.astype(F32) for m in moves), pair.astype(F32)).astype(BF16)
     theirs = lax.ppermute(mine, "core", swap)
     white, white_weight = pl.pallas_call(

time: 52.4 us -> 52.3 us (level)
  Pallas kernels: 14.4 us -> 13.7 us
    all_to_all x1, waiting for transfers between devices: 4.51 us -> 5.42 us  [per_device(): images_all = lax.all_to_all(copies, LIB, 0, 0, tiled=False)]
    ppermute x1, waiting for transfers between devices: 0.89 us -> 0.01 us  [per_device(): lax.ppermute(send, 'core', swap).astype(F32)]
    pallas_call x2, Pallas kernels: 2.33 us -> 1.6 us  [gain(): pl.pallas_call(functools.partial(gain_kernel, t), out_shape=[pltpu.VMEM(p...]
    ppermute x1, waiting for transfers between devices: 0.01 us -> 0.64 us  [per_device(): theirs = lax.ppermute(mine, 'core', swap)]
  transfers between devices with their start and end apart: 11 -> 11, of which waited for: 4 -> 4; matrix products, arithmetic and copies ran while one was open for 0% -> 0% of each run, Pallas kernels for 21% -> 20%
where the time goes in v14:
time: 52.3 us; the launch traced here: 51.8 us
  starting transfers between devices  24.5 us (47%)
  Pallas kernels  13.7 us (26%)
  waiting for transfers between devices  10.8 us (21%)
  other arithmetic  0.94 us (2%)
  between operations  0.92 us (2%)
  local copies, waits for them, and re-layouts  0.88 us (2%)
    all_to_all x1, starting transfers between devices, per_device(): images_all = lax.all_to_all(copies, LIB, 0, 0, tiled=False)  8.22 us
    pallas_call x2, Pallas kernels, match(): pl.pallas_call(functools.partial(match_kernel, t), out_shape=pltpu.VMEM((...  7.22 us
    all_to_all x1, waiting for transfers between devices, per_device(): images_all = lax.all_to_all(copies, LIB, 0, 0, tiled=False)  5.42 us
    ppermute x1, waiting for transfers between devices, per_device(): got = lax.ppermute(match(1, BF16, 'match_other'), 'xhi', swap)  4.26 us
    ppermute x3, starting transfers between devices, per_device(): lax.ppermute(pair, 'z', [(z, (z + dz) % deep) for z in range(deep)])  3.94 us
    ppermute x1, starting transfers between devices, per_device(): received = lax.ppermute(tile, 'xhi', swap)  3.57 us
    ppermute x2, starting transfers between devices, per_device(): far = [lax.ppermute(part, 'core', swap) for part in near]  3.17 us
    ppermute x1, starting transfers between devices, per_device(): got = lax.ppermute(match(1, BF16, 'match_other'), 'xhi', swap)  1.99 us
  transfers between devices with their start and end apart: 11, of which 4 were waited for; matrix products, arithmetic and copies ran while one was open for 0% of the time, Pallas kernels for 20%

profile of v14, /device:TPU:1, one launch (start us, length us, event | category | flops | bytes accessed | tf_op | source)
XLA Modules:
  0.0 51.8 jit_solution(12047219918899289508)
XLA Ops:
  0.0 3.6 %collective-permute-start = (bf16[384,384]{1,0:T(8,128)(2,1)}, bf16[384,384]{1,0:T(8,128)(2,1)S(1)}, u32[]{:S(2)}, u32[]{:S(2)}) collective-permute-start(bf16[384,384]{1,0:T(8,128)(2,1)} %bitcast.12), channel_id=1, source_target_pairs={{0,2},{2,0},{1,3},{3,1},{4,6},{6,4},{5,7},{7,5},{8,10},{10,8},{9,1... | collective-permute-start | bytes 884744 | tf_op jit(solution)/shard_map/ppermute | solution.py:300
  3.6 1.8 %copies.1 = bf16[32,48,384]{2,1,0:T(8,128)(2,1)} custom-call(bf16[48,384]{1,0:T(8,128)(2,1)} %bitcast.14), custom_call_target="tpu_custom_call" | custom-call | bytes 1048576 | tf_op jit(solution)/shard_map/copies/pallas_call | solution.py:301
  5.4 0.0 copy-start.8
  5.4 0.0 copy-start.9
  5.5 0.0 copy-start.10
  5.5 0.0 copy-start.11
  5.5 0.0 copy-start
  5.5 0.0 copy-start.1
  5.5 8.2 %all-to-all-start = ((bf16[32,48,384]{2,1,0:T(8,128)(2,1)}), bf16[32,48,384]{2,1,0:T(8,128)(2,1)S(1)}, u32[]{:S(2)}, u32[]{:S(2)}) async-start(bf16[32,48,384]{2,1,0:T(8,128)(2,1)} %copies.1), calls=%async_computation | async-start | bytes 2359296 | tf_op jit(solution)/shard_map/all_to_all | solution.py:315
  14.4 0.0 copy-done.8
  14.4 0.0 copy-done.9
  14.4 0.0 copy-done.10
  14.4 0.0 copy-done.11
  14.4 0.0 collective-permute-done.other_ref
  14.5 0.0 copy-done
  14.5 0.0 copy-done.1
  14.5 0.0 copy-start.2
  14.5 0.0 copy-start.3
  14.5 0.9 %tile.1 = (f32[2,2,200,384]{3,2,1,0:T(8,128)S(1)}, bf16[104,384]{1,0:T(8,128)(2,1)S(1)}, bf16[104,384]{1,0:T(8,128)(2,1)S(1)}) custom-call(s32[1,1]{1,0:T(1,128)} %bitcast.core_ref, bf16[384,384]{1,0:T(8,128)(2,1)S(1)} %bitcast.13, bf16[384,384]{1,0:T(8,128)(2,1)S(1)} %collective-permute-done.other_ref, bf16[1168,256]{1,0:T(8,128)(2,1)S(1)} %copy-done), custom_call_target="tpu_custom_call" | custom-call | flops 31457280000 | bytes 3145728 | tf_op jit(solution)/shard_map/tile/pallas_call | solution.py:317
  15.4 0.0 copy-start.4
  15.4 1.3 %collective-permute-start.1 = (bf16[104,384]{1,0:T(8,128)(2,1)S(1)}, bf16[104,384]{1,0:T(8,128)(2,1)S(1)}, u32[]{:S(2)}, u32[]{:S(2)}) collective-permute-start(bf16[104,384]{1,0:T(8,128)(2,1)S(1)} %get-tuple-element.26), channel_id=1, source_target_pairs={{0,1},{1,0},{2,3},{3,2},{4,5},{5,4},{6,7},{7,6},{8,9},{9,8},{10,11... | collective-permute-start | bytes 239624 | tf_op jit(solution)/shard_map/ppermute | solution.py:333
  16.7 0.0 copy-done.2
  16.7 0.0 copy-done.3
  16.7 0.8 %gain_own.1 = (f32[2,200,384]{2,1,0:T(8,128)S(1)}, f32[200,384]{1,0:T(8,128)S(1)}, f32[8,128]{1,0:T(8,128)S(1)}) custom-call(s32[1,1]{1,0:T(1,128)S(6)} %copy.11.row_ref, f32[8,128]{1,0:T(8,128)S(1)} %select_maximum_fusion.table_ref, f32[2,2,200,384]{3,2,1,0:T(8,128)S(1)} %get-tuple-element.27.tile_ref, bf16[1168,256]{1,0:T(8,128)(2,1)S(1)} %copy-done, ...), custom_call_target="tpu_custom_call" | custom-call | flops 1258291200 | bytes 3145728 | tf_op jit(solution)/shard_map/gain_own/pallas_call | solution.py:342
  17.5 0.0 copy-done.4
  17.5 0.0 copy-start.6
  17.5 0.8 %copy-done.6 = f32[2,200,384]{2,1,0:T(8,128)} copy-done((f32[2,200,384]{2,1,0:T(8,128)}, f32[2,200,384]{2,1,0:T(8,128)S(1)}, u32[]{:S(2)}) %copy-start.6) | copy-done | bytes 614424
  18.3 1.7 %collective-permute-start.5 = (f32[8,128]{1,0:T(8,128)S(1)}, f32[8,128]{1,0:T(8,128)S(1)}, u32[]{:S(2)}, u32[]{:S(2)}) collective-permute-start(f32[8,128]{1,0:T(8,128)S(1)} %get-tuple-element.31), channel_id=1, source_target_pairs={{0,2},{2,0},{1,3},{3,1},{4,6},{6,4},{5,7},{7,5},{8,10},{10,8},{9,1... | collective-permute-start | bytes 12296 | tf_op jit(solution)/shard_map/ppermute | solution.py:358
  20.1 0.0 collective-permute-done.1
  20.1 2.8 %collective-permute-start.4 = (bf16[104,384]{1,0:T(8,128)(2,1)S(1)}, bf16[104,384]{1,0:T(8,128)(2,1)S(1)}, u32[]{:S(2)}, u32[]{:S(2)}) collective-permute-start(bf16[104,384]{1,0:T(8,128)(2,1)S(1)} %add_convert_fusion.1), channel_id=1, source_target_pairs={{0,12},{4,0},{8,4},{12,8},{1,13},{5,1},{9,5},{13,9},{2,14},{6,2},{... | collective-permute-start | bytes 239624 | tf_op jit(solution)/shard_map/ppermute | solution.py:335
  22.9 0.6 %collective-permute-start.3 = (bf16[104,384]{1,0:T(8,128)(2,1)S(1)}, bf16[104,384]{1,0:T(8,128)(2,1)S(1)}, u32[]{:S(2)}, u32[]{:S(2)}) collective-permute-start(bf16[104,384]{1,0:T(8,128)(2,1)S(1)} %add_convert_fusion.1), channel_id=1, source_target_pairs={{0,8},{4,12},{8,0},{12,4},{1,9},{5,13},{9,1},{13,5},{2,10},{6,14},... | collective-permute-start | bytes 239624 | tf_op jit(solution)/shard_map/ppermute | solution.py:335
  23.5 0.6 %collective-permute-start.2 = (bf16[104,384]{1,0:T(8,128)(2,1)S(1)}, bf16[104,384]{1,0:T(8,128)(2,1)S(1)}, u32[]{:S(2)}, u32[]{:S(2)}) collective-permute-start(bf16[104,384]{1,0:T(8,128)(2,1)S(1)} %add_convert_fusion.1), channel_id=1, source_target_pairs={{0,4},{4,8},{8,12},{12,0},{1,5},{5,9},{9,13},{13,1},{2,6},{6,10},{... | collective-permute-start | bytes 239624 | tf_op jit(solution)/shard_map/ppermute | solution.py:335
  24.1 5.4 %all-to-all-done = bf16[32,48,384]{2,1,0:T(8,128)(2,1)S(1)} async-done(((bf16[32,48,384]{2,1,0:T(8,128)(2,1)}), bf16[32,48,384]{2,1,0:T(8,128)(2,1)S(1)}, u32[]{:S(2)}, u32[]{:S(2)}) %all-to-all-start) | async-done | bytes 1179680 | tf_op jit(solution)/shard_map/all_to_all | solution.py:315
  29.5 0.8 %library.3.refs_1_ = bf16[2,2,200,384]{3,2,1,0:T(8,128)(2,1)S(1)} custom-call(bf16[8,4,48,384]{3,2,1,0:T(8,128)(2,1)S(1)} %bitcast.10, bf16[1168,256]{1,0:T(8,128)(2,1)S(1)} %copy-done), custom_call_target="tpu_custom_call" | custom-call | flops 3460300800 | bytes 3145728 | tf_op jit(solution)/shard_map/library/pallas_call | solution.py:363
  30.3 0.0 copy-start.5
  30.3 0.8 %library.2.refs_0_ = bf16[2,2,200,384]{3,2,1,0:T(8,128)(2,1)S(1)} custom-call(bf16[8,4,48,384]{3,2,1,0:T(8,128)(2,1)S(1)} %bitcast.11, bf16[1168,256]{1,0:T(8,128)(2,1)S(1)} %copy-done), custom_call_target="tpu_custom_call" | custom-call | flops 314572800 | bytes 3145728 | tf_op jit(solution)/shard_map/library/pallas_call | solution.py:363
  31.2 3.1 %collective-permute-start.6 = (bf16[2,2,200,384]{3,2,1,0:T(8,128)(2,1)S(1)}, bf16[2,2,200,384]{3,2,1,0:T(8,128)(2,1)S(1)}, u32[]{:S(2)}, u32[]{:S(2)}) collective-permute-start(bf16[2,2,200,384]{3,2,1,0:T(8,128)(2,1)S(1)} %library.2.refs_0_), channel_id=1, source_target_pairs={{0,1},{1,0},{2,3},{3,2},{4,5},{5,4},{6,7},{7,6},{8,9},{9,8},{10,11... | collective-permute-start | bytes 1843208 | tf_op jit(solution)/shard_map/ppermute | solution.py:374
  34.3 0.0 collective-permute-done.5.row_ref
  34.3 0.1 collective-permute-start.7
  34.4 0.0 collective-permute-done.4
  34.4 0.0 collective-permute-done.3
  34.4 0.5 collective-permute-done.2
  34.9 0.0 copy-start.7
  34.9 0.6 %collective-permute-start.8 = (bf16[104,384]{1,0:T(8,128)(2,1)S(1)}, bf16[104,384]{1,0:T(8,128)(2,1)S(1)}, u32[]{:S(2)}, u32[]{:S(2)}) collective-permute-start(bf16[104,384]{1,0:T(8,128)(2,1)S(1)} %add_convert_fusion.mine_ref), channel_id=1, source_target_pairs={{0,1},{1,0},{2,3},{3,2},{4,5},{5,4},{6,7},{7,6},{8,9},{9,8},{10,11... | collective-permute-start | bytes 239624 | tf_op jit(solution)/shard_map/ppermute | solution.py:379
  35.5 0.0 copy-done.5
  35.5 0.8 %gain_other.1 = (f32[2,200,384]{2,1,0:T(8,128)S(1)}, f32[200,384]{1,0:T(8,128)S(1)}, f32[8,128]{1,0:T(8,128)}) custom-call(f32[8,128]{1,0:T(8,128)S(1)} %collective-permute-done.5.row_ref, f32[8,128]{1,0:T(8,128)S(1)} %select_maximum_fusion.table_ref, f32[2,2,200,384]{3,2,1,0:T(8,128)S(1)} %copy-done.5), custom_call_target="tpu_custom_call" | custom-call | flops 1258291200 | bytes 3145728 | tf_op jit(solution)/shard_map/gain_other/pallas_call | solution.py:342
  36.3 0.6 %collective-permute-done.8.theirs_ref = bf16[104,384]{1,0:T(8,128)(2,1)S(1)} collective-permute-done((bf16[104,384]{1,0:T(8,128)(2,1)S(1)}, bf16[104,384]{1,0:T(8,128)(2,1)S(1)}, u32[]{:S(2)}, u32[]{:S(2)}) %collective-permute-start.8) | collective-permute-done | bytes 79904 | tf_op jit(solution)/shard_map/ppermute | solution.py:379
  36.9 0.0 copy-done.7
  36.9 0.5 whiten.1
  37.4 0.0 collective-permute-done.6.refs_2_
  37.4 0.0 collective-permute-done.7.refs_3_
  37.4 3.5 %match_other.1 = bf16[384,384]{1,0:T(8,128)(2,1)S(1)} custom-call(bf16[2,2,200,384]{3,2,1,0:T(8,128)(2,1)S(1)} %library.2.refs_0_, bf16[2,2,200,384]{3,2,1,0:T(8,128)(2,1)S(1)} %library.3.refs_1_, bf16[2,2,200,384]{3,2,1,0:T(8,128)(2,1)S(1)} %collective-permute-done.6.refs_2_, bf16[2,2,200,384]{3,2,1,0:T(8,128)(2,1)S(1)} %collective-permute-done.7.refs_3_, ...), custom_call_target="tpu_custom_call" | custom-call | flops 2516582400 | bytes 6291456 | tf_op jit(solution)/shard_map/match_other/pallas_call | solution.py:394
  40.9 2.0 %collective-permute-start.9 = (bf16[384,384]{1,0:T(8,128)(2,1)S(1)}, bf16[384,384]{1,0:T(8,128)(2,1)S(1)}, u32[]{:S(2)}, u32[]{:S(2)}) collective-permute-start(bf16[384,384]{1,0:T(8,128)(2,1)S(1)} %match_other.1), channel_id=1, source_target_pairs={{0,2},{2,0},{1,3},{3,1},{4,6},{6,4},{5,7},{7,5},{8,10},{10,8},{9,1... | collective-permute-start | bytes 884744 | tf_op jit(solution)/shard_map/ppermute | solution.py:409
  42.9 3.7 %match_own.1 = f32[384,384]{1,0:T(8,128)S(1)} custom-call(bf16[2,2,200,384]{3,2,1,0:T(8,128)(2,1)S(1)} %library.2.refs_0_, bf16[2,2,200,384]{3,2,1,0:T(8,128)(2,1)S(1)} %library.3.refs_1_, bf16[2,2,200,384]{3,2,1,0:T(8,128)(2,1)S(1)} %collective-permute-done.6.refs_2_, bf16[2,2,200,384]{3,2,1,0:T(8,128)(2,1)S(1)} %collective-permute-done.7.refs_3_, ...), custom_call_target="tpu_custom_call" | custom-call | flops 2516582400 | bytes 6291456 | tf_op jit(solution)/shard_map/match_own/pallas_call | solution.py:394
  46.7 4.3 %collective-permute-done.9 = bf16[384,384]{1,0:T(8,128)(2,1)S(1)} collective-permute-done((bf16[384,384]{1,0:T(8,128)(2,1)S(1)}, bf16[384,384]{1,0:T(8,128)(2,1)S(1)}, u32[]{:S(2)}, u32[]{:S(2)}) %collective-permute-start.9) | collective-permute-done | bytes 294944 | tf_op jit(solution)/shard_map/ppermute | solution.py:409
  50.9 0.9 %maximum_bitcast_fusion = f32[1,1,384,384]{3,2,1,0:T(8,128)} fusion(f32[384,384]{1,0:T(8,128)S(1)} %match_own.1, bf16[384,384]{1,0:T(8,128)(2,1)S(1)} %collective-permute-done.9), kind=kLoop, calls=%fused_computation | loop fusion | flops 294912 | bytes 1474560 | tf_op jit(solution)/shard_map/broadcast_in_dim | solution.py:411
  (3 shorter events, 0.1 us)
Async XLA Ops:
  0.0 14.4 %collective-permute-start = (bf16[384,384]{1,0:T(8,128)(2,1)}, bf16[384,384]{1,0:T(8,128)(2,1)S(1)}, u32[]{:S(2)}, u32[]{:S(2)}) collective-permute-start(bf16[384,384]{1,0:T(8,128)(2,1)} %bitcast.12), channel_id=1, source_target_pairs={{0,2},{2,0},{1,3},{3,1},{4,6},{6,4},{5,7},{7,5},{8,10},{10,8},{9,1... | collective-permute-start | bytes 884744 | tf_op jit(solution)/shard_map/ppermute | solution.py:300
  5.4 9.0 %copy-start.8 = (f32[64]{0:T(128)S(1)}, f32[64]{0:T(128)}, u32[]{:S(2)}) copy-start(f32[64]{0:T(128)} %param.16) | copy-start | bytes 772
  5.4 9.0 %copy-start.9 = (f32[64]{0:T(128)S(1)}, f32[64]{0:T(128)}, u32[]{:S(2)}) copy-start(f32[64]{0:T(128)} %param.15) | copy-start | bytes 772
  5.5 9.0 %copy-start.10 = (f32[64]{0:T(128)S(1)}, f32[64]{0:T(128)}, u32[]{:S(2)}) copy-start(f32[64]{0:T(128)} %param.14) | copy-start | bytes 772
  5.5 9.0 %copy-start.11 = (f32[64]{0:T(128)S(1)}, f32[64]{0:T(128)}, u32[]{:S(2)}) copy-start(f32[64]{0:T(128)} %param.13) | copy-start | bytes 772
  5.5 9.0 %copy-start = (bf16[1168,256]{1,0:T(8,128)(2,1)S(1)}, bf16[1168,256]{1,0:T(8,128)(2,1)}, u32[]{:S(2)}) copy-start(bf16[1168,256]{1,0:T(8,128)(2,1)} %constant.13.clone.tab_ref.refs_0_) | copy-start | bytes 1794052
  5.5 9.0 %copy-start.1 = (bf16[1,1,384,384]{3,2,1,0:T(8,128)(2,1)S(1)}, bf16[1,1,384,384]{3,2,1,0:T(8,128)(2,1)}, u32[]{:S(2)}) copy-start(bf16[1,1,384,384]{3,2,1,0:T(8,128)(2,1)} %param.10) | copy-start | bytes 884740
  5.5 24.0 %all-to-all-start = ((bf16[32,48,384]{2,1,0:T(8,128)(2,1)}), bf16[32,48,384]{2,1,0:T(8,128)(2,1)S(1)}, u32[]{:S(2)}, u32[]{:S(2)}) async-start(bf16[32,48,384]{2,1,0:T(8,128)(2,1)} %copies.1), calls=%async_computation | async-start | bytes 2359296 | tf_op jit(solution)/shard_map/all_to_all | solution.py:315
  14.5 2.2 %copy-start.2 = (bf16[1184,256]{1,0:T(8,128)(2,1)S(1)}, bf16[1184,256]{1,0:T(8,128)(2,1)}, u32[]{:S(2)}) copy-start(bf16[1184,256]{1,0:T(8,128)(2,1)} %constant.14.clone.refs_1_.refs_0_.refs_6_) | copy-start | bytes 1818628
  14.5 2.2 %copy-start.3 = (bf16[192,400]{1,0:T(8,128)(2,1)S(1)}, bf16[192,400]{1,0:T(8,128)(2,1)}, u32[]{:S(2)}) copy-start(bf16[192,400]{1,0:T(8,128)(2,1)} %constant.15.clone.refs_2_.refs_1_.refs_7_) | copy-start | bytes 460804
  15.4 2.2 %copy-start.4 = (f32[2,2,200,384]{3,2,1,0:T(8,128)}, f32[2,2,200,384]{3,2,1,0:T(8,128)S(1)}, u32[]{:S(2)}) copy-start(f32[2,2,200,384]{3,2,1,0:T(8,128)S(1)} %get-tuple-element.27.tile_ref) | copy-start | bytes 3686404
  15.4 4.7 %collective-permute-start.1 = (bf16[104,384]{1,0:T(8,128)(2,1)S(1)}, bf16[104,384]{1,0:T(8,128)(2,1)S(1)}, u32[]{:S(2)}, u32[]{:S(2)}) collective-permute-start(bf16[104,384]{1,0:T(8,128)(2,1)S(1)} %get-tuple-element.26), channel_id=1, source_target_pairs={{0,1},{1,0},{2,3},{3,2},{4,5},{5,4},{6,7},{7,6},{8,9},{9,8},{10,11... | collective-permute-start | bytes 239624 | tf_op jit(solution)/shard_map/ppermute | solution.py:333
  17.5 0.8 %copy-start.6 = (f32[2,200,384]{2,1,0:T(8,128)}, f32[2,200,384]{2,1,0:T(8,128)S(1)}, u32[]{:S(2)}) copy-start(f32[2,200,384]{2,1,0:T(8,128)S(1)} %get-tuple-element.34.own_ref) | copy-start | bytes 1843204
  18.3 15.9 %collective-permute-start.5 = (f32[8,128]{1,0:T(8,128)S(1)}, f32[8,128]{1,0:T(8,128)S(1)}, u32[]{:S(2)}, u32[]{:S(2)}) collective-permute-start(f32[8,128]{1,0:T(8,128)S(1)} %get-tuple-element.31), channel_id=1, source_target_pairs={{0,2},{2,0},{1,3},{3,1},{4,6},{6,4},{5,7},{7,5},{8,10},{10,8},{9,1... | collective-permute-start | bytes 12296 | tf_op jit(solution)/shard_map/ppermute | solution.py:358
  20.1 14.3 %collective-permute-start.4 = (bf16[104,384]{1,0:T(8,128)(2,1)S(1)}, bf16[104,384]{1,0:T(8,128)(2,1)S(1)}, u32[]{:S(2)}, u32[]{:S(2)}) collective-permute-start(bf16[104,384]{1,0:T(8,128)(2,1)S(1)} %add_convert_fusion.1), channel_id=1, source_target_pairs={{0,12},{4,0},{8,4},{12,8},{1,13},{5,1},{9,5},{13,9},{2,14},{6,2},{... | collective-permute-start | bytes 239624 | tf_op jit(solution)/shard_map/ppermute | solution.py:335
  22.9 11.5 %collective-permute-start.3 = (bf16[104,384]{1,0:T(8,128)(2,1)S(1)}, bf16[104,384]{1,0:T(8,128)(2,1)S(1)}, u32[]{:S(2)}, u32[]{:S(2)}) collective-permute-start(bf16[104,384]{1,0:T(8,128)(2,1)S(1)} %add_convert_fusion.1), channel_id=1, source_target_pairs={{0,8},{4,12},{8,0},{12,4},{1,9},{5,13},{9,1},{13,5},{2,10},{6,14},... | collective-permute-start | bytes 239624 | tf_op jit(solution)/shard_map/ppermute | solution.py:335
  23.5 11.4 %collective-permute-start.2 = (bf16[104,384]{1,0:T(8,128)(2,1)S(1)}, bf16[104,384]{1,0:T(8,128)(2,1)S(1)}, u32[]{:S(2)}, u32[]{:S(2)}) collective-permute-start(bf16[104,384]{1,0:T(8,128)(2,1)S(1)} %add_convert_fusion.1), channel_id=1, source_target_pairs={{0,4},{4,8},{8,12},{12,0},{1,5},{5,9},{9,13},{13,1},{2,6},{6,10},{... | collective-permute-start | bytes 239624 | tf_op jit(solution)/shard_map/ppermute | solution.py:335
  30.3 5.2 %copy-start.5 = (f32[2,2,200,384]{3,2,1,0:T(8,128)S(1)}, f32[2,2,200,384]{3,2,1,0:T(8,128)}, u32[]{:S(2)}) copy-start(f32[2,2,200,384]{3,2,1,0:T(8,128)} %copy-done.4) | copy-start | bytes 3686404
  31.2 6.2 %collective-permute-start.6 = (bf16[2,2,200,384]{3,2,1,0:T(8,128)(2,1)S(1)}, bf16[2,2,200,384]{3,2,1,0:T(8,128)(2,1)S(1)}, u32[]{:S(2)}, u32[]{:S(2)}) collective-permute-start(bf16[2,2,200,384]{3,2,1,0:T(8,128)(2,1)S(1)} %library.2.refs_0_), channel_id=1, source_target_pairs={{0,1},{1,0},{2,3},{3,2},{4,5},{5,4},{6,7},{7,6},{8,9},{9,8},{10,11... | collective-permute-start | bytes 1843208 | tf_op jit(solution)/shard_map/ppermute | solution.py:374
  34.3 3.2 %collective-permute-start.7 = (bf16[2,2,200,384]{3,2,1,0:T(8,128)(2,1)S(1)}, bf16[2,2,200,384]{3,2,1,0:T(8,128)(2,1)S(1)}, u32[]{:S(2)}, u32[]{:S(2)}) collective-permute-start(bf16[2,2,200,384]{3,2,1,0:T(8,128)(2,1)S(1)} %library.3.refs_1_), channel_id=1, source_target_pairs={{0,1},{1,0},{2,3},{3,2},{4,5},{5,4},{6,7},{7,6},{8,9},{9,8},{10,11... | collective-permute-start | bytes 1843208 | tf_op jit(solution)/shard_map/ppermute | solution.py:374
  34.9 2.0 %copy-start.7 = (f32[2,200,384]{2,1,0:T(8,128)S(1)}, f32[2,200,384]{2,1,0:T(8,128)}, u32[]{:S(2)}) copy-start(f32[2,200,384]{2,1,0:T(8,128)} %copy-done.6) | copy-start | bytes 1843204
  34.9 2.0 %collective-permute-start.8 = (bf16[104,384]{1,0:T(8,128)(2,1)S(1)}, bf16[104,384]{1,0:T(8,128)(2,1)S(1)}, u32[]{:S(2)}, u32[]{:S(2)}) collective-permute-start(bf16[104,384]{1,0:T(8,128)(2,1)S(1)} %add_convert_fusion.mine_ref), channel_id=1, source_target_pairs={{0,1},{1,0},{2,3},{3,2},{4,5},{5,4},{6,7},{7,6},{8,9},{9,8},{10,11... | collective-permute-start | bytes 239624 | tf_op jit(solution)/shard_map/ppermute | solution.py:379
  40.9 10.0 %collective-permute-start.9 = (bf16[384,384]{1,0:T(8,128)(2,1)S(1)}, bf16[384,384]{1,0:T(8,128)(2,1)S(1)}, u32[]{:S(2)}, u32[]{:S(2)}) collective-permute-start(bf16[384,384]{1,0:T(8,128)(2,1)S(1)} %match_other.1), channel_id=1, source_target_pairs={{0,2},{2,0},{1,3},{3,1},{4,6},{6,4},{5,7},{7,5},{8,10},{10,8},{9,1... | collective-permute-start | bytes 884744 | tf_op jit(solution)/shard_map/ppermute | solution.py:409

commit v15 on v14

--- a/solution.py
+++ b/solution.py
@@ -359,6 +359,7 @@
     images_all, pair, own = lax.optimization_barrier((images_all, pair, own))
 
     images_all = images_all.reshape(groups, deep, N // groups, N)
+    held, mate = lax.optimization_barrier((images_all, mate))
     near = [
         pl.pallas_call(
             functools.partial(library_kernel, first),
@@ -366,9 +367,9 @@
             in_specs=kept * 2,
             out_specs=kept[0],
             compiler_params=params(12),
-            cost_estimate=cost(deep // 2 * work * (1 + 5 * first), 3 << 20),
+            cost_estimate=cost(deep // 2 * work, 3 << 20),
             name="library",
-        )(images_all, ahead)
+        )(held if first else images_all, ahead)
         for first in (0, deep // 2)
     ]
     far = [lax.ppermute(part, "core", swap) for part in near]

time: 52.3 us -> 52.1 us (level)
    all_to_all x1, waiting for transfers between devices: 5.42 us -> 4.51 us  [per_device(): images_all = lax.all_to_all(copies, LIB, 0, 0, tiled=False)]
    ppermute x1, waiting for transfers between devices: 0.01 us -> 0.89 us  [per_device(): lax.ppermute(send, 'core', swap).astype(F32)]
  transfers between devices with their start and end apart: 11 -> 11, of which waited for: 4 -> 5; matrix products, arithmetic and copies ran while one was open for 0% -> 0% of each run, Pallas kernels for 20% -> 20%
where the time goes in v15:
time: 52.1 us; the launch traced here: 51.8 us
  starting transfers between devices  24.6 us (47%)
  Pallas kernels  13.7 us (26%)
  waiting for transfers between devices  10.7 us (21%)
  other arithmetic  0.95 us (2%)
  between operations  0.9 us (2%)
  local copies, waits for them, and re-layouts  0.88 us (2%)
    all_to_all x1, starting transfers between devices, per_device(): images_all = lax.all_to_all(copies, LIB, 0, 0, tiled=False)  8.22 us
    pallas_call x2, Pallas kernels, match(): pl.pallas_call(functools.partial(match_kernel, t), out_shape=pltpu.VMEM((...  7.22 us
    ppermute x1, waiting for transfers between devices, per_device(): got = lax.ppermute(match(1, BF16, 'match_other'), 'xhi', swap)  4.53 us
    all_to_all x1, waiting for transfers between devices, per_device(): images_all = lax.all_to_all(copies, LIB, 0, 0, tiled=False)  4.51 us
    ppermute x3, starting transfers between devices, per_device(): lax.ppermute(pair, 'z', [(z, (z + dz) % deep) for z in range(deep)])  3.95 us
    ppermute x1, starting transfers between devices, per_device(): received = lax.ppermute(tile, 'xhi', swap)  3.57 us
    ppermute x2, starting transfers between devices, per_device(): far = [lax.ppermute(part, 'core', swap) for part in near]  3.41 us
    ppermute x1, starting transfers between devices, per_device(): got = lax.ppermute(match(1, BF16, 'match_other'), 'xhi', swap)  1.98 us
  transfers between devices with their start and end apart: 11, of which 5 were waited for; matrix products, arithmetic and copies ran while one was open for 0% of the time, Pallas kernels for 20%

profile of v15, /device:TPU:1, one launch (start us, length us, event | category | flops | bytes accessed | tf_op | source)
XLA Modules:
  0.0 51.8 jit_solution(16928975494122362433)
XLA Ops:
  0.0 3.6 %collective-permute-start = (bf16[384,384]{1,0:T(8,128)(2,1)}, bf16[384,384]{1,0:T(8,128)(2,1)S(1)}, u32[]{:S(2)}, u32[]{:S(2)}) collective-permute-start(bf16[384,384]{1,0:T(8,128)(2,1)} %bitcast.12), channel_id=1, source_target_pairs={{0,2},{2,0},{1,3},{3,1},{4,6},{6,4},{5,7},{7,5},{8,10},{10,8},{9,1... | collective-permute-start | bytes 884744 | tf_op jit(solution)/shard_map/ppermute | solution.py:300
  3.6 1.8 %copies.1 = bf16[32,48,384]{2,1,0:T(8,128)(2,1)} custom-call(bf16[48,384]{1,0:T(8,128)(2,1)} %bitcast.14), custom_call_target="tpu_custom_call" | custom-call | bytes 1048576 | tf_op jit(solution)/shard_map/copies/pallas_call | solution.py:301
  5.4 0.0 copy-start
  5.4 0.0 copy-start.1
  5.5 8.2 %all-to-all-start = ((bf16[32,48,384]{2,1,0:T(8,128)(2,1)}), bf16[32,48,384]{2,1,0:T(8,128)(2,1)S(1)}, u32[]{:S(2)}, u32[]{:S(2)}) async-start(bf16[32,48,384]{2,1,0:T(8,128)(2,1)} %copies.1), calls=%async_computation | async-start | bytes 2359296 | tf_op jit(solution)/shard_map/all_to_all | solution.py:315
  14.3 0.0 collective-permute-done.other_ref
  14.4 0.0 copy-done
  14.4 0.0 copy-done.1
  14.4 0.0 copy-start.8
  14.4 0.0 copy-start.9
  14.4 0.0 copy-start.10
  14.4 0.0 copy-start.11
  14.4 0.0 copy-start.2
  14.4 0.0 copy-start.3
  14.4 0.9 %tile.1 = (f32[2,2,200,384]{3,2,1,0:T(8,128)S(1)}, bf16[104,384]{1,0:T(8,128)(2,1)S(1)}, bf16[104,384]{1,0:T(8,128)(2,1)S(1)}) custom-call(s32[1,1]{1,0:T(1,128)} %bitcast.core_ref, bf16[384,384]{1,0:T(8,128)(2,1)S(1)} %bitcast.13, bf16[384,384]{1,0:T(8,128)(2,1)S(1)} %collective-permute-done.other_ref, bf16[1168,256]{1,0:T(8,128)(2,1)S(1)} %copy-done), custom_call_target="tpu_custom_call" | custom-call | flops 31457280000 | bytes 3145728 | tf_op jit(solution)/shard_map/tile/pallas_call | solution.py:317
  15.3 0.0 copy-start.4
  15.3 1.3 %collective-permute-start.1 = (bf16[104,384]{1,0:T(8,128)(2,1)S(1)}, bf16[104,384]{1,0:T(8,128)(2,1)S(1)}, u32[]{:S(2)}, u32[]{:S(2)}) collective-permute-start(bf16[104,384]{1,0:T(8,128)(2,1)S(1)} %get-tuple-element.28), channel_id=1, source_target_pairs={{0,1},{1,0},{2,3},{3,2},{4,5},{5,4},{6,7},{7,6},{8,9},{9,8},{10,11... | collective-permute-start | bytes 239624 | tf_op jit(solution)/shard_map/ppermute | solution.py:333
  16.6 0.0 copy-done.8
  16.6 0.0 copy-done.9
  16.6 0.0 copy-done.10
  16.6 0.0 copy-done.11
  16.7 0.9 %collective-permute-done.1 = bf16[104,384]{1,0:T(8,128)(2,1)S(1)} collective-permute-done((bf16[104,384]{1,0:T(8,128)(2,1)S(1)}, bf16[104,384]{1,0:T(8,128)(2,1)S(1)}, u32[]{:S(2)}, u32[]{:S(2)}) %collective-permute-start.1) | collective-permute-done | bytes 79904 | tf_op jit(solution)/shard_map/ppermute | solution.py:333
  17.6 2.8 %collective-permute-start.4 = (bf16[104,384]{1,0:T(8,128)(2,1)S(1)}, bf16[104,384]{1,0:T(8,128)(2,1)S(1)}, u32[]{:S(2)}, u32[]{:S(2)}) collective-permute-start(bf16[104,384]{1,0:T(8,128)(2,1)S(1)} %add_convert_fusion.1), channel_id=1, source_target_pairs={{0,12},{4,0},{8,4},{12,8},{1,13},{5,1},{9,5},{13,9},{2,14},{6,2},{... | collective-permute-start | bytes 239624 | tf_op jit(solution)/shard_map/ppermute | solution.py:335
  20.4 0.6 %collective-permute-start.3 = (bf16[104,384]{1,0:T(8,128)(2,1)S(1)}, bf16[104,384]{1,0:T(8,128)(2,1)S(1)}, u32[]{:S(2)}, u32[]{:S(2)}) collective-permute-start(bf16[104,384]{1,0:T(8,128)(2,1)S(1)} %add_convert_fusion.1), channel_id=1, source_target_pairs={{0,8},{4,12},{8,0},{12,4},{1,9},{5,13},{9,1},{13,5},{2,10},{6,14},... | collective-permute-start | bytes 239624 | tf_op jit(solution)/shard_map/ppermute | solution.py:335
  20.9 0.6 %collective-permute-start.2 = (bf16[104,384]{1,0:T(8,128)(2,1)S(1)}, bf16[104,384]{1,0:T(8,128)(2,1)S(1)}, u32[]{:S(2)}, u32[]{:S(2)}) collective-permute-start(bf16[104,384]{1,0:T(8,128)(2,1)S(1)} %add_convert_fusion.1), channel_id=1, source_target_pairs={{0,4},{4,8},{8,12},{12,0},{1,5},{5,9},{9,13},{13,1},{2,6},{6,10},{... | collective-permute-start | bytes 239624 | tf_op jit(solution)/shard_map/ppermute | solution.py:335
  21.5 0.0 copy-done.2
  21.5 0.0 copy-done.3
  21.5 0.8 %gain_own.1 = (f32[2,200,384]{2,1,0:T(8,128)S(1)}, f32[200,384]{1,0:T(8,128)S(1)}, f32[8,128]{1,0:T(8,128)S(1)}) custom-call(s32[1,1]{1,0:T(1,128)S(6)} %copy.11.row_ref, f32[8,128]{1,0:T(8,128)S(1)} %select_maximum_fusion.table_ref, f32[2,2,200,384]{3,2,1,0:T(8,128)S(1)} %get-tuple-element.29.tile_ref, bf16[1168,256]{1,0:T(8,128)(2,1)S(1)} %copy-done, ...), custom_call_target="tpu_custom_call" | custom-call | flops 1258291200 | bytes 3145728 | tf_op jit(solution)/shard_map/gain_own/pallas_call | solution.py:342
  22.4 0.0 copy-done.4
  22.4 0.0 copy-start.6
  22.4 0.8 %copy-done.6 = f32[2,200,384]{2,1,0:T(8,128)} copy-done((f32[2,200,384]{2,1,0:T(8,128)}, f32[2,200,384]{2,1,0:T(8,128)S(1)}, u32[]{:S(2)}) %copy-start.6) | copy-done | bytes 614424
  23.2 1.7 %collective-permute-start.5 = (f32[8,128]{1,0:T(8,128)S(1)}, f32[8,128]{1,0:T(8,128)S(1)}, u32[]{:S(2)}, u32[]{:S(2)}) collective-permute-start(f32[8,128]{1,0:T(8,128)S(1)} %get-tuple-element.33), channel_id=1, source_target_pairs={{0,2},{2,0},{1,3},{3,1},{4,6},{6,4},{5,7},{7,5},{8,10},{10,8},{9,1... | collective-permute-start | bytes 12296 | tf_op jit(solution)/shard_map/ppermute | solution.py:358
  24.9 4.5 %all-to-all-done = bf16[32,48,384]{2,1,0:T(8,128)(2,1)S(1)} async-done(((bf16[32,48,384]{2,1,0:T(8,128)(2,1)}), bf16[32,48,384]{2,1,0:T(8,128)(2,1)S(1)}, u32[]{:S(2)}, u32[]{:S(2)}) %all-to-all-start) | async-done | bytes 1179680 | tf_op jit(solution)/shard_map/all_to_all | solution.py:315
  29.4 0.0 collective-permute-done.5.row_ref
  29.4 0.8 %library.2.refs_0_ = bf16[2,2,200,384]{3,2,1,0:T(8,128)(2,1)S(1)} custom-call(bf16[8,4,48,384]{3,2,1,0:T(8,128)(2,1)S(1)} %bitcast.10, bf16[1168,256]{1,0:T(8,128)(2,1)S(1)} %copy-done), custom_call_target="tpu_custom_call" | custom-call | flops 314572800 | bytes 3145728 | tf_op jit(solution)/shard_map/library/pallas_call | solution.py:364
  30.3 0.0 copy-start.5
  30.3 3.3 %collective-permute-start.6 = (bf16[2,2,200,384]{3,2,1,0:T(8,128)(2,1)S(1)}, bf16[2,2,200,384]{3,2,1,0:T(8,128)(2,1)S(1)}, u32[]{:S(2)}, u32[]{:S(2)}) collective-permute-start(bf16[2,2,200,384]{3,2,1,0:T(8,128)(2,1)S(1)} %library.2.refs_0_), channel_id=1, source_target_pairs={{0,1},{1,0},{2,3},{3,2},{4,5},{5,4},{6,7},{7,6},{8,9},{9,8},{10,11... | collective-permute-start | bytes 1843208 | tf_op jit(solution)/shard_map/ppermute | solution.py:375
  33.6 0.8 %library.3.refs_1_ = bf16[2,2,200,384]{3,2,1,0:T(8,128)(2,1)S(1)} custom-call(bf16[8,4,48,384]{3,2,1,0:T(8,128)(2,1)S(1)} %bitcast.11, bf16[1168,256]{1,0:T(8,128)(2,1)S(1)} %copy-done), custom_call_target="tpu_custom_call" | custom-call | flops 314572800 | bytes 3145728 | tf_op jit(solution)/shard_map/library/pallas_call | solution.py:364
  34.5 0.1 collective-permute-start.7
  34.6 0.0 collective-permute-done.4
  34.6 0.0 collective-permute-done.3
  34.6 0.3 collective-permute-done.2
  35.0 0.0 copy-start.7
  35.0 0.5 collective-permute-start.8
  35.4 0.0 copy-done.5
  35.4 0.8 %gain_other.1 = (f32[2,200,384]{2,1,0:T(8,128)S(1)}, f32[200,384]{1,0:T(8,128)S(1)}, f32[8,128]{1,0:T(8,128)}) custom-call(f32[8,128]{1,0:T(8,128)S(1)} %collective-permute-done.5.row_ref, f32[8,128]{1,0:T(8,128)S(1)} %select_maximum_fusion.table_ref, f32[2,2,200,384]{3,2,1,0:T(8,128)S(1)} %copy-done.5), custom_call_target="tpu_custom_call" | custom-call | flops 1258291200 | bytes 3145728 | tf_op jit(solution)/shard_map/gain_other/pallas_call | solution.py:342
  36.2 0.5 collective-permute-done.8.theirs_ref
  36.7 0.0 copy-done.7
  36.7 0.5 whiten.1
  37.2 0.0 collective-permute-done.6.refs_2_
  37.2 0.0 collective-permute-done.7.refs_3_
  37.2 3.5 %match_other.1 = bf16[384,384]{1,0:T(8,128)(2,1)S(1)} custom-call(bf16[2,2,200,384]{3,2,1,0:T(8,128)(2,1)S(1)} %library.2.refs_0_, bf16[2,2,200,384]{3,2,1,0:T(8,128)(2,1)S(1)} %library.3.refs_1_, bf16[2,2,200,384]{3,2,1,0:T(8,128)(2,1)S(1)} %collective-permute-done.6.refs_2_, bf16[2,2,200,384]{3,2,1,0:T(8,128)(2,1)S(1)} %collective-permute-done.7.refs_3_, ...), custom_call_target="tpu_custom_call" | custom-call | flops 2516582400 | bytes 6291456 | tf_op jit(solution)/shard_map/match_other/pallas_call | solution.py:395
  40.7 2.0 %collective-permute-start.9 = (bf16[384,384]{1,0:T(8,128)(2,1)S(1)}, bf16[384,384]{1,0:T(8,128)(2,1)S(1)}, u32[]{:S(2)}, u32[]{:S(2)}) collective-permute-start(bf16[384,384]{1,0:T(8,128)(2,1)S(1)} %match_other.1), channel_id=1, source_target_pairs={{0,2},{2,0},{1,3},{3,1},{4,6},{6,4},{5,7},{7,5},{8,10},{10,8},{9,1... | collective-permute-start | bytes 884744 | tf_op jit(solution)/shard_map/ppermute | solution.py:410
  42.7 3.7 %match_own.1 = f32[384,384]{1,0:T(8,128)S(1)} custom-call(bf16[2,2,200,384]{3,2,1,0:T(8,128)(2,1)S(1)} %library.2.refs_0_, bf16[2,2,200,384]{3,2,1,0:T(8,128)(2,1)S(1)} %library.3.refs_1_, bf16[2,2,200,384]{3,2,1,0:T(8,128)(2,1)S(1)} %collective-permute-done.6.refs_2_, bf16[2,2,200,384]{3,2,1,0:T(8,128)(2,1)S(1)} %collective-permute-done.7.refs_3_, ...), custom_call_target="tpu_custom_call" | custom-call | flops 2516582400 | bytes 6291456 | tf_op jit(solution)/shard_map/match_own/pallas_call | solution.py:395
  46.4 4.5 %collective-permute-done.9 = bf16[384,384]{1,0:T(8,128)(2,1)S(1)} collective-permute-done((bf16[384,384]{1,0:T(8,128)(2,1)S(1)}, bf16[384,384]{1,0:T(8,128)(2,1)S(1)}, u32[]{:S(2)}, u32[]{:S(2)}) %collective-permute-start.9) | collective-permute-done | bytes 294944 | tf_op jit(solution)/shard_map/ppermute | solution.py:410
  50.9 0.9 %maximum_bitcast_fusion = f32[1,1,384,384]{3,2,1,0:T(8,128)} fusion(f32[384,384]{1,0:T(8,128)S(1)} %match_own.1, bf16[384,384]{1,0:T(8,128)(2,1)S(1)} %collective-permute-done.9), kind=kLoop, calls=%fused_computation | loop fusion | flops 294912 | bytes 1474560 | tf_op jit(solution)/shard_map/broadcast_in_dim | solution.py:412
  (3 shorter events, 0.1 us)
Async XLA Ops:
  0.0 14.3 %collective-permute-start = (bf16[384,384]{1,0:T(8,128)(2,1)}, bf16[384,384]{1,0:T(8,128)(2,1)S(1)}, u32[]{:S(2)}, u32[]{:S(2)}) collective-permute-start(bf16[384,384]{1,0:T(8,128)(2,1)} %bitcast.12), channel_id=1, source_target_pairs={{0,2},{2,0},{1,3},{3,1},{4,6},{6,4},{5,7},{7,5},{8,10},{10,8},{9,1... | collective-permute-start | bytes 884744 | tf_op jit(solution)/shard_map/ppermute | solution.py:300
  5.4 8.9 %copy-start = (bf16[1168,256]{1,0:T(8,128)(2,1)S(1)}, bf16[1168,256]{1,0:T(8,128)(2,1)}, u32[]{:S(2)}) copy-start(bf16[1168,256]{1,0:T(8,128)(2,1)} %constant.13.clone.tab_ref.refs_0_) | copy-start | bytes 1794052
  5.4 8.9 %copy-start.1 = (bf16[1,1,384,384]{3,2,1,0:T(8,128)(2,1)S(1)}, bf16[1,1,384,384]{3,2,1,0:T(8,128)(2,1)}, u32[]{:S(2)}) copy-start(bf16[1,1,384,384]{3,2,1,0:T(8,128)(2,1)} %param.10) | copy-start | bytes 884740
  5.5 24.0 %all-to-all-start = ((bf16[32,48,384]{2,1,0:T(8,128)(2,1)}), bf16[32,48,384]{2,1,0:T(8,128)(2,1)S(1)}, u32[]{:S(2)}, u32[]{:S(2)}) async-start(bf16[32,48,384]{2,1,0:T(8,128)(2,1)} %copies.1), calls=%async_computation | async-start | bytes 2359296 | tf_op jit(solution)/shard_map/all_to_all | solution.py:315
  14.4 2.3 %copy-start.8 = (f32[64]{0:T(128)S(1)}, f32[64]{0:T(128)}, u32[]{:S(2)}) copy-start(f32[64]{0:T(128)} %param.16) | copy-start | bytes 772
  14.4 2.2 %copy-start.9 = (f32[64]{0:T(128)S(1)}, f32[64]{0:T(128)}, u32[]{:S(2)}) copy-start(f32[64]{0:T(128)} %param.15) | copy-start | bytes 772
  14.4 2.2 %copy-start.10 = (f32[64]{0:T(128)S(1)}, f32[64]{0:T(128)}, u32[]{:S(2)}) copy-start(f32[64]{0:T(128)} %param.14) | copy-start | bytes 772
  14.4 2.2 %copy-start.11 = (f32[64]{0:T(128)S(1)}, f32[64]{0:T(128)}, u32[]{:S(2)}) copy-start(f32[64]{0:T(128)} %param.13) | copy-start | bytes 772
  14.4 7.1 %copy-start.2 = (bf16[1184,256]{1,0:T(8,128)(2,1)S(1)}, bf16[1184,256]{1,0:T(8,128)(2,1)}, u32[]{:S(2)}) copy-start(bf16[1184,256]{1,0:T(8,128)(2,1)} %constant.14.clone.refs_1_.refs_0_.refs_6_) | copy-start | bytes 1818628
  14.4 7.1 %copy-start.3 = (bf16[192,400]{1,0:T(8,128)(2,1)S(1)}, bf16[192,400]{1,0:T(8,128)(2,1)}, u32[]{:S(2)}) copy-start(bf16[192,400]{1,0:T(8,128)(2,1)} %constant.15.clone.refs_2_.refs_1_.refs_7_) | copy-start | bytes 460804
  15.3 7.1 %copy-start.4 = (f32[2,2,200,384]{3,2,1,0:T(8,128)}, f32[2,2,200,384]{3,2,1,0:T(8,128)S(1)}, u32[]{:S(2)}) copy-start(f32[2,2,200,384]{3,2,1,0:T(8,128)S(1)} %get-tuple-element.29.tile_ref) | copy-start | bytes 3686404
  15.3 2.2 %collective-permute-start.1 = (bf16[104,384]{1,0:T(8,128)(2,1)S(1)}, bf16[104,384]{1,0:T(8,128)(2,1)S(1)}, u32[]{:S(2)}, u32[]{:S(2)}) collective-permute-start(bf16[104,384]{1,0:T(8,128)(2,1)S(1)} %get-tuple-element.28), channel_id=1, source_target_pairs={{0,1},{1,0},{2,3},{3,2},{4,5},{5,4},{6,7},{7,6},{8,9},{9,8},{10,11... | collective-permute-start | bytes 239624 | tf_op jit(solution)/shard_map/ppermute | solution.py:333
  17.6 17.0 %collective-permute-start.4 = (bf16[104,384]{1,0:T(8,128)(2,1)S(1)}, bf16[104,384]{1,0:T(8,128)(2,1)S(1)}, u32[]{:S(2)}, u32[]{:S(2)}) collective-permute-start(bf16[104,384]{1,0:T(8,128)(2,1)S(1)} %add_convert_fusion.1), channel_id=1, source_target_pairs={{0,12},{4,0},{8,4},{12,8},{1,13},{5,1},{9,5},{13,9},{2,14},{6,2},{... | collective-permute-start | bytes 239624 | tf_op jit(solution)/shard_map/ppermute | solution.py:335
  20.4 14.2 %collective-permute-start.3 = (bf16[104,384]{1,0:T(8,128)(2,1)S(1)}, bf16[104,384]{1,0:T(8,128)(2,1)S(1)}, u32[]{:S(2)}, u32[]{:S(2)}) collective-permute-start(bf16[104,384]{1,0:T(8,128)(2,1)S(1)} %add_convert_fusion.1), channel_id=1, source_target_pairs={{0,8},{4,12},{8,0},{12,4},{1,9},{5,13},{9,1},{13,5},{2,10},{6,14},... | collective-permute-start | bytes 239624 | tf_op jit(solution)/shard_map/ppermute | solution.py:335
  20.9 14.0 %collective-permute-start.2 = (bf16[104,384]{1,0:T(8,128)(2,1)S(1)}, bf16[104,384]{1,0:T(8,128)(2,1)S(1)}, u32[]{:S(2)}, u32[]{:S(2)}) collective-permute-start(bf16[104,384]{1,0:T(8,128)(2,1)S(1)} %add_convert_fusion.1), channel_id=1, source_target_pairs={{0,4},{4,8},{8,12},{12,0},{1,5},{5,9},{9,13},{13,1},{2,6},{6,10},{... | collective-permute-start | bytes 239624 | tf_op jit(solution)/shard_map/ppermute | solution.py:335
  22.4 0.8 %copy-start.6 = (f32[2,200,384]{2,1,0:T(8,128)}, f32[2,200,384]{2,1,0:T(8,128)S(1)}, u32[]{:S(2)}) copy-start(f32[2,200,384]{2,1,0:T(8,128)S(1)} %get-tuple-element.38.own_ref) | copy-start | bytes 1843204
  23.2 6.2 %collective-permute-start.5 = (f32[8,128]{1,0:T(8,128)S(1)}, f32[8,128]{1,0:T(8,128)S(1)}, u32[]{:S(2)}, u32[]{:S(2)}) collective-permute-start(f32[8,128]{1,0:T(8,128)S(1)} %get-tuple-element.33), channel_id=1, source_target_pairs={{0,2},{2,0},{1,3},{3,1},{4,6},{6,4},{5,7},{7,5},{8,10},{10,8},{9,1... | collective-permute-start | bytes 12296 | tf_op jit(solution)/shard_map/ppermute | solution.py:358
  30.3 5.2 %copy-start.5 = (f32[2,2,200,384]{3,2,1,0:T(8,128)S(1)}, f32[2,2,200,384]{3,2,1,0:T(8,128)}, u32[]{:S(2)}) copy-start(f32[2,2,200,384]{3,2,1,0:T(8,128)} %copy-done.4) | copy-start | bytes 3686404
  30.3 6.9 %collective-permute-start.6 = (bf16[2,2,200,384]{3,2,1,0:T(8,128)(2,1)S(1)}, bf16[2,2,200,384]{3,2,1,0:T(8,128)(2,1)S(1)}, u32[]{:S(2)}, u32[]{:S(2)}) collective-permute-start(bf16[2,2,200,384]{3,2,1,0:T(8,128)(2,1)S(1)} %library.2.refs_0_), channel_id=1, source_target_pairs={{0,1},{1,0},{2,3},{3,2},{4,5},{5,4},{6,7},{7,6},{8,9},{9,8},{10,11... | collective-permute-start | bytes 1843208 | tf_op jit(solution)/shard_map/ppermute | solution.py:375
  34.5 2.8 %collective-permute-start.7 = (bf16[2,2,200,384]{3,2,1,0:T(8,128)(2,1)S(1)}, bf16[2,2,200,384]{3,2,1,0:T(8,128)(2,1)S(1)}, u32[]{:S(2)}, u32[]{:S(2)}) collective-permute-start(bf16[2,2,200,384]{3,2,1,0:T(8,128)(2,1)S(1)} %library.3.refs_1_), channel_id=1, source_target_pairs={{0,1},{1,0},{2,3},{3,2},{4,5},{5,4},{6,7},{7,6},{8,9},{9,8},{10,11... | collective-permute-start | bytes 1843208 | tf_op jit(solution)/shard_map/ppermute | solution.py:375
  35.0 1.7 %copy-start.7 = (f32[2,200,384]{2,1,0:T(8,128)S(1)}, f32[2,200,384]{2,1,0:T(8,128)}, u32[]{:S(2)}) copy-start(f32[2,200,384]{2,1,0:T(8,128)} %copy-done.6) | copy-start | bytes 1843204
  35.0 1.7 %collective-permute-start.8 = (bf16[104,384]{1,0:T(8,128)(2,1)S(1)}, bf16[104,384]{1,0:T(8,128)(2,1)S(1)}, u32[]{:S(2)}, u32[]{:S(2)}) collective-permute-start(bf16[104,384]{1,0:T(8,128)(2,1)S(1)} %add_convert_fusion.mine_ref), channel_id=1, source_target_pairs={{0,1},{1,0},{2,3},{3,2},{4,5},{5,4},{6,7},{7,6},{8,9},{9,8},{10,11... | collective-permute-start | bytes 239624 | tf_op jit(solution)/shard_map/ppermute | solution.py:380
  40.7 10.2 %collective-permute-start.9 = (bf16[384,384]{1,0:T(8,128)(2,1)S(1)}, bf16[384,384]{1,0:T(8,128)(2,1)S(1)}, u32[]{:S(2)}, u32[]{:S(2)}) collective-permute-start(bf16[384,384]{1,0:T(8,128)(2,1)S(1)} %match_other.1), channel_id=1, source_target_pairs={{0,2},{2,0},{1,3},{3,1},{4,6},{6,4},{5,7},{7,5},{8,10},{10,8},{9,1... | collective-permute-start | bytes 884744 | tf_op jit(solution)/shard_map/ppermute | solution.py:410

commit v16 on v14

--- a/solution.py
+++ b/solution.py
@@ -366,7 +366,7 @@
             in_specs=kept * 2,
             out_specs=kept[0],
             compiler_params=params(12),
-            cost_estimate=cost(deep // 2 * work * (1 + 5 * first), 3 << 20),
+            cost_estimate=cost(deep // 2 * work, 3 << 20),
             name="library",
         )(images_all, ahead)
         for first in (0, deep // 2)

time: 52.3 us -> 52.3 us (level)
    all_to_all x1, waiting for transfers between devices: 5.42 us -> 4.51 us  [per_device(): images_all = lax.all_to_all(copies, LIB, 0, 0, tiled=False)]
    ppermute x1, waiting for transfers between devices: 0.01 us -> 0.89 us  [per_device(): lax.ppermute(send, 'core', swap).astype(F32)]
  transfers between devices with their start and end apart: 11 -> 11, of which waited for: 4 -> 5; matrix products, arithmetic and copies ran while one was open for 0% -> 0% of each run, Pallas kernels for 20% -> 20%
where the time goes in v16:
time: 52.3 us; the launch traced here: 52 us
  starting transfers between devices  24.7 us (47%)
  Pallas kernels  13.7 us (26%)
  waiting for transfers between devices  10.9 us (21%)
  other arithmetic  0.95 us (2%)
  between operations  0.89 us (2%)
  local copies, waits for them, and re-layouts  0.88 us (2%)
    all_to_all x1, starting transfers between devices, per_device(): images_all = lax.all_to_all(copies, LIB, 0, 0, tiled=False)  8.22 us
    pallas_call x2, Pallas kernels, match(): pl.pallas_call(functools.partial(match_kernel, t), out_shape=pltpu.VMEM((...  7.22 us
    all_to_all x1, waiting for transfers between devices, per_device(): images_all = lax.all_to_all(copies, LIB, 0, 0, tiled=False)  4.51 us
    ppermute x1, waiting for transfers between devices, per_device(): got = lax.ppermute(match(1, BF16, 'match_other'), 'xhi', swap)  4.26 us
    ppermute x3, starting transfers between devices, per_device(): lax.ppermute(pair, 'z', [(z, (z + dz) % deep) for z in range(deep)])  3.95 us
    ppermute x1, starting transfers between devices, per_device(): received = lax.ppermute(tile, 'xhi', swap)  3.57 us
    ppermute x2, starting transfers between devices, per_device(): far = [lax.ppermute(part, 'core', swap) for part in near]  3.41 us
    ppermute x1, starting transfers between devices, per_device(): got = lax.ppermute(match(1, BF16, 'match_other'), 'xhi', swap)  1.99 us
  transfers between devices with their start and end apart: 11, of which 5 were waited for; matrix products, arithmetic and copies ran while one was open for 0% of the time, Pallas kernels for 20%

profile of v16, /device:TPU:1, one launch (start us, length us, event | category | flops | bytes accessed | tf_op | source)
XLA Modules:
  0.0 52.0 jit_solution(11008678780652698039)
XLA Ops:
  0.0 3.6 %collective-permute-start = (bf16[384,384]{1,0:T(8,128)(2,1)}, bf16[384,384]{1,0:T(8,128)(2,1)S(1)}, u32[]{:S(2)}, u32[]{:S(2)}) collective-permute-start(bf16[384,384]{1,0:T(8,128)(2,1)} %bitcast.12), channel_id=1, source_target_pairs={{0,2},{2,0},{1,3},{3,1},{4,6},{6,4},{5,7},{7,5},{8,10},{10,8},{9,1... | collective-permute-start | bytes 884744 | tf_op jit(solution)/shard_map/ppermute | solution.py:300
  3.6 1.8 %copies.1 = bf16[32,48,384]{2,1,0:T(8,128)(2,1)} custom-call(bf16[48,384]{1,0:T(8,128)(2,1)} %bitcast.14), custom_call_target="tpu_custom_call" | custom-call | bytes 1048576 | tf_op jit(solution)/shard_map/copies/pallas_call | solution.py:301
  5.4 0.0 copy-start
  5.4 0.0 copy-start.1
  5.5 8.2 %all-to-all-start = ((bf16[32,48,384]{2,1,0:T(8,128)(2,1)}), bf16[32,48,384]{2,1,0:T(8,128)(2,1)S(1)}, u32[]{:S(2)}, u32[]{:S(2)}) async-start(bf16[32,48,384]{2,1,0:T(8,128)(2,1)} %copies.1), calls=%async_computation | async-start | bytes 2359296 | tf_op jit(solution)/shard_map/all_to_all | solution.py:315
  14.3 0.0 collective-permute-done.other_ref
  14.4 0.0 copy-done
  14.4 0.0 copy-done.1
  14.4 0.0 copy-start.8
  14.4 0.0 copy-start.9
  14.4 0.0 copy-start.10
  14.4 0.0 copy-start.11
  14.4 0.0 copy-start.2
  14.4 0.0 copy-start.3
  14.4 0.9 %tile.1 = (f32[2,2,200,384]{3,2,1,0:T(8,128)S(1)}, bf16[104,384]{1,0:T(8,128)(2,1)S(1)}, bf16[104,384]{1,0:T(8,128)(2,1)S(1)}) custom-call(s32[1,1]{1,0:T(1,128)} %bitcast.core_ref, bf16[384,384]{1,0:T(8,128)(2,1)S(1)} %bitcast.13, bf16[384,384]{1,0:T(8,128)(2,1)S(1)} %collective-permute-done.other_ref, bf16[1168,256]{1,0:T(8,128)(2,1)S(1)} %copy-done), custom_call_target="tpu_custom_call" | custom-call | flops 31457280000 | bytes 3145728 | tf_op jit(solution)/shard_map/tile/pallas_call | solution.py:317
  15.3 0.0 copy-start.4
  15.3 1.3 %collective-permute-start.1 = (bf16[104,384]{1,0:T(8,128)(2,1)S(1)}, bf16[104,384]{1,0:T(8,128)(2,1)S(1)}, u32[]{:S(2)}, u32[]{:S(2)}) collective-permute-start(bf16[104,384]{1,0:T(8,128)(2,1)S(1)} %get-tuple-element.26), channel_id=1, source_target_pairs={{0,1},{1,0},{2,3},{3,2},{4,5},{5,4},{6,7},{7,6},{8,9},{9,8},{10,11... | collective-permute-start | bytes 239624 | tf_op jit(solution)/shard_map/ppermute | solution.py:333
  16.6 0.0 copy-done.8
  16.6 0.0 copy-done.9
  16.6 0.0 copy-done.10
  16.6 0.0 copy-done.11
  16.7 0.9 %collective-permute-done.1 = bf16[104,384]{1,0:T(8,128)(2,1)S(1)} collective-permute-done((bf16[104,384]{1,0:T(8,128)(2,1)S(1)}, bf16[104,384]{1,0:T(8,128)(2,1)S(1)}, u32[]{:S(2)}, u32[]{:S(2)}) %collective-permute-start.1) | collective-permute-done | bytes 79904 | tf_op jit(solution)/shard_map/ppermute | solution.py:333
  17.6 2.8 %collective-permute-start.4 = (bf16[104,384]{1,0:T(8,128)(2,1)S(1)}, bf16[104,384]{1,0:T(8,128)(2,1)S(1)}, u32[]{:S(2)}, u32[]{:S(2)}) collective-permute-start(bf16[104,384]{1,0:T(8,128)(2,1)S(1)} %add_convert_fusion.1), channel_id=1, source_target_pairs={{0,12},{4,0},{8,4},{12,8},{1,13},{5,1},{9,5},{13,9},{2,14},{6,2},{... | collective-permute-start | bytes 239624 | tf_op jit(solution)/shard_map/ppermute | solution.py:335
  20.4 0.6 %collective-permute-start.3 = (bf16[104,384]{1,0:T(8,128)(2,1)S(1)}, bf16[104,384]{1,0:T(8,128)(2,1)S(1)}, u32[]{:S(2)}, u32[]{:S(2)}) collective-permute-start(bf16[104,384]{1,0:T(8,128)(2,1)S(1)} %add_convert_fusion.1), channel_id=1, source_target_pairs={{0,8},{4,12},{8,0},{12,4},{1,9},{5,13},{9,1},{13,5},{2,10},{6,14},... | collective-permute-start | bytes 239624 | tf_op jit(solution)/shard_map/ppermute | solution.py:335
  20.9 0.6 %collective-permute-start.2 = (bf16[104,384]{1,0:T(8,128)(2,1)S(1)}, bf16[104,384]{1,0:T(8,128)(2,1)S(1)}, u32[]{:S(2)}, u32[]{:S(2)}) collective-permute-start(bf16[104,384]{1,0:T(8,128)(2,1)S(1)} %add_convert_fusion.1), channel_id=1, source_target_pairs={{0,4},{4,8},{8,12},{12,0},{1,5},{5,9},{9,13},{13,1},{2,6},{6,10},{... | collective-permute-start | bytes 239624 | tf_op jit(solution)/shard_map/ppermute | solution.py:335
  21.5 0.0 copy-done.2
  21.5 0.0 copy-done.3
  21.5 0.8 %gain_own.1 = (f32[2,200,384]{2,1,0:T(8,128)S(1)}, f32[200,384]{1,0:T(8,128)S(1)}, f32[8,128]{1,0:T(8,128)S(1)}) custom-call(s32[1,1]{1,0:T(1,128)S(6)} %copy.11.row_ref, f32[8,128]{1,0:T(8,128)S(1)} %select_maximum_fusion.table_ref, f32[2,2,200,384]{3,2,1,0:T(8,128)S(1)} %get-tuple-element.27.tile_ref, bf16[1168,256]{1,0:T(8,128)(2,1)S(1)} %copy-done, ...), custom_call_target="tpu_custom_call" | custom-call | flops 1258291200 | bytes 3145728 | tf_op jit(solution)/shard_map/gain_own/pallas_call | solution.py:342
  22.4 0.0 copy-done.4
  22.4 0.0 copy-start.6
  22.4 0.8 %copy-done.6 = f32[2,200,384]{2,1,0:T(8,128)} copy-done((f32[2,200,384]{2,1,0:T(8,128)}, f32[2,200,384]{2,1,0:T(8,128)S(1)}, u32[]{:S(2)}) %copy-start.6) | copy-done | bytes 614424
  23.2 1.7 %collective-permute-start.5 = (f32[8,128]{1,0:T(8,128)S(1)}, f32[8,128]{1,0:T(8,128)S(1)}, u32[]{:S(2)}, u32[]{:S(2)}) collective-permute-start(f32[8,128]{1,0:T(8,128)S(1)} %get-tuple-element.31), channel_id=1, source_target_pairs={{0,2},{2,0},{1,3},{3,1},{4,6},{6,4},{5,7},{7,5},{8,10},{10,8},{9,1... | collective-permute-start | bytes 12296 | tf_op jit(solution)/shard_map/ppermute | solution.py:358
  24.9 4.5 %all-to-all-done = bf16[32,48,384]{2,1,0:T(8,128)(2,1)S(1)} async-done(((bf16[32,48,384]{2,1,0:T(8,128)(2,1)}), bf16[32,48,384]{2,1,0:T(8,128)(2,1)S(1)}, u32[]{:S(2)}, u32[]{:S(2)}) %all-to-all-start) | async-done | bytes 1179680 | tf_op jit(solution)/shard_map/all_to_all | solution.py:315
  29.4 0.8 %library.3.refs_1_ = bf16[2,2,200,384]{3,2,1,0:T(8,128)(2,1)S(1)} custom-call(bf16[8,4,48,384]{3,2,1,0:T(8,128)(2,1)S(1)} %bitcast.10, bf16[1168,256]{1,0:T(8,128)(2,1)S(1)} %copy-done), custom_call_target="tpu_custom_call" | custom-call | flops 314572800 | bytes 3145728 | tf_op jit(solution)/shard_map/library/pallas_call | solution.py:363
  30.3 0.0 copy-start.5
  30.3 0.8 %library.2.refs_0_ = bf16[2,2,200,384]{3,2,1,0:T(8,128)(2,1)S(1)} custom-call(bf16[8,4,48,384]{3,2,1,0:T(8,128)(2,1)S(1)} %bitcast.11, bf16[1168,256]{1,0:T(8,128)(2,1)S(1)} %copy-done), custom_call_target="tpu_custom_call" | custom-call | flops 314572800 | bytes 3145728 | tf_op jit(solution)/shard_map/library/pallas_call | solution.py:363
  31.1 3.3 %collective-permute-start.6 = (bf16[2,2,200,384]{3,2,1,0:T(8,128)(2,1)S(1)}, bf16[2,2,200,384]{3,2,1,0:T(8,128)(2,1)S(1)}, u32[]{:S(2)}, u32[]{:S(2)}) collective-permute-start(bf16[2,2,200,384]{3,2,1,0:T(8,128)(2,1)S(1)} %library.2.refs_0_), channel_id=1, source_target_pairs={{0,1},{1,0},{2,3},{3,2},{4,5},{5,4},{6,7},{7,6},{8,9},{9,8},{10,11... | collective-permute-start | bytes 1843208 | tf_op jit(solution)/shard_map/ppermute | solution.py:374
  34.5 0.0 collective-permute-done.5.row_ref
  34.5 0.1 collective-permute-start.7
  34.6 0.0 collective-permute-done.4
  34.6 0.0 collective-permute-done.3
  34.6 0.3 collective-permute-done.2
  35.0 0.0 copy-start.7
  35.0 0.5 collective-permute-start.8
  35.4 0.0 copy-done.5
  35.4 0.8 %gain_other.1 = (f32[2,200,384]{2,1,0:T(8,128)S(1)}, f32[200,384]{1,0:T(8,128)S(1)}, f32[8,128]{1,0:T(8,128)}) custom-call(f32[8,128]{1,0:T(8,128)S(1)} %collective-permute-done.5.row_ref, f32[8,128]{1,0:T(8,128)S(1)} %select_maximum_fusion.table_ref, f32[2,2,200,384]{3,2,1,0:T(8,128)S(1)} %copy-done.5), custom_call_target="tpu_custom_call" | custom-call | flops 1258291200 | bytes 3145728 | tf_op jit(solution)/shard_map/gain_other/pallas_call | solution.py:342
  36.2 0.9 %collective-permute-done.8.theirs_ref = bf16[104,384]{1,0:T(8,128)(2,1)S(1)} collective-permute-done((bf16[104,384]{1,0:T(8,128)(2,1)S(1)}, bf16[104,384]{1,0:T(8,128)(2,1)S(1)}, u32[]{:S(2)}, u32[]{:S(2)}) %collective-permute-start.8) | collective-permute-done | bytes 79904 | tf_op jit(solution)/shard_map/ppermute | solution.py:379
  37.1 0.0 copy-done.7
  37.1 0.5 whiten.1
  37.6 0.0 collective-permute-done.6.refs_2_
  37.6 0.0 collective-permute-done.7.refs_3_
  37.6 3.5 %match_other.1 = bf16[384,384]{1,0:T(8,128)(2,1)S(1)} custom-call(bf16[2,2,200,384]{3,2,1,0:T(8,128)(2,1)S(1)} %library.2.refs_0_, bf16[2,2,200,384]{3,2,1,0:T(8,128)(2,1)S(1)} %library.3.refs_1_, bf16[2,2,200,384]{3,2,1,0:T(8,128)(2,1)S(1)} %collective-permute-done.6.refs_2_, bf16[2,2,200,384]{3,2,1,0:T(8,128)(2,1)S(1)} %collective-permute-done.7.refs_3_, ...), custom_call_target="tpu_custom_call" | custom-call | flops 2516582400 | bytes 6291456 | tf_op jit(solution)/shard_map/match_other/pallas_call | solution.py:394
  41.1 2.0 %collective-permute-start.9 = (bf16[384,384]{1,0:T(8,128)(2,1)S(1)}, bf16[384,384]{1,0:T(8,128)(2,1)S(1)}, u32[]{:S(2)}, u32[]{:S(2)}) collective-permute-start(bf16[384,384]{1,0:T(8,128)(2,1)S(1)} %match_other.1), channel_id=1, source_target_pairs={{0,2},{2,0},{1,3},{3,1},{4,6},{6,4},{5,7},{7,5},{8,10},{10,8},{9,1... | collective-permute-start | bytes 884744 | tf_op jit(solution)/shard_map/ppermute | solution.py:409
  43.1 3.7 %match_own.1 = f32[384,384]{1,0:T(8,128)S(1)} custom-call(bf16[2,2,200,384]{3,2,1,0:T(8,128)(2,1)S(1)} %library.2.refs_0_, bf16[2,2,200,384]{3,2,1,0:T(8,128)(2,1)S(1)} %library.3.refs_1_, bf16[2,2,200,384]{3,2,1,0:T(8,128)(2,1)S(1)} %collective-permute-done.6.refs_2_, bf16[2,2,200,384]{3,2,1,0:T(8,128)(2,1)S(1)} %collective-permute-done.7.refs_3_, ...), custom_call_target="tpu_custom_call" | custom-call | flops 2516582400 | bytes 6291456 | tf_op jit(solution)/shard_map/match_own/pallas_call | solution.py:394
  46.9 4.3 %collective-permute-done.9 = bf16[384,384]{1,0:T(8,128)(2,1)S(1)} collective-permute-done((bf16[384,384]{1,0:T(8,128)(2,1)S(1)}, bf16[384,384]{1,0:T(8,128)(2,1)S(1)}, u32[]{:S(2)}, u32[]{:S(2)}) %collective-permute-start.9) | collective-permute-done | bytes 294944 | tf_op jit(solution)/shard_map/ppermute | solution.py:409
  51.1 0.9 %maximum_bitcast_fusion = f32[1,1,384,384]{3,2,1,0:T(8,128)} fusion(f32[384,384]{1,0:T(8,128)S(1)} %match_own.1, bf16[384,384]{1,0:T(8,128)(2,1)S(1)} %collective-permute-done.9), kind=kLoop, calls=%fused_computation | loop fusion | flops 294912 | bytes 1474560 | tf_op jit(solution)/shard_map/broadcast_in_dim | solution.py:411
  (3 shorter events, 0.1 us)
Async XLA Ops:
  0.0 14.3 %collective-permute-start = (bf16[384,384]{1,0:T(8,128)(2,1)}, bf16[384,384]{1,0:T(8,128)(2,1)S(1)}, u32[]{:S(2)}, u32[]{:S(2)}) collective-permute-start(bf16[384,384]{1,0:T(8,128)(2,1)} %bitcast.12), channel_id=1, source_target_pairs={{0,2},{2,0},{1,3},{3,1},{4,6},{6,4},{5,7},{7,5},{8,10},{10,8},{9,1... | collective-permute-start | bytes 884744 | tf_op jit(solution)/shard_map/ppermute | solution.py:300
  5.4 8.9 %copy-start = (bf16[1168,256]{1,0:T(8,128)(2,1)S(1)}, bf16[1168,256]{1,0:T(8,128)(2,1)}, u32[]{:S(2)}) copy-start(bf16[1168,256]{1,0:T(8,128)(2,1)} %constant.13.clone.tab_ref.refs_0_) | copy-start | bytes 1794052
  5.4 8.9 %copy-start.1 = (bf16[1,1,384,384]{3,2,1,0:T(8,128)(2,1)S(1)}, bf16[1,1,384,384]{3,2,1,0:T(8,128)(2,1)}, u32[]{:S(2)}) copy-start(bf16[1,1,384,384]{3,2,1,0:T(8,128)(2,1)} %param.10) | copy-start | bytes 884740
  5.5 24.0 %all-to-all-start = ((bf16[32,48,384]{2,1,0:T(8,128)(2,1)}), bf16[32,48,384]{2,1,0:T(8,128)(2,1)S(1)}, u32[]{:S(2)}, u32[]{:S(2)}) async-start(bf16[32,48,384]{2,1,0:T(8,128)(2,1)} %copies.1), calls=%async_computation | async-start | bytes 2359296 | tf_op jit(solution)/shard_map/all_to_all | solution.py:315
  14.4 2.3 %copy-start.8 = (f32[64]{0:T(128)S(1)}, f32[64]{0:T(128)}, u32[]{:S(2)}) copy-start(f32[64]{0:T(128)} %param.16) | copy-start | bytes 772
  14.4 2.2 %copy-start.9 = (f32[64]{0:T(128)S(1)}, f32[64]{0:T(128)}, u32[]{:S(2)}) copy-start(f32[64]{0:T(128)} %param.15) | copy-start | bytes 772
  14.4 2.2 %copy-start.10 = (f32[64]{0:T(128)S(1)}, f32[64]{0:T(128)}, u32[]{:S(2)}) copy-start(f32[64]{0:T(128)} %param.14) | copy-start | bytes 772
  14.4 2.2 %copy-start.11 = (f32[64]{0:T(128)S(1)}, f32[64]{0:T(128)}, u32[]{:S(2)}) copy-start(f32[64]{0:T(128)} %param.13) | copy-start | bytes 772
  14.4 7.1 %copy-start.2 = (bf16[1184,256]{1,0:T(8,128)(2,1)S(1)}, bf16[1184,256]{1,0:T(8,128)(2,1)}, u32[]{:S(2)}) copy-start(bf16[1184,256]{1,0:T(8,128)(2,1)} %constant.14.clone.refs_1_.refs_0_.refs_6_) | copy-start | bytes 1818628
  14.4 7.1 %copy-start.3 = (bf16[192,400]{1,0:T(8,128)(2,1)S(1)}, bf16[192,400]{1,0:T(8,128)(2,1)}, u32[]{:S(2)}) copy-start(bf16[192,400]{1,0:T(8,128)(2,1)} %constant.15.clone.refs_2_.refs_1_.refs_7_) | copy-start | bytes 460804
  15.3 7.1 %copy-start.4 = (f32[2,2,200,384]{3,2,1,0:T(8,128)}, f32[2,2,200,384]{3,2,1,0:T(8,128)S(1)}, u32[]{:S(2)}) copy-start(f32[2,2,200,384]{3,2,1,0:T(8,128)S(1)} %get-tuple-element.27.tile_ref) | copy-start | bytes 3686404
  15.3 2.2 %collective-permute-start.1 = (bf16[104,384]{1,0:T(8,128)(2,1)S(1)}, bf16[104,384]{1,0:T(8,128)(2,1)S(1)}, u32[]{:S(2)}, u32[]{:S(2)}) collective-permute-start(bf16[104,384]{1,0:T(8,128)(2,1)S(1)} %get-tuple-element.26), channel_id=1, source_target_pairs={{0,1},{1,0},{2,3},{3,2},{4,5},{5,4},{6,7},{7,6},{8,9},{9,8},{10,11... | collective-permute-start | bytes 239624 | tf_op jit(solution)/shard_map/ppermute | solution.py:333
  17.6 17.0 %collective-permute-start.4 = (bf16[104,384]{1,0:T(8,128)(2,1)S(1)}, bf16[104,384]{1,0:T(8,128)(2,1)S(1)}, u32[]{:S(2)}, u32[]{:S(2)}) collective-permute-start(bf16[104,384]{1,0:T(8,128)(2,1)S(1)} %add_convert_fusion.1), channel_id=1, source_target_pairs={{0,12},{4,0},{8,4},{12,8},{1,13},{5,1},{9,5},{13,9},{2,14},{6,2},{... | collective-permute-start | bytes 239624 | tf_op jit(solution)/shard_map/ppermute | solution.py:335
  20.4 14.2 %collective-permute-start.3 = (bf16[104,384]{1,0:T(8,128)(2,1)S(1)}, bf16[104,384]{1,0:T(8,128)(2,1)S(1)}, u32[]{:S(2)}, u32[]{:S(2)}) collective-permute-start(bf16[104,384]{1,0:T(8,128)(2,1)S(1)} %add_convert_fusion.1), channel_id=1, source_target_pairs={{0,8},{4,12},{8,0},{12,4},{1,9},{5,13},{9,1},{13,5},{2,10},{6,14},... | collective-permute-start | bytes 239624 | tf_op jit(solution)/shard_map/ppermute | solution.py:335
  20.9 14.0 %collective-permute-start.2 = (bf16[104,384]{1,0:T(8,128)(2,1)S(1)}, bf16[104,384]{1,0:T(8,128)(2,1)S(1)}, u32[]{:S(2)}, u32[]{:S(2)}) collective-permute-start(bf16[104,384]{1,0:T(8,128)(2,1)S(1)} %add_convert_fusion.1), channel_id=1, source_target_pairs={{0,4},{4,8},{8,12},{12,0},{1,5},{5,9},{9,13},{13,1},{2,6},{6,10},{... | collective-permute-start | bytes 239624 | tf_op jit(solution)/shard_map/ppermute | solution.py:335
  22.4 0.8 %copy-start.6 = (f32[2,200,384]{2,1,0:T(8,128)}, f32[2,200,384]{2,1,0:T(8,128)S(1)}, u32[]{:S(2)}) copy-start(f32[2,200,384]{2,1,0:T(8,128)S(1)} %get-tuple-element.34.own_ref) | copy-start | bytes 1843204
  23.2 11.3 %collective-permute-start.5 = (f32[8,128]{1,0:T(8,128)S(1)}, f32[8,128]{1,0:T(8,128)S(1)}, u32[]{:S(2)}, u32[]{:S(2)}) collective-permute-start(f32[8,128]{1,0:T(8,128)S(1)} %get-tuple-element.31), channel_id=1, source_target_pairs={{0,2},{2,0},{1,3},{3,1},{4,6},{6,4},{5,7},{7,5},{8,10},{10,8},{9,1... | collective-permute-start | bytes 12296 | tf_op jit(solution)/shard_map/ppermute | solution.py:358
  30.3 5.2 %copy-start.5 = (f32[2,2,200,384]{3,2,1,0:T(8,128)S(1)}, f32[2,2,200,384]{3,2,1,0:T(8,128)}, u32[]{:S(2)}) copy-start(f32[2,2,200,384]{3,2,1,0:T(8,128)} %copy-done.4) | copy-start | bytes 3686404
  31.1 6.5 %collective-permute-start.6 = (bf16[2,2,200,384]{3,2,1,0:T(8,128)(2,1)S(1)}, bf16[2,2,200,384]{3,2,1,0:T(8,128)(2,1)S(1)}, u32[]{:S(2)}, u32[]{:S(2)}) collective-permute-start(bf16[2,2,200,384]{3,2,1,0:T(8,128)(2,1)S(1)} %library.2.refs_0_), channel_id=1, source_target_pairs={{0,1},{1,0},{2,3},{3,2},{4,5},{5,4},{6,7},{7,6},{8,9},{9,8},{10,11... | collective-permute-start | bytes 1843208 | tf_op jit(solution)/shard_map/ppermute | solution.py:374
  34.5 3.2 %collective-permute-start.7 = (bf16[2,2,200,384]{3,2,1,0:T(8,128)(2,1)S(1)}, bf16[2,2,200,384]{3,2,1,0:T(8,128)(2,1)S(1)}, u32[]{:S(2)}, u32[]{:S(2)}) collective-permute-start(bf16[2,2,200,384]{3,2,1,0:T(8,128)(2,1)S(1)} %library.3.refs_1_), channel_id=1, source_target_pairs={{0,1},{1,0},{2,3},{3,2},{4,5},{5,4},{6,7},{7,6},{8,9},{9,8},{10,11... | collective-permute-start | bytes 1843208 | tf_op jit(solution)/shard_map/ppermute | solution.py:374
  35.0 2.2 %copy-start.7 = (f32[2,200,384]{2,1,0:T(8,128)S(1)}, f32[2,200,384]{2,1,0:T(8,128)}, u32[]{:S(2)}) copy-start(f32[2,200,384]{2,1,0:T(8,128)} %copy-done.6) | copy-start | bytes 1843204
  35.0 2.1 %collective-permute-start.8 = (bf16[104,384]{1,0:T(8,128)(2,1)S(1)}, bf16[104,384]{1,0:T(8,128)(2,1)S(1)}, u32[]{:S(2)}, u32[]{:S(2)}) collective-permute-start(bf16[104,384]{1,0:T(8,128)(2,1)S(1)} %add_convert_fusion.mine_ref), channel_id=1, source_target_pairs={{0,1},{1,0},{2,3},{3,2},{4,5},{5,4},{6,7},{7,6},{8,9},{9,8},{10,11... | collective-permute-start | bytes 239624 | tf_op jit(solution)/shard_map/ppermute | solution.py:379
  41.1 10.0 %collective-permute-start.9 = (bf16[384,384]{1,0:T(8,128)(2,1)S(1)}, bf16[384,384]{1,0:T(8,128)(2,1)S(1)}, u32[]{:S(2)}, u32[]{:S(2)}) collective-permute-start(bf16[384,384]{1,0:T(8,128)(2,1)S(1)} %match_other.1), channel_id=1, source_target_pairs={{0,2},{2,0},{1,3},{3,1},{4,6},{6,4},{5,7},{7,5},{8,10},{10,8},{9,1... | collective-permute-start | bytes 884744 | tf_op jit(solution)/shard_map/ppermute | solution.py:409
